TPU v7x, 32 devices: a whole 2x2x4 slice. The times are simulated.
32 devices in a mesh: dp: 2 (over y), mp: 4 (over x, core), tensor: 4 (over z).
Axes of the slice: x: 2, y: 2, z: 4, core: 2. Of those that a mesh axis runs over, the one named last changes fastest.
Arguments:
- tokens: bfloat16 [4096, 2048], P(('dp', 'mp', 'tensor')), may hold values from -6 to 6
- norm_gain: float32 [2048], replicated, may hold values from 0.1 to 1.9
- w_proj: bfloat16 [4, 2048, 2048], P(None, 'mp', 'tensor'), may hold values from -0.125 to 0.125
- w_beta: bfloat16 [2048, 16], P('mp', 'tensor'), may hold values from -0.125 to 0.125
- conv_weight: float32 [3, 4, 4, 4, 128], P(None, None, 'tensor', 'mp'), may hold values from -3 to 3
- out_gain: float32 [128], replicated, may hold values from 0.1 to 1.9
- w_out: bfloat16 [2048, 2048], P('tensor', 'mp'), may hold values from -0.25 to 0.25
- mlp_gain: float32 [2048], replicated, may hold values from 0.1 to 1.9
- w_in: bfloat16 [2, 2048, 5632], P(None, 'mp', 'tensor'), may hold values from -0.125 to 0.125
- w_down: bfloat16 [5632, 2048], P('tensor', 'mp'), may hold values from -0.078125 to 0.078125
- cotangent: bfloat16 [4096, 2048], P(('dp', 'mp', 'tensor')), may hold values from -6 to 6
- starts: int32 [2, 8], P('dp'), may hold values from 0 to 2047, as said below
- lengths: int32 [2], P('dp'), may hold values from 1024 to 2048
Outputs:
- output: bfloat16 [4096, 2048], P(('dp', 'mp', 'tensor'))
- d_tokens: float32 [4096, 2048], P(('dp', 'mp', 'tensor'))
- g_norm_gain: float32 [2048], replicated
- g_proj: float32 [4, 2048, 2048], P(None, 'mp', 'tensor')
- g_beta: float32 [2048, 16], P('mp', 'tensor')
- g_conv: float32 [3, 4, 4, 4, 128], P(None, None, 'tensor', 'mp')
- g_out_gain: float32 [128], replicated
- g_out: float32 [2048, 2048], P('tensor', 'mp')
- g_mlp_gain: float32 [2048], replicated
- g_in: float32 [2, 2048, 5632], P(None, 'mp', 'tensor')
- g_down: float32 [5632, 2048], P('tensor', 'mp')
- state_norm: float32 [], replicated
Inputs may be any that keep to these rules, and one draw needn't show every extreme that they name: `starts`: row s rises strictly from 0 and lists where the 8 documents of sequence s begin.
All inputs are finite; a program needn't handle non-finite values.
Results may differ from a plain program's by a relative error of at most 0.014.
Values may be sent and summed in bfloat16 or wider, within the bound.
No kernel may reach another device: no remote copies, remote signals or barrier semaphores. Data moves between devices by JAX's collectives and lax.ppermute only.
A program may use at most 256 MiB of HBM per device.

v0:
```python
import jax
import jax.numpy as jnp
from jax import lax
from jax.sharding import PartitionSpec as P

HEADS = 16
BLOCK = 64


def shortened(value):

    def short(part):
        return part.astype(jnp.bfloat16) if part.dtype == jnp.float32 else part

    return jax.tree.map(short, value)


def rms_rows(values, epsilon):
    return values * lax.rsqrt(jnp.mean(values * values, axis=-1, keepdims=True) + epsilon)


def scaled_norm(values, gain_row):
    return rms_rows(values, 1e-05) * gain_row


def short_conv(values, taps, doc_ids):
    taps_count = taps.shape[0]
    summed = values * taps[taps_count - 1]
    for offset in range(1, taps_count):
        shifted = jnp.concatenate(
            [jnp.zeros((offset, values.shape[1]), jnp.float32), values[:-offset]], axis=0
        )
        prior_doc = jnp.concatenate([jnp.full((offset,), -1, jnp.int32), doc_ids[:-offset]])
        summed = (
            summed
            + jnp.where((prior_doc == doc_ids)[:, None], shifted, 0.0)
            * taps[taps_count - 1 - offset]
        )
    return summed


def block_delta(query, key_vec, value, beta, doc_ids):
    highest = lax.Precision.HIGHEST
    seq_len = query.shape[0]
    width = BLOCK
    count = seq_len // width
    q_blocks = query.reshape(count, width, -1)
    k_blocks = key_vec.reshape(count, width, -1)
    v_blocks = value.reshape(count, width, -1)
    b_blocks = beta.reshape(count, width)
    d_blocks = doc_ids.reshape(count, width)
    prior_doc = jnp.concatenate([jnp.full((1,), -1, jnp.int32), doc_ids[width - 1 : -1 : width]])
    keep_rows = (d_blocks == prior_doc[:, None]).astype(jnp.float32)
    same_doc = d_blocks[:, :, None] == d_blocks[:, None, :]
    row_ids = lax.broadcasted_iota(jnp.int32, (width, width), 0)
    col_ids = lax.broadcasted_iota(jnp.int32, (width, width), 1)
    strict_mask = same_doc & (row_ids > col_ids)[None]
    upto_mask = same_doc & (row_ids >= col_ids)[None]
    gram_mat = jnp.einsum("mik,mjk->mij", k_blocks, k_blocks, precision=highest)
    neg_mat = jnp.where(strict_mask, -b_blocks[:, :, None] * gram_mat, 0.0)
    inverse = jnp.eye(width, dtype=jnp.float32)[None] + neg_mat
    power_mat = neg_mat
    for rounds in range(width.bit_length() - 2):
        power_mat = jnp.einsum("mij,mjk->mik", power_mat, power_mat, precision=highest)
        inverse = inverse + jnp.einsum("mij,mjk->mik", inverse, power_mat, precision=highest)
    w_mat = jnp.einsum(
        "mij,mjk->mik", inverse, (b_blocks * keep_rows)[:, :, None] * k_blocks, precision=highest
    )
    u_mat = jnp.einsum("mij,mjk->mik", inverse, b_blocks[:, :, None] * v_blocks, precision=highest)
    scores = jnp.where(
        upto_mask, jnp.einsum("mik,mjk->mij", q_blocks, k_blocks, precision=highest), 0.0
    )
    last_doc = (d_blocks == d_blocks[:, -1:]).astype(jnp.float32)

    def advance(state, pieces):
        w_part, u_part, q_part, s_part, k_part, keep_part, last_part = pieces
        pseudo = u_part - jnp.dot(w_part, state, precision=highest)
        result = keep_part[:, None] * jnp.dot(q_part, state, precision=highest) + jnp.dot(
            s_part, pseudo, precision=highest
        )
        new_state = keep_part[-1] * state + jnp.dot(
            (k_part * last_part[:, None]).T, pseudo, precision=highest
        )
        return (new_state, (result, jnp.sqrt(jnp.sum(new_state * new_state) + 1e-12)))

    start_state = jnp.zeros((k_blocks.shape[2], v_blocks.shape[2]), jnp.float32)
    final_state, (results, norm_list) = lax.scan(
        jax.checkpoint(advance),
        start_state,
        (w_mat, u_mat, q_blocks, scores, k_blocks, keep_rows, last_doc),
    )
    return (results.reshape(seq_len, -1), jnp.sum(norm_list))


def head_piece(pieces, beta_logit, conv_flat, gain_row, doc_ids, valid):
    seq_len = pieces.shape[1]
    head_count = beta_logit.shape[1]
    conv_q = short_conv(pieces[0], conv_flat[0], doc_ids)
    conv_k = short_conv(pieces[1], conv_flat[1], doc_ids)
    conv_v = short_conv(pieces[2], conv_flat[2], doc_ids)
    query = jax.nn.silu(conv_q).reshape(seq_len, head_count, -1)
    query = query * lax.rsqrt(jnp.sum(query * query, axis=-1, keepdims=True) + 1e-06)
    key_rows = jax.nn.silu(conv_k).reshape(seq_len, head_count, -1)
    key_rows = key_rows * lax.rsqrt(jnp.sum(key_rows * key_rows, axis=-1, keepdims=True) + 1e-06)
    values = jax.nn.silu(conv_v).reshape(seq_len, head_count, -1)
    beta_rows = jax.nn.sigmoid(beta_logit) * valid[:, None]
    mixed_out, norm_sums = jax.vmap(block_delta, in_axes=(1, 1, 1, 1, None), out_axes=(1, 0))(
        query, key_rows, values, beta_rows, doc_ids
    )
    gate_rows = pieces[3].reshape(seq_len, head_count, -1)
    mixed = rms_rows(mixed_out, 1e-05) * gain_row * jax.nn.silu(gate_rows) * valid[:, None, None]
    return (mixed.reshape(seq_len, -1), jnp.sum(norm_sums))


def spread(values):
    return lax.all_gather(values, "tensor", axis=0, tiled=True)


def collect(values):
    return lax.psum_scatter(values, "tensor", scatter_dimension=0, tiled=True)


def shards(
    tokens,
    norm_gain,
    w_proj,
    w_beta,
    conv_weight,
    out_gain,
    w_out,
    mlp_gain,
    w_in,
    w_down,
    cotangent,
    starts,
    lengths,
):
    f32 = jnp.float32
    bf16 = jnp.bfloat16
    full_proj, full_beta, full_out, full_in, full_down = (
        lax.all_gather(w_proj, "mp", axis=1, tiled=True),
        lax.all_gather(w_beta, "mp", axis=0, tiled=True),
        lax.all_gather(w_out, "mp", axis=1, tiled=True),
        lax.all_gather(w_in, "mp", axis=1, tiled=True),
        lax.all_gather(w_down, "mp", axis=1, tiled=True),
    )
    inputs = tokens.astype(f32)
    normed_local, first_back = jax.vjp(scaled_norm, inputs, norm_gain)
    normed = spread(normed_local.astype(bf16))
    projected = jnp.einsum("nd,sdc->snc", normed, full_proj, preferred_element_type=f32).astype(
        bf16
    )
    beta_logit = jnp.dot(normed, full_beta, preferred_element_type=f32).astype(bf16)[None]
    heads_proj, heads_beta = (
        lax.all_to_all(projected, "mp", split_axis=2, concat_axis=1, tiled=True),
        lax.all_to_all(beta_logit, "mp", split_axis=2, concat_axis=1, tiled=True),
    )
    seq_count = starts.shape[0]
    seq_len = heads_proj.shape[1] // seq_count
    channels = heads_proj.shape[2]
    places = lax.broadcasted_iota(jnp.int32, (seq_count, seq_len), 1)
    doc_ids = jnp.sum((starts[:, :, None] <= places[:, None, :]).astype(jnp.int32), axis=1) - 1
    valid = (places < lengths[:, None]).astype(f32)
    conv_flat = conv_weight.reshape(3, conv_weight.shape[1], channels)
    head_inputs = heads_proj.astype(f32).reshape(4, seq_count, seq_len, channels)
    beta_inputs = heads_beta.astype(f32)

    def mixer(piece_in, beta_in, conv_in, gain_in):
        mixed_seq, norm_seq = jax.vmap(head_piece, in_axes=(1, 0, None, None, 0, 0))(
            piece_in, beta_in, conv_in, gain_in, doc_ids, valid
        )
        return (mixed_seq, jnp.sum(norm_seq))

    mixed_heads, mixer_back, norm_total = jax.vjp(
        mixer, head_inputs, beta_inputs, conv_flat, out_gain, has_aux=True
    )
    mixed_low = mixed_heads.astype(bf16).reshape(1, seq_count * seq_len, channels)
    mixed_tok = lax.all_to_all(
        shortened(mixed_low), "mp", split_axis=1, concat_axis=2, tiled=True
    ).astype(mixed_low.dtype)[0]
    branch = collect(jnp.dot(mixed_tok, full_out, preferred_element_type=f32))
    middle = inputs + branch
    normed_local_two, second_back = jax.vjp(scaled_norm, middle, mlp_gain)
    normed_two = spread(normed_local_two.astype(bf16))
    gate_up = jnp.einsum("nd,sdf->snf", normed_two, full_in, preferred_element_type=f32)
    gate_val = gate_up[0]
    up_val = gate_up[1]
    activated = jax.nn.silu(gate_val)
    hidden = (activated * up_val).astype(bf16)
    feed_out = collect(jnp.dot(hidden, full_down, preferred_element_type=f32))
    output = (middle + feed_out).astype(bf16)
    grad_rows_all = spread(cotangent)
    g_down = jnp.einsum("nf,nd->fd", hidden, grad_rows_all, preferred_element_type=f32)
    d_hidden = jnp.einsum("nd,fd->nf", grad_rows_all, full_down, preferred_element_type=f32)
    sigma = jax.nn.sigmoid(gate_val)
    d_gate = (d_hidden * up_val * sigma * (1.0 + gate_val * (1.0 - sigma))).astype(bf16)
    d_up = (d_hidden * activated).astype(bf16)
    d_gate_up = jnp.stack([d_gate, d_up])
    g_in = jnp.einsum("nd,snf->sdf", normed_two, d_gate_up, preferred_element_type=f32)
    d_normed_two = collect(
        jnp.einsum("snf,sdf->nd", d_gate_up, full_in, preferred_element_type=f32)
    )
    d_mid_norm, g_mlp_gain = second_back(d_normed_two)
    d_middle = cotangent.astype(f32) + d_mid_norm
    d_middle_all = spread(d_middle.astype(bf16))
    g_out = jnp.einsum("nc,nd->cd", mixed_tok, d_middle_all, preferred_element_type=f32)
    d_mixed = jnp.einsum("nd,cd->nc", d_middle_all, full_out, preferred_element_type=f32).astype(
        bf16
    )[None]
    d_mixed_heads = lax.all_to_all(d_mixed, "mp", split_axis=2, concat_axis=1, tiled=True)
    d_pieces, d_betas, g_conv_flat, g_out_gain = mixer_back(
        d_mixed_heads.astype(f32).reshape(seq_count, seq_len, channels)
    )
    d_proj_heads = d_pieces.reshape(4, seq_count * seq_len, channels).astype(bf16)
    d_beta_heads = d_betas.reshape(1, seq_count * seq_len, d_betas.shape[2]).astype(bf16)
    d_proj_tok, d_beta_tok = (
        lax.all_to_all(
            shortened(d_proj_heads), "mp", split_axis=1, concat_axis=2, tiled=True
        ).astype(d_proj_heads.dtype),
        lax.all_to_all(
            shortened(d_beta_heads), "mp", split_axis=1, concat_axis=2, tiled=True
        ).astype(d_beta_heads.dtype),
    )
    g_proj = jnp.einsum("nd,snc->sdc", normed, d_proj_tok, preferred_element_type=f32)
    g_beta = jnp.einsum("nd,nh->dh", normed, d_beta_tok[0], preferred_element_type=f32)
    d_normed_part = jnp.einsum("snc,sdc->nd", d_proj_tok, full_proj, preferred_element_type=f32)
    d_normed_part = d_normed_part + jnp.einsum(
        "nh,dh->nd", d_beta_tok[0], full_beta, preferred_element_type=f32
    )
    d_normed = collect(d_normed_part)
    d_in_norm, g_norm_gain = first_back(d_normed)
    d_tokens = d_middle + d_in_norm
    g_conv = g_conv_flat.reshape(conv_weight.shape)
    rows_proj, rows_beta, rows_out, rows_in, rows_down = (
        lax.psum_scatter(g_proj, "mp", scatter_dimension=1, tiled=True),
        lax.psum_scatter(g_beta, "mp", scatter_dimension=0, tiled=True),
        lax.psum_scatter(g_out, "mp", scatter_dimension=1, tiled=True),
        lax.psum_scatter(g_in, "mp", scatter_dimension=1, tiled=True),
        lax.psum_scatter(g_down, "mp", scatter_dimension=1, tiled=True),
    )
    sum_proj, sum_beta, sum_out, sum_in, sum_down, sum_conv = lax.psum(
        (rows_proj, rows_beta, rows_out, rows_in, rows_down, g_conv), "dp"
    )
    gain_one, gain_two, gain_head, norm_all = lax.psum(
        (g_norm_gain, g_mlp_gain, g_out_gain, norm_total), ("dp", "mp", "tensor")
    )
    state_norm = norm_all / (HEADS * seq_count * lax.axis_size("dp") * (seq_len // BLOCK))
    return (
        output,
        d_tokens,
        gain_one,
        sum_proj,
        sum_beta,
        sum_conv,
        gain_head,
        sum_out,
        gain_two,
        sum_in,
        sum_down,
        state_norm,
    )


def solution(mesh):
    placed = (
        P(("dp", "mp", "tensor"), None),
        P(),
        P(None, "mp", "tensor"),
        P("mp", "tensor"),
        P(None, None, "tensor", "mp", None),
        P(),
        P("tensor", "mp"),
        P(),
        P(None, "mp", "tensor"),
        P("tensor", "mp"),
        P(("dp", "mp", "tensor"), None),
        P("dp", None),
        P("dp"),
    )
    return jax.shard_map(
        shards,
        mesh=mesh,
        in_specs=placed,
        out_specs=(
            P(("dp", "mp", "tensor"), None),
            P(("dp", "mp", "tensor"), None),
            P(),
            P(None, "mp", "tensor"),
            P("mp", "tensor"),
            P(None, None, "tensor", "mp", None),
            P(),
            P("tensor", "mp"),
            P(),
            P(None, "mp", "tensor"),
            P("tensor", "mp"),
            P(),
        ),
        check_vma=False,
    )
```

profile of v0, /device:TPU:0, one launch (start us, length us, event | category | flops | bytes accessed | tf_op | source)
XLA Modules:
  0.0 2314.6 jit_solution(12100505633663045501)
XLA Ops:
  12.6 6.2 all_gather.29
  19.5 39.6 %all-gather.9.cloned.1.call-done = bf16[512,2048]{1,0:T(8,128)(2,1)} async-done(((bf16[128,2048]{1,0:T(8,128)(2,1)}), bf16[512,2048]{1,0:T(8,128)(2,1)}) %all-gather.9.cloned.1.call-update) | async-done | bytes 2097168 | tf_op jit(solution)/shard_map/all_gather | solution.py:116
  63.1 3.3 all-to-all-start.1
  66.4 51.3 %all-gather.11.cloned.1.call-done = bf16[4,2048,512]{2,1,0:T(8,128)(2,1)} async-done(((bf16[4,512,512]{2,1,0:T(8,128)(2,1)}), bf16[4,2048,512]{2,1,0:T(8,128)(2,1)}) %all-gather.11.cloned.1.call-update) | async-done | bytes 8388624 | tf_op jit(solution)/shard_map/all_gather | solution.py:141
  117.7 8.5 convert_bitcast_fusion.1
  126.3 3.1 copy.403
  129.3 3.7 all-to-all-start
  134.8 28.1 %all-to-all-done = bf16[4,512,512]{1,0,2:T(4,128)(2,1)S(1)} async-done(((bf16[4,512,512]{1,0,2:T(4,128)(2,1)}), bf16[4,512,512]{1,0,2:T(4,128)(2,1)S(1)}, u32[]{:S(2)}, u32[]{:S(2)}) %all-to-all-start) | async-done | bytes 2097184 | tf_op jit(solution)/shard_map/all_to_all | solution.py:155
  165.8 5.2 copy.406
  171.1 4.1 fusion.237
  185.7 4.0 multiply_reduce_fusion.17
  212.3 3.9 multiply_reduce_fusion.16
  217.2 3.1 convolution_bitcast_fusion.31
  220.4 3.6 convolution_bitcast_fusion.30
  227.9 4.1 fusion.79
  235.7 250.8 %while.42 = (s32[]{:T(128)}, f32[1,1,128,128]{3,2,1,0:T(8,128)S(1)}, f32[32,1,1,64,128]{4,3,2,1,0:T(8,128)}, f32[32,1,1]{0,2,1:T(1,128)S(1)}, f32[32,1,1,128,128...) while((s32[]{:T(128)}, ...), condition=%wide.region_6.7_spmd.clone, body=%wide.region_4.6_spmd.clone.sunk | while | flops 44204032 | bytes 758749 | solution.py:87
  492.7 8.9 copy.593
  501.6 13.4 reduce.46
  516.9 13.0 all_to_all.75
  529.9 3.5 reshape.2087
  537.5 5.1 fusion.245
  543.2 76.3 %reduce-scatter.12.cloned.1.call-done = f32[128,2048]{1,0:T(8,128)} async-done(((f32[512,2048]{1,0:T(8,128)}), f32[128,2048]{1,0:T(8,128)}) %reduce-scatter.12.cloned.1.call-update) | async-done | bytes 1048592 | tf_op jit(solution)/shard_map/reduce_scatter | solution.py:120
  624.6 73.0 %all-gather.17.cloned.1.call-done = bf16[2,2048,1408]{2,1,0:T(8,128)(2,1)} async-done(((bf16[2,512,1408]{2,1,0:T(8,128)(2,1)}), bf16[2,2048,1408]{2,1,0:T(8,128)(2,1)}) %all-gather.17.cloned.1.call-update) | async-done | bytes 11534352 | tf_op jit(solution)/shard_map/all_gather | solution.py:144
  697.6 47.7 %all-gather.15.cloned.1.call-done = bf16[512,2048]{1,0:T(8,128)(2,1)} async-done(((bf16[128,2048]{1,0:T(8,128)(2,1)}), bf16[512,2048]{1,0:T(8,128)(2,1)}) %all-gather.15.cloned.1.call-update) | async-done | bytes 2097168 | tf_op jit(solution)/shard_map/all_gather | solution.py:116
  745.3 12.9 convolution_bitcast_fusion.10
  758.2 33.2 %all-gather.21.cloned.1.call-done = bf16[512,2048]{1,0:T(8,128)(2,1)} async-done(((bf16[128,2048]{1,0:T(8,128)(2,1)}), bf16[512,2048]{1,0:T(8,128)(2,1)}) %all-gather.21.cloned.1.call-update) | async-done | bytes 2097168 | tf_op jit(solution)/shard_map/all_gather | solution.py:116
  791.4 43.8 %all-gather.19.cloned.1.call-done = bf16[1408,2048]{1,0:T(8,128)(2,1)} async-done(((bf16[1408,512]{1,0:T(8,128)(2,1)}), bf16[1408,2048]{1,0:T(8,128)(2,1)}) %all-gather.19.cloned.1.call-update) | async-done | bytes 5767184 | tf_op jit(solution)/shard_map/all_gather | solution.py:145
  835.1 10.4 fusion.76
  847.1 10.3 convolution_bitcast_fusion.11
  857.5 76.9 %reduce-scatter.16.cloned.1.call-done = f32[128,2048]{1,0:T(8,128)} async-done(((f32[512,2048]{1,0:T(8,128)}), f32[128,2048]{1,0:T(8,128)}) %reduce-scatter.16.cloned.1.call-update) | async-done | bytes 1048592 | tf_op jit(solution)/shard_map/reduce_scatter | solution.py:120
  939.7 46.3 %all-gather.23.cloned.1.call-done = bf16[512,2048]{1,0:T(8,128)(2,1)} async-done(((bf16[128,2048]{1,0:T(8,128)(2,1)}), bf16[512,2048]{1,0:T(8,128)(2,1)}) %all-gather.23.cloned.1.call-update) | async-done | bytes 2097168 | tf_op jit(solution)/shard_map/all_gather | solution.py:116
  986.0 5.0 fusion.249
  991.3 10.5 fusion.250
  1003.7 4.3 fusion.100
  1008.0 3.6 copy.433
  1011.7 5.6 reduce.47
  1019.5 4.1 all-to-all-start.3
  1023.7 13.0 convolution_bitcast_fusion.8
  1038.4 3.5 reshape.2089
  1046.9 3.8 fusion.139
  1057.8 486.7 %while.43 = (s32[]{:T(128)}, f32[1,1,128,128]{2,3,1,0:T(8,128)S(1)}, f32[32,1,1,64,128]{4,3,2,1,0:T(8,128)}, f32[32,1,1,64,128]{4,3,2,1,0:T(8,128)}, f32[32,1,1,...) while((s32[]{:T(128)}, ...), condition=%wide.region_15.16_spmd.clone, body=%wide.region_14.15_spmd.clone.sunk | while | flops 100794368 | bytes 1952515 | solution.py:87
  1544.6 3.5 fusion.134
  1593.4 5.7 multiply_reduce_fusion.4
  1604.6 9.9 copy.469
  1614.6 28.1 %all_to_all.76 = bf16[4,2048,128]{2,0,1:T(4,128)(2,1)S(1)} all-to-all(bf16[4,2048,128]{2,0,1:T(4,128)(2,1)S(1)} %copy.469), channel_id=1, replica_groups=mesh['dp'=2,'mp'=4,'tensor'=4] {'mp'}, dimensions={1} | all-to-all | bytes 4194304 | tf_op jit(solution)/shard_map/all_to_all | solution.py:217
  1642.7 2.9 copy.592
  1645.7 4.2 all_to_all.65
  1649.9 9.7 convolution_bitcast_fusion.9
  1661.5 15.9 reduce.48
  1677.4 6.3 all_to_all.77
  1685.0 15.3 bitcast_reduce_fusion.1
  1702.1 7.9 fusion.248
  1714.1 7.8 fusion.246
  1722.1 60.2 %reduce-scatter.20.cloned.1.call-done = f32[4,512,512]{1,2,0:T(8,128)} async-done(((f32[4,2048,512]{1,2,0:T(8,128)}), f32[4,512,512]{1,2,0:T(8,128)}) %reduce-scatter.20.cloned.1.call-update) | async-done | bytes 4194320 | tf_op jit(solution)/shard_map/reduce_scatter | solution.py:235
  1783.6 26.4 %reduce-scatter.28.cloned.1.call-done = f32[512,4]{1,0:T(8,128)} async-done(((f32[2048,4]{1,0:T(8,128)}), f32[512,4]{1,0:T(8,128)}) %reduce-scatter.28.cloned.1.call-update) | async-done | bytes 8208
  1811.1 8.7 all-reduce.40
  1819.8 69.8 %reduce-scatter.18.cloned.1.call-done = f32[128,2048]{1,0:T(8,128)} async-done(((f32[512,2048]{1,0:T(8,128)}), f32[128,2048]{1,0:T(8,128)}) %reduce-scatter.18.cloned.1.call-update) | async-done | bytes 1048592 | tf_op jit(solution)/shard_map/reduce_scatter | solution.py:120
  1891.2 44.1 %all-reduce.39 = (f32[2048]{0:T(1024)}, f32[128]{0:T(128)}, f32[2048]{0:T(1024)}, f32[]{:T(128)}) all-reduce(f32[2048]{0:T(1024)S(1)} %get-tuple-element.794, f32[128]{0:T(128)S(1)} %copy-done.141, f32[2048]{0:T(1024)S(1)} %copy-done.98, f32[]{:T(128)} %reduce_sum.323), channel_id=1, replica_groups=mesh['dp'=2,'mp'=4,'tensor'=4] {'dp','mp','tensor'}, use_global_device_ids=true, to_apply=%region_24.25 | all-reduce | flops 4225 | bytes 33800 | tf_op jit(solution)/shard_map/psum | solution.py:244
  1936.0 34.7 %reduce-scatter.14.cloned.1.call-done = f32[128,2048]{1,0:T(8,128)} async-done(((f32[512,2048]{1,0:T(8,128)}), f32[128,2048]{1,0:T(8,128)}) %reduce-scatter.14.cloned.1.call-update) | async-done | bytes 1048592 | tf_op jit(solution)/shard_map/reduce_scatter | solution.py:120
  1970.7 3.2 fusion.115
  1973.9 316.1 %all-reduce.44.cloned.1.call-done = (f32[4,512,512]{1,2,0:T(8,128)}, f32[512,512]{1,0:T(8,128)}, f32[2,512,1408]{1,2,0:T(8,128)}, f32[1408,512]{1,0:T(8,128)}) async-done(((f32[4,512,512]{1,2,0:T(8,128)}, f32[512,512]{1,0:T(8,128)}, f32[2,512,1408]{1,2,0:T(8,128)}, f32[1408,512]{1,0:T(8,128)}), (f32[4,512,512]{1,2,0:T(8,128)}, f32[512,512]{1,0:T(8,128)}, f32[2,512,1408]{1,2,0:T(8,128)}, ...) | async-done | bytes 13893648 | tf_op jit(solution)/shard_map/psum | solution.py:241
  2290.0 5.2 copy.475
  2295.2 6.3 copy.477
  2302.5 3.7 copy.646
  (1292 shorter events, 875.2 us)
Async XLA Ops:
  7.2 51.9 %all-gather.9.cloned.1.call-start = ((), (), s32[]{:S(2)}) async-start(), calls=%async_computation.15 | async-start | bytes 2621440 | tf_op jit(solution)/shard_map/all_gather | solution.py:116
  8.5 52.9 %copy-start.142 = (f32[128]{0:T(128)}, f32[128]{0:T(128)S(1)}, u32[]{:S(2)}) copy-start(f32[128]{0:T(128)S(1)} %fusion.116) | copy-start | bytes 1540
  8.5 52.8 %copy-start.110 = (f32[128]{0:T(128)}, f32[128]{0:T(128)S(1)}, u32[]{:S(2)}) copy-start(f32[128]{0:T(128)S(1)} %fusion.222) | copy-start | bytes 1540
  10.6 107.2 %all-gather.11.cloned.1.call-start = ((), (), s32[]{:S(2)}) async-start(), calls=%async_computation.16 | async-start | bytes 10485760 | tf_op jit(solution)/shard_map/all_gather | solution.py:141
  11.3 526.2 %all-gather.13.cloned.1.call-start = ((), (), s32[]{:S(2)}) async-start(), calls=%async_computation.17 | async-start | bytes 2621440 | tf_op jit(solution)/shard_map/all_gather | solution.py:143
  12.2 121.5 %copy-start.66 = (s32[2048]{0:T(1024)}, s32[2048]{0:T(1024)S(1)}, u32[]{:S(2)}) copy-start(s32[2048]{0:T(1024)S(1)} %broadcast_add_fusion) | copy-start | bytes 24580
  12.4 215.5 %copy-start.77 = (pred[64,64]{0,1:T(8,128)(4,1)}, pred[64,64]{0,1:T(8,128)(4,1)S(1)}, u32[]{:S(2)}) copy-start(pred[64,64]{0,1:T(8,128)(4,1)S(1)} %iota_compare_fusion.1) | copy-start | bytes 12292
  18.8 107.4 %copy-start.74 = (bf16[2048,4]{0,1:T(4,128)(2,1)}, bf16[2048,4]{0,1:T(4,128)(2,1)S(1)}, u32[]{:S(2)}) copy-start(bf16[2048,4]{0,1:T(4,128)(2,1)S(1)} %all_gather.29) | copy-start | bytes 49156
  63.1 66.2 %all-to-all-start.1 = ((bf16[4,2,256]{2,1,0:T(2,128)(2,1)}), bf16[4,2,256]{2,1,0:T(2,128)(2,1)S(1)}, u32[]{:S(2)}, u32[]{:S(2)}) async-start(bf16[4,2,256]{2,1,0:T(2,128)(2,1)} %reshape.2084), calls=%async_computation.1 | async-start | bytes 8192 | tf_op jit(solution)/shard_map/all_to_all | solution.py:156
  129.3 33.5 %all-to-all-start = ((bf16[4,512,512]{1,0,2:T(4,128)(2,1)}), bf16[4,512,512]{1,0,2:T(4,128)(2,1)S(1)}, u32[]{:S(2)}, u32[]{:S(2)}) async-start(bf16[4,512,512]{1,0,2:T(4,128)(2,1)} %copy.403), calls=%async_computation | async-start | bytes 4194304 | tf_op jit(solution)/shard_map/all_to_all | solution.py:155
  133.1 486.4 %reduce-scatter.12.cloned.1.call-start = ((), (), s32[]{:S(2)}) async-start(), calls=%async_computation.18 | async-start | bytes 5242880 | tf_op jit(solution)/shard_map/reduce_scatter | solution.py:120
  133.2 357.5 %copy-start.82 = (f32[2048]{0:T(1024)}, f32[2048]{0:T(1024)S(1)}, u32[]{:S(2)}) copy-start(f32[2048]{0:T(1024)S(1)} %fusion.217) | copy-start | bytes 24580
  133.4 63.4 %copy-start.68 = (f32[64,64]{0,1:T(8,128)}, f32[64,64]{0,1:T(8,128)S(1)}, u32[]{:S(2)}) copy-start(f32[64,64]{0,1:T(8,128)S(1)} %fusion.210) | copy-start | bytes 49156
  133.6 868.9 %copy-start.92 = (pred[2048]{0:T(1024)(128)(4,1)}, pred[2048]{0:T(1024)(128)(4,1)S(1)}, u32[]{:S(2)}) copy-start(pred[2048]{0:T(1024)(128)(4,1)S(1)} %get-tuple-element.808) | copy-start | bytes 6148
  133.6 869.5 %copy-start.94 = (pred[2048]{0:T(1024)(128)(4,1)}, pred[2048]{0:T(1024)(128)(4,1)S(1)}, u32[]{:S(2)}) copy-start(pred[2048]{0:T(1024)(128)(4,1)S(1)} %get-tuple-element.809) | copy-start | bytes 6148
  133.6 52.0 %copy-start.116 = (f32[128]{0:T(128)}, f32[128]{0:T(128)S(1)}, u32[]{:S(2)}) copy-start(f32[128]{0:T(128)S(1)} %get-tuple-element.946) | copy-start | bytes 1540
  133.6 52.0 %copy-start.120 = (f32[128]{0:T(128)}, f32[128]{0:T(128)S(1)}, u32[]{:S(2)}) copy-start(f32[128]{0:T(128)S(1)} %get-tuple-element.943) | copy-start | bytes 1540
  133.6 52.0 %copy-start.126 = (f32[128]{0:T(128)}, f32[128]{0:T(128)S(1)}, u32[]{:S(2)}) copy-start(f32[128]{0:T(128)S(1)} %get-tuple-element.944) | copy-start | bytes 1540
  133.6 52.0 %copy-start.134 = (f32[128]{0:T(128)}, f32[128]{0:T(128)S(1)}, u32[]{:S(2)}) copy-start(f32[128]{0:T(128)S(1)} %get-tuple-element.945) | copy-start | bytes 1540
  133.6 78.5 %copy-start.114 = (f32[128]{0:T(128)}, f32[128]{0:T(128)S(1)}, u32[]{:S(2)}) copy-start(f32[128]{0:T(128)S(1)} %get-tuple-element.937) | copy-start | bytes 1540
  133.7 78.5 %copy-start.118 = (f32[128]{0:T(128)}, f32[128]{0:T(128)S(1)}, u32[]{:S(2)}) copy-start(f32[128]{0:T(128)S(1)} %get-tuple-element.939) | copy-start | bytes 1540
  133.7 78.5 %copy-start.122 = (f32[128]{0:T(128)}, f32[128]{0:T(128)S(1)}, u32[]{:S(2)}) copy-start(f32[128]{0:T(128)S(1)} %get-tuple-element.947) | copy-start | bytes 1540
  133.7 78.5 %copy-start.124 = (f32[128]{0:T(128)}, f32[128]{0:T(128)S(1)}, u32[]{:S(2)}) copy-start(f32[128]{0:T(128)S(1)} %get-tuple-element.940) | copy-start | bytes 1540
  133.7 78.5 %copy-start.128 = (f32[128]{0:T(128)}, f32[128]{0:T(128)S(1)}, u32[]{:S(2)}) copy-start(f32[128]{0:T(128)S(1)} %get-tuple-element.948) | copy-start | bytes 1540
  133.7 78.5 %copy-start.130 = (f32[128]{0:T(128)}, f32[128]{0:T(128)S(1)}, u32[]{:S(2)}) copy-start(f32[128]{0:T(128)S(1)} %get-tuple-element.938) | copy-start | bytes 1540
  133.7 78.5 %copy-start.132 = (f32[128]{0:T(128)}, f32[128]{0:T(128)S(1)}, u32[]{:S(2)}) copy-start(f32[128]{0:T(128)S(1)} %get-tuple-element.941) | copy-start | bytes 1540
  133.7 78.5 %copy-start.136 = (f32[128]{0:T(128)}, f32[128]{0:T(128)S(1)}, u32[]{:S(2)}) copy-start(f32[128]{0:T(128)S(1)} %get-tuple-element.942) | copy-start | bytes 1540
  133.8 868.0 %copy-start.96 = (pred[2048]{0:T(1024)(128)(4,1)}, pred[2048]{0:T(1024)(128)(4,1)S(1)}, u32[]{:S(2)}) copy-start(pred[2048]{0:T(1024)(128)(4,1)S(1)} %add_compare_fusion.1) | copy-start | bytes 6148
  134.8 85.6 %copy-start.72 = (f32[32,64]{1,0:T(8,128)}, f32[32,64]{1,0:T(8,128)S(1)}, u32[]{:S(2)}) copy-start(f32[32,64]{1,0:T(8,128)S(1)} %get-tuple-element.892) | copy-start | bytes 24580
  176.7 9.0 copy-start.44
  216.2 9.0 copy-start.90
  225.3 9.3 copy-start.86
  225.3 9.2 copy-start.70
  235.7 255.0 %copy-start.107 = (f32[128]{0:T(128)S(1)}, f32[128]{0:T(128)}, u32[]{:S(2)}) copy-start(f32[128]{0:T(128)} %param.22) | copy-start | bytes 1540
  490.7 24.2 %copy-start.80 = (f32[2048]{0:T(1024)}, f32[2048]{0:T(1024)S(1)}, u32[]{:S(2)}) copy-start(f32[2048]{0:T(1024)S(1)} %rsqrt.72) | copy-start | bytes 24580
  542.6 79.5 %copy-start.76 = (f32[2048]{0:T(1024)S(1)}, f32[2048]{0:T(1024)}, u32[]{:S(2)}) copy-start(f32[2048]{0:T(1024)} %param.24) | copy-start | bytes 24580
  542.6 155.0 %all-gather.17.cloned.1.call-start = ((), (), s32[]{:S(2)}) async-start(), calls=%async_computation.20 | async-start | bytes 14417920 | tf_op jit(solution)/shard_map/all_gather | solution.py:144
  543.2 202.1 %all-gather.15.cloned.1.call-start = ((), (), s32[]{:S(2)}) async-start(), calls=%async_computation.19 | async-start | bytes 2621440 | tf_op jit(solution)/shard_map/all_gather | solution.py:116
  621.1 315.7 %copy-start.105 = (f32[128]{0:T(128)}, f32[128]{0:T(128)S(1)}, u32[]{:S(2)}) copy-start(f32[128]{0:T(128)S(1)} %fusion.223) | copy-start | bytes 1540
  623.1 168.3 %all-gather.21.cloned.1.call-start = ((), (), s32[]{:S(2)}) async-start(), calls=%async_computation.23 | async-start | bytes 2621440 | tf_op jit(solution)/shard_map/all_gather | solution.py:116
  623.9 211.3 %all-gather.19.cloned.1.call-start = ((), (), s32[]{:S(2)}) async-start(), calls=%async_computation.21 | async-start | bytes 7208960 | tf_op jit(solution)/shard_map/all_gather | solution.py:145
  624.6 309.8 %reduce-scatter.16.cloned.1.call-start = ((), (), s32[]{:S(2)}) async-start(), calls=%async_computation.24 | async-start | bytes 5242880 | tf_op jit(solution)/shard_map/reduce_scatter | solution.py:120
  857.5 128.5 %all-gather.23.cloned.1.call-start = ((), (), s32[]{:S(2)}) async-start(), calls=%async_computation.25 | async-start | bytes 2621440 | tf_op jit(solution)/shard_map/all_gather | solution.py:116
  936.8 54.2 %copy-start.139 = (f32[128]{0:T(128)}, f32[128]{0:T(128)S(1)}, u32[]{:S(2)}) copy-start(f32[128]{0:T(128)S(1)} %multiply_multiply_fusion.5) | copy-start | bytes 1540
  939.7 782.3 %reduce-scatter.22.cloned.1.call-start = ((), (), s32[]{:S(2)}) async-start(), calls=%async_computation.28 | async-start | bytes 5242880 | tf_op jit(solution)/shard_map/reduce_scatter | solution.py:237
  991.1 730.9 %reduce-scatter.26.cloned.1.call-start = ((), (), s32[]{:S(2)}) async-start(), calls=%async_computation.30 | async-start | bytes 14417920 | tf_op jit(solution)/shard_map/reduce_scatter | solution.py:239
  1019.5 19.0 all-to-all-start.3
  1023.6 698.4 %reduce-scatter.24.cloned.1.call-start = ((), (), s32[]{:S(2)}) async-start(), calls=%async_computation.29 | async-start | bytes 28835840 | tf_op jit(solution)/shard_map/reduce_scatter | solution.py:238
  1036.6 745.7 %reduce-scatter.20.cloned.1.call-start = ((), (), s32[]{:S(2)}) async-start(), calls=%async_computation.27 | async-start | bytes 20971520 | tf_op jit(solution)/shard_map/reduce_scatter | solution.py:235
  1659.6 150.4 %reduce-scatter.28.cloned.1.call-start = ((), (), s32[]{:S(2)}) async-start(), calls=%async_computation.31 | async-start | bytes 1310720
  1702.0 187.6 %reduce-scatter.18.cloned.1.call-start = ((), (), s32[]{:S(2)}) async-start(), calls=%async_computation.26 | async-start | bytes 5242880 | tf_op jit(solution)/shard_map/reduce_scatter | solution.py:120
  1712.8 257.9 %reduce-scatter.14.cloned.1.call-start = ((), (), s32[]{:S(2)}) async-start(), calls=%async_computation.22 | async-start | bytes 5242880 | tf_op jit(solution)/shard_map/reduce_scatter | solution.py:120
  1721.9 568.0 %all-reduce.44.cloned.1.call-start = ((), (), s32[]{:S(2)}) async-start(), calls=%async_computation.32 | async-start | bytes 27787264 | tf_op jit(solution)/shard_map/psum | solution.py:241
  1782.3 107.3 %copy-start.21 = (bf16[128,2048]{1,0:T(8,128)(2,1)S(1)}, bf16[128,2048]{1,0:T(8,128)(2,1)}, u32[]{:S(2)}) copy-start(bf16[128,2048]{1,0:T(8,128)(2,1)} %param.17) | copy-start | bytes 1572868
  1782.3 107.3 %copy-start.79 = (f32[2048]{0:T(1024)S(1)}, f32[2048]{0:T(1024)}, u32[]{:S(2)}) copy-start(f32[2048]{0:T(1024)} %param.18) | copy-start | bytes 24580
  1782.3 107.3 %copy-start.111 = (f32[128]{0:T(128)S(1)}, f32[128]{0:T(128)}, u32[]{:S(2)}) copy-start(f32[128]{0:T(128)} %copy-done.110) | copy-start | bytes 1540
  1782.3 108.9 %copy-start.98 = (f32[2048]{0:T(1024)S(1)}, f32[2048]{0:T(1024)}, u32[]{:S(2)}) copy-start(f32[2048]{0:T(1024)} %get-tuple-element.790) | copy-start | bytes 24580
  1782.3 108.9 %copy-start.141 = (f32[128]{0:T(128)S(1)}, f32[128]{0:T(128)}, u32[]{:S(2)}) copy-start(f32[128]{0:T(128)} %get-tuple-element.792) | copy-start | bytes 1540
  1782.3 153.6 %copy-start.143 = (f32[128]{0:T(128)S(1)}, f32[128]{0:T(128)}, u32[]{:S(2)}) copy-start(f32[128]{0:T(128)} %copy-done.142) | copy-start | bytes 1540
  1782.3 188.4 %copy-start.10 = (f32[128,2048]{1,0:T(8,128)S(1)}, f32[128,2048]{1,0:T(8,128)}, u32[]{:S(2)}) copy-start(f32[128,2048]{1,0:T(8,128)} %copy-done.9) | copy-start | bytes 3145732
  1782.3 188.4 %copy-start.39 = (f32[128,2048]{1,0:T(8,128)S(1)}, f32[128,2048]{1,0:T(8,128)}, u32[]{:S(2)}) copy-start(f32[128,2048]{1,0:T(8,128)} %reduce-scatter.16.cloned.1.call-done) | copy-start | bytes 3145732
  1782.4 188.4 %copy-start.61 = (bf16[128,2048]{1,0:T(8,128)(2,1)S(1)}, bf16[128,2048]{1,0:T(8,128)(2,1)}, u32[]{:S(2)}) copy-start(bf16[128,2048]{1,0:T(8,128)(2,1)} %param.27) | copy-start | bytes 1572868
  1782.4 188.3 %copy-start.106 = (f32[128]{0:T(128)S(1)}, f32[128]{0:T(128)}, u32[]{:S(2)}) copy-start(f32[128]{0:T(128)} %copy-done.105) | copy-start | bytes 1540
  1782.4 188.3 %copy-start.140 = (f32[128]{0:T(128)S(1)}, f32[128]{0:T(128)}, u32[]{:S(2)}) copy-start(f32[128]{0:T(128)} %copy-done.139) | copy-start | bytes 1540
  (107 other events, 344.4 us)
Sparse Core Ops, SparseCore 0:
  10.7 48.3 all-gather.8
  60.6 57.0 all-gather.10
  119.3 26.7 all-gather.12
  542.7 76.7 reduce-scatter.11
  621.0 76.6 all-gather.16
  699.6 45.6 all-gather.14
  746.9 44.4 all-gather.20
  792.9 42.1 all-gather.18
  857.6 76.7 reduce-scatter.15
  939.8 46.1 all-gather.22
  991.2 48.8 reduce-scatter.21
  1042.5 90.7 reduce-scatter.25
  1135.9 162.9 reduce-scatter.23
  1659.7 122.5 reduce-scatter.19
  1785.2 24.7 reduce-scatter.27
  1812.8 76.7 reduce-scatter.17
  1892.3 78.3 reduce-scatter.13
  1973.2 316.7 all-reduce.43
where the time goes:
time: 2350 us; the launch traced here: 2310 us
  waiting for transfers between devices  1030 us (44%)
  matrix products  651 us (28%)
  local copies, waits for them, and re-layouts  363 us (15%)
  other arithmetic  109 us (5%)
  blocking collectives  107 us (5%)
  loops' own time  24.5 us (1%)
    psum x1, waiting for transfers between devices, shards(): lax.psum((rows_proj, rows_beta, rows_out, rows_in, rows_down, g_conv), 'dp')  316 us
    reduce_scatter x4, waiting for transfers between devices, collect(): return lax.psum_scatter(values, 'tensor', scatter_dimension=0, tiled=True)  258 us
    all_gather x4, waiting for transfers between devices, spread(): return lax.all_gather(values, 'tensor', axis=0, tiled=True)  167 us
    squeeze x192, local copies, waits for them, and re-layouts, block_delta(): lax.scan(jax.checkpoint(advance), start_state, (w_mat, u_mat, q_blocks, s...  166 us
    dot_general x96, matrix products, advance(): jnp.dot((k_part * last_part[:, None]).T, pseudo, precision=highest)  153 us
    dot_general x96, matrix products, advance(): jnp.dot(q_part, state, precision=highest)  134 us
    dot_general x96, matrix products, advance(): jnp.dot(s_part, pseudo, precision=highest)  102 us
    dot_general x128, matrix products, advance(): pseudo = u_part - jnp.dot(w_part, state, precision=highest)  73.5 us
  transfers between devices with their start and end apart: 21, of which 16 were waited for; matrix products, arithmetic and copies ran while one was open for 46% of the time, Pallas kernels for 0%

commit v1 on v0

v1 whole, which is shorter than its diff:
```python
import jax
import jax.numpy as jnp
from jax import lax
from jax.experimental import pallas as pl
from jax.experimental.pallas import tpu as pltpu
from jax.sharding import PartitionSpec as P

HEADS = 16


def shortened(value):

    def short(part):
        return part.astype(jnp.bfloat16) if part.dtype == jnp.float32 else part

    return jax.tree.map(short, value)


def rms_rows(values, epsilon):
    return values * lax.rsqrt(jnp.mean(values * values, axis=-1, keepdims=True) + epsilon)


def scaled_norm(values, gain_row):
    return rms_rows(values, 1e-05) * gain_row


BLOCK = 64
PAIR = 2 * BLOCK
LANES = 128
f32 = jnp.float32
bf16 = jnp.bfloat16


def halves(a):
    hi = a.astype(bf16)
    return hi, (a - hi.astype(f32)).astype(bf16)


def product(a, b, dims):
    return lax.dot_general(a, b, (dims, ((), ())), preferred_element_type=f32)


def close_dot(a, b, dims=((1,), (0,))):
    a_hi, a_lo = a if isinstance(a, tuple) else halves(a)
    b_hi, b_lo = b if isinstance(b, tuple) else halves(b)
    return product(a_hi, b_hi, dims) + (product(a_hi, b_lo, dims) + product(a_lo, b_hi, dims))


NN = ((1,), (0,))
NT = ((1,), (1,))
TN = ((0,), (0,))


def doc_start(places, starts_ref):
    found = jnp.zeros_like(places)
    for j in range(1, starts_ref.shape[0]):
        begin = starts_ref[j]
        found = jnp.where(places >= begin, begin, found)
    return found


def place_rows(base, rows, width=LANES):
    return base + lax.broadcasted_iota(jnp.int32, (rows, width), 0)


def pair_masks(base, begins):
    rows = lax.broadcasted_iota(jnp.int32, (PAIR, PAIR), 0)
    cols = lax.broadcasted_iota(jnp.int32, (PAIR, PAIR), 1)
    heads = (rows // BLOCK) * BLOCK
    lower = jnp.maximum(begins - base, heads)
    upto = (cols >= lower) & (cols <= rows)
    strict = (cols >= lower) & (cols < rows)
    keep = begins < base + heads
    return upto, strict, keep, (rows == cols).astype(f32)


def forward_body(starts_ref, length_ref, x_ref, before_ref, logit_ref, taps_ref, gain_ref,
                 mixed_ref, norm_ref, conv_ref, wu_ref, t_ref, a_ref, c_ref, m_ref, s_ref, o_ref,
                 state_ref, square_ref):
    step = pl.program_id(0)
    rows = x_ref.shape[1]
    base = step * rows

    @pl.when(step == 0)
    def _():
        state_ref[...] = jnp.zeros_like(state_ref)

    places = place_rows(base, rows)
    begins = doc_start(places, starts_ref)
    since = places - begins
    valid = (places < length_ref[0]).astype(f32)
    parts = []
    for p in range(3):
        now = x_ref[p].astype(f32)
        tall = jnp.concatenate([before_ref[p].astype(f32), now], axis=0)
        lead = tall.shape[0] - rows
        summed = now * taps_ref[p, 3:4, :]
        for j in range(1, 4):
            moved = pltpu.roll(tall, j, 0)[lead:]
            summed = summed + jnp.where(since >= j, moved, 0.0) * taps_ref[p, 3 - j:4 - j, :]
        conv_ref[p] = summed
        act = summed * jax.nn.sigmoid(summed)
        if p < 2:
            act = act * lax.rsqrt(jnp.sum(act * act, axis=1, keepdims=True) + 1e-06)
        parts.append(act)
    beta = jax.nn.sigmoid(logit_ref[...].astype(f32)) * valid
    gates = x_ref[3].astype(f32)
    gates = gates * jax.nn.sigmoid(gates) * valid * gain_ref[...]
    pairs = rows // PAIR
    blocks = []
    for g in range(pairs):
        at = slice(g * PAIR, (g + 1) * PAIR)
        start = base + g * PAIR
        q, k, v, b = parts[0][at], parts[1][at], parts[2][at], beta[at]
        upto, strict, keep, eye = pair_masks(start, begins[at])
        kb = b * k
        k_two = halves(k)
        neg = jnp.where(strict, -close_dot(kb, k_two, NT), 0.0)
        inverse = eye + neg
        power = neg
        for _ in range(BLOCK.bit_length() - 2):
            power_two = halves(power)
            power = close_dot(power_two, power_two)
            inverse = inverse + close_dot(inverse, power)
        wu = close_dot(inverse, jnp.concatenate([jnp.where(keep, kb, 0.0), b * v], axis=1))
        wu_two = halves(wu)
        scores = jnp.where(upto, close_dot(q, k_two, NT), 0.0)
        cd = close_dot(scores, wu_two)
        c = jnp.where(keep, q, 0.0) - cd[:, :LANES]
        wu_ref[at] = wu
        t_ref[at] = inverse
        a_ref[at] = scores
        c_ref[at] = c
        for h in range(2):
            inner = slice(h * BLOCK, (h + 1) * BLOCK)
            first = start + h * BLOCK
            final = doc_start(first + BLOCK - 1, starts_ref)
            tail = place_rows(first, BLOCK) >= final
            k_last = jnp.where(tail, k[inner], 0.0)
            mb = close_dot(k_last, (wu_two[0][inner], wu_two[1][inner]), TN)
            kept = jnp.where(final < first, 1.0, 0.0)
            m = kept * eye - mb[:, :LANES]
            m_ref[g * 2 + h] = m
            blocks.append((halves(m), mb[:, LANES:], c[inner], cd[inner, LANES:]))
    state = state_ref[...]
    results = []
    for n, (m_two, addend, c, d) in enumerate(blocks):
        s_ref[n] = state
        s_two = halves(state)
        results.append(close_dot(c, s_two) + d)
        state = close_dot(m_two, s_two) + addend
        square_ref[pl.ds(step * len(blocks) + n, 1), :] = jnp.sum(state * state, axis=0, keepdims=True)
    state_ref[...] = state
    result = jnp.concatenate(results, axis=0)
    o_ref[...] = result
    unit = result * lax.rsqrt(jnp.mean(result * result, axis=1, keepdims=True) + 1e-05)
    mixed_ref[...] = (unit * gates).astype(bf16)

    @pl.when(step == pl.num_programs(0) - 1)
    def _():
        sizes = jnp.sqrt(jnp.sum(square_ref[...], axis=1, keepdims=True) + 1e-12)
        norm_ref[...] = jnp.broadcast_to(jnp.sum(sizes, axis=0, keepdims=True), norm_ref.shape)


def backward_body(starts_ref, length_ref, x_ref, logit_ref, taps_ref, gain_ref, grad_ref,
                  conv_ref, wu_ref, t_ref, a_ref, c_ref, m_ref, s_ref, o_ref,
                  dx_ref, dlogit_ref, dtaps_ref, dgain_ref, dstate_ref, after_ref):
    step = pl.program_id(0)
    rows = x_ref.shape[1]
    base = (pl.num_programs(0) - 1 - step) * rows

    @pl.when(step == 0)
    def _():
        dstate_ref[...] = jnp.zeros_like(dstate_ref)
        after_ref[...] = jnp.zeros_like(after_ref)
        dtaps_ref[...] = jnp.zeros_like(dtaps_ref)
        dgain_ref[...] = jnp.zeros_like(dgain_ref)

    lead = after_ref.shape[1]
    places_tall = place_rows(base, rows + lead)
    begins_tall = doc_start(places_tall, starts_ref)
    since_tall = places_tall - begins_tall
    places, begins = places_tall[:rows], begins_tall[:rows]
    valid = (places < length_ref[0]).astype(f32)
    gain = gain_ref[...]
    gate = x_ref[3].astype(f32)
    gate_sig = jax.nn.sigmoid(gate)
    gate_act = gate * gate_sig
    o = o_ref[...]
    r = lax.rsqrt(jnp.mean(o * o, axis=1, keepdims=True) + 1e-05)
    unit = o * r
    grad = grad_ref[...].astype(f32) * valid
    gu = grad * unit
    dgain_ref[0:1, :] += jnp.sum(gu * gate_act, axis=0, keepdims=True)
    dx_ref[3] = (gu * gain * (gate_sig * (1.0 + gate * (1.0 - gate_sig)))).astype(bf16)
    dunit = grad * gain * gate_act
    d_o = r * (dunit - unit * jnp.mean(dunit * unit, axis=1, keepdims=True))
    convs, sigs, acts, scales, units = [], [], [], [], []
    for p in range(3):
        conv = conv_ref[p]
        sig = jax.nn.sigmoid(conv)
        act = conv * sig
        convs.append(conv)
        sigs.append(sig)
        if p < 2:
            scale = lax.rsqrt(jnp.sum(act * act, axis=1, keepdims=True) + 1e-06)
            scales.append(scale)
            units.append(act * scale)
        else:
            units.append(act)
    logit_sig = jax.nn.sigmoid(logit_ref[...].astype(f32))
    beta = logit_sig * valid
    pairs = rows // PAIR
    do_two = halves(d_o)
    pieces = [None] * (2 * pairs)
    for n in range(2 * pairs):
        inner = slice(n * BLOCK, (n + 1) * BLOCK)
        pieces[n] = close_dot(c_ref[inner, :], (do_two[0][inner], do_two[1][inner]), TN)
    dstate = dstate_ref[...]
    dstates = [None] * (2 * pairs)
    for n in reversed(range(2 * pairs)):
        d_two = halves(dstate)
        dstates[n] = d_two
        dstate = close_dot(m_ref[n], d_two, TN) + pieces[n]
    dstate_ref[...] = dstate
    grads = [[], [], []]
    dbetas = []
    for g in range(pairs):
        at = slice(g * PAIR, (g + 1) * PAIR)
        start = base + g * PAIR
        q, k, v, b = units[0][at], units[1][at], units[2][at], beta[at]
        upto, strict, keep, eye = pair_masks(start, begins[at])
        wu = wu_ref[at, :]
        wu_two = halves(wu)
        a_two = halves(a_ref[at, :])
        k_two = halves(k)
        do_pair = (do_two[0][at], do_two[1][at])
        p_rows, dp_rows, dq_rows, dk_rows, dw_rows = [], [], [], [], []
        later = close_dot(a_two, do_pair, TN)
        for h in range(2):
            n = g * 2 + h
            inner = slice(h * BLOCK, (h + 1) * BLOCK)
            first = start + h * BLOCK
            final = doc_start(first + BLOCK - 1, starts_ref)
            tail = place_rows(first, BLOCK) >= final
            s_two = halves(s_ref[n])
            ds_two = dstates[n]
            wu_in = (wu_two[0][inner, :LANES], wu_two[1][inner, :LANES])
            p = wu[inner, LANES:] - close_dot(wu_in, s_two)
            p_two = halves(p)
            k_last = jnp.where(tail, k[inner], 0.0)
            dp = later[inner] + close_dot(k_last, ds_two)
            dp_two = halves(dp)
            p_rows.append(p_two)
            dp_rows.append(dp)
            do_in = (do_pair[0][inner], do_pair[1][inner])
            dq_rows.append(close_dot(do_in, s_two, NT))
            dk_rows.append(jnp.where(tail, close_dot(p_two, ds_two, NT), 0.0))
            dw_rows.append(-close_dot(dp_two, s_two, NT))
        p_two = tuple(jnp.concatenate([p_rows[0][i], p_rows[1][i]], axis=0) for i in range(2))
        dp = jnp.concatenate(dp_rows, axis=0)
        da_two = halves(jnp.where(upto, close_dot(do_pair, p_two, NT), 0.0))
        q_two = halves(q)
        dq = jnp.where(keep, jnp.concatenate(dq_rows, axis=0), 0.0) + close_dot(da_two, k_two)
        dk = jnp.concatenate(dk_rows, axis=0) + close_dot(da_two, q_two, TN)
        dwu = jnp.concatenate([jnp.concatenate(dw_rows, axis=0), dp], axis=1)
        dbkv = close_dot(t_ref[at, :], dwu, TN)
        dl_two = halves(jnp.where(strict, -close_dot(dbkv, wu_two, NT), 0.0))
        dkb = close_dot(dl_two, k_two) + jnp.where(keep, dbkv[:, :LANES], 0.0)
        dbv = dbkv[:, LANES:]
        dk = dk + b * dkb + close_dot(dl_two, b * k, TN)
        grads[0].append(dq)
        grads[1].append(dk)
        grads[2].append(b * dbv)
        dbetas.append(jnp.sum(k * dkb + v * dbv, axis=1, keepdims=True))
    dbeta = jnp.concatenate(dbetas, axis=0)
    dlogit_ref[...] = dbeta * (beta * (1.0 - logit_sig))[:, :1]
    for p in range(3):
        dact = jnp.concatenate(grads[p], axis=0)
        if p < 2:
            dact = scales[p] * (dact - units[p] * jnp.sum(dact * units[p], axis=1, keepdims=True))
        dconv = dact * (sigs[p] * (1.0 + convs[p] * (1.0 - sigs[p])))
        tall = jnp.concatenate([dconv, after_ref[p]], axis=0)
        after_ref[p] = dconv[:lead]
        x = x_ref[p].astype(f32)
        dx = dconv * taps_ref[p, 3:4, :]
        dtaps_ref[p, 3:4, :] += jnp.sum(dconv * x, axis=0, keepdims=True)
        for j in range(1, 4):
            moved = pltpu.roll(jnp.where(since_tall >= j, tall, 0.0), rows + lead - j, 0)[:rows]
            dx = dx + moved * taps_ref[p, 3 - j:4 - j, :]
            dtaps_ref[p, 3 - j:4 - j, :] += jnp.sum(moved * x, axis=0, keepdims=True)
        dx_ref[p] = dx.astype(bf16)


def head_forward(x, logit, taps, gain, starts, length, rows=256):
    count = x.shape[1]
    rows = min(rows, count)
    steps = count // rows
    per = rows // BLOCK
    whole = lambda shape: pl.BlockSpec(shape, lambda i, *_: (0,) * len(shape))
    flat = lambda width: pl.BlockSpec((rows, width), lambda i, *_: (i, 0))
    square = pl.BlockSpec((per, LANES, LANES), lambda i, *_: (i, 0, 0))
    halo = 16
    s = jax.ShapeDtypeStruct
    outs = pl.pallas_call(
        forward_body,
        grid_spec=pltpu.PrefetchScalarGridSpec(
            num_scalar_prefetch=2,
            grid=(steps,),
            in_specs=[
                pl.BlockSpec((4, rows, LANES), lambda i, *_: (0, i, 0)),
                pl.BlockSpec((3, halo, LANES), lambda i, *_: (0, jnp.maximum(i * (rows // halo) - 1, 0), 0)),
                pl.BlockSpec((rows, 1), lambda i, *_: (i, 0)),
                whole(taps.shape),
                whole(gain.shape),
            ],
            out_specs=[
                flat(LANES),
                whole((8, LANES)),
                pl.BlockSpec((3, rows, LANES), lambda i, *_: (0, i, 0)),
                flat(2 * LANES), flat(PAIR), flat(PAIR), flat(LANES),
                square, square, flat(LANES),
            ],
            scratch_shapes=[pltpu.VMEM((LANES, LANES), f32), pltpu.VMEM((count // BLOCK, LANES), f32)],
        ),
        out_shape=[
            s((count, LANES), bf16), s((8, LANES), f32), s((3, count, LANES), f32),
            s((count, 2 * LANES), f32), s((count, PAIR), f32), s((count, PAIR), f32), s((count, LANES), f32),
            s((count // BLOCK, LANES, LANES), f32), s((count // BLOCK, LANES, LANES), f32),
            s((count, LANES), f32),
        ],
        name="head_forward",
    )(starts, length, x, x, logit, taps, gain)
    return outs[0], outs[1][0, 0], tuple(outs[2:])


def head_backward(grad, x, logit, taps, gain, starts, length, kept, rows=256):
    count = x.shape[1]
    rows = min(rows, count)
    steps = count // rows
    per = rows // BLOCK
    whole = lambda shape: pl.BlockSpec(shape, lambda i, *_: (0,) * len(shape))
    flat = lambda width: pl.BlockSpec((rows, width), lambda i, *_: (steps - 1 - i, 0))
    deep = lambda d: pl.BlockSpec((d, rows, LANES), lambda i, *_: (0, steps - 1 - i, 0))
    square = pl.BlockSpec((per, LANES, LANES), lambda i, *_: (steps - 1 - i, 0, 0))
    s = jax.ShapeDtypeStruct
    return pl.pallas_call(
        backward_body,
        grid_spec=pltpu.PrefetchScalarGridSpec(
            num_scalar_prefetch=2,
            grid=(steps,),
            in_specs=[
                deep(4), flat(1), whole(taps.shape), whole(gain.shape), flat(LANES),
                deep(3), flat(2 * LANES), flat(PAIR), flat(PAIR), flat(LANES), square, square, flat(LANES),
            ],
            out_specs=[deep(4), flat(1), whole(taps.shape), whole((8, LANES))],
            scratch_shapes=[pltpu.VMEM((LANES, LANES), f32), pltpu.VMEM((3, 8, LANES), f32)],
        ),
        out_shape=[s((4, count, LANES), bf16), s((count, 1), f32), s(taps.shape, f32), s((8, LANES), f32)],
        name="head_backward",
    )(starts, length, x, logit, taps, gain, grad, *kept)

def spread(values):
    return lax.all_gather(values, "tensor", axis=0, tiled=True)


def collect(values):
    return lax.psum_scatter(values, "tensor", scatter_dimension=0, tiled=True)


def shards(
    tokens,
    norm_gain,
    w_proj,
    w_beta,
    conv_weight,
    out_gain,
    w_out,
    mlp_gain,
    w_in,
    w_down,
    cotangent,
    starts,
    lengths,
):
    f32 = jnp.float32
    bf16 = jnp.bfloat16
    full_proj, full_beta, full_out, full_in, full_down = (
        lax.all_gather(w_proj, "mp", axis=1, tiled=True),
        lax.all_gather(w_beta, "mp", axis=0, tiled=True),
        lax.all_gather(w_out, "mp", axis=1, tiled=True),
        lax.all_gather(w_in, "mp", axis=1, tiled=True),
        lax.all_gather(w_down, "mp", axis=1, tiled=True),
    )
    inputs = tokens.astype(f32)
    normed_local, first_back = jax.vjp(scaled_norm, inputs, norm_gain)
    normed = spread(normed_local.astype(bf16))
    projected = jnp.einsum("nd,sdc->snc", normed, full_proj, preferred_element_type=f32).astype(
        bf16
    )
    beta_logit = jnp.dot(normed, full_beta, preferred_element_type=f32).astype(bf16)[None]
    heads_proj, heads_beta = (
        lax.all_to_all(projected, "mp", split_axis=2, concat_axis=1, tiled=True),
        lax.all_to_all(beta_logit, "mp", split_axis=2, concat_axis=1, tiled=True),
    )
    seq_count = starts.shape[0]
    seq_len = heads_proj.shape[1] // seq_count
    channels = heads_proj.shape[2]
    assert seq_count == 1 and channels == LANES
    conv_flat = conv_weight.reshape(3, conv_weight.shape[1], channels)
    logit = heads_beta[0].astype(f32)
    head_args = (heads_proj, logit, conv_flat, out_gain[None], starts[0], lengths)
    mixed_low, norm_total, kept = head_forward(*head_args)
    mixed_tok = lax.all_to_all(mixed_low, "mp", split_axis=0, concat_axis=1, tiled=True)
    branch = collect(jnp.dot(mixed_tok, full_out, preferred_element_type=f32))
    middle = inputs + branch
    normed_local_two, second_back = jax.vjp(scaled_norm, middle, mlp_gain)
    normed_two = spread(normed_local_two.astype(bf16))
    gate_up = jnp.einsum("nd,sdf->snf", normed_two, full_in, preferred_element_type=f32)
    gate_val = gate_up[0]
    up_val = gate_up[1]
    activated = jax.nn.silu(gate_val)
    hidden = (activated * up_val).astype(bf16)
    feed_out = collect(jnp.dot(hidden, full_down, preferred_element_type=f32))
    output = (middle + feed_out).astype(bf16)
    grad_rows_all = spread(cotangent)
    g_down = jnp.einsum("nf,nd->fd", hidden, grad_rows_all, preferred_element_type=f32)
    d_hidden = jnp.einsum("nd,fd->nf", grad_rows_all, full_down, preferred_element_type=f32)
    sigma = jax.nn.sigmoid(gate_val)
    d_gate = (d_hidden * up_val * sigma * (1.0 + gate_val * (1.0 - sigma))).astype(bf16)
    d_up = (d_hidden * activated).astype(bf16)
    d_gate_up = jnp.stack([d_gate, d_up])
    g_in = jnp.einsum("nd,snf->sdf", normed_two, d_gate_up, preferred_element_type=f32)
    d_normed_two = collect(
        jnp.einsum("snf,sdf->nd", d_gate_up, full_in, preferred_element_type=f32)
    )
    d_mid_norm, g_mlp_gain = second_back(d_normed_two)
    d_middle = cotangent.astype(f32) + d_mid_norm
    d_middle_all = spread(d_middle.astype(bf16))
    g_out = jnp.einsum("nc,nd->cd", mixed_tok, d_middle_all, preferred_element_type=f32)
    d_mixed = jnp.einsum("nd,cd->nc", d_middle_all, full_out, preferred_element_type=f32).astype(
        bf16
    )[None]
    d_mixed_heads = lax.all_to_all(d_mixed, "mp", split_axis=2, concat_axis=1, tiled=True)
    d_proj_heads, d_betas, g_conv_flat, g_out_gain = head_backward(
        d_mixed_heads[0], *head_args, kept
    )
    g_out_gain = g_out_gain[0]
    d_beta_heads = d_betas.astype(bf16)[None]
    d_proj_tok, d_beta_tok = (
        lax.all_to_all(
            shortened(d_proj_heads), "mp", split_axis=1, concat_axis=2, tiled=True
        ).astype(d_proj_heads.dtype),
        lax.all_to_all(
            shortened(d_beta_heads), "mp", split_axis=1, concat_axis=2, tiled=True
        ).astype(d_beta_heads.dtype),
    )
    g_proj = jnp.einsum("nd,snc->sdc", normed, d_proj_tok, preferred_element_type=f32)
    g_beta = jnp.einsum("nd,nh->dh", normed, d_beta_tok[0], preferred_element_type=f32)
    d_normed_part = jnp.einsum("snc,sdc->nd", d_proj_tok, full_proj, preferred_element_type=f32)
    d_normed_part = d_normed_part + jnp.einsum(
        "nh,dh->nd", d_beta_tok[0], full_beta, preferred_element_type=f32
    )
    d_normed = collect(d_normed_part)
    d_in_norm, g_norm_gain = first_back(d_normed)
    d_tokens = d_middle + d_in_norm
    g_conv = g_conv_flat.reshape(conv_weight.shape)
    rows_proj, rows_beta, rows_out, rows_in, rows_down = (
        lax.psum_scatter(g_proj, "mp", scatter_dimension=1, tiled=True),
        lax.psum_scatter(g_beta, "mp", scatter_dimension=0, tiled=True),
        lax.psum_scatter(g_out, "mp", scatter_dimension=1, tiled=True),
        lax.psum_scatter(g_in, "mp", scatter_dimension=1, tiled=True),
        lax.psum_scatter(g_down, "mp", scatter_dimension=1, tiled=True),
    )
    sum_proj, sum_beta, sum_out, sum_in, sum_down, sum_conv = lax.psum(
        (rows_proj, rows_beta, rows_out, rows_in, rows_down, g_conv), "dp"
    )
    gain_one, gain_two, gain_head, norm_all = lax.psum(
        (g_norm_gain, g_mlp_gain, g_out_gain, norm_total), ("dp", "mp", "tensor")
    )
    state_norm = norm_all / (HEADS * seq_count * lax.axis_size("dp") * (seq_len // BLOCK))
    return (
        output,
        d_tokens,
        gain_one,
        sum_proj,
        sum_beta,
        sum_conv,
        gain_head,
        sum_out,
        gain_two,
        sum_in,
        sum_down,
        state_norm,
    )


def solution(mesh):
    placed = (
        P(("dp", "mp", "tensor"), None),
        P(),
        P(None, "mp", "tensor"),
        P("mp", "tensor"),
        P(None, None, "tensor", "mp", None),
        P(),
        P("tensor", "mp"),
        P(),
        P(None, "mp", "tensor"),
        P("tensor", "mp"),
        P(("dp", "mp", "tensor"), None),
        P("dp", None),
        P("dp"),
    )
    return jax.shard_map(
        shards,
        mesh=mesh,
        in_specs=placed,
        out_specs=(
            P(("dp", "mp", "tensor"), None),
            P(("dp", "mp", "tensor"), None),
            P(),
            P(None, "mp", "tensor"),
            P("mp", "tensor"),
            P(None, None, "tensor", "mp", None),
            P(),
            P("tensor", "mp"),
            P(),
            P(None, "mp", "tensor"),
            P("tensor", "mp"),
            P(),
        ),
        check_vma=False,
    )
```

time: 2350 us -> 1670 us (0.71)
  matrix products: 651 us -> 121 us
  local copies, waits for them, and re-layouts: 363 us -> 84.9 us
  waiting for transfers between devices: 1030 us -> 1180 us
  Pallas kernels: 0 us -> 73.2 us
  other arithmetic: 109 us -> 38.4 us
  loops' own time: 24.5 us -> 0 us
    dot_general x458 -> x0, matrix products: 539 us -> none  [the longest x96 153 us: advance(): jnp.dot((k_part * last_part[:, None]).T, pseudo, precision=highest)]
    squeeze x192 -> x1, local copies, waits for them, and re-layouts: 166 us -> 0.69 us  [shards(): g_out_gain = g_out_gain[0]]
    reduce_scatter x1, waiting for transfers between devices: 0.02 us -> 77.6 us  [shards(): lax.psum_scatter(g_in, 'mp', scatter_dimension=1, tiled=True)]
    slice x74 -> x1, local copies, waits for them, and re-layouts: 78.2 us -> 1.2 us  [head_forward(): return (outs[0], outs[1][0, 0], tuple(outs[2:]))]
    pallas_call x0 -> x2, Pallas kernels: none -> 73.2 us  [the longest x1 39.1 us: head_forward(): pl.pallas_call(forward_body, grid_spec=pltpu.PrefetchScalarGridSpec(num_s...]
    reduce_scatter x1, waiting for transfers between devices: 60.2 us -> 127 us  [shards(): lax.psum_scatter(g_proj, 'mp', scatter_dimension=1, tiled=True)]
    convert_element_type x5 -> x1, local copies, waits for them, and re-layouts: 27.5 us -> 1.35 us  [shards(): logit = heads_beta[0].astype(f32)]
    another operation x2 -> x0, loops' own time: 24.5 us -> none  [block_delta(): lax.scan(jax.checkpoint(advance), start_state, (w_mat, u_mat, q_blocks, s...]
  transfers between devices with their start and end apart: 21 -> 21, of which waited for: 16 -> 17; matrix products, arithmetic and copies ran while one was open for 46% -> 11% of each run, Pallas kernels for 0% -> 4%
where the time goes in v1:
time: 1670 us; the launch traced here: 1660 us
  waiting for transfers between devices  1180 us (71%)
  blocking collectives  130 us (8%)
  matrix products  121 us (7%)
  local copies, waits for them, and re-layouts  84.9 us (5%)
  Pallas kernels  73.2 us (4%)
  other arithmetic  38.4 us (2%)
  between operations  17.4 us (1%)
    psum x1, waiting for transfers between devices, shards(): lax.psum((rows_proj, rows_beta, rows_out, rows_in, rows_down, g_conv), 'dp')  316 us
    reduce_scatter x4, waiting for transfers between devices, collect(): return lax.psum_scatter(values, 'tensor', scatter_dimension=0, tiled=True)  258 us
    all_gather x4, waiting for transfers between devices, spread(): return lax.all_gather(values, 'tensor', axis=0, tiled=True)  168 us
    reduce_scatter x1, waiting for transfers between devices, shards(): lax.psum_scatter(g_proj, 'mp', scatter_dimension=1, tiled=True)  127 us
    reduce_scatter x1, waiting for transfers between devices, shards(): lax.psum_scatter(g_in, 'mp', scatter_dimension=1, tiled=True)  77.6 us
    all_gather x1, waiting for transfers between devices, shards(): lax.all_gather(w_in, 'mp', axis=1, tiled=True)  73.9 us
    all_gather x1, waiting for transfers between devices, shards(): lax.all_gather(w_proj, 'mp', axis=1, tiled=True)  51.3 us
    all_to_all x1, blocking collectives, shards(): lax.all_to_all(shortened(d_proj_heads), 'mp', split_axis=1, concat_axis=2...  51 us
  transfers between devices with their start and end apart: 21, of which 17 were waited for; matrix products, arithmetic and copies ran while one was open for 11% of the time, Pallas kernels for 4%

profile of v1, /device:TPU:0, one launch (start us, length us, event | category | flops | bytes accessed | tf_op | source)
XLA Modules:
  0.0 1656.3 jit_solution(6751153285618311248)
XLA Ops:
  8.5 2.0 fusion.14
  12.0 6.2 all_gather.29
  18.3 40.8 %all-gather.9.cloned.1.call-done = bf16[512,2048]{1,0:T(8,128)(2,1)} async-done(((bf16[128,2048]{1,0:T(8,128)(2,1)}), bf16[512,2048]{1,0:T(8,128)(2,1)}) %all-gather.9.cloned.1.call-update) | async-done | bytes 2097168 | tf_op jit(solution)/shard_map/all_gather | solution.py:364
  59.1 2.2 fusion.13
  63.1 3.3 all-to-all-start.1
  66.4 51.3 %all-gather.11.cloned.1.call-done = bf16[4,2048,512]{2,1,0:T(8,128)(2,1)} async-done(((bf16[4,512,512]{2,1,0:T(8,128)(2,1)}), bf16[4,2048,512]{2,1,0:T(8,128)(2,1)}) %all-gather.11.cloned.1.call-update) | async-done | bytes 8388624 | tf_op jit(solution)/shard_map/all_gather | solution.py:389
  117.7 9.8 convert_bitcast_fusion
  127.6 4.5 copy.71
  132.1 4.5 all-to-all-start
  138.6 24.4 %all-to-all-done = bf16[4,512,512]{1,0,2:T(4,128)(2,1)} async-done(((bf16[4,512,512]{1,0,2:T(4,128)(2,1)}), bf16[4,512,512]{1,0,2:T(4,128)(2,1)}, u32[]{:S(2)}, u32[]{:S(2)}) %all-to-all-start) | async-done | bytes 2097184 | tf_op jit(solution)/shard_map/all_to_all | solution.py:403
  162.9 4.5 copy.72
  167.4 39.1 %head_forward.1 = (bf16[2048,128]{1,0:T(8,128)(2,1)}, f32[8,128]{1,0:T(8,128)}, f32[3,2048,128]{2,1,0:T(8,128)}, f32[2048,256]{1,0:T(8,128)}, f32[2048,128]{1,0:...) custom-call(s32[8]{0:T(128)} %bitcast.140, ...), custom_call_target="tpu_custom_call" | custom-call | tf_op jit(solution)/shard_map/head_forward/pallas_call | solution.py:305
  206.5 2.0 copy.75
  208.5 3.5 all-to-all-start.2
  212.1 8.7 all-to-all-done.2
  220.8 5.1 fusion.28
  226.6 76.3 %reduce-scatter.12.cloned.1.call-done = f32[128,2048]{1,0:T(8,128)} async-done(((f32[512,2048]{1,0:T(8,128)}), f32[128,2048]{1,0:T(8,128)}) %reduce-scatter.12.cloned.1.call-update) | async-done | bytes 1048592 | tf_op jit(solution)/shard_map/reduce_scatter | solution.py:368
  307.1 73.9 %all-gather.17.cloned.1.call-done = bf16[2,2048,1408]{2,1,0:T(8,128)(2,1)} async-done(((bf16[2,512,1408]{2,1,0:T(8,128)(2,1)}), bf16[2,2048,1408]{2,1,0:T(8,128)(2,1)}) %all-gather.17.cloned.1.call-update) | async-done | bytes 11534352 | tf_op jit(solution)/shard_map/all_gather | solution.py:392
  380.9 47.7 %all-gather.15.cloned.1.call-done = bf16[512,2048]{1,0:T(8,128)(2,1)} async-done(((bf16[128,2048]{1,0:T(8,128)(2,1)}), bf16[512,2048]{1,0:T(8,128)(2,1)}) %all-gather.15.cloned.1.call-update) | async-done | bytes 2097168 | tf_op jit(solution)/shard_map/all_gather | solution.py:364
  428.6 12.5 convolution_bitcast_fusion.2
  441.1 33.6 %all-gather.21.cloned.1.call-done = bf16[512,2048]{1,0:T(8,128)(2,1)} async-done(((bf16[128,2048]{1,0:T(8,128)(2,1)}), bf16[512,2048]{1,0:T(8,128)(2,1)}) %all-gather.21.cloned.1.call-update) | async-done | bytes 2097168 | tf_op jit(solution)/shard_map/all_gather | solution.py:364
  474.7 43.8 %all-gather.19.cloned.1.call-done = bf16[1408,2048]{1,0:T(8,128)(2,1)} async-done(((bf16[1408,512]{1,0:T(8,128)(2,1)}), bf16[1408,2048]{1,0:T(8,128)(2,1)}) %all-gather.19.cloned.1.call-update) | async-done | bytes 5767184 | tf_op jit(solution)/shard_map/all_gather | solution.py:393
  518.5 10.4 fusion.9
  530.5 10.3 convolution_bitcast_fusion.3
  540.9 76.9 %reduce-scatter.16.cloned.1.call-done = f32[128,2048]{1,0:T(8,128)} async-done(((f32[512,2048]{1,0:T(8,128)}), f32[128,2048]{1,0:T(8,128)}) %reduce-scatter.16.cloned.1.call-update) | async-done | bytes 1048592 | tf_op jit(solution)/shard_map/reduce_scatter | solution.py:368
  620.6 46.3 %all-gather.23.cloned.1.call-done = bf16[512,2048]{1,0:T(8,128)(2,1)} async-done(((bf16[128,2048]{1,0:T(8,128)(2,1)}), bf16[512,2048]{1,0:T(8,128)(2,1)}) %all-gather.23.cloned.1.call-update) | async-done | bytes 2097168 | tf_op jit(solution)/shard_map/all_gather | solution.py:364
  666.8 5.0 fusion.31
  672.3 10.4 fusion.32
  682.8 13.3 convolution_bitcast_fusion
  696.2 4.3 fusion.12
  700.5 3.6 copy.76
  704.1 5.6 reduce.5
  709.6 2.2 reshape.106
  711.9 13.2 all_to_all.94
  725.0 3.5 reshape.107
  728.6 2.5 copy.91
  731.0 2.2 copy.77
  733.3 34.1 %head_backward.1 = (bf16[4,2048,128]{2,1,0:T(8,128)(2,1)}, f32[2048,1]{1,0:T(8,128)}, f32[3,4,128]{2,1,0:T(4,128)}, f32[8,128]{1,0:T(8,128)}) custom-call(s32[8]{0:T(128)} %bitcast.141, s32[1]{0:T(128)S(6)} %copy.100.length_ref, bf16[4,2048,128]{2,1,0:T(8,128)(2,1)} %bitcast.125, f32[2048,1]{1,0:T(8,128)} %copy.74.logit_ref, f32[3,4,128]{2,1,0:T(4,128)} %bitcast.138, ...), custom_call_target="tpu_custom_call" | custom-call | tf_op jit(solution)/shard_map/head_backward/pallas_call | solution.py:347
  767.4 3.4 copy.79
  770.9 51.0 %all_to_all.95 = bf16[4,2048,128]{2,0,1:T(4,128)(2,1)S(1)} all-to-all(bf16[4,2048,128]{2,0,1:T(4,128)(2,1)S(1)} %copy.79), channel_id=1, replica_groups=mesh['dp'=2,'mp'=4,'tensor'=4] {'mp'}, dimensions={1} | all-to-all | bytes 4194304 | tf_op jit(solution)/shard_map/all_to_all | solution.py:451
  821.9 2.9 copy.94
  824.8 4.1 all_to_all.84
  828.9 15.0 convolution_bitcast_fusion.1
  846.2 7.5 reshape_bitcast_fusion
  853.7 17.0 %reduce.6 = bf16[2048]{0:T(1024)(128)(2,1)S(1)} reduce(bf16[2048,1,1]{2,1,0:T(2,128)(2,1)} %reshape_bitcast_fusion, bf16[]{:T(256)} %broadcast.95), dimensions={1,2}, to_apply=%reshape_bitcast_fusion.reduce_sub_computation | reduce | bytes 8194
  870.8 6.5 all_to_all.96
  877.3 2.3 reshape.109
  879.6 16.3 bitcast_reduce_fusion
  895.9 3.5 fusion.20
  899.5 7.6 fusion.30
  907.1 2.8 bitcast_add_fusion
  910.0 8.8 fusion.29
  919.0 77.6 %reduce-scatter.24.cloned.1.call-done = f32[2,512,1408]{1,2,0:T(8,128)} async-done(((f32[2,2048,1408]{1,2,0:T(8,128)}), f32[2,512,1408]{1,2,0:T(8,128)}) %reduce-scatter.24.cloned.1.call-update) | async-done | bytes 5767184 | tf_op jit(solution)/shard_map/reduce_scatter | solution.py:472
  996.6 127.4 %reduce-scatter.20.cloned.1.call-done = f32[4,512,512]{1,2,0:T(8,128)} async-done(((f32[4,2048,512]{1,2,0:T(8,128)}), f32[4,512,512]{1,2,0:T(8,128)}) %reduce-scatter.20.cloned.1.call-update) | async-done | bytes 4194320 | tf_op jit(solution)/shard_map/reduce_scatter | solution.py:469
  1125.8 25.9 %reduce-scatter.28.cloned.1.call-done = f32[512,4]{1,0:T(8,128)} async-done(((f32[2048,4]{1,0:T(8,128)}), f32[512,4]{1,0:T(8,128)}) %reduce-scatter.28.cloned.1.call-update) | async-done | bytes 8208
  1152.8 8.7 all-reduce.1
  1161.5 69.8 %reduce-scatter.18.cloned.1.call-done = f32[128,2048]{1,0:T(8,128)} async-done(((f32[512,2048]{1,0:T(8,128)}), f32[128,2048]{1,0:T(8,128)}) %reduce-scatter.18.cloned.1.call-update) | async-done | bytes 1048592 | tf_op jit(solution)/shard_map/reduce_scatter | solution.py:368
  1232.9 44.1 %all-reduce = (f32[2048]{0:T(1024)}, f32[128]{0:T(128)}, f32[2048]{0:T(1024)}, f32[]{:T(128)}) all-reduce(f32[2048]{0:T(1024)S(1)} %get-tuple-element.102, f32[128]{0:T(128)S(1)} %slice_bitcast_fusion.2, f32[2048]{0:T(1024)S(1)} %get-tuple-element.100, f32[]{:T(128)} %bitcast.40), channel_id=1, replica_groups=mesh['dp'=2,'mp'=4,'tensor'=4] {'dp','mp','tensor'}, use_global_device_ids=true, to_apply=%region_9.10 | all-reduce | flops 4225 | bytes 33800 | tf_op jit(solution)/shard_map/psum | solution.py:478
  1277.6 34.7 %reduce-scatter.14.cloned.1.call-done = f32[128,2048]{1,0:T(8,128)} async-done(((f32[512,2048]{1,0:T(8,128)}), f32[128,2048]{1,0:T(8,128)}) %reduce-scatter.14.cloned.1.call-update) | async-done | bytes 1048592 | tf_op jit(solution)/shard_map/reduce_scatter | solution.py:368
  1312.4 3.1 fusion.17
  1315.5 316.1 %all-reduce.5.cloned.1.call-done = (f32[4,512,512]{1,2,0:T(8,128)}, f32[512,512]{1,0:T(8,128)}, f32[2,512,1408]{1,2,0:T(8,128)}, f32[1408,512]{1,0:T(8,128)}) async-done(((f32[4,512,512]{1,2,0:T(8,128)}, f32[512,512]{1,0:T(8,128)}, f32[2,512,1408]{1,2,0:T(8,128)}, f32[1408,512]{1,0:T(8,128)}), (f32[4,512,512]{1,2,0:T(8,128)}, f32[512,512]{1,0:T(8,128)}, f32[2,512,1408]{1,2,0:T(8,128)}, ...) | async-done | bytes 13893648 | tf_op jit(solution)/shard_map/psum | solution.py:475
  1631.6 5.2 copy.84
  1636.9 6.3 copy.86
  1644.1 3.7 copy.102
  (86 shorter events, 23.8 us)
Async XLA Ops:
  7.2 51.9 %all-gather.9.cloned.1.call-start = ((), (), s32[]{:S(2)}) async-start(), calls=%async_computation.15 | async-start | bytes 2621440 | tf_op jit(solution)/shard_map/all_gather | solution.py:364
  8.5 3.6 copy-start.8
  10.5 107.2 %all-gather.11.cloned.1.call-start = ((), (), s32[]{:S(2)}) async-start(), calls=%async_computation.16 | async-start | bytes 10485760 | tf_op jit(solution)/shard_map/all_gather | solution.py:389
  11.3 200.8 %all-gather.13.cloned.1.call-start = ((), (), s32[]{:S(2)}) async-start(), calls=%async_computation.17 | async-start | bytes 2621440 | tf_op jit(solution)/shard_map/all_gather | solution.py:391
  63.1 68.9 %all-to-all-start.1 = ((bf16[4,2,256]{2,1,0:T(2,128)(2,1)}), bf16[4,2,256]{2,1,0:T(2,128)(2,1)S(1)}, u32[]{:S(2)}, u32[]{:S(2)}) async-start(bf16[4,2,256]{2,1,0:T(2,128)(2,1)} %reshape.104), calls=%async_computation.1 | async-start | bytes 8192 | tf_op jit(solution)/shard_map/all_to_all | solution.py:404
  132.1 30.9 %all-to-all-start = ((bf16[4,512,512]{1,0,2:T(4,128)(2,1)}), bf16[4,512,512]{1,0,2:T(4,128)(2,1)}, u32[]{:S(2)}, u32[]{:S(2)}) async-start(bf16[4,512,512]{1,0,2:T(4,128)(2,1)} %copy.71), calls=%async_computation | async-start | bytes 4194304 | tf_op jit(solution)/shard_map/all_to_all | solution.py:403
  208.5 12.3 all-to-all-start.2
  212.0 90.8 %reduce-scatter.12.cloned.1.call-start = ((), (), s32[]{:S(2)}) async-start(), calls=%async_computation.18 | async-start | bytes 5242880 | tf_op jit(solution)/shard_map/reduce_scatter | solution.py:368
  220.8 5.1 copy-start.3
  225.9 77.0 %copy-start = (bf16[128,2048]{1,0:T(8,128)(2,1)S(1)}, bf16[128,2048]{1,0:T(8,128)(2,1)}, u32[]{:S(2)}) copy-start(bf16[128,2048]{1,0:T(8,128)(2,1)} %param.13) | copy-start | bytes 1572868
  225.9 78.4 %copy-start.5 = (f32[2048]{0:T(1024)S(1)}, f32[2048]{0:T(1024)}, u32[]{:S(2)}) copy-start(f32[2048]{0:T(1024)} %param.20) | copy-start | bytes 24580
  225.9 155.0 %all-gather.17.cloned.1.call-start = ((), (), s32[]{:S(2)}) async-start(), calls=%async_computation.20 | async-start | bytes 14417920 | tf_op jit(solution)/shard_map/all_gather | solution.py:392
  226.5 202.1 %all-gather.15.cloned.1.call-start = ((), (), s32[]{:S(2)}) async-start(), calls=%async_computation.19 | async-start | bytes 2621440 | tf_op jit(solution)/shard_map/all_gather | solution.py:364
  305.3 169.4 %all-gather.21.cloned.1.call-start = ((), (), s32[]{:S(2)}) async-start(), calls=%async_computation.23 | async-start | bytes 2621440 | tf_op jit(solution)/shard_map/all_gather | solution.py:364
  306.1 212.4 %all-gather.19.cloned.1.call-start = ((), (), s32[]{:S(2)}) async-start(), calls=%async_computation.21 | async-start | bytes 7208960 | tf_op jit(solution)/shard_map/all_gather | solution.py:393
  306.8 311.0 %reduce-scatter.16.cloned.1.call-start = ((), (), s32[]{:S(2)}) async-start(), calls=%async_computation.24 | async-start | bytes 5242880 | tf_op jit(solution)/shard_map/reduce_scatter | solution.py:368
  528.9 1.1 copy-start.9
  528.9 1.6 copy-start.10
  540.8 78.5 %copy-start.2 = (bf16[128,2048]{1,0:T(8,128)(2,1)S(1)}, bf16[128,2048]{1,0:T(8,128)(2,1)}, u32[]{:S(2)}) copy-start(bf16[128,2048]{1,0:T(8,128)(2,1)} %param.23) | copy-start | bytes 1572868
  540.8 126.0 %all-gather.23.cloned.1.call-start = ((), (), s32[]{:S(2)}) async-start(), calls=%async_computation.25 | async-start | bytes 2621440 | tf_op jit(solution)/shard_map/all_gather | solution.py:364
  617.8 1.6 copy-start.1
  620.5 298.4 %reduce-scatter.22.cloned.1.call-start = ((), (), s32[]{:S(2)}) async-start(), calls=%async_computation.28 | async-start | bytes 5242880 | tf_op jit(solution)/shard_map/reduce_scatter | solution.py:471
  671.9 247.1 %reduce-scatter.26.cloned.1.call-start = ((), (), s32[]{:S(2)}) async-start(), calls=%async_computation.30 | async-start | bytes 14417920 | tf_op jit(solution)/shard_map/reduce_scatter | solution.py:473
  682.8 313.8 %reduce-scatter.24.cloned.1.call-start = ((), (), s32[]{:S(2)}) async-start(), calls=%async_computation.29 | async-start | bytes 28835840 | tf_op jit(solution)/shard_map/reduce_scatter | solution.py:472
  696.2 427.8 %reduce-scatter.20.cloned.1.call-start = ((), (), s32[]{:S(2)}) async-start(), calls=%async_computation.27 | async-start | bytes 20971520 | tf_op jit(solution)/shard_map/reduce_scatter | solution.py:469
  844.0 307.7 %reduce-scatter.28.cloned.1.call-start = ((), (), s32[]{:S(2)}) async-start(), calls=%async_computation.31 | async-start | bytes 1310720
  899.4 331.8 %reduce-scatter.18.cloned.1.call-start = ((), (), s32[]{:S(2)}) async-start(), calls=%async_computation.26 | async-start | bytes 5242880 | tf_op jit(solution)/shard_map/reduce_scatter | solution.py:368
  909.9 402.4 %reduce-scatter.14.cloned.1.call-start = ((), (), s32[]{:S(2)}) async-start(), calls=%async_computation.22 | async-start | bytes 5242880 | tf_op jit(solution)/shard_map/reduce_scatter | solution.py:368
  918.9 712.8 %all-reduce.5.cloned.1.call-start = ((), (), s32[]{:S(2)}) async-start(), calls=%async_computation.32 | async-start | bytes 27787264 | tf_op jit(solution)/shard_map/psum | solution.py:475
  1123.9 28.8 %copy-start.7 = (f32[3,4,128]{2,1,0:T(4,128)S(1)}, f32[3,4,128]{2,1,0:T(4,128)}, u32[]{:S(2)}) copy-start(f32[3,4,128]{2,1,0:T(4,128)} %get-tuple-element.37) | copy-start | bytes 18436
  1123.9 107.3 %copy-start.6 = (f32[2048]{0:T(1024)S(1)}, f32[2048]{0:T(1024)}, u32[]{:S(2)}) copy-start(f32[2048]{0:T(1024)} %param.14) | copy-start | bytes 24580
  1636.9 6.3 copy-start.4
Sparse Core Ops, SparseCore 0:
  10.7 48.3 all-gather.8
  60.6 57.0 all-gather.10
  119.3 23.2 all-gather.12
  226.0 76.7 reduce-scatter.11
  304.3 76.6 all-gather.16
  382.9 45.6 all-gather.14
  430.2 44.4 all-gather.20
  476.2 42.1 all-gather.18
  540.9 76.7 reduce-scatter.15
  620.7 46.1 all-gather.22
  672.0 43.1 reduce-scatter.21
  717.7 113.1 reduce-scatter.25
  833.5 163.0 reduce-scatter.23
  999.0 124.8 reduce-scatter.19
  1126.9 24.7 reduce-scatter.27
  1154.4 76.7 reduce-scatter.17
  1234.0 78.3 reduce-scatter.13
  1314.8 316.7 all-reduce.4

commit v2 on v1

v2 whole, which is shorter than its diff:
```python
import jax
import jax.numpy as jnp
from jax import lax
from jax.experimental import pallas as pl
from jax.experimental.pallas import tpu as pltpu
from jax.sharding import PartitionSpec as P

BLOCK = 64
PAIR = 2 * BLOCK
LANES = 128
f32 = jnp.float32
bf16 = jnp.bfloat16


def halves(a):
    hi = a.astype(bf16)
    return hi, (a - hi.astype(f32)).astype(bf16)


def product(a, b, dims):
    return lax.dot_general(a, b, (dims, ((), ())), preferred_element_type=f32)


def close_dot(a, b, dims=((1,), (0,))):
    a_hi, a_lo = a if isinstance(a, tuple) else halves(a)
    b_hi, b_lo = b if isinstance(b, tuple) else halves(b)
    return product(a_hi, b_hi, dims) + (product(a_hi, b_lo, dims) + product(a_lo, b_hi, dims))


NN = ((1,), (0,))
NT = ((1,), (1,))
TN = ((0,), (0,))


def doc_start(places, starts_ref):
    found = jnp.zeros_like(places)
    for j in range(1, starts_ref.shape[0]):
        begin = starts_ref[j]
        found = jnp.where(places >= begin, begin, found)
    return found


def place_rows(base, rows, width=LANES):
    return base + lax.broadcasted_iota(jnp.int32, (rows, width), 0)


def pair_masks(base, begins):
    rows = lax.broadcasted_iota(jnp.int32, (PAIR, PAIR), 0)
    cols = lax.broadcasted_iota(jnp.int32, (PAIR, PAIR), 1)
    heads = (rows // BLOCK) * BLOCK
    lower = jnp.maximum(begins - base, heads)
    upto = (cols >= lower) & (cols <= rows)
    strict = (cols >= lower) & (cols < rows)
    keep = begins < base + heads
    return upto, strict, keep, (rows == cols).astype(f32)


HALO = 16


def place_of(chunk, info_ref):
    return chunk ^ info_ref[1]


def in_order(step, count, info_ref, refs, target_ref, first):
    local = place_of(step * count, info_ref)
    near = local < pl.num_programs(0) * count // 2
    for n in range(count):
        inside = (local ^ n) % count

        @pl.when(near)
        def _():
            target_ref[first + n * PAIR:first + (n + 1) * PAIR, :] = refs[0][
                pl.ds(pl.multiple_of(inside * PAIR, PAIR), PAIR), :]

        @pl.when(jnp.logical_not(near))
        def _():
            target_ref[first + n * PAIR:first + (n + 1) * PAIR, :] = refs[1][
                pl.ds(pl.multiple_of(inside * PAIR, PAIR), PAIR), :]


def out_of_order(step, count, info_ref, value, target_ref, width):
    local = place_of(step * count, info_ref)
    for n in range(count):
        inside = pl.multiple_of(((local ^ n) % count) * PAIR, PAIR)
        target_ref[pl.ds(inside, PAIR), width] = value[n * PAIR:(n + 1) * PAIR]


def column(row):
    eye = lax.broadcasted_iota(jnp.int32, (PAIR, PAIR), 0) == lax.broadcasted_iota(jnp.int32, (PAIR, PAIR), 1)
    return jnp.sum(jnp.where(eye, row, 0.0), axis=1, keepdims=True)


def columns(step, count, info_ref, ref):
    return jnp.concatenate(
        [column(ref[pl.ds(place_of(step * count + n, info_ref), 1), :]) for n in range(count)], axis=0)


def forward_body(starts_ref, info_ref, near_ref, far_ref, before_near_ref, before_far_ref, logit_ref, taps_ref,
                 gain_ref, mixed_ref, norm_ref, conv_ref, wu_ref, t_ref, a_ref, c_ref, m_ref, s_ref, o_ref,
                 state_ref, square_ref, x_ref):
    step = pl.program_id(0)
    rows = near_ref.shape[0]
    base = step * rows
    count = rows // PAIR
    half_chunks = pl.num_programs(0) * count // 2
    before = place_of(jnp.maximum(step * count - 1, 0), info_ref)

    @pl.when(before < half_chunks)
    def _():
        x_ref[:HALO, :] = before_near_ref[...]

    @pl.when(before >= half_chunks)
    def _():
        x_ref[:HALO, :] = before_far_ref[...]

    in_order(step, count, info_ref, (near_ref, far_ref), x_ref, HALO)

    @pl.when(step == 0)
    def _():
        state_ref[...] = jnp.zeros_like(state_ref)

    places = place_rows(base, rows)
    begins = doc_start(places, starts_ref)
    since = places - begins
    valid = (places < info_ref[0]).astype(f32)
    parts = []
    for p in range(3):
        tall = x_ref[:, p * LANES:(p + 1) * LANES].astype(f32)
        now = tall[HALO:]
        summed = now * taps_ref[p, 3:4, :]
        for j in range(1, 4):
            moved = pltpu.roll(tall, j, 0)[HALO:]
            summed = summed + jnp.where(since >= j, moved, 0.0) * taps_ref[p, 3 - j:4 - j, :]
        conv_ref[p] = summed
        act = summed * jax.nn.sigmoid(summed)
        if p < 2:
            act = act * lax.rsqrt(jnp.sum(act * act, axis=1, keepdims=True) + 1e-06)
        parts.append(act)
    beta = jax.nn.sigmoid(columns(step, count, info_ref, logit_ref)) * valid
    gates = x_ref[HALO:, 3 * LANES:].astype(f32)
    gates = gates * jax.nn.sigmoid(gates) * valid * gain_ref[...]
    pairs = rows // PAIR
    blocks = []
    for g in range(pairs):
        at = slice(g * PAIR, (g + 1) * PAIR)
        start = base + g * PAIR
        q, k, v, b = parts[0][at], parts[1][at], parts[2][at], beta[at]
        upto, strict, keep, eye = pair_masks(start, begins[at])
        kb = b * k
        k_two = halves(k)
        neg = jnp.where(strict, -close_dot(kb, k_two, NT), 0.0)
        inverse = eye + neg
        power = neg
        for _ in range(BLOCK.bit_length() - 2):
            power_two = halves(power)
            power = close_dot(power_two, power_two)
            inverse = inverse + close_dot(inverse, power)
        wu = close_dot(inverse, jnp.concatenate([jnp.where(keep, kb, 0.0), b * v], axis=1))
        wu_two = halves(wu)
        scores = jnp.where(upto, close_dot(q, k_two, NT), 0.0)
        cd = close_dot(scores, wu_two)
        c = jnp.where(keep, q, 0.0) - cd[:, :LANES]
        wu_ref[at] = wu
        t_ref[at] = inverse
        a_ref[at] = scores
        c_ref[at] = c
        for h in range(2):
            inner = slice(h * BLOCK, (h + 1) * BLOCK)
            first = start + h * BLOCK
            final = doc_start(first + BLOCK - 1, starts_ref)
            tail = place_rows(first, BLOCK) >= final
            k_last = jnp.where(tail, k[inner], 0.0)
            mb = close_dot(k_last, (wu_two[0][inner], wu_two[1][inner]), TN)
            kept = jnp.where(final < first, 1.0, 0.0)
            m = kept * eye - mb[:, :LANES]
            m_ref[g * 2 + h] = m
            blocks.append((halves(m), mb[:, LANES:], c[inner], cd[inner, LANES:]))
    state = state_ref[...]
    results = []
    for n, (m_two, addend, c, d) in enumerate(blocks):
        s_ref[n] = state
        s_two = halves(state)
        results.append(close_dot(c, s_two) + d)
        state = close_dot(m_two, s_two) + addend
        square_ref[pl.ds(step * len(blocks) + n, 1), :] = jnp.sum(state * state, axis=0, keepdims=True)
    state_ref[...] = state
    result = jnp.concatenate(results, axis=0)
    o_ref[...] = result
    unit = result * lax.rsqrt(jnp.mean(result * result, axis=1, keepdims=True) + 1e-05)
    out_of_order(step, count, info_ref, (unit * gates).astype(bf16), mixed_ref, slice(None))

    @pl.when(step == pl.num_programs(0) - 1)
    def _():
        sizes = jnp.sqrt(jnp.sum(square_ref[...], axis=1, keepdims=True) + 1e-12)
        norm_ref[...] = jnp.broadcast_to(jnp.sum(sizes, axis=0, keepdims=True), norm_ref.shape)


def backward_body(starts_ref, info_ref, near_ref, far_ref, logit_ref, taps_ref, gain_ref, grad_near_ref,
                  grad_far_ref, conv_ref, wu_ref, t_ref, a_ref, c_ref, m_ref, s_ref, o_ref,
                  dx_ref, dlogit_ref, dtaps_ref, dgain_ref, dstate_ref, after_ref, x_ref, grad_ref):
    step = pl.num_programs(0) - 1 - pl.program_id(0)
    rows = near_ref.shape[0]
    base = step * rows
    count = rows // PAIR
    in_order(step, count, info_ref, (near_ref, far_ref), x_ref, 0)
    in_order(step, count, info_ref, (grad_near_ref, grad_far_ref), grad_ref, 0)

    @pl.when(pl.program_id(0) == 0)
    def _():
        dstate_ref[...] = jnp.zeros_like(dstate_ref)
        after_ref[...] = jnp.zeros_like(after_ref)
        dtaps_ref[...] = jnp.zeros_like(dtaps_ref)
        dgain_ref[...] = jnp.zeros_like(dgain_ref)

    lead = after_ref.shape[1]
    places_tall = place_rows(base, rows + lead)
    begins_tall = doc_start(places_tall, starts_ref)
    since_tall = places_tall - begins_tall
    places, begins = places_tall[:rows], begins_tall[:rows]
    valid = (places < info_ref[0]).astype(f32)
    gain = gain_ref[...]
    gate = x_ref[:, 3 * LANES:].astype(f32)
    gate_sig = jax.nn.sigmoid(gate)
    gate_act = gate * gate_sig
    o = o_ref[...]
    r = lax.rsqrt(jnp.mean(o * o, axis=1, keepdims=True) + 1e-05)
    unit = o * r
    grad = grad_ref[...].astype(f32) * valid
    gu = grad * unit
    dgain_ref[0:1, :] += jnp.sum(gu * gate_act, axis=0, keepdims=True)
    dgate = (gu * gain * (gate_sig * (1.0 + gate * (1.0 - gate_sig)))).astype(bf16)
    out_of_order(step, count, info_ref, dgate, dx_ref, slice(3 * LANES, 4 * LANES))
    dunit = grad * gain * gate_act
    d_o = r * (dunit - unit * jnp.mean(dunit * unit, axis=1, keepdims=True))
    convs, sigs, acts, scales, units = [], [], [], [], []
    for p in range(3):
        conv = conv_ref[p]
        sig = jax.nn.sigmoid(conv)
        act = conv * sig
        convs.append(conv)
        sigs.append(sig)
        if p < 2:
            scale = lax.rsqrt(jnp.sum(act * act, axis=1, keepdims=True) + 1e-06)
            scales.append(scale)
            units.append(act * scale)
        else:
            units.append(act)
    logit_sig = jax.nn.sigmoid(columns(step, count, info_ref, logit_ref))
    beta = logit_sig * valid
    pairs = rows // PAIR
    do_two = halves(d_o)
    pieces = [None] * (2 * pairs)
    for n in range(2 * pairs):
        inner = slice(n * BLOCK, (n + 1) * BLOCK)
        pieces[n] = close_dot(c_ref[inner, :], (do_two[0][inner], do_two[1][inner]), TN)
    dstate = dstate_ref[...]
    dstates = [None] * (2 * pairs)
    for n in reversed(range(2 * pairs)):
        d_two = halves(dstate)
        dstates[n] = d_two
        dstate = close_dot(m_ref[n], d_two, TN) + pieces[n]
    dstate_ref[...] = dstate
    grads = [[], [], []]
    dbetas = []
    for g in range(pairs):
        at = slice(g * PAIR, (g + 1) * PAIR)
        start = base + g * PAIR
        q, k, v, b = units[0][at], units[1][at], units[2][at], beta[at]
        upto, strict, keep, eye = pair_masks(start, begins[at])
        wu = wu_ref[at, :]
        wu_two = halves(wu)
        a_two = halves(a_ref[at, :])
        k_two = halves(k)
        do_pair = (do_two[0][at], do_two[1][at])
        p_rows, dp_rows, dq_rows, dk_rows, dw_rows = [], [], [], [], []
        later = close_dot(a_two, do_pair, TN)
        for h in range(2):
            n = g * 2 + h
            inner = slice(h * BLOCK, (h + 1) * BLOCK)
            first = start + h * BLOCK
            final = doc_start(first + BLOCK - 1, starts_ref)
            tail = place_rows(first, BLOCK) >= final
            s_two = halves(s_ref[n])
            ds_two = dstates[n]
            wu_in = (wu_two[0][inner, :LANES], wu_two[1][inner, :LANES])
            p = wu[inner, LANES:] - close_dot(wu_in, s_two)
            p_two = halves(p)
            k_last = jnp.where(tail, k[inner], 0.0)
            dp = later[inner] + close_dot(k_last, ds_two)
            dp_two = halves(dp)
            p_rows.append(p_two)
            dp_rows.append(dp)
            do_in = (do_pair[0][inner], do_pair[1][inner])
            dq_rows.append(close_dot(do_in, s_two, NT))
            dk_rows.append(jnp.where(tail, close_dot(p_two, ds_two, NT), 0.0))
            dw_rows.append(-close_dot(dp_two, s_two, NT))
        p_two = tuple(jnp.concatenate([p_rows[0][i], p_rows[1][i]], axis=0) for i in range(2))
        dp = jnp.concatenate(dp_rows, axis=0)
        da_two = halves(jnp.where(upto, close_dot(do_pair, p_two, NT), 0.0))
        q_two = halves(q)
        dq = jnp.where(keep, jnp.concatenate(dq_rows, axis=0), 0.0) + close_dot(da_two, k_two)
        dk = jnp.concatenate(dk_rows, axis=0) + close_dot(da_two, q_two, TN)
        dwu = jnp.concatenate([jnp.concatenate(dw_rows, axis=0), dp], axis=1)
        dbkv = close_dot(t_ref[at, :], dwu, TN)
        dl_two = halves(jnp.where(strict, -close_dot(dbkv, wu_two, NT), 0.0))
        dkb = close_dot(dl_two, k_two) + jnp.where(keep, dbkv[:, :LANES], 0.0)
        dbv = dbkv[:, LANES:]
        dk = dk + b * dkb + close_dot(dl_two, b * k, TN)
        grads[0].append(dq)
        grads[1].append(dk)
        grads[2].append(b * dbv)
        dbetas.append(jnp.sum(k * dkb + v * dbv, axis=1, keepdims=True))
    dbeta = jnp.concatenate(dbetas, axis=0)
    dlogit = dbeta * (beta * (1.0 - logit_sig))
    eye = lax.broadcasted_iota(jnp.int32, (PAIR, PAIR), 0) == lax.broadcasted_iota(jnp.int32, (PAIR, PAIR), 1)
    for n in range(count):
        row = jnp.sum(jnp.where(eye, dlogit[n * PAIR:(n + 1) * PAIR], 0.0), axis=0, keepdims=True)
        dlogit_ref[pl.ds(place_of(step * count + n, info_ref), 1), :] = row
    for p in range(3):
        dact = jnp.concatenate(grads[p], axis=0)
        if p < 2:
            dact = scales[p] * (dact - units[p] * jnp.sum(dact * units[p], axis=1, keepdims=True))
        dconv = dact * (sigs[p] * (1.0 + convs[p] * (1.0 - sigs[p])))
        tall = jnp.concatenate([dconv, after_ref[p]], axis=0)
        after_ref[p] = dconv[:lead]
        x = x_ref[:, p * LANES:(p + 1) * LANES].astype(f32)
        dx = dconv * taps_ref[p, 3:4, :]
        dtaps_ref[p, 3:4, :] += jnp.sum(dconv * x, axis=0, keepdims=True)
        for j in range(1, 4):
            moved = pltpu.roll(jnp.where(since_tall >= j, tall, 0.0), rows + lead - j, 0)[:rows]
            dx = dx + moved * taps_ref[p, 3 - j:4 - j, :]
            dtaps_ref[p, 3 - j:4 - j, :] += jnp.sum(moved * x, axis=0, keepdims=True)
        out_of_order(step, count, info_ref, dx.astype(bf16), dx_ref, slice(p * LANES, (p + 1) * LANES))


def half_specs(rows, width, steps, order):
    count = rows // PAIR

    def pair(i, info):
        return place_of(order(i) * count, info) // count

    return [
        pl.BlockSpec((rows, width), lambda i, _, info: (jnp.minimum(pair(i, info), steps // 2 - 1), 0)),
        pl.BlockSpec((rows, width), lambda i, _, info: (jnp.maximum(pair(i, info) - steps // 2, 0), 0)),
    ]


def whole_spec(shape):
    return pl.BlockSpec(shape, lambda i, *_: (0,) * len(shape))


def head_forward(near, far, logit, taps, gain, starts, info, rows=256):
    total = 2 * near.shape[0]
    steps = total // rows
    count = rows // PAIR
    per = rows // BLOCK
    chunks = total // PAIR
    flat = lambda width: pl.BlockSpec((rows, width), lambda i, *_: (i, 0))
    square = pl.BlockSpec((per, LANES, LANES), lambda i, *_: (i, 0, 0))
    fine = PAIR // HALO

    def before(i, info):
        return place_of(jnp.maximum(i * count - 1, 0), info)

    s = jax.ShapeDtypeStruct
    outs = pl.pallas_call(
        forward_body,
        grid_spec=pltpu.PrefetchScalarGridSpec(
            num_scalar_prefetch=2,
            grid=(steps,),
            in_specs=[
                *half_specs(rows, 4 * LANES, steps, lambda i: i),
                pl.BlockSpec((HALO, 4 * LANES), lambda i, _, info: (
                    jnp.minimum(before(i, info), chunks // 2 - 1) * fine + fine - 1, 0)),
                pl.BlockSpec((HALO, 4 * LANES), lambda i, _, info: (
                    jnp.maximum(before(i, info) - chunks // 2, 0) * fine + fine - 1, 0)),
                whole_spec(logit.shape),
                whole_spec(taps.shape),
                whole_spec(gain.shape),
            ],
            out_specs=[
                pl.BlockSpec((rows, LANES), lambda i, _, info: (place_of(i * count, info) // count, 0)),
                whole_spec((8, LANES)),
                pl.BlockSpec((3, rows, LANES), lambda i, *_: (0, i, 0)),
                flat(2 * LANES), flat(PAIR), flat(PAIR), flat(LANES),
                square, square, flat(LANES),
            ],
            scratch_shapes=[
                pltpu.VMEM((LANES, LANES), f32), pltpu.VMEM((total // BLOCK, LANES), f32),
                pltpu.VMEM((rows + HALO, 4 * LANES), bf16),
            ],
        ),
        out_shape=[
            s((total, LANES), bf16), s((8, LANES), f32), s((3, total, LANES), f32),
            s((total, 2 * LANES), f32), s((total, PAIR), f32), s((total, PAIR), f32), s((total, LANES), f32),
            s((total // BLOCK, LANES, LANES), f32), s((total // BLOCK, LANES, LANES), f32),
            s((total, LANES), f32),
        ],
        name="head_forward",
    )(starts, info, near, far, near, far, logit, taps, gain)
    return outs[0], outs[1][0, 0], tuple(outs[2:])


def head_backward(grad_near, grad_far, near, far, logit, taps, gain, starts, info, kept, rows=256):
    total = 2 * near.shape[0]
    steps = total // rows
    count = rows // PAIR
    per = rows // BLOCK
    back = lambda i: steps - 1 - i
    flat = lambda width: pl.BlockSpec((rows, width), lambda i, *_: (back(i), 0))
    square = pl.BlockSpec((per, LANES, LANES), lambda i, *_: (back(i), 0, 0))
    s = jax.ShapeDtypeStruct
    return pl.pallas_call(
        backward_body,
        grid_spec=pltpu.PrefetchScalarGridSpec(
            num_scalar_prefetch=2,
            grid=(steps,),
            in_specs=[
                *half_specs(rows, 4 * LANES, steps, back),
                whole_spec(logit.shape), whole_spec(taps.shape), whole_spec(gain.shape),
                *half_specs(rows, LANES, steps, back),
                pl.BlockSpec((3, rows, LANES), lambda i, *_: (0, back(i), 0)),
                flat(2 * LANES), flat(PAIR), flat(PAIR), flat(LANES), square, square, flat(LANES),
            ],
            out_specs=[
                pl.BlockSpec((rows, 4 * LANES), lambda i, _, info: (place_of(back(i) * count, info) // count, 0)),
                whole_spec(logit.shape), whole_spec(taps.shape), whole_spec((8, LANES)),
            ],
            scratch_shapes=[
                pltpu.VMEM((LANES, LANES), f32), pltpu.VMEM((3, 8, LANES), f32),
                pltpu.VMEM((rows, 4 * LANES), bf16), pltpu.VMEM((rows, LANES), bf16),
            ],
        ),
        out_shape=[s((total, 4 * LANES), bf16), s(logit.shape, f32), s(taps.shape, f32), s((8, LANES), f32)],
        name="head_backward",
    )(starts, info, near, far, logit, taps, gain, grad_near, grad_far, *kept)


def other(value, axis, bit):
    size = lax.axis_size(axis)
    return lax.ppermute(value, axis, [(i, i ^ bit) for i in range(size)])


def after(value, *done):
    return lax.optimization_barrier((value, *done))[0]


def own_order(value, index, axis, parts=4):
    size = value.shape[axis] // parts
    return jnp.concatenate(
        [lax.dynamic_slice_in_dim(value, (p ^ index) * size, size, axis) for p in range(parts)], axis
    )


def neighbour_order(value, axis, bit, parts=4):
    size = value.shape[axis] // parts
    return jnp.concatenate(
        [lax.slice_in_dim(value, (p ^ bit) * size, ((p ^ bit) + 1) * size, axis=axis) for p in range(parts)], axis
    )


def matmul(a, b, dims=((1,), (0,))):
    return lax.dot_general(a, b, (dims, ((), ())), preferred_element_type=f32)


def norm_rows(values, gain):
    scale = lax.rsqrt(jnp.mean(values * values, axis=-1, keepdims=True) + 1e-05)
    unit = values * scale
    return unit * gain, unit, scale


def norm_back(grad, unit, scale, gain):
    pulled = grad * gain
    inner = jnp.mean(pulled * unit, axis=-1, keepdims=True)
    return scale * (pulled - unit * inner), jnp.sum(grad * unit, axis=0)


def spread(values):
    mine = [values] + [other(values, "tensor", s) for s in range(1, lax.axis_size("tensor"))]
    theirs = [neighbour_order(other(v, "mp", 1), 1, 1) for v in mine]
    return jnp.concatenate(mine + theirs, axis=0)


def collect(partial):
    ways = lax.axis_size("tensor")
    rows = partial.rows // 2
    theirs = partial(rows, 2 * rows).astype(bf16)
    back = neighbour_order(other(theirs, "mp", 1), 1, 1)
    joined = partial(0, rows) + back.astype(f32)
    piece = rows // ways
    total = joined[:piece]
    for s in range(1, ways):
        total = total + other(joined[s * piece:(s + 1) * piece].astype(bf16), "tensor", s).astype(f32)
    return total


class Rows:
    def __init__(self, rows, body):
        self.rows = rows
        self.body = body

    def __call__(self, start, stop):
        return self.body(start, stop)


def over_dp(value):
    bit = 1
    while bit < lax.axis_size("dp"):
        low = value.astype(bf16)
        value = low.astype(f32) + other(low, "dp", bit).astype(f32)
        bit *= 2
    return value


def shards(
    tokens,
    norm_gain,
    w_proj,
    w_beta,
    conv_weight,
    out_gain,
    w_out,
    mlp_gain,
    w_in,
    w_down,
    cotangent,
    starts,
    lengths,
):
    assert lax.axis_size("mp") == 4 and starts.shape[0] == 1
    m = lax.axis_index("mp")
    core = m & 1
    place = m * lax.axis_size("tensor") + lax.axis_index("tensor")
    block = w_proj.shape[1]
    near_blocks = 2 * block

    inputs = own_order(tokens, m, 1).astype(f32)
    gain_one = own_order(norm_gain, m, 0)
    gain_two = own_order(mlp_gain, m, 0)
    scaled, unit_one, scale_one = norm_rows(inputs, gain_one)
    scaled = scaled.astype(bf16)

    pieces, _, wide = w_proj.shape
    head = wide // 4
    heads = [
        lax.dynamic_slice_in_dim(w_proj, (j ^ m) * head, head, 2).transpose(1, 0, 2).reshape(block, pieces * head)
        for j in range(4)
    ]
    pair = lambda values, i, j, axis: jnp.concatenate([values[i], values[j]], axis)
    full_proj = jnp.concatenate(
        [
            pair(heads, 0, 2, 1),
            other(pair(heads, 1, 3, 1), "mp", 1),
            other(pair(heads, 2, 0, 1), "mp", 2),
            other(pair(heads, 3, 1, 1), "mp", 3),
        ],
        axis=0,
    )
    beta_rows = w_beta.T
    full_beta = own_order(
        jnp.concatenate([beta_rows] + [other(beta_rows, "mp", s) for s in range(1, 4)], axis=1), m, 0
    )
    full_beta = jnp.concatenate([full_beta[0:1], full_beta[2:3]], axis=0)

    normed = spread(scaled)
    far_out = matmul(normed, full_proj[:, pieces * head:]).astype(bf16)
    logits = matmul(full_beta, normed, ((1,), (1,))).astype(bf16)
    far = other(far_out, "mp", 2)
    far_logit = other(logits[1:2], "mp", 2)
    near = matmul(normed, full_proj[:, : pieces * head]).astype(bf16)
    chunk_rows = (-1, LANES)
    logit = jnp.concatenate([logits[0].reshape(chunk_rows), far_logit.reshape(chunk_rows)], axis=0).astype(f32)

    w_out, w_in, w_down = after((w_out, w_in, w_down), far)
    out_rows = [lax.dynamic_slice_in_dim(w_out, (j ^ m) * head, head, 0) for j in range(4)]
    full_out = jnp.concatenate(
        [
            pair(out_rows, 0, 2, 0),
            other(pair(out_rows, 1, 3, 0), "mp", 1),
            other(pair(out_rows, 2, 0, 0), "mp", 2),
            other(pair(out_rows, 3, 1, 0), "mp", 3),
        ],
        axis=1,
    )
    units = w_down.shape[0]
    half = LANES * ((units // LANES + 1) // 2)
    ours_in = lax.dynamic_slice_in_dim(w_in, core * (units - half), half, 2)
    theirs_in = lax.dynamic_slice_in_dim(w_in, (1 - core) * (units - half), half, 2)
    far_in = other(ours_in, "mp", 2)
    diag_in = other(theirs_in, "mp", 3)
    full_in = jnp.concatenate([ours_in, other(theirs_in, "mp", 1), far_in, diag_in], axis=1)
    w_down = after(w_down, far_in, diag_in)
    ours_down = lax.dynamic_slice_in_dim(w_down, core * (units - half), half, 0)
    theirs_down = lax.dynamic_slice_in_dim(w_down, (1 - core) * (units - half), half, 0)
    full_down = jnp.concatenate(
        [ours_down, other(theirs_down, "mp", 1), other(ours_down, "mp", 2), other(theirs_down, "mp", 3)], axis=1
    )
    live = (lax.broadcasted_iota(jnp.int32, (1, half), 1) >= core * (2 * half - units)).astype(f32)

    taps = conv_weight.reshape(3, conv_weight.shape[1], head)
    info = jnp.stack([lengths[0], place]).astype(jnp.int32)
    head_args = (near, far, logit, taps, out_gain[None], starts[0], info)
    mixed, norm_total, kept = head_forward(*head_args)
    count = near.shape[0]
    mixed_tok = jnp.concatenate([mixed[:count], other(mixed[count:], "mp", 2)], axis=1)
    branch = collect(Rows(count, lambda a, b: matmul(mixed_tok[a:b], full_out)))
    middle = inputs + branch
    scaled_two, unit_two, scale_two = norm_rows(middle, gain_two)
    normed_two = spread(scaled_two.astype(bf16))

    cot_own = own_order(cotangent, m, 1)
    cot_all = spread(after(cot_own, normed))
    gate = matmul(normed_two, full_in[0])
    up = matmul(normed_two, full_in[1])
    sigma = jax.nn.sigmoid(gate)
    activated = gate * sigma
    hidden = (activated * up * live).astype(bf16)
    d_hidden = matmul(cot_all, full_down, ((1,), (1,)))
    d_hidden = d_hidden * live
    d_gate = (d_hidden * up * sigma * (1.0 + gate * (1.0 - sigma))).astype(bf16)
    d_up = (d_hidden * activated).astype(bf16)
    d_normed_two = collect(
        Rows(
            count,
            lambda a, b: matmul(d_gate[a:b], full_in[0], ((1,), (1,))) + matmul(d_up[a:b], full_in[1], ((1,), (1,))),
        )
    )
    d_mid_norm, g_mlp = norm_back(d_normed_two, unit_two, scale_two, gain_two)
    d_middle = cot_own.astype(f32) + d_mid_norm
    feed = collect(Rows(count, lambda a, b: matmul(hidden[a:b], full_down)))
    output = own_order((middle + feed).astype(bf16), m, 1)

    tn = ((0,), (0,))

    def joined_units(mine, theirs, axis):
        gap = units - half
        low = jnp.where(core == 0, mine, theirs)
        high = jnp.where(core == 0, theirs, mine)
        zero = jnp.zeros_like(lax.slice_in_dim(low, 0, gap, axis=axis))
        return jnp.concatenate([low, zero], axis) + jnp.concatenate([zero, high], axis)

    def far_sum(product, lhs, rhs, axis, swap=None):
        cut = lambda v, a, b: lax.slice_in_dim(v, a, b, axis=1)
        if axis == 0:
            sent = product(cut(lhs, near_blocks, 2 * near_blocks), rhs).astype(bf16)
            held = product(cut(lhs, 0, near_blocks), rhs)
        else:
            sent = product(lhs, cut(rhs, near_blocks, 2 * near_blocks)).astype(bf16)
            held = product(lhs, cut(rhs, 0, near_blocks))
        back = other(sent, "mp", 2)
        if swap is not None:
            back = neighbour_order(back, swap, 1, 2)
        return (held + back.astype(f32)).astype(bf16)

    grad_dot = lambda a, b: matmul(a, b, tn)
    down_two = far_sum(grad_dot, hidden, cot_all, 1)
    down_mine = down_two[:, :block]
    g_down = over_dp(joined_units(down_mine, other(down_two[:, block:], "mp", 1), 0))
    in_sums = []
    for grad in (d_gate, d_up):
        in_two = far_sum(grad_dot, normed_two, grad, 0)
        in_sums.append(over_dp(joined_units(in_two[:block], other(in_two[block:], "mp", 1), 1)))
    g_in = jnp.stack(in_sums)

    d_mid_all = spread(d_middle.astype(bf16))
    d_mixed = matmul(d_mid_all, full_out, ((1,), (1,))).astype(bf16)
    d_far = other(d_mixed[:, head:], "mp", 2)
    out_two = far_sum(grad_dot, mixed_tok, d_mid_all, 1, swap=0)
    out_theirs = other(out_two[:, block:], "mp", 1)
    out_mine = out_two[:, :block]
    g_out = over_dp(
        own_order(
            jnp.concatenate([out_mine[:head], out_theirs[:head], out_mine[head:], out_theirs[head:]], axis=0), m, 0
        )
    )
    d_heads, d_logit, d_taps, g_head_gain = head_backward(d_mixed[:, :head], d_far, *head_args, kept)
    d_proj = jnp.concatenate([d_heads[:count], other(d_heads[count:], "mp", 2)], axis=1)
    d_logit = d_logit.astype(bf16)
    half_chunks = d_logit.shape[0] // 2
    d_logits = jnp.concatenate(
        [d_logit[:half_chunks].reshape(1, count), other(d_logit[half_chunks:], "mp", 2).reshape(1, count)], axis=0
    )
    d_normed = collect(
        Rows(
            count,
            lambda a, b: matmul(d_proj[a:b], full_proj, ((1,), (1,))) + matmul(d_logits[:, a:b], full_beta, tn),
        )
    )
    proj_two = far_sum(grad_dot, normed, d_proj, 0, swap=1)
    proj_mine = proj_two[:block]
    proj_theirs = other(proj_two[block:], "mp", 1)
    span = pieces * head
    g_proj = over_dp(
        jnp.concatenate(
            [proj_mine[:, :span], proj_theirs[:, :span], proj_mine[:, span:], proj_theirs[:, span:]], axis=1
        )
    )
    g_proj = jnp.concatenate(
        [
            lax.dynamic_slice_in_dim(g_proj, (h ^ m) * span, span, 1).reshape(block, pieces, head).transpose(1, 0, 2)
            for h in range(4)
        ],
        axis=2,
    )
    beta_part = matmul(d_logits, normed)
    beta_back = neighbour_order(neighbour_order(other(beta_part, "mp", 2), 0, 1, 2), 1, 1, 2)
    beta_two = beta_part + beta_back
    beta_theirs = other(beta_two[:, block:near_blocks], "mp", 1)
    beta_rows = own_order(
        jnp.concatenate([beta_two[:1, :block], beta_theirs[:1], beta_two[1:, :block], beta_theirs[1:]], axis=0), m, 0
    )
    bit = 1
    while bit < lax.axis_size("dp"):
        beta_rows = beta_rows + other(beta_rows, "dp", bit)
        d_taps = d_taps + other(d_taps, "dp", bit)
        bit *= 2
    d_in_norm, g_norm = norm_back(d_normed, unit_one, scale_one, gain_one)
    d_tokens = own_order(d_middle + d_in_norm, m, 1)
    sum_norm, sum_mlp, sum_head, norm_all = lax.psum(
        (own_order(g_norm, m, 0), own_order(g_mlp, m, 0), g_head_gain[0], norm_total), ("dp", "mp", "tensor")
    )
    ways = lax.axis_size("mp") * lax.axis_size("tensor")
    state_norm = norm_all / (ways * lax.axis_size("dp") * (2 * count // BLOCK))
    return (
        output,
        d_tokens,
        sum_norm,
        g_proj,
        beta_rows.T,
        d_taps.reshape(conv_weight.shape),
        sum_head,
        g_out,
        sum_mlp,
        g_in,
        g_down,
        state_norm,
    )


def solution(mesh):
    placed = (
        P(("dp", "mp", "tensor"), None),
        P(),
        P(None, "mp", "tensor"),
        P("mp", "tensor"),
        P(None, None, "tensor", "mp", None),
        P(),
        P("tensor", "mp"),
        P(),
        P(None, "mp", "tensor"),
        P("tensor", "mp"),
        P(("dp", "mp", "tensor"), None),
        P("dp", None),
        P("dp"),
    )
    return jax.shard_map(
        shards,
        mesh=mesh,
        in_specs=placed,
        out_specs=(
            P(("dp", "mp", "tensor"), None),
            P(("dp", "mp", "tensor"), None),
            P(),
            P(None, "mp", "tensor"),
            P("mp", "tensor"),
            P(None, None, "tensor", "mp", None),
            P(),
            P("tensor", "mp"),
            P(),
            P(None, "mp", "tensor"),
            P("tensor", "mp"),
            P(),
        ),
        check_vma=False,
    )
```

time: 1670 us -> 871 us (0.52)
  waiting for transfers between devices: 1180 us -> 484 us
  blocking collectives: 130 us -> 38.3 us
  starting transfers between devices: 12.8 us -> 103 us
  local copies, waits for them, and re-layouts: 84.9 us -> 37.6 us
  matrix products: 121 us -> 82.2 us
    ppermute x0 -> x84, waiting for transfers between devices: none -> 484 us  [other(): return lax.ppermute(value, axis, [(i, i ^ bit) for i in range(size)])]
    reduce_scatter x8 -> x0, waiting for transfers between devices: 463 us -> none  [the longest x4 258 us: collect(): return lax.psum_scatter(values, 'tensor', scatter_dimension=0, tiled=True)]
    all_gather x8 -> x0, waiting for transfers between devices: 337 us -> none  [the longest x4 168 us: spread(): return lax.all_gather(values, 'tensor', axis=0, tiled=True)]
    psum x1 -> x0, waiting for transfers between devices: 316 us -> none  [shards(): lax.psum((rows_proj, rows_beta, rows_out, rows_in, rows_down, g_conv), 'dp')]
    ppermute x0 -> x84, starting transfers between devices: none -> 103 us  [other(): return lax.ppermute(value, axis, [(i, i ^ bit) for i in range(size)])]
    all_to_all x3 -> x0, blocking collectives: 70.7 us -> none  [the longest x1 51 us: shards(): lax.all_to_all(shortened(d_proj_heads), 'mp', split_axis=1, concat_axis=2...]
    dot_general x14 -> x30, matrix products: 118 us -> 82.2 us  [matmul(): return lax.dot_general(a, b, (dims, ((), ())), preferred_element_type=f32)]
    all_to_all x3 -> x0, waiting for transfers between devices: 33.1 us -> none  [the longest x1 24.4 us: shards(): lax.all_to_all(projected, 'mp', split_axis=2, concat_axis=1, tiled=True)]
  transfers between devices with their start and end apart: 21 -> 84, of which waited for: 17 -> 32; matrix products, arithmetic and copies ran while one was open for 11% -> 13% of each run, Pallas kernels for 4% -> 9%
where the time goes in v2:
time: 871 us; the launch traced here: 865 us
  waiting for transfers between devices  484 us (56%)
  starting transfers between devices  103 us (12%)
  matrix products  82.2 us (9%)
  Pallas kernels  74.8 us (9%)
  other arithmetic  39.8 us (5%)
  blocking collectives  38.3 us (4%)
  local copies, waits for them, and re-layouts  37.6 us (4%)
    ppermute x84, waiting for transfers between devices, other(): return lax.ppermute(value, axis, [(i, i ^ bit) for i in range(size)])  484 us
    ppermute x84, starting transfers between devices, other(): return lax.ppermute(value, axis, [(i, i ^ bit) for i in range(size)])  103 us
    dot_general x30, matrix products, matmul(): return lax.dot_general(a, b, (dims, ((), ())), preferred_element_type=f32)  82.2 us
    pallas_call x1, Pallas kernels, head_forward(): pl.pallas_call(forward_body, grid_spec=pltpu.PrefetchScalarGridSpec(num_s...  40.4 us
    psum x1, blocking collectives, shards(): lax.psum((own_order(g_norm, m, 0), own_order(g_mlp, m, 0), g_head_gain[0]...  38.3 us
    pallas_call x1, Pallas kernels, head_backward(): pl.pallas_call(backward_body, grid_spec=pltpu.PrefetchScalarGridSpec(num_...  34.5 us
    unnamed x141, local copies, waits for them, and re-layouts  22.2 us
  transfers between devices with their start and end apart: 84, of which 32 were waited for; matrix products, arithmetic and copies ran while one was open for 13% of the time, Pallas kernels for 9%

profile of v2, /device:TPU:0, one launch (start us, length us, event | category | flops | bytes accessed | tf_op | source)
XLA Modules:
  0.0 865.5 jit_solution(14139064816200657523)
XLA Ops:
  4.9 3.1 collective-permute-start
  7.9 2.6 collective-permute-start.1
  24.8 6.4 collective-permute-done
  34.8 10.4 %collective-permute-done.1 = bf16[128,2048]{1,0:T(8,128)(2,1)} collective-permute-done((bf16[128,2048]{1,0:T(8,128)(2,1)}, bf16[128,2048]{1,0:T(8,128)(2,1)}, u32[]{:S(2)}, u32[]{:S(2)}) %collective-permute-start.1) | collective-permute-done | bytes 524320 | tf_op jit(solution)/shard_map/ppermute | solution.py:442
  52.5 18.8 %collective-permute-done.8 = bf16[512,1024]{0,1:T(8,128)(2,1)S(1)} collective-permute-done((bf16[512,1024]{0,1:T(8,128)(2,1)}, bf16[512,1024]{0,1:T(8,128)(2,1)S(1)}, u32[]{:S(2)}, u32[]{:S(2)}) %collective-permute-start.8) | collective-permute-done | bytes 1048608 | tf_op jit(solution)/shard_map/ppermute | solution.py:442
  71.3 5.1 pad_maximum_fusion.2
  76.5 3.3 fusion.54.near_ref.before_near_ref
  79.8 3.3 fusion.57
  88.1 3.5 collective-permute-start.41
  91.7 16.4 %collective-permute-done.14 = bf16[1,1024]{1,0:T(2,128)(2,1)S(1)} collective-permute-done((bf16[1,1024]{1,0:T(2,128)(2,1)S(1)}, bf16[1,1024]{1,0:T(2,128)(2,1)S(1)}, u32[]{:S(2)}, u32[]{:S(2)}) %collective-permute-start.14) | collective-permute-done | bytes 2080 | tf_op jit(solution)/shard_map/ppermute | solution.py:442
  111.6 40.4 %head_forward.1 = (bf16[2048,128]{1,0:T(8,128)(2,1)}, f32[8,128]{1,0:T(8,128)}, f32[3,2048,128]{2,1,0:T(8,128)}, f32[2048,256]{1,0:T(8,128)}, f32[2048,128]{1,0:...) custom-call(s32[8]{0:T(128)} %bitcast.114, ...), custom_call_target="tpu_custom_call" | custom-call | tf_op jit(solution)/shard_map/head_forward/pallas_call | solution.py:367
  159.9 2.4 collective-permute-done.15
  162.3 4.7 collective-permute-done.18
  167.7 5.3 collective-permute-done.17
  181.2 30.6 %collective-permute-done.32 = bf16[2,512,768]{2,1,0:T(8,128)(2,1)S(1)} collective-permute-done((bf16[2,512,768]{2,1,0:T(8,128)(2,1)S(1)}, bf16[2,512,768]{2,1,0:T(8,128)(2,1)S(1)}, u32[]{:S(2)}, u32[]{:S(2)}) %collective-permute-start.32) | collective-permute-done | bytes 1572896 | tf_op jit(solution)/shard_map/ppermute | solution.py:442
  211.8 33.9 %collective-permute-done.31 = bf16[2,512,768]{2,1,0:T(8,128)(2,1)S(1)} collective-permute-done((bf16[2,512,768]{2,1,0:T(8,128)(2,1)S(1)}, bf16[2,512,768]{2,1,0:T(8,128)(2,1)S(1)}, u32[]{:S(2)}, u32[]{:S(2)}) %collective-permute-start.31) | collective-permute-done | bytes 1572896 | tf_op jit(solution)/shard_map/ppermute | solution.py:442
  248.6 3.7 collective-permute-start.22
  253.5 11.9 %collective-permute-done.22 = bf16[128,2048]{1,0:T(8,128)(2,1)S(1)} collective-permute-done((bf16[128,2048]{1,0:T(8,128)(2,1)S(1)}, bf16[128,2048]{1,0:T(8,128)(2,1)S(1)}, u32[]{:S(2)}, u32[]{:S(2)}) %collective-permute-start.22) | collective-permute-done | bytes 524320 | tf_op jit(solution)/shard_map/ppermute | solution.py:442
  266.0 30.4 %collective-permute-done.21 = bf16[128,2048]{1,0:T(8,128)(2,1)S(1)} collective-permute-done((bf16[128,2048]{1,0:T(8,128)(2,1)S(1)}, bf16[128,2048]{1,0:T(8,128)(2,1)S(1)}, u32[]{:S(2)}, u32[]{:S(2)}) %collective-permute-start.21) | collective-permute-done | bytes 524320 | tf_op jit(solution)/shard_map/ppermute | solution.py:442
  297.2 3.0 collective-permute-start.24
  301.6 5.1 fusion.136
  306.7 13.7 %collective-permute-done.23 = bf16[128,2048]{1,0:T(8,128)(2,1)S(1)} collective-permute-done((bf16[128,2048]{1,0:T(8,128)(2,1)S(1)}, bf16[128,2048]{1,0:T(8,128)(2,1)S(1)}, u32[]{:S(2)}, u32[]{:S(2)}) %collective-permute-start.23) | collective-permute-done | bytes 524320 | tf_op jit(solution)/shard_map/ppermute | solution.py:442
  320.4 15.0 %collective-permute-done.24 = bf16[128,2048]{1,0:T(8,128)(2,1)S(1)} collective-permute-done((bf16[128,2048]{1,0:T(8,128)(2,1)S(1)}, bf16[128,2048]{1,0:T(8,128)(2,1)S(1)}, u32[]{:S(2)}, u32[]{:S(2)}) %collective-permute-start.24) | collective-permute-done | bytes 524320 | tf_op jit(solution)/shard_map/ppermute | solution.py:442
  338.2 3.4 fusion.5
  341.6 7.4 multiply_convert_fusion.1
  349.0 3.8 fusion.3
  355.4 4.0 add_convert_fusion.2
  365.5 4.1 convolution_convert_fusion.1
  369.7 3.8 fusion.4
  373.5 18.6 %collective-permute-done.78 = bf16[1024,768]{1,0:T(8,128)(2,1)S(1)} collective-permute-done((bf16[1024,768]{1,0:T(8,128)(2,1)S(1)}, bf16[1024,768]{1,0:T(8,128)(2,1)S(1)}, u32[]{:S(2)}, u32[]{:S(2)}) %collective-permute-start.78) | collective-permute-done | bytes 1572896 | tf_op jit(solution)/shard_map/ppermute | solution.py:442
  392.1 1.9 add_convert_fusion.4
  394.2 31.7 %collective-permute-done.75 = bf16[1024,768]{1,0:T(8,128)(2,1)} collective-permute-done((bf16[1024,768]{1,0:T(8,128)(2,1)S(1)}, bf16[1024,768]{1,0:T(8,128)(2,1)}, u32[]{:S(2)}, u32[]{:S(2)}) %collective-permute-start.75) | collective-permute-done | bytes 1572896 | tf_op jit(solution)/shard_map/ppermute | solution.py:442
  425.9 3.3 add_convert_fusion.5
  429.4 29.3 %collective-permute-done.81 = bf16[768,1024]{1,0:T(8,128)(2,1)S(1)} collective-permute-done((bf16[768,1024]{1,0:T(8,128)(2,1)S(1)}, bf16[768,1024]{1,0:T(8,128)(2,1)S(1)}, u32[]{:S(2)}, u32[]{:S(2)}) %collective-permute-start.81) | collective-permute-done | bytes 1572896 | tf_op jit(solution)/shard_map/ppermute | solution.py:442
  460.9 4.8 fusion.181
  465.9 2.5 collective-permute-start.50
  468.4 8.5 collective-permute-start.49
  477.1 3.0 fusion.182
  480.5 2.4 collective-permute-start.39
  484.4 21.2 %collective-permute-start.37 = (bf16[128,2048]{1,0:T(8,128)(2,1)S(1)}, bf16[128,2048]{1,0:T(8,128)(2,1)S(1)}, u32[]{:S(2)}, u32[]{:S(2)}) collective-permute-start(bf16[128,2048]{1,0:T(8,128)(2,1)S(1)} %get-tuple-element.128), channel_id=1, source_target_pairs={{0,1},{1,0},{2,3},{3,2},{4,5},{5,4},{6,7},{7,6},{8,9},{9,8},{10,11... | collective-permute-start | bytes 1572872 | tf_op jit(solution)/shard_map/ppermute | solution.py:442
  505.8 32.4 %collective-permute-done.49 = bf16[128,2048]{1,0:T(8,128)(2,1)S(1)} collective-permute-done((bf16[128,2048]{1,0:T(8,128)(2,1)S(1)}, bf16[128,2048]{1,0:T(8,128)(2,1)S(1)}, u32[]{:S(2)}, u32[]{:S(2)}) %collective-permute-start.49) | collective-permute-done | bytes 524320 | tf_op jit(solution)/shard_map/ppermute | solution.py:442
  540.3 20.4 %collective-permute-done.38 = bf16[128,2048]{1,0:T(8,128)(2,1)S(1)} collective-permute-done((bf16[128,2048]{1,0:T(8,128)(2,1)S(1)}, bf16[128,2048]{1,0:T(8,128)(2,1)S(1)}, u32[]{:S(2)}, u32[]{:S(2)}) %collective-permute-start.38) | collective-permute-done | bytes 524320 | tf_op jit(solution)/shard_map/ppermute | solution.py:442
  563.1 3.0 collective-permute-start.52
  568.5 19.2 %collective-permute-done.51 = bf16[128,2048]{1,0:T(8,128)(2,1)S(1)} collective-permute-done((bf16[128,2048]{1,0:T(8,128)(2,1)S(1)}, bf16[128,2048]{1,0:T(8,128)(2,1)S(1)}, u32[]{:S(2)}, u32[]{:S(2)}) %collective-permute-start.51) | collective-permute-done | bytes 524320 | tf_op jit(solution)/shard_map/ppermute | solution.py:442
  587.8 13.7 %collective-permute-done.52 = bf16[128,2048]{1,0:T(8,128)(2,1)S(1)} collective-permute-done((bf16[128,2048]{1,0:T(8,128)(2,1)S(1)}, bf16[128,2048]{1,0:T(8,128)(2,1)S(1)}, u32[]{:S(2)}, u32[]{:S(2)}) %collective-permute-start.52) | collective-permute-done | bytes 524320 | tf_op jit(solution)/shard_map/ppermute | solution.py:442
  612.6 21.0 %collective-permute-done.83 = bf16[1408,512]{1,0:T(8,128)(2,1)S(1)} collective-permute-done((bf16[1408,512]{1,0:T(8,128)(2,1)S(1)}, bf16[1408,512]{1,0:T(8,128)(2,1)S(1)}, u32[]{:S(2)}, u32[]{:S(2)}) %collective-permute-start.83) | collective-permute-done | bytes 1441824 | tf_op jit(solution)/shard_map/ppermute | solution.py:442
  633.6 2.0 convert_add_fusion.5
  635.6 2.9 pad_maximum_fusion.1
  639.2 34.5 %head_backward.1 = (bf16[2048,512]{1,0:T(8,128)(2,1)}, f32[16,128]{1,0:T(8,128)}, f32[3,4,128]{2,1,0:T(4,128)}, f32[8,128]{1,0:T(8,128)}) custom-call(s32[8]{0:T(128)} %bitcast.115, s32[2]{0:T(128)} %pad_add_fusion.3.info_ref, bf16[1024,512]{1,0:T(8,128)(2,1)} %fusion.54.near_ref.before_near_ref, bf16[1024,512]{1,0:T(8,128)(2,1)} %copy-done.2, ...), custom_call_target="tpu_custom_call" | custom-call | tf_op jit(solution)/shard_map/head_backward/pallas_call | solution.py:414
  684.0 15.9 %collective-permute-done.68 = f32[2,2048]{1,0:T(2,128)S(1)} collective-permute-done((f32[2,2048]{1,0:T(2,128)S(1)}, f32[2,2048]{1,0:T(2,128)S(1)}, u32[]{:S(2)}, u32[]{:S(2)}) %collective-permute-start.68) | collective-permute-done | bytes 16416 | tf_op jit(solution)/shard_map/ppermute | solution.py:442
  701.3 3.8 fusion.22
  706.6 2.3 add_convert_fusion.1
  709.0 2.3 fusion.66
  715.3 37.7 %collective-permute-done.65 = bf16[1024,1024]{0,1:T(8,128)(2,1)S(1)} collective-permute-done((bf16[1024,1024]{0,1:T(8,128)(2,1)}, bf16[1024,1024]{0,1:T(8,128)(2,1)S(1)}, u32[]{:S(2)}, u32[]{:S(2)}) %collective-permute-start.65) | collective-permute-done | bytes 2097184 | tf_op jit(solution)/shard_map/ppermute | solution.py:442
  753.2 2.6 add_convert_fusion
  756.1 5.4 fusion.183
  761.7 2.6 collective-permute-start.64
  771.5 7.0 collective-permute-done.64
  778.5 30.4 %collective-permute-done.63 = bf16[128,2048]{1,0:T(8,128)(2,1)S(1)} collective-permute-done((bf16[128,2048]{1,0:T(8,128)(2,1)S(1)}, bf16[128,2048]{1,0:T(8,128)(2,1)S(1)}, u32[]{:S(2)}, u32[]{:S(2)}) %collective-permute-start.63) | collective-permute-done | bytes 524320 | tf_op jit(solution)/shard_map/ppermute | solution.py:442
  809.0 2.6 fusion.74
  811.7 38.3 %all-reduce.6 = (f32[2048]{0:T(1024)}, f32[128]{0:T(128)}, f32[2048]{0:T(1024)}, f32[]{:T(128)}) all-reduce(f32[2048]{0:T(1024)S(1)} %pad_maximum_fusion.30, f32[128]{0:T(128)S(1)} %slice_bitcast_fusion.11, f32[2048]{0:T(1024)S(1)} %pad_maximum_fusion.33, f32[]{:T(128)} %bitcast.33), channel_id=1, replica_groups=mesh['dp'=2,'mp'=4,'tensor'=4] {'dp','mp','tensor'}, use_global_device_ids=true, to_apply=%region_5.6 | all-reduce | flops 4225 | bytes 33800 | tf_op jit(solution)/shard_map/psum | solution.py:720
  853.7 2.2 convert_add_fusion
  856.4 2.5 pad_maximum_fusion.3
  858.8 5.2 copy.32
  (407 shorter events, 123.4 us)
Async XLA Ops:
  4.9 26.4 %collective-permute-start = (bf16[128,2048]{1,0:T(8,128)(2,1)}, bf16[128,2048]{1,0:T(8,128)(2,1)}, u32[]{:S(2)}, u32[]{:S(2)}) collective-permute-start(bf16[128,2048]{1,0:T(8,128)(2,1)} %get-tuple-element.92), channel_id=1, source_target_pairs={{0,1},{1,0},{2,3},{3,2},{4,5},{5,4},{6,7},{7,6},{8,9},{9,8},{10,11... | collective-permute-start | bytes 1572872 | tf_op jit(solution)/shard_map/ppermute | solution.py:442
  7.9 37.3 %collective-permute-start.1 = (bf16[128,2048]{1,0:T(8,128)(2,1)}, bf16[128,2048]{1,0:T(8,128)(2,1)}, u32[]{:S(2)}, u32[]{:S(2)}) collective-permute-start(bf16[128,2048]{1,0:T(8,128)(2,1)} %get-tuple-element.92), channel_id=1, source_target_pairs={{0,2},{1,3},{2,0},{3,1},{4,6},{5,7},{6,4},{7,5},{8,10},{9,11},{10,... | collective-permute-start | bytes 1572872 | tf_op jit(solution)/shard_map/ppermute | solution.py:442
  22.9 24.1 %collective-permute-start.2 = (bf16[128,2048]{1,0:T(8,128)(2,1)}, bf16[128,2048]{1,0:T(8,128)(2,1)S(1)}, u32[]{:S(2)}, u32[]{:S(2)}) collective-permute-start(bf16[128,2048]{1,0:T(8,128)(2,1)} %get-tuple-element.92), channel_id=1, source_target_pairs={{0,3},{1,2},{2,1},{3,0},{4,7},{5,6},{6,5},{7,4},{8,11},{9,10},{10,... | collective-permute-start | bytes 1572872 | tf_op jit(solution)/shard_map/ppermute | solution.py:442
  23.0 25.5 %collective-permute-start.3 = (bf16[128,2048]{1,0:T(8,128)(2,1)}, bf16[128,2048]{1,0:T(8,128)(2,1)S(1)}, u32[]{:S(2)}, u32[]{:S(2)}) collective-permute-start(bf16[128,2048]{1,0:T(8,128)(2,1)} %get-tuple-element.92), channel_id=1, source_target_pairs={{0,4},{4,0},{8,12},{12,8},{1,5},{5,1},{9,13},{13,9},{2,6},{6,2},{1... | collective-permute-start | bytes 1572872 | tf_op jit(solution)/shard_map/ppermute | solution.py:442
  23.2 29.4 %collective-permute-start.9 = (bf16[512,1024]{0,1:T(8,128)(2,1)}, bf16[512,1024]{0,1:T(8,128)(2,1)S(1)}, u32[]{:S(2)}, u32[]{:S(2)}) collective-permute-start(bf16[512,1024]{0,1:T(8,128)(2,1)} %get-tuple-element.156), channel_id=1, source_target_pairs={{0,12},{4,8},{8,4},{12,0},{1,13},{5,9},{9,5},{13,1},{2,14},{6,10},... | collective-permute-start | bytes 3145736 | tf_op jit(solution)/shard_map/ppermute | solution.py:442
  31.3 40.0 %collective-permute-start.8 = (bf16[512,1024]{0,1:T(8,128)(2,1)}, bf16[512,1024]{0,1:T(8,128)(2,1)S(1)}, u32[]{:S(2)}, u32[]{:S(2)}) collective-permute-start(bf16[512,1024]{0,1:T(8,128)(2,1)} %pad_maximum_fusion.10), channel_id=1, source_target_pairs={{0,8},{4,12},{8,0},{12,4},{1,9},{5,13},{9,1},{13,5},{2,10},{6,14},... | collective-permute-start | bytes 3145736 | tf_op jit(solution)/shard_map/ppermute | solution.py:442
  45.2 26.1 %collective-permute-start.7 = (bf16[512,1024]{0,1:T(8,128)(2,1)}, bf16[512,1024]{0,1:T(8,128)(2,1)S(1)}, u32[]{:S(2)}, u32[]{:S(2)}) collective-permute-start(bf16[512,1024]{0,1:T(8,128)(2,1)} %get-tuple-element.155), channel_id=1, source_target_pairs={{0,4},{4,0},{8,12},{12,8},{1,5},{5,1},{9,13},{13,9},{2,6},{6,2},{1... | collective-permute-start | bytes 3145736 | tf_op jit(solution)/shard_map/ppermute | solution.py:442
  83.2 27.4 %collective-permute-start.10 = (bf16[1024,512]{1,0:T(8,128)(2,1)}, bf16[1024,512]{1,0:T(8,128)(2,1)S(1)}, u32[]{:S(2)}, u32[]{:S(2)}) collective-permute-start(bf16[1024,512]{1,0:T(8,128)(2,1)} %fusion.57), channel_id=1, source_target_pairs={{0,8},{4,12},{8,0},{12,4},{1,9},{5,13},{9,1},{13,5},{2,10},{6,14},... | collective-permute-start | bytes 3145736 | tf_op jit(solution)/shard_map/ppermute | solution.py:442
  84.7 24.0 %collective-permute-start.40 = (bf16[128,2048]{1,0:T(8,128)(2,1)S(1)}, bf16[128,2048]{1,0:T(8,128)(2,1)}, u32[]{:S(2)}, u32[]{:S(2)}) collective-permute-start(bf16[128,2048]{1,0:T(8,128)(2,1)S(1)} %pad_maximum_fusion.17), channel_id=1, source_target_pairs={{0,1},{1,0},{2,3},{3,2},{4,5},{5,4},{6,7},{7,6},{8,9},{9,8},{10,11... | collective-permute-start | bytes 1572872 | tf_op jit(solution)/shard_map/ppermute | solution.py:442
  86.6 21.5 %collective-permute-start.14 = (bf16[1,1024]{1,0:T(2,128)(2,1)S(1)}, bf16[1,1024]{1,0:T(2,128)(2,1)S(1)}, u32[]{:S(2)}, u32[]{:S(2)}) collective-permute-start(bf16[1,1024]{1,0:T(2,128)(2,1)S(1)} %get-tuple-element.284), channel_id=1, source_target_pairs={{0,8},{4,12},{8,0},{12,4},{1,9},{5,13},{9,1},{13,5},{2,10},{6,14},... | collective-permute-start | bytes 6152 | tf_op jit(solution)/shard_map/ppermute | solution.py:442
  88.1 67.1 %collective-permute-start.41 = (bf16[128,2048]{1,0:T(8,128)(2,1)S(1)}, bf16[128,2048]{1,0:T(8,128)(2,1)}, u32[]{:S(2)}, u32[]{:S(2)}) collective-permute-start(bf16[128,2048]{1,0:T(8,128)(2,1)S(1)} %pad_maximum_fusion.17), channel_id=1, source_target_pairs={{0,2},{1,3},{2,0},{3,1},{4,6},{5,7},{6,4},{7,5},{8,10},{9,11},{10,... | collective-permute-start | bytes 1572872 | tf_op jit(solution)/shard_map/ppermute | solution.py:442
  91.6 82.3 %collective-permute-start.42 = (bf16[128,2048]{1,0:T(8,128)(2,1)S(1)}, bf16[128,2048]{1,0:T(8,128)(2,1)}, u32[]{:S(2)}, u32[]{:S(2)}) collective-permute-start(bf16[128,2048]{1,0:T(8,128)(2,1)S(1)} %pad_maximum_fusion.17), channel_id=1, source_target_pairs={{0,3},{1,2},{2,1},{3,0},{4,7},{5,6},{6,5},{7,4},{8,11},{9,10},{10,... | collective-permute-start | bytes 1572872 | tf_op jit(solution)/shard_map/ppermute | solution.py:442
  108.1 48.6 %collective-permute-start.43 = (bf16[128,2048]{1,0:T(8,128)(2,1)S(1)}, bf16[128,2048]{1,0:T(8,128)(2,1)}, u32[]{:S(2)}, u32[]{:S(2)}) collective-permute-start(bf16[128,2048]{1,0:T(8,128)(2,1)S(1)} %pad_maximum_fusion.17), channel_id=1, source_target_pairs={{0,4},{4,0},{8,12},{12,8},{1,5},{5,1},{9,13},{13,9},{2,6},{6,2},{1... | collective-permute-start | bytes 1572872 | tf_op jit(solution)/shard_map/ppermute | solution.py:442
  155.2 17.9 %collective-permute-start.17 = (bf16[256,512]{1,0:T(8,128)(2,1)S(1)}, bf16[256,512]{1,0:T(8,128)(2,1)S(1)}, u32[]{:S(2)}, u32[]{:S(2)}) collective-permute-start(bf16[256,512]{1,0:T(8,128)(2,1)S(1)} %pad_maximum_fusion.23), channel_id=1, source_target_pairs={{0,8},{4,12},{8,0},{12,4},{1,9},{5,13},{9,1},{13,5},{2,10},{6,14},... | collective-permute-start | bytes 786440 | tf_op jit(solution)/shard_map/ppermute | solution.py:442
  156.7 16.4 %collective-permute-start.16 = (bf16[256,512]{1,0:T(8,128)(2,1)S(1)}, bf16[256,512]{1,0:T(8,128)(2,1)S(1)}, u32[]{:S(2)}, u32[]{:S(2)}) collective-permute-start(bf16[256,512]{1,0:T(8,128)(2,1)S(1)} %get-tuple-element.251), channel_id=1, source_target_pairs={{0,4},{4,0},{8,12},{12,8},{1,5},{5,1},{9,13},{13,9},{2,6},{6,2},{1... | collective-permute-start | bytes 786440 | tf_op jit(solution)/shard_map/ppermute | solution.py:442
  162.3 15.3 %collective-permute-start.44 = (bf16[128,2048]{1,0:T(8,128)(2,1)}, bf16[128,2048]{1,0:T(8,128)(2,1)S(1)}, u32[]{:S(2)}, u32[]{:S(2)}) collective-permute-start(bf16[128,2048]{1,0:T(8,128)(2,1)} %collective-permute-done.40), channel_id=1, source_target_pairs={{0,4},{4,0},{8,12},{12,8},{1,5},{5,1},{9,13},{13,9},{2,6},{6,2},{1... | collective-permute-start | bytes 1572872 | tf_op jit(solution)/shard_map/ppermute | solution.py:442
  173.8 73.7 %collective-permute-start.19 = (bf16[512,2048]{1,0:T(8,128)(2,1)S(1)}, bf16[512,2048]{1,0:T(8,128)(2,1)S(1)}, u32[]{:S(2)}, u32[]{:S(2)}) collective-permute-start(bf16[512,2048]{1,0:T(8,128)(2,1)S(1)} %convolution_convert_fusion), channel_id=1, source_target_pairs={{0,4},{4,0},{8,12},{12,8},{1,5},{5,1},{9,13},{13,9},{2,6},{6,2},{1... | collective-permute-start | bytes 6291464 | tf_op jit(solution)/shard_map/ppermute | solution.py:442
  175.3 36.5 %collective-permute-start.32 = (bf16[2,512,768]{2,1,0:T(8,128)(2,1)S(1)}, bf16[2,512,768]{2,1,0:T(8,128)(2,1)S(1)}, u32[]{:S(2)}, u32[]{:S(2)}) collective-permute-start(bf16[2,512,768]{2,1,0:T(8,128)(2,1)S(1)} %get-tuple-element.101), channel_id=1, source_target_pairs={{0,12},{4,8},{8,4},{12,0},{1,13},{5,9},{9,5},{13,1},{2,14},{6,10},... | collective-permute-start | bytes 4718600 | tf_op jit(solution)/shard_map/ppermute | solution.py:442
  177.0 68.7 %collective-permute-start.31 = (bf16[2,512,768]{2,1,0:T(8,128)(2,1)S(1)}, bf16[2,512,768]{2,1,0:T(8,128)(2,1)S(1)}, u32[]{:S(2)}, u32[]{:S(2)}) collective-permute-start(bf16[2,512,768]{2,1,0:T(8,128)(2,1)S(1)} %get-tuple-element.100), channel_id=1, source_target_pairs={{0,8},{4,12},{8,0},{12,4},{1,9},{5,13},{9,1},{13,5},{2,10},{6,14},... | collective-permute-start | bytes 4718600 | tf_op jit(solution)/shard_map/ppermute | solution.py:442
  177.8 74.5 %collective-permute-start.30 = (bf16[2,512,768]{2,1,0:T(8,128)(2,1)S(1)}, bf16[2,512,768]{2,1,0:T(8,128)(2,1)S(1)}, u32[]{:S(2)}, u32[]{:S(2)}) collective-permute-start(bf16[2,512,768]{2,1,0:T(8,128)(2,1)S(1)} %get-tuple-element.101), channel_id=1, source_target_pairs={{0,4},{4,0},{8,12},{12,8},{1,5},{5,1},{9,13},{13,9},{2,6},{6,2},{1... | collective-permute-start | bytes 4718600 | tf_op jit(solution)/shard_map/ppermute | solution.py:442
  245.9 54.3 %collective-permute-start.35 = (bf16[768,512]{1,0:T(8,128)(2,1)S(1)}, bf16[768,512]{1,0:T(8,128)(2,1)S(1)}, u32[]{:S(2)}, u32[]{:S(2)}) collective-permute-start(bf16[768,512]{1,0:T(8,128)(2,1)S(1)} %get-tuple-element.147), channel_id=1, source_target_pairs={{0,12},{4,8},{8,4},{12,0},{1,13},{5,9},{9,5},{13,1},{2,14},{6,10},... | collective-permute-start | bytes 2359304 | tf_op jit(solution)/shard_map/ppermute | solution.py:442
  246.4 55.2 %collective-permute-start.33 = (bf16[768,512]{1,0:T(8,128)(2,1)S(1)}, bf16[768,512]{1,0:T(8,128)(2,1)S(1)}, u32[]{:S(2)}, u32[]{:S(2)}) collective-permute-start(bf16[768,512]{1,0:T(8,128)(2,1)S(1)} %get-tuple-element.147), channel_id=1, source_target_pairs={{0,4},{4,0},{8,12},{12,8},{1,5},{5,1},{9,13},{13,9},{2,6},{6,2},{1... | collective-permute-start | bytes 2359304 | tf_op jit(solution)/shard_map/ppermute | solution.py:442
  248.6 16.8 %collective-permute-start.22 = (bf16[128,2048]{1,0:T(8,128)(2,1)S(1)}, bf16[128,2048]{1,0:T(8,128)(2,1)S(1)}, u32[]{:S(2)}, u32[]{:S(2)}) collective-permute-start(bf16[128,2048]{1,0:T(8,128)(2,1)S(1)} %get-tuple-element.136), channel_id=1, source_target_pairs={{0,3},{1,2},{2,1},{3,0},{4,7},{5,6},{6,5},{7,4},{8,11},{9,10},{10,... | collective-permute-start | bytes 1572872 | tf_op jit(solution)/shard_map/ppermute | solution.py:442
  252.3 44.1 %collective-permute-start.21 = (bf16[128,2048]{1,0:T(8,128)(2,1)S(1)}, bf16[128,2048]{1,0:T(8,128)(2,1)S(1)}, u32[]{:S(2)}, u32[]{:S(2)}) collective-permute-start(bf16[128,2048]{1,0:T(8,128)(2,1)S(1)} %get-tuple-element.137), channel_id=1, source_target_pairs={{0,2},{1,3},{2,0},{3,1},{4,6},{5,7},{6,4},{7,5},{8,10},{9,11},{10,... | collective-permute-start | bytes 1572872 | tf_op jit(solution)/shard_map/ppermute | solution.py:442
  252.3 44.0 %collective-permute-start.20 = (bf16[128,2048]{1,0:T(8,128)(2,1)S(1)}, bf16[128,2048]{1,0:T(8,128)(2,1)S(1)}, u32[]{:S(2)}, u32[]{:S(2)}) collective-permute-start(bf16[128,2048]{1,0:T(8,128)(2,1)S(1)} %get-tuple-element.135), channel_id=1, source_target_pairs={{0,1},{1,0},{2,3},{3,2},{4,5},{5,4},{6,7},{7,6},{8,9},{9,8},{10,11... | collective-permute-start | bytes 1572872 | tf_op jit(solution)/shard_map/ppermute | solution.py:442
  265.4 36.1 %collective-permute-start.34 = (bf16[768,512]{1,0:T(8,128)(2,1)S(1)}, bf16[768,512]{1,0:T(8,128)(2,1)S(1)}, u32[]{:S(2)}, u32[]{:S(2)}) collective-permute-start(bf16[768,512]{1,0:T(8,128)(2,1)S(1)} %get-tuple-element.146), channel_id=1, source_target_pairs={{0,8},{4,12},{8,0},{12,4},{1,9},{5,13},{9,1},{13,5},{2,10},{6,14},... | collective-permute-start | bytes 2359304 | tf_op jit(solution)/shard_map/ppermute | solution.py:442
  297.1 23.3 %collective-permute-start.23 = (bf16[128,2048]{1,0:T(8,128)(2,1)S(1)}, bf16[128,2048]{1,0:T(8,128)(2,1)S(1)}, u32[]{:S(2)}, u32[]{:S(2)}) collective-permute-start(bf16[128,2048]{1,0:T(8,128)(2,1)S(1)} %get-tuple-element.88), channel_id=1, source_target_pairs={{0,1},{1,0},{2,3},{3,2},{4,5},{5,4},{6,7},{7,6},{8,9},{9,8},{10,11... | collective-permute-start | bytes 1572872 | tf_op jit(solution)/shard_map/ppermute | solution.py:442
  297.2 38.3 %collective-permute-start.24 = (bf16[128,2048]{1,0:T(8,128)(2,1)S(1)}, bf16[128,2048]{1,0:T(8,128)(2,1)S(1)}, u32[]{:S(2)}, u32[]{:S(2)}) collective-permute-start(bf16[128,2048]{1,0:T(8,128)(2,1)S(1)} %get-tuple-element.88), channel_id=1, source_target_pairs={{0,2},{1,3},{2,0},{3,1},{4,6},{5,7},{6,4},{7,5},{8,10},{9,11},{10,... | collective-permute-start | bytes 1572872 | tf_op jit(solution)/shard_map/ppermute | solution.py:442
  300.2 35.3 %collective-permute-start.25 = (bf16[128,2048]{1,0:T(8,128)(2,1)S(1)}, bf16[128,2048]{1,0:T(8,128)(2,1)S(1)}, u32[]{:S(2)}, u32[]{:S(2)}) collective-permute-start(bf16[128,2048]{1,0:T(8,128)(2,1)S(1)} %get-tuple-element.88), channel_id=1, source_target_pairs={{0,3},{1,2},{2,1},{3,0},{4,7},{5,6},{6,5},{7,4},{8,11},{9,10},{10,... | collective-permute-start | bytes 1572872 | tf_op jit(solution)/shard_map/ppermute | solution.py:442
  306.7 28.8 %collective-permute-start.26 = (bf16[128,2048]{1,0:T(8,128)(2,1)S(1)}, bf16[128,2048]{1,0:T(8,128)(2,1)S(1)}, u32[]{:S(2)}, u32[]{:S(2)}) collective-permute-start(bf16[128,2048]{1,0:T(8,128)(2,1)S(1)} %get-tuple-element.88), channel_id=1, source_target_pairs={{0,4},{4,0},{8,12},{12,8},{1,5},{5,1},{9,13},{13,9},{2,6},{6,2},{1... | collective-permute-start | bytes 1572872 | tf_op jit(solution)/shard_map/ppermute | solution.py:442
  320.3 15.9 %collective-permute-start.27 = (bf16[128,2048]{1,0:T(8,128)(2,1)S(1)}, bf16[128,2048]{1,0:T(8,128)(2,1)S(1)}, u32[]{:S(2)}, u32[]{:S(2)}) collective-permute-start(bf16[128,2048]{1,0:T(8,128)(2,1)S(1)} %collective-permute-done.23), channel_id=1, source_target_pairs={{0,4},{4,0},{8,12},{12,8},{1,5},{5,1},{9,13},{13,9},{2,6},{6,2},{1... | collective-permute-start | bytes 1572872 | tf_op jit(solution)/shard_map/ppermute | solution.py:442
  354.8 37.3 %collective-permute-start.78 = (bf16[1024,768]{1,0:T(8,128)(2,1)S(1)}, bf16[1024,768]{1,0:T(8,128)(2,1)S(1)}, u32[]{:S(2)}, u32[]{:S(2)}) collective-permute-start(bf16[1024,768]{1,0:T(8,128)(2,1)S(1)} %fusion.36), channel_id=1, source_target_pairs={{0,8},{4,12},{8,0},{12,4},{1,9},{5,13},{9,1},{13,5},{2,10},{6,14},... | collective-permute-start | bytes 4718600 | tf_op jit(solution)/shard_map/ppermute | solution.py:442
  361.3 99.4 %collective-permute-start.47 = (bf16[512,2048]{1,0:T(8,128)(2,1)S(1)}, bf16[512,2048]{1,0:T(8,128)(2,1)S(1)}, u32[]{:S(2)}, u32[]{:S(2)}) collective-permute-start(bf16[512,2048]{1,0:T(8,128)(2,1)S(1)} %add_convert_fusion.2), channel_id=1, source_target_pairs={{0,4},{4,0},{8,12},{12,8},{1,5},{5,1},{9,13},{13,9},{2,6},{6,2},{1... | collective-permute-start | bytes 6291464 | tf_op jit(solution)/shard_map/ppermute | solution.py:442
  361.4 64.5 %collective-permute-start.75 = (bf16[1024,768]{1,0:T(8,128)(2,1)S(1)}, bf16[1024,768]{1,0:T(8,128)(2,1)}, u32[]{:S(2)}, u32[]{:S(2)}) collective-permute-start(bf16[1024,768]{1,0:T(8,128)(2,1)S(1)} %fusion.33), channel_id=1, source_target_pairs={{0,8},{4,12},{8,0},{12,4},{1,9},{5,13},{9,1},{13,5},{2,10},{6,14},... | collective-permute-start | bytes 4718600 | tf_op jit(solution)/shard_map/ppermute | solution.py:442
  364.8 93.8 %collective-permute-start.81 = (bf16[768,1024]{1,0:T(8,128)(2,1)S(1)}, bf16[768,1024]{1,0:T(8,128)(2,1)S(1)}, u32[]{:S(2)}, u32[]{:S(2)}) collective-permute-start(bf16[768,1024]{1,0:T(8,128)(2,1)S(1)} %fusion.39), channel_id=1, source_target_pairs={{0,8},{4,12},{8,0},{12,4},{1,9},{5,13},{9,1},{13,5},{2,10},{6,14},... | collective-permute-start | bytes 4718600 | tf_op jit(solution)/shard_map/ppermute | solution.py:442
  369.6 98.8 %collective-permute-start.36 = (bf16[512,2048]{1,0:T(8,128)(2,1)}, bf16[512,2048]{1,0:T(8,128)(2,1)S(1)}, u32[]{:S(2)}, u32[]{:S(2)}) collective-permute-start(bf16[512,2048]{1,0:T(8,128)(2,1)} %convolution_convert_fusion.1), channel_id=1, source_target_pairs={{0,4},{4,0},{8,12},{12,8},{1,5},{5,1},{9,13},{13,9},{2,6},{6,2},{1... | collective-permute-start | bytes 6291464 | tf_op jit(solution)/shard_map/ppermute | solution.py:442
  394.1 86.1 %collective-permute-start.79 = (bf16[512,768]{1,0:T(8,128)(2,1)S(1)}, bf16[512,768]{1,0:T(8,128)(2,1)S(1)}, u32[]{:S(2)}, u32[]{:S(2)}) collective-permute-start(bf16[512,768]{1,0:T(8,128)(2,1)S(1)} %slice.824), channel_id=1, source_target_pairs={{0,4},{4,0},{8,12},{12,8},{1,5},{5,1},{9,13},{13,9},{2,6},{6,2},{1... | collective-permute-start | bytes 2359304 | tf_op jit(solution)/shard_map/ppermute | solution.py:442
  429.3 51.2 %collective-permute-start.76 = (bf16[512,768]{1,0:T(8,128)(2,1)S(1)}, bf16[512,768]{1,0:T(8,128)(2,1)S(1)}, u32[]{:S(2)}, u32[]{:S(2)}) collective-permute-start(bf16[512,768]{1,0:T(8,128)(2,1)S(1)} %slice.822), channel_id=1, source_target_pairs={{0,4},{4,0},{8,12},{12,8},{1,5},{5,1},{9,13},{13,9},{2,6},{6,2},{1... | collective-permute-start | bytes 2359304 | tf_op jit(solution)/shard_map/ppermute | solution.py:442
  460.7 22.5 %collective-permute-start.82 = (bf16[768,512]{1,0:T(8,128)(2,1)S(1)}, bf16[768,512]{1,0:T(8,128)(2,1)S(1)}, u32[]{:S(2)}, u32[]{:S(2)}) collective-permute-start(bf16[768,512]{1,0:T(8,128)(2,1)S(1)} %slice.828), channel_id=1, source_target_pairs={{0,4},{4,0},{8,12},{12,8},{1,5},{5,1},{9,13},{13,9},{2,6},{6,2},{1... | collective-permute-start | bytes 2359304 | tf_op jit(solution)/shard_map/ppermute | solution.py:442
  465.9 18.6 %collective-permute-start.50 = (bf16[128,2048]{1,0:T(8,128)(2,1)S(1)}, bf16[128,2048]{1,0:T(8,128)(2,1)S(1)}, u32[]{:S(2)}, u32[]{:S(2)}) collective-permute-start(bf16[128,2048]{1,0:T(8,128)(2,1)S(1)} %get-tuple-element.122), channel_id=1, source_target_pairs={{0,3},{1,2},{2,1},{3,0},{4,7},{5,6},{6,5},{7,4},{8,11},{9,10},{10,... | collective-permute-start | bytes 1572872 | tf_op jit(solution)/shard_map/ppermute | solution.py:442
  468.4 69.9 %collective-permute-start.49 = (bf16[128,2048]{1,0:T(8,128)(2,1)S(1)}, bf16[128,2048]{1,0:T(8,128)(2,1)S(1)}, u32[]{:S(2)}, u32[]{:S(2)}) collective-permute-start(bf16[128,2048]{1,0:T(8,128)(2,1)S(1)} %get-tuple-element.123), channel_id=1, source_target_pairs={{0,2},{1,3},{2,0},{3,1},{4,6},{5,7},{6,4},{7,5},{8,10},{9,11},{10,... | collective-permute-start | bytes 1572872 | tf_op jit(solution)/shard_map/ppermute | solution.py:442
  480.2 59.6 %collective-permute-start.48 = (bf16[128,2048]{1,0:T(8,128)(2,1)S(1)}, bf16[128,2048]{1,0:T(8,128)(2,1)S(1)}, u32[]{:S(2)}, u32[]{:S(2)}) collective-permute-start(bf16[128,2048]{1,0:T(8,128)(2,1)S(1)} %get-tuple-element.121), channel_id=1, source_target_pairs={{0,1},{1,0},{2,3},{3,2},{4,5},{5,4},{6,7},{7,6},{8,9},{9,8},{10,11... | collective-permute-start | bytes 1572872 | tf_op jit(solution)/shard_map/ppermute | solution.py:442
  480.5 59.8 %collective-permute-start.39 = (bf16[128,2048]{1,0:T(8,128)(2,1)S(1)}, bf16[128,2048]{1,0:T(8,128)(2,1)S(1)}, u32[]{:S(2)}, u32[]{:S(2)}) collective-permute-start(bf16[128,2048]{1,0:T(8,128)(2,1)S(1)} %get-tuple-element.129), channel_id=1, source_target_pairs={{0,3},{1,2},{2,1},{3,0},{4,7},{5,6},{6,5},{7,4},{8,11},{9,10},{10,... | collective-permute-start | bytes 1572872 | tf_op jit(solution)/shard_map/ppermute | solution.py:442
  483.2 77.5 %collective-permute-start.38 = (bf16[128,2048]{1,0:T(8,128)(2,1)S(1)}, bf16[128,2048]{1,0:T(8,128)(2,1)S(1)}, u32[]{:S(2)}, u32[]{:S(2)}) collective-permute-start(bf16[128,2048]{1,0:T(8,128)(2,1)S(1)} %get-tuple-element.130), channel_id=1, source_target_pairs={{0,2},{1,3},{2,0},{3,1},{4,6},{5,7},{6,4},{7,5},{8,10},{9,11},{10,... | collective-permute-start | bytes 1572872 | tf_op jit(solution)/shard_map/ppermute | solution.py:442
  484.4 76.3 %collective-permute-start.37 = (bf16[128,2048]{1,0:T(8,128)(2,1)S(1)}, bf16[128,2048]{1,0:T(8,128)(2,1)S(1)}, u32[]{:S(2)}, u32[]{:S(2)}) collective-permute-start(bf16[128,2048]{1,0:T(8,128)(2,1)S(1)} %get-tuple-element.128), channel_id=1, source_target_pairs={{0,1},{1,0},{2,3},{3,2},{4,5},{5,4},{6,7},{7,6},{8,9},{9,8},{10,11... | collective-permute-start | bytes 1572872 | tf_op jit(solution)/shard_map/ppermute | solution.py:442
  538.3 73.7 %collective-permute-start.80 = (bf16[512,1408]{1,0:T(8,128)(2,1)S(1)}, bf16[512,1408]{1,0:T(8,128)(2,1)S(1)}, u32[]{:S(2)}, u32[]{:S(2)}) collective-permute-start(bf16[512,1408]{1,0:T(8,128)(2,1)S(1)} %pad_add_fusion.1), channel_id=1, source_target_pairs={{0,16},{16,0},{1,17},{17,1},{2,18},{18,2},{3,19},{19,3},{4,20},{20... | collective-permute-start | bytes 4325384 | tf_op jit(solution)/shard_map/ppermute | solution.py:442
  539.8 72.5 %collective-permute-start.77 = (bf16[512,1408]{1,0:T(8,128)(2,1)S(1)}, bf16[512,1408]{1,0:T(8,128)(2,1)S(1)}, u32[]{:S(2)}, u32[]{:S(2)}) collective-permute-start(bf16[512,1408]{1,0:T(8,128)(2,1)S(1)} %pad_add_fusion.2), channel_id=1, source_target_pairs={{0,16},{16,0},{1,17},{17,1},{2,18},{18,2},{3,19},{19,3},{4,20},{20... | collective-permute-start | bytes 4325384 | tf_op jit(solution)/shard_map/ppermute | solution.py:442
  563.1 24.6 %collective-permute-start.51 = (bf16[128,2048]{1,0:T(8,128)(2,1)S(1)}, bf16[128,2048]{1,0:T(8,128)(2,1)S(1)}, u32[]{:S(2)}, u32[]{:S(2)}) collective-permute-start(bf16[128,2048]{1,0:T(8,128)(2,1)S(1)} %get-tuple-element.84), channel_id=1, source_target_pairs={{0,1},{1,0},{2,3},{3,2},{4,5},{5,4},{6,7},{7,6},{8,9},{9,8},{10,11... | collective-permute-start | bytes 1572872 | tf_op jit(solution)/shard_map/ppermute | solution.py:442
  563.1 38.3 %collective-permute-start.52 = (bf16[128,2048]{1,0:T(8,128)(2,1)S(1)}, bf16[128,2048]{1,0:T(8,128)(2,1)S(1)}, u32[]{:S(2)}, u32[]{:S(2)}) collective-permute-start(bf16[128,2048]{1,0:T(8,128)(2,1)S(1)} %get-tuple-element.84), channel_id=1, source_target_pairs={{0,2},{1,3},{2,0},{3,1},{4,6},{5,7},{6,4},{7,5},{8,10},{9,11},{10,... | collective-permute-start | bytes 1572872 | tf_op jit(solution)/shard_map/ppermute | solution.py:442
  566.1 36.8 %collective-permute-start.53 = (bf16[128,2048]{1,0:T(8,128)(2,1)S(1)}, bf16[128,2048]{1,0:T(8,128)(2,1)S(1)}, u32[]{:S(2)}, u32[]{:S(2)}) collective-permute-start(bf16[128,2048]{1,0:T(8,128)(2,1)S(1)} %get-tuple-element.84), channel_id=1, source_target_pairs={{0,3},{1,2},{2,1},{3,0},{4,7},{5,6},{6,5},{7,4},{8,11},{9,10},{10,... | collective-permute-start | bytes 1572872 | tf_op jit(solution)/shard_map/ppermute | solution.py:442
  587.7 15.4 %collective-permute-start.54 = (bf16[128,2048]{1,0:T(8,128)(2,1)S(1)}, bf16[128,2048]{1,0:T(8,128)(2,1)S(1)}, u32[]{:S(2)}, u32[]{:S(2)}) collective-permute-start(bf16[128,2048]{1,0:T(8,128)(2,1)S(1)} %get-tuple-element.84), channel_id=1, source_target_pairs={{0,4},{4,0},{8,12},{12,8},{1,5},{5,1},{9,13},{13,9},{2,6},{6,2},{1... | collective-permute-start | bytes 1572872 | tf_op jit(solution)/shard_map/ppermute | solution.py:442
  601.4 32.2 %collective-permute-start.83 = (bf16[1408,512]{1,0:T(8,128)(2,1)S(1)}, bf16[1408,512]{1,0:T(8,128)(2,1)S(1)}, u32[]{:S(2)}, u32[]{:S(2)}) collective-permute-start(bf16[1408,512]{1,0:T(8,128)(2,1)S(1)} %pad_add_fusion), channel_id=1, source_target_pairs={{0,16},{16,0},{1,17},{17,1},{2,18},{18,2},{3,19},{19,3},{4,20},{20... | collective-permute-start | bytes 4325384 | tf_op jit(solution)/shard_map/ppermute | solution.py:442
  609.2 29.4 %collective-permute-start.58 = (bf16[1024,128]{1,0:T(8,128)(2,1)S(1)}, bf16[1024,128]{1,0:T(8,128)(2,1)S(1)}, u32[]{:S(2)}, u32[]{:S(2)}) collective-permute-start(bf16[1024,128]{1,0:T(8,128)(2,1)S(1)} %get-tuple-element.165), channel_id=1, source_target_pairs={{0,8},{4,12},{8,0},{12,4},{1,9},{5,13},{9,1},{13,5},{2,10},{6,14},... | collective-permute-start | bytes 786440 | tf_op jit(solution)/shard_map/ppermute | solution.py:442
  610.4 90.7 %collective-permute-start.72 = (bf16[256,1024]{1,0:T(8,128)(2,1)S(1)}, bf16[256,1024]{1,0:T(8,128)(2,1)S(1)}, u32[]{:S(2)}, u32[]{:S(2)}) collective-permute-start(bf16[256,1024]{1,0:T(8,128)(2,1)S(1)} %fusion.63), channel_id=1, source_target_pairs={{0,8},{4,12},{8,0},{12,4},{1,9},{5,13},{9,1},{13,5},{2,10},{6,14},... | collective-permute-start | bytes 1572872 | tf_op jit(solution)/shard_map/ppermute | solution.py:442
  676.8 24.4 %collective-permute-start.59 = (bf16[1024,512]{1,0:T(8,128)(2,1)S(1)}, bf16[1024,512]{1,0:T(8,128)(2,1)S(1)}, u32[]{:S(2)}, u32[]{:S(2)}) collective-permute-start(bf16[1024,512]{1,0:T(8,128)(2,1)S(1)} %get-tuple-element.119), channel_id=1, source_target_pairs={{0,8},{4,12},{8,0},{12,4},{1,9},{5,13},{9,1},{13,5},{2,10},{6,14},... | collective-permute-start | bytes 3145736 | tf_op jit(solution)/shard_map/ppermute | solution.py:442
  682.0 17.8 %collective-permute-start.68 = (f32[2,2048]{1,0:T(2,128)S(1)}, f32[2,2048]{1,0:T(2,128)S(1)}, u32[]{:S(2)}, u32[]{:S(2)}) collective-permute-start(f32[2,2048]{1,0:T(2,128)S(1)} %fusion.108), channel_id=1, source_target_pairs={{0,8},{4,12},{8,0},{12,4},{1,9},{5,13},{9,1},{13,5},{2,10},{6,14},... | collective-permute-start | bytes 49160 | tf_op jit(solution)/shard_map/ppermute | solution.py:442
  705.1 47.9 %collective-permute-start.65 = (bf16[1024,1024]{0,1:T(8,128)(2,1)}, bf16[1024,1024]{0,1:T(8,128)(2,1)S(1)}, u32[]{:S(2)}, u32[]{:S(2)}) collective-permute-start(bf16[1024,1024]{0,1:T(8,128)(2,1)} %fusion.22), channel_id=1, source_target_pairs={{0,8},{4,12},{8,0},{12,4},{1,9},{5,13},{9,1},{13,5},{2,10},{6,14},... | collective-permute-start | bytes 6291464 | tf_op jit(solution)/shard_map/ppermute | solution.py:442
  709.0 47.0 %collective-permute-start.61 = (bf16[512,2048]{1,0:T(8,128)(2,1)S(1)}, bf16[512,2048]{1,0:T(8,128)(2,1)S(1)}, u32[]{:S(2)}, u32[]{:S(2)}) collective-permute-start(bf16[512,2048]{1,0:T(8,128)(2,1)S(1)} %add_convert_fusion.1), channel_id=1, source_target_pairs={{0,4},{4,0},{8,12},{12,8},{1,5},{5,1},{9,13},{13,9},{2,6},{6,2},{1... | collective-permute-start | bytes 6291464 | tf_op jit(solution)/shard_map/ppermute | solution.py:442
  712.0 56.3 %collective-permute-start.70 = (f32[4,512]{1,0:T(4,128)S(1)}, f32[4,512]{1,0:T(4,128)S(1)}, u32[]{:S(2)}, u32[]{:S(2)}) collective-permute-start(f32[4,512]{1,0:T(4,128)S(1)} %pad_maximum_fusion.32), channel_id=1, source_target_pairs={{0,16},{16,0},{1,17},{17,1},{2,18},{18,2},{3,19},{19,3},{4,20},{20... | collective-permute-start | bytes 24584 | tf_op jit(solution)/shard_map/ppermute | solution.py:442
  713.8 56.6 %collective-permute-start.74 = (bf16[512,512]{1,0:T(8,128)(2,1)S(1)}, bf16[512,512]{1,0:T(8,128)(2,1)S(1)}, u32[]{:S(2)}, u32[]{:S(2)}) collective-permute-start(bf16[512,512]{1,0:T(8,128)(2,1)S(1)} %pad_maximum_fusion.19), channel_id=1, source_target_pairs={{0,16},{16,0},{1,17},{17,1},{2,18},{18,2},{3,19},{19,3},{4,20},{20... | collective-permute-start | bytes 1572872 | tf_op jit(solution)/shard_map/ppermute | solution.py:442
  761.7 16.8 %collective-permute-start.64 = (bf16[128,2048]{1,0:T(8,128)(2,1)S(1)}, bf16[128,2048]{1,0:T(8,128)(2,1)S(1)}, u32[]{:S(2)}, u32[]{:S(2)}) collective-permute-start(bf16[128,2048]{1,0:T(8,128)(2,1)S(1)} %get-tuple-element.113), channel_id=1, source_target_pairs={{0,3},{1,2},{2,1},{3,0},{4,7},{5,6},{6,5},{7,4},{8,11},{9,10},{10,... | collective-permute-start | bytes 1572872 | tf_op jit(solution)/shard_map/ppermute | solution.py:442
  764.3 44.6 %collective-permute-start.63 = (bf16[128,2048]{1,0:T(8,128)(2,1)S(1)}, bf16[128,2048]{1,0:T(8,128)(2,1)S(1)}, u32[]{:S(2)}, u32[]{:S(2)}) collective-permute-start(bf16[128,2048]{1,0:T(8,128)(2,1)S(1)} %get-tuple-element.114), channel_id=1, source_target_pairs={{0,2},{1,3},{2,0},{3,1},{4,6},{5,7},{6,4},{7,5},{8,10},{9,11},{10,... | collective-permute-start | bytes 1572872 | tf_op jit(solution)/shard_map/ppermute | solution.py:442
  764.8 44.2 %collective-permute-start.62 = (bf16[128,2048]{1,0:T(8,128)(2,1)S(1)}, bf16[128,2048]{1,0:T(8,128)(2,1)S(1)}, u32[]{:S(2)}, u32[]{:S(2)}) collective-permute-start(bf16[128,2048]{1,0:T(8,128)(2,1)S(1)} %get-tuple-element.112), channel_id=1, source_target_pairs={{0,1},{1,0},{2,3},{3,2},{4,5},{5,4},{6,7},{7,6},{8,9},{9,8},{10,11... | collective-permute-start | bytes 1572872 | tf_op jit(solution)/shard_map/ppermute | solution.py:442
  768.2 85.5 %collective-permute-start.67 = (bf16[512,2048]{0,1:T(8,128)(2,1)}, bf16[512,2048]{0,1:T(8,128)(2,1)}, u32[]{:S(2)}, u32[]{:S(2)}) collective-permute-start(bf16[512,2048]{0,1:T(8,128)(2,1)} %pad_maximum_fusion.6), channel_id=1, source_target_pairs={{0,16},{16,0},{1,17},{17,1},{2,18},{18,2},{3,19},{19,3},{4,20},{20... | collective-permute-start | bytes 6291464 | tf_op jit(solution)/shard_map/ppermute | solution.py:442
  (80 other events, 2906.7 us)

commit v3 on v2

--- a/solution.py
+++ b/solution.py
@@ -476,32 +476,58 @@
     return scale * (pulled - unit * inner), jnp.sum(grad * unit, axis=0)
 
 
+def tensor_tree():
+    return lax.axis_size("tensor") == 4
+
+
+def inner_place():
+    index = lax.axis_index("tensor")
+    return (index == 1) | (index == 2)
+
+
+def along_tensor(value, pairs):
+    return lax.ppermute(value, "tensor", pairs)
+
+
+def gather_tensor(value):
+    if not tensor_tree():
+        return [value] + [other(value, "tensor", s) for s in range(1, lax.axis_size("tensor"))]
+    two = other(value, "tensor", 2)
+    one = other(value, "tensor", 1)
+    passed = along_tensor(two, [(2, 3), (1, 0)])
+    middle = along_tensor(after(value, one), [(1, 2), (2, 1)])
+    return [value, one, two, jnp.where(inner_place(), middle, passed)]
+
+
 def spread(values):
-    mine = [values] + [other(values, "tensor", s) for s in range(1, lax.axis_size("tensor"))]
+    mine = gather_tensor(values)
     theirs = [neighbour_order(other(v, "mp", 1), 1, 1) for v in mine]
     return jnp.concatenate(mine + theirs, axis=0)
 
 
-def collect(partial):
+def partials(rows, body):
+    return body(rows // 2, rows).astype(bf16), body(0, rows // 2)
+
+
+def collect(parts):
+    theirs, mine = parts
     ways = lax.axis_size("tensor")
-    rows = partial.rows // 2
-    theirs = partial(rows, 2 * rows).astype(bf16)
-    back = neighbour_order(other(theirs, "mp", 1), 1, 1)
-    joined = partial(0, rows) + back.astype(f32)
-    piece = rows // ways
-    total = joined[:piece]
-    for s in range(1, ways):
-        total = total + other(joined[s * piece:(s + 1) * piece].astype(bf16), "tensor", s).astype(f32)
-    return total
-
-
-class Rows:
-    def __init__(self, rows, body):
-        self.rows = rows
-        self.body = body
-
-    def __call__(self, start, stop):
-        return self.body(start, stop)
+    piece = mine.shape[0] // ways
+    last = (ways - 1) * piece
+    tail = mine[last:] + neighbour_order(other(theirs[last:], "mp", 1), 1, 1).astype(f32)
+    rest = mine[:last] + neighbour_order(other(theirs[:last], "mp", 1), 1, 1).astype(f32)
+    if not tensor_tree():
+        joined = jnp.concatenate([rest, tail], axis=0)
+        total = joined[:piece]
+        for s in range(1, ways):
+            total = total + other(joined[s * piece:(s + 1) * piece].astype(bf16), "tensor", s).astype(f32)
+        return total
+    low = tail.astype(bf16)
+    passed = along_tensor(low, [(3, 2), (0, 1)])
+    middle = along_tensor(low, [(1, 2), (2, 1)])
+    two = other((rest[2 * piece:] + passed.astype(f32)).astype(bf16), "tensor", 2)
+    one = other(rest[piece:2 * piece].astype(bf16), "tensor", 1)
+    return rest[:piece] + middle.astype(f32) + one.astype(f32) + two.astype(f32)
 
 
 def over_dp(value):
@@ -510,6 +536,15 @@
         low = value.astype(bf16)
         value = low.astype(f32) + other(low, "dp", bit).astype(f32)
         bit *= 2
+    return value
+
+
+def over_all(value):
+    for axis in ("mp", "tensor", "dp"):
+        bit = 1
+        while bit < lax.axis_size(axis):
+            value = value + other(value, axis, bit)
+            bit *= 2
     return value
 
 
@@ -543,74 +578,81 @@
 
     pieces, _, wide = w_proj.shape
     head = wide // 4
+    span = pieces * head
     heads = [
-        lax.dynamic_slice_in_dim(w_proj, (j ^ m) * head, head, 2).transpose(1, 0, 2).reshape(block, pieces * head)
+        lax.dynamic_slice_in_dim(w_proj, (j ^ m) * head, head, 2).transpose(1, 0, 2).reshape(block, span)
         for j in range(4)
     ]
+    beta_rows = own_order(w_beta.T, m, 0)
     pair = lambda values, i, j, axis: jnp.concatenate([values[i], values[j]], axis)
-    full_proj = jnp.concatenate(
-        [
-            pair(heads, 0, 2, 1),
-            other(pair(heads, 1, 3, 1), "mp", 1),
-            other(pair(heads, 2, 0, 1), "mp", 2),
-            other(pair(heads, 3, 1, 1), "mp", 3),
-        ],
-        axis=0,
-    )
-    beta_rows = w_beta.T
-    full_beta = own_order(
-        jnp.concatenate([beta_rows] + [other(beta_rows, "mp", s) for s in range(1, 4)], axis=1), m, 0
-    )
-    full_beta = jnp.concatenate([full_beta[0:1], full_beta[2:3]], axis=0)
-
-    normed = spread(scaled)
-    far_out = matmul(normed, full_proj[:, pieces * head:]).astype(bf16)
+
+    def with_beta(i, j):
+        row = jnp.concatenate([beta_rows[i], beta_rows[j]])[None]
+        return jnp.concatenate([pair(heads, i, j, 1), jnp.pad(row, ((0, HALO - 1), (0, 2 * span - 2 * block)))], 0)
+
+    far_sent, across_sent, core_sent = with_beta(2, 0), with_beta(3, 1), with_beta(1, 3)
+    far_got = other(far_sent, "mp", 2)
+    across_got = other(across_sent, "mp", 3)
+    core_got = other(core_sent, "mp", 1)
+    own_pair = pair(heads, 0, 2, 1)
+    normed = spread(after(scaled, far_sent, across_sent, core_sent))
+    full_proj = jnp.concatenate([own_pair, core_got[:block], far_got[:block], across_got[:block]], axis=0)
+    full_beta = jnp.concatenate(
+        [jnp.stack([beta_rows[0], beta_rows[2]])]
+        + [v[block, : 2 * block].reshape(2, block) for v in (core_got, far_got, across_got)],
+        axis=1,
+    )
     logits = matmul(full_beta, normed, ((1,), (1,))).astype(bf16)
-    far = other(far_out, "mp", 2)
-    far_logit = other(logits[1:2], "mp", 2)
-    near = matmul(normed, full_proj[:, : pieces * head]).astype(bf16)
+    far_out = matmul(normed, full_proj[:, span:]).astype(bf16)
+    count = far_out.shape[0]
+    logit_rows = count // span
+    far_sent = jnp.concatenate([far_out, jnp.pad(logits[1].reshape(logit_rows, span), ((0, HALO - logit_rows), (0, 0)))], 0)
+    far = other(far_sent, "mp", 2)
+    near = matmul(normed, full_proj[:, :span]).astype(bf16)
     chunk_rows = (-1, LANES)
-    logit = jnp.concatenate([logits[0].reshape(chunk_rows), far_logit.reshape(chunk_rows)], axis=0).astype(f32)
-
-    w_out, w_in, w_down = after((w_out, w_in, w_down), far)
-    out_rows = [lax.dynamic_slice_in_dim(w_out, (j ^ m) * head, head, 0) for j in range(4)]
-    full_out = jnp.concatenate(
-        [
-            pair(out_rows, 0, 2, 0),
-            other(pair(out_rows, 1, 3, 0), "mp", 1),
-            other(pair(out_rows, 2, 0, 0), "mp", 2),
-            other(pair(out_rows, 3, 1, 0), "mp", 3),
-        ],
-        axis=1,
-    )
+    logit = jnp.concatenate(
+        [logits[0].reshape(chunk_rows), far[count:count + logit_rows].reshape(chunk_rows)], axis=0
+    ).astype(f32)
+
     units = w_down.shape[0]
     half = LANES * ((units // LANES + 1) // 2)
-    ours_in = lax.dynamic_slice_in_dim(w_in, core * (units - half), half, 2)
-    theirs_in = lax.dynamic_slice_in_dim(w_in, (1 - core) * (units - half), half, 2)
-    far_in = other(ours_in, "mp", 2)
-    diag_in = other(theirs_in, "mp", 3)
-    full_in = jnp.concatenate([ours_in, other(theirs_in, "mp", 1), far_in, diag_in], axis=1)
-    w_down = after(w_down, far_in, diag_in)
-    ours_down = lax.dynamic_slice_in_dim(w_down, core * (units - half), half, 0)
-    theirs_down = lax.dynamic_slice_in_dim(w_down, (1 - core) * (units - half), half, 0)
+    ours = lambda v, axis: lax.dynamic_slice_in_dim(v, core * (units - half), half, axis)
+    theirs = lambda v, axis: lax.dynamic_slice_in_dim(v, (1 - core) * (units - half), half, axis)
+    live = (lax.broadcasted_iota(jnp.int32, (1, half), 1) >= core * (2 * half - units)).astype(f32)
+    w_out = after(w_out, far)
+    out_blocks = lambda v: [lax.dynamic_slice_in_dim(v, (j ^ m) * head, head, 0) for j in range(4)]
+    out_mine, out_far = out_blocks(w_out), out_blocks(other(w_out, "mp", 2))
+    w_down = after(w_down, far)
+    down_far = other(w_down, "mp", 2)
+    out_core = other(jnp.concatenate([pair(out_mine, 1, 3, 0), pair(out_far, 1, 3, 0)], axis=1), "mp", 1)
+    full_out = jnp.concatenate(
+        [pair(out_mine, 0, 2, 0), out_core[:, :block], pair(out_far, 0, 2, 0), out_core[:, block:]], axis=1
+    )
+    down_core = other(jnp.concatenate([theirs(w_down, 0), theirs(down_far, 0)], axis=1), "mp", 1)
     full_down = jnp.concatenate(
-        [ours_down, other(theirs_down, "mp", 1), other(ours_down, "mp", 2), other(theirs_down, "mp", 3)], axis=1
-    )
-    live = (lax.broadcasted_iota(jnp.int32, (1, half), 1) >= core * (2 * half - units)).astype(f32)
+        [ours(w_down, 0), down_core[:, :block], ours(down_far, 0), down_core[:, block:]], axis=1
+    )
+    cot_own = own_order(cotangent, m, 1)
+    cot_all = spread(after(cot_own, normed))
 
     taps = conv_weight.reshape(3, conv_weight.shape[1], head)
     info = jnp.stack([lengths[0], place]).astype(jnp.int32)
     head_args = (near, far, logit, taps, out_gain[None], starts[0], info)
     mixed, norm_total, kept = head_forward(*head_args)
-    count = near.shape[0]
-    mixed_tok = jnp.concatenate([mixed[:count], other(mixed[count:], "mp", 2)], axis=1)
-    branch = collect(Rows(count, lambda a, b: matmul(mixed_tok[a:b], full_out)))
+    mixed_far = other(mixed[count:], "mp", 2)
+    mixed_tok = jnp.concatenate([mixed[:count], mixed_far], axis=1)
+    branch = collect(partials(count, lambda a, b: matmul(mixed_tok[a:b], full_out)))
+
+    w_in = after(w_in, mixed_far)
+    in_far = other(w_in, "mp", 2)
+    in_core = other(theirs(w_in, 2), "mp", 1)
+    in_across = other(theirs(in_far, 2), "mp", 1)
+    full_in = jnp.concatenate([ours(w_in, 2), in_core, ours(in_far, 2), in_across], axis=1)
+
     middle = inputs + branch
     scaled_two, unit_two, scale_two = norm_rows(middle, gain_two)
     normed_two = spread(scaled_two.astype(bf16))
 
-    cot_own = own_order(cotangent, m, 1)
-    cot_all = spread(after(cot_own, normed))
     gate = matmul(normed_two, full_in[0])
     up = matmul(normed_two, full_in[1])
     sigma = jax.nn.sigmoid(gate)
@@ -621,17 +663,21 @@
     d_gate = (d_hidden * up * sigma * (1.0 + gate * (1.0 - sigma))).astype(bf16)
     d_up = (d_hidden * activated).astype(bf16)
     d_normed_two = collect(
-        Rows(
+        partials(
             count,
             lambda a, b: matmul(d_gate[a:b], full_in[0], ((1,), (1,))) + matmul(d_up[a:b], full_in[1], ((1,), (1,))),
         )
     )
     d_mid_norm, g_mlp = norm_back(d_normed_two, unit_two, scale_two, gain_two)
     d_middle = cot_own.astype(f32) + d_mid_norm
-    feed = collect(Rows(count, lambda a, b: matmul(hidden[a:b], full_down)))
+    d_mid_all = spread(d_middle.astype(bf16))
+    d_mixed = matmul(d_mid_all, full_out, ((1,), (1,))).astype(bf16)
+    d_far = other(d_mixed[:, head:], "mp", 2)
+    feed = collect(after(partials(count, lambda a, b: matmul(hidden[a:b], full_down)), d_mid_all))
     output = own_order((middle + feed).astype(bf16), m, 1)
 
     tn = ((0,), (0,))
+    grad_dot = lambda a, b: matmul(a, b, tn)
 
     def joined_units(mine, theirs, axis):
         gap = units - half
@@ -640,33 +686,26 @@
         zero = jnp.zeros_like(lax.slice_in_dim(low, 0, gap, axis=axis))
         return jnp.concatenate([low, zero], axis) + jnp.concatenate([zero, high], axis)
 
-    def far_sum(product, lhs, rhs, axis, swap=None):
-        cut = lambda v, a, b: lax.slice_in_dim(v, a, b, axis=1)
-        if axis == 0:
-            sent = product(cut(lhs, near_blocks, 2 * near_blocks), rhs).astype(bf16)
-            held = product(cut(lhs, 0, near_blocks), rhs)
-        else:
-            sent = product(lhs, cut(rhs, near_blocks, 2 * near_blocks)).astype(bf16)
-            held = product(lhs, cut(rhs, 0, near_blocks))
-        back = other(sent, "mp", 2)
-        if swap is not None:
-            back = neighbour_order(back, swap, 1, 2)
-        return (held + back.astype(f32)).astype(bf16)
-
-    grad_dot = lambda a, b: matmul(a, b, tn)
-    down_two = far_sum(grad_dot, hidden, cot_all, 1)
-    down_mine = down_two[:, :block]
-    g_down = over_dp(joined_units(down_mine, other(down_two[:, block:], "mp", 1), 0))
-    in_sums = []
-    for grad in (d_gate, d_up):
-        in_two = far_sum(grad_dot, normed_two, grad, 0)
-        in_sums.append(over_dp(joined_units(in_two[:block], other(in_two[block:], "mp", 1), 1)))
-    g_in = jnp.stack(in_sums)
-
-    d_mid_all = spread(d_middle.astype(bf16))
-    d_mixed = matmul(d_mid_all, full_out, ((1,), (1,))).astype(bf16)
-    d_far = other(d_mixed[:, head:], "mp", 2)
-    out_two = far_sum(grad_dot, mixed_tok, d_mid_all, 1, swap=0)
+    def units_grad(product, axis, *before):
+        cut = lambda v, p: lax.slice_in_dim(v, p * block, (p + 1) * block, axis=axis)
+        two = lambda i, j: jnp.concatenate([cut(product, i), cut(product, j)], axis)
+        joined = joined_units(two(0, 2), other(two(1, 3), "mp", 1), 1 - axis)
+        sent = cut(joined, 1)
+        if before:
+            sent = after(sent, *before)
+        return over_dp(cut(joined, 0).astype(f32) + other(sent, "mp", 2).astype(f32))
+
+    g_down = units_grad(grad_dot(hidden, cot_all).astype(bf16), 1)
+    g_in = jnp.stack(
+        [
+            units_grad(grad_dot(normed_two, d_gate).astype(bf16), 0),
+            units_grad(grad_dot(normed_two, d_up).astype(bf16), 0, d_far),
+        ]
+    )
+
+    out_grad = grad_dot(mixed_tok, d_mid_all)
+    out_back = neighbour_order(other(after(out_grad[:, near_blocks:].astype(bf16), d_far), "mp", 2), 0, 1, 2)
+    out_two = (out_grad[:, :near_blocks] + out_back.astype(f32)).astype(bf16)
     out_theirs = other(out_two[:, block:], "mp", 1)
     out_mine = out_two[:, :block]
     g_out = over_dp(
@@ -675,63 +714,84 @@
         )
     )
     d_heads, d_logit, d_taps, g_head_gain = head_backward(d_mixed[:, :head], d_far, *head_args, kept)
-    d_proj = jnp.concatenate([d_heads[:count], other(d_heads[count:], "mp", 2)], axis=1)
     d_logit = d_logit.astype(bf16)
     half_chunks = d_logit.shape[0] // 2
+    d_sent = jnp.concatenate(
+        [
+            d_heads[count:],
+            jnp.pad(d_logit[half_chunks:].reshape(logit_rows, span), ((0, HALO - logit_rows), (0, 0))),
+        ],
+        axis=0,
+    )
+    d_got = other(d_sent, "mp", 2)
+    d_own = d_heads[:count]
+    d_proj = jnp.concatenate([d_own, d_got[:count]], axis=1)
     d_logits = jnp.concatenate(
-        [d_logit[:half_chunks].reshape(1, count), other(d_logit[half_chunks:], "mp", 2).reshape(1, count)], axis=0
+        [d_logit[:half_chunks].reshape(1, count), d_got[count:count + logit_rows].reshape(1, count)], axis=0
     )
     d_normed = collect(
-        Rows(
+        partials(
             count,
             lambda a, b: matmul(d_proj[a:b], full_proj, ((1,), (1,))) + matmul(d_logits[:, a:b], full_beta, tn),
         )
     )
-    proj_two = far_sum(grad_dot, normed, d_proj, 0, swap=1)
-    proj_mine = proj_two[:block]
-    proj_theirs = other(proj_two[block:], "mp", 1)
-    span = pieces * head
-    g_proj = over_dp(
-        jnp.concatenate(
-            [proj_mine[:, :span], proj_theirs[:, :span], proj_mine[:, span:], proj_theirs[:, span:]], axis=1
-        )
-    )
-    g_proj = jnp.concatenate(
-        [
-            lax.dynamic_slice_in_dim(g_proj, (h ^ m) * span, span, 1).reshape(block, pieces, head).transpose(1, 0, 2)
-            for h in range(4)
-        ],
-        axis=2,
+    own_grad = grad_dot(normed, d_own)
+    far_grad = grad_dot(normed, d_got[:count])
+    own_back = other(own_grad[near_blocks:].astype(bf16), "mp", 2)
+    far_back = other(after(far_grad[near_blocks:].astype(bf16), own_back), "mp", 2)
+
+    def proj_part(held, back):
+        two = (held[:near_blocks] + back.astype(f32)).astype(bf16)
+        return over_dp(jnp.concatenate([two[:block], other(two[block:], "mp", 1)], axis=1))
+
+    part_far = proj_part(far_grad, own_back)
+    part_own = proj_part(own_grad, far_back)
+    g_heads = [part_own[:, :span], part_own[:, span:], part_far[:, :span], part_far[:, span:]]
+    g_proj = own_order(
+        jnp.concatenate([v.reshape(block, pieces, head).transpose(1, 0, 2) for v in g_heads], axis=2), m, 2
     )
     beta_part = matmul(d_logits, normed)
     beta_back = neighbour_order(neighbour_order(other(beta_part, "mp", 2), 0, 1, 2), 1, 1, 2)
     beta_two = beta_part + beta_back
     beta_theirs = other(beta_two[:, block:near_blocks], "mp", 1)
-    beta_rows = own_order(
+    g_beta = own_order(
         jnp.concatenate([beta_two[:1, :block], beta_theirs[:1], beta_two[1:, :block], beta_theirs[1:]], axis=0), m, 0
     )
+    small = jnp.concatenate([g_beta.reshape(-1, LANES), d_taps.reshape(-1, LANES)], axis=0)
     bit = 1
     while bit < lax.axis_size("dp"):
-        beta_rows = beta_rows + other(beta_rows, "dp", bit)
-        d_taps = d_taps + other(d_taps, "dp", bit)
+        small = small + other(small, "dp", bit)
         bit *= 2
+    cut = g_beta.size // LANES
+    g_beta = small[:cut].reshape(g_beta.shape)
+    d_taps = small[cut:]
     d_in_norm, g_norm = norm_back(d_normed, unit_one, scale_one, gain_one)
     d_tokens = own_order(d_middle + d_in_norm, m, 1)
-    sum_norm, sum_mlp, sum_head, norm_all = lax.psum(
-        (own_order(g_norm, m, 0), own_order(g_mlp, m, 0), g_head_gain[0], norm_total), ("dp", "mp", "tensor")
-    )
+    row = lambda v: v.reshape(-1, LANES)
+    sums = over_all(
+        jnp.concatenate(
+            [
+                row(own_order(g_norm, m, 0)),
+                row(own_order(g_mlp, m, 0)),
+                g_head_gain[:1],
+                jnp.full((1, LANES), norm_total),
+            ],
+            axis=0,
+        )
+    )
+    lines = g_norm.shape[0] // LANES
     ways = lax.axis_size("mp") * lax.axis_size("tensor")
-    state_norm = norm_all / (ways * lax.axis_size("dp") * (2 * count // BLOCK))
+    state_norm = sums[2 * lines + 1, 0] / (ways * lax.axis_size("dp") * (2 * count // BLOCK))
     return (
         output,
         d_tokens,
-        sum_norm,
+        sums[:lines].reshape(-1),
         g_proj,
-        beta_rows.T,
+        g_beta.T,
         d_taps.reshape(conv_weight.shape),
-        sum_head,
+        sums[2 * lines],
         g_out,
-        sum_mlp,
+        sums[lines:2 * lines].reshape(-1),
         g_in,
         g_down,
         state_norm,

time: 871 us -> 710 us (0.82)
  waiting for transfers between devices: 484 us -> 282 us
  local copies, waits for them, and re-layouts: 37.6 us -> 92.2 us
  other arithmetic: 39.8 us -> 81.8 us
  blocking collectives: 38.3 us -> 0 us
  starting transfers between devices: 103 us -> 87.1 us
    ppermute x84 -> x80, waiting for transfers between devices: 484 us -> 234 us  [other(): return lax.ppermute(value, axis, [(i, i ^ bit) for i in range(size)])]
    ppermute x0 -> x16, waiting for transfers between devices: none -> 48.2 us  [along_tensor(): return lax.ppermute(value, 'tensor', pairs)]
    ppermute x84 -> x80, starting transfers between devices: 103 us -> 64.2 us  [other(): return lax.ppermute(value, axis, [(i, i ^ bit) for i in range(size)])]
    psum x1 -> x0, blocking collectives: 38.3 us -> none  [shards(): lax.psum((own_order(g_norm, m, 0), own_order(g_mlp, m, 0), g_head_gain[0]...]
    ppermute x0 -> x16, starting transfers between devices: none -> 23 us  [along_tensor(): return lax.ppermute(value, 'tensor', pairs)]
    slice x12 -> x38, local copies, waits for them, and re-layouts: 3.99 us -> 26.2 us  [the longest x3 3.94 us: shards(): v[block, :2 * block].reshape(2, block)]
    convert_element_type x1 -> x17, other arithmetic: 0.6 us -> 17.3 us  [the longest x3 6.21 us: over_dp(): low = value.astype(bf16)]
    dot_general x30 -> x26, matrix products: 82.2 us -> 80.1 us  [matmul(): return lax.dot_general(a, b, (dims, ((), ())), preferred_element_type=f32)]
  transfers between devices with their start and end apart: 84 -> 96, of which waited for: 32 -> 38; matrix products, arithmetic and copies ran while one was open for 13% -> 27% of each run, Pallas kernels for 9% -> 11%
where the time goes in v3:
time: 710 us; the launch traced here: 704 us
  waiting for transfers between devices  282 us (40%)
  local copies, waits for them, and re-layouts  92.2 us (13%)
  starting transfers between devices  87.1 us (12%)
  other arithmetic  81.8 us (12%)
  matrix products  80.1 us (11%)
  Pallas kernels  74.7 us (11%)
    ppermute x80, waiting for transfers between devices, other(): return lax.ppermute(value, axis, [(i, i ^ bit) for i in range(size)])  234 us
    dot_general x26, matrix products, matmul(): return lax.dot_general(a, b, (dims, ((), ())), preferred_element_type=f32)  80.1 us
    ppermute x80, starting transfers between devices, other(): return lax.ppermute(value, axis, [(i, i ^ bit) for i in range(size)])  64.2 us
    ppermute x16, waiting for transfers between devices, along_tensor(): return lax.ppermute(value, 'tensor', pairs)  48.2 us
    pallas_call x1, Pallas kernels, head_forward(): pl.pallas_call(forward_body, grid_spec=pltpu.PrefetchScalarGridSpec(num_s...  40.3 us
    pallas_call x1, Pallas kernels, head_backward(): pl.pallas_call(backward_body, grid_spec=pltpu.PrefetchScalarGridSpec(num_...  34.3 us
    unnamed x218, local copies, waits for them, and re-layouts  23.5 us
    ppermute x16, starting transfers between devices, along_tensor(): return lax.ppermute(value, 'tensor', pairs)  23 us
  transfers between devices with their start and end apart: 96, of which 38 were waited for; matrix products, arithmetic and copies ran while one was open for 27% of the time, Pallas kernels for 11%

profile of v3, /device:TPU:0, one launch (start us, length us, event | category | flops | bytes accessed | tf_op | source)
XLA Modules:
  0.0 704.5 jit_solution(2657148335523975425)
XLA Ops:
  12.0 3.0 fusion.31
  15.1 3.1 collective-permute-start
  18.1 2.6 collective-permute-start.1
  20.7 2.4 copy.55
  34.0 7.4 %collective-permute-done = bf16[128,2048]{1,0:T(8,128)(2,1)} collective-permute-done((bf16[128,2048]{1,0:T(8,128)(2,1)}, bf16[128,2048]{1,0:T(8,128)(2,1)}, u32[]{:S(2)}, u32[]{:S(2)}) %collective-permute-start) | collective-permute-done | bytes 524320 | tf_op jit(solution)/shard_map/ppermute | solution.py:442
  52.0 5.3 collective-permute-done.3
  64.3 12.6 %collective-permute-done.9 = bf16[528,1024]{1,0:T(8,128)(2,1)} collective-permute-done((bf16[528,1024]{1,0:T(8,128)(2,1)S(1)}, bf16[528,1024]{1,0:T(8,128)(2,1)}, u32[]{:S(2)}, u32[]{:S(2)}) %collective-permute-start.9) | collective-permute-done | bytes 1081376 | tf_op jit(solution)/shard_map/ppermute | solution.py:442
  83.1 2.4 slice.908
  91.7 5.1 pad_maximum_fusion.2
  98.0 3.6 collective-permute-start.34
  102.4 2.4 fusion.23
  104.8 3.3 fusion.20.near_ref.before_near_ref
  112.1 10.3 %collective-permute-done.34 = bf16[128,2048]{1,0:T(8,128)(2,1)} collective-permute-done((bf16[128,2048]{1,0:T(8,128)(2,1)}, bf16[128,2048]{1,0:T(8,128)(2,1)}, u32[]{:S(2)}, u32[]{:S(2)}) %collective-permute-start.34) | collective-permute-done | bytes 524320 | tf_op jit(solution)/shard_map/ppermute | solution.py:442
  123.1 2.7 collective-permute-done.35
  129.8 9.8 %collective-permute-done.37 = bf16[128,2048]{1,0:T(8,128)(2,1)S(1)} collective-permute-done((bf16[128,2048]{1,0:T(8,128)(2,1)}, bf16[128,2048]{1,0:T(8,128)(2,1)S(1)}, u32[]{:S(2)}, u32[]{:S(2)}) %collective-permute-start.37) | collective-permute-done | bytes 524320 | tf_op jit(solution)/shard_map/ppermute | solution.py:489
  146.9 8.9 %collective-permute-done.13 = bf16[512,512]{1,0:T(8,128)(2,1)S(1)} collective-permute-done((bf16[512,512]{1,0:T(8,128)(2,1)}, bf16[512,512]{1,0:T(8,128)(2,1)S(1)}, u32[]{:S(2)}, u32[]{:S(2)}) %collective-permute-start.13) | collective-permute-done | bytes 524320 | tf_op jit(solution)/shard_map/ppermute | solution.py:442
  157.3 40.3 %head_forward.1 = (bf16[2048,128]{1,0:T(8,128)(2,1)}, f32[8,128]{1,0:T(8,128)}, f32[3,2048,128]{2,1,0:T(8,128)}, f32[2048,256]{1,0:T(8,128)}, f32[2048,128]{1,0:...) custom-call(s32[8]{0:T(128)} %bitcast.125, ...), custom_call_target="tpu_custom_call" | custom-call | tf_op jit(solution)/shard_map/head_forward/pallas_call | solution.py:367
  205.3 2.7 collective-permute-done.12
  218.9 9.9 %collective-permute-done.19 = bf16[128,2048]{1,0:T(8,128)(2,1)S(1)} collective-permute-done((bf16[128,2048]{1,0:T(8,128)(2,1)S(1)}, bf16[128,2048]{1,0:T(8,128)(2,1)S(1)}, u32[]{:S(2)}, u32[]{:S(2)}) %collective-permute-start.19) | collective-permute-done | bytes 524320 | tf_op jit(solution)/shard_map/ppermute | solution.py:489
  229.0 2.4 collective-permute-start.20
  233.7 20.8 %collective-permute-done.20 = bf16[128,2048]{1,0:T(8,128)(2,1)S(1)} collective-permute-done((bf16[128,2048]{1,0:T(8,128)(2,1)S(1)}, bf16[128,2048]{1,0:T(8,128)(2,1)S(1)}, u32[]{:S(2)}, u32[]{:S(2)}) %collective-permute-start.20) | collective-permute-done | bytes 524320 | tf_op jit(solution)/shard_map/ppermute | solution.py:442
  258.1 7.3 %fusion.113 = f32[1024,768]{1,0:T(8,128)} fusion(bf16[1024,2048]{1,0:T(8,128)(2,1)} %maximum_dynamic-update-slice_fusion.8, bf16[768,512]{1,0:T(8,128)(2,1)S(1)} %get-tuple-element.147, bf16[768,512]{1,0:T(8,128)(2,1)S(1)} %get-tuple-element.154, bf16[768,512]{1,0:T(8,128)(2,1)S(1)} %get-tuple-element.146, bf16[768,512]{1,0:T(8,128)(2,1)S(1)} %get-tuple-element.152), kind=kOutput, calls=%fused_computation.341 | convolution fusion | flops 3233808384 | bytes 10485760 | tf_op jit(solution)/shard_map/dot_general | solution.py:464
  265.4 9.4 %collective-permute-done.30 = bf16[2,512,1408]{2,1,0:T(8,128)(2,1)S(1)} collective-permute-done((bf16[2,512,1408]{2,1,0:T(8,128)(2,1)S(1)}, bf16[2,512,1408]{2,1,0:T(8,128)(2,1)S(1)}, u32[]{:S(2)}, u32[]{:S(2)}) %collective-permute-start.30) | collective-permute-done | bytes 2883616 | tf_op jit(solution)/shard_map/ppermute | solution.py:442
  275.1 3.8 collective-permute-done.21
  282.8 11.0 %collective-permute-done.24 = bf16[128,2048]{1,0:T(8,128)(2,1)S(1)} collective-permute-done((bf16[128,2048]{1,0:T(8,128)(2,1)S(1)}, bf16[128,2048]{1,0:T(8,128)(2,1)S(1)}, u32[]{:S(2)}, u32[]{:S(2)}) %collective-permute-start.24) | collective-permute-done | bytes 524320 | tf_op jit(solution)/shard_map/ppermute | solution.py:489
  296.6 3.4 fusion.7
  300.1 4.7 multiply_convert_fusion.1
  304.8 3.9 convolution_convert_fusion.1
  310.6 3.8 fusion.6
  314.4 4.2 convolution_convert_fusion.2
  322.7 3.7 convolution_convert_fusion
  326.4 4.1 fusion.66
  330.4 2.8 convolution_convert_fusion.4
  335.7 4.0 convolution_add_fusion
  339.8 2.7 collective-permute-done.43
  347.1 8.5 %collective-permute-done.46 = bf16[128,2048]{1,0:T(8,128)(2,1)S(1)} collective-permute-done((bf16[128,2048]{1,0:T(8,128)(2,1)S(1)}, bf16[128,2048]{1,0:T(8,128)(2,1)S(1)}, u32[]{:S(2)}, u32[]{:S(2)}) %collective-permute-start.46) | collective-permute-done | bytes 524320 | tf_op jit(solution)/shard_map/ppermute | solution.py:489
  355.8 2.9 collective-permute-start.47
  359.9 21.4 %collective-permute-done.47 = bf16[128,2048]{1,0:T(8,128)(2,1)S(1)} collective-permute-done((bf16[128,2048]{1,0:T(8,128)(2,1)S(1)}, bf16[128,2048]{1,0:T(8,128)(2,1)S(1)}, u32[]{:S(2)}, u32[]{:S(2)}) %collective-permute-start.47) | collective-permute-done | bytes 524320 | tf_op jit(solution)/shard_map/ppermute | solution.py:442
  388.7 18.0 %collective-permute-done.48 = bf16[128,2048]{1,0:T(8,128)(2,1)S(1)} collective-permute-done((bf16[128,2048]{1,0:T(8,128)(2,1)S(1)}, bf16[128,2048]{1,0:T(8,128)(2,1)S(1)}, u32[]{:S(2)}, u32[]{:S(2)}) %collective-permute-start.48) | collective-permute-done | bytes 524320 | tf_op jit(solution)/shard_map/ppermute | solution.py:442
  417.3 3.6 collective-permute-done.51
  431.3 4.4 collective-permute-done.62.grad_far_ref
  436.5 34.3 %head_backward.1 = (bf16[2048,512]{1,0:T(8,128)(2,1)}, f32[16,128]{1,0:T(8,128)}, f32[3,4,128]{2,1,0:T(4,128)}, f32[8,128]{1,0:T(8,128)}) custom-call(s32[8]{0:T(128)} %bitcast.126, s32[2]{0:T(128)} %pad_add_fusion.3.info_ref, bf16[1024,512]{1,0:T(8,128)(2,1)} %fusion.20.near_ref.before_near_ref, bf16[1040,512]{1,0:T(8,128)(2,1)} %copy-done.6, ...), custom_call_target="tpu_custom_call" | custom-call | tf_op jit(solution)/shard_map/head_backward/pallas_call | solution.py:414
  471.5 6.9 fusion.111
  487.2 3.8 convert_add_fusion.1
  491.0 5.7 collective-permute-done.84
  498.3 3.6 add_bitcast_fusion.1
  502.0 4.9 collective-permute-start.60
  508.0 11.5 %collective-permute-done.63 = bf16[1040,512]{1,0:T(8,128)(2,1)S(1)} collective-permute-done((bf16[1040,512]{1,0:T(8,128)(2,1)S(1)}, bf16[1040,512]{1,0:T(8,128)(2,1)S(1)}, u32[]{:S(2)}, u32[]{:S(2)}) %collective-permute-start.63) | collective-permute-done | bytes 1064992 | tf_op jit(solution)/shard_map/ppermute | solution.py:442
  523.8 7.7 %add_convert_fusion = bf16[512,2048]{1,0:T(8,128)(2,1)} fusion(f32[512,2048]{1,0:T(8,128)S(1)} %fusion.83, bf16[1024,512]{1,0:T(8,128)(2,1)S(1)} %slice.1026, bf16[1024,512]{1,0:T(8,128)(2,1)S(1)} %get-tuple-element.128, bf16[512,1024]{0,1:T(8,128)(2,1)S(1)} %copy-done.28, bf16[512,1024]{0,1:T(8,128)(2,1)S(1)} %copy-done.29, ...), kind=kOutput, calls=%fused_computation.5 | convolution fusion | flops 2172649472 | bytes 12582912 | tf_op jit(solution)/shard_map/dot_general | solution.py:464
  531.5 2.5 fusion.109
  534.8 4.3 convolution_add_fusion.1
  549.2 2.7 slice.1285
  558.4 2.4 convert_add_fusion
  562.2 5.9 collective-permute-done.86
  570.8 2.9 add_convert_fusion.3
  583.4 16.2 %collective-permute-done.61 = bf16[128,2048]{1,0:T(8,128)(2,1)S(1)} collective-permute-done((bf16[128,2048]{1,0:T(8,128)(2,1)S(1)}, bf16[128,2048]{1,0:T(8,128)(2,1)S(1)}, u32[]{:S(2)}, u32[]{:S(2)}) %collective-permute-start.61) | collective-permute-done | bytes 524320 | tf_op jit(solution)/shard_map/ppermute | solution.py:442
  606.5 29.4 %collective-permute-done.80 = bf16[512,1024]{0,1:T(8,128)(2,1)S(1)} collective-permute-done((bf16[512,1024]{0,1:T(8,128)(2,1)S(1)}, bf16[512,1024]{0,1:T(8,128)(2,1)S(1)}, u32[]{:S(2)}, u32[]{:S(2)}) %collective-permute-start.80) | collective-permute-done | bytes 1048608 | tf_op jit(solution)/shard_map/ppermute | solution.py:442
  647.6 3.7 add_bitcast_fusion
  651.3 16.7 %collective-permute-done.69 = bf16[128,2048]{1,0:T(8,128)(2,1)S(1)} collective-permute-done((bf16[128,2048]{1,0:T(8,128)(2,1)S(1)}, bf16[128,2048]{1,0:T(8,128)(2,1)S(1)}, u32[]{:S(2)}, u32[]{:S(2)}) %collective-permute-start.69) | collective-permute-done | bytes 524320 | tf_op jit(solution)/shard_map/ppermute | solution.py:442
  668.1 2.5 fusion.39
  671.5 4.9 pad_maximum_fusion.1
  677.5 2.7 collective-permute-done.71
  681.6 2.4 collective-permute-done.72
  686.0 2.8 collective-permute-done.73
  (591 shorter events, 229.1 us)
Async XLA Ops:
  15.1 26.4 %collective-permute-start = (bf16[128,2048]{1,0:T(8,128)(2,1)}, bf16[128,2048]{1,0:T(8,128)(2,1)}, u32[]{:S(2)}, u32[]{:S(2)}) collective-permute-start(bf16[128,2048]{1,0:T(8,128)(2,1)} %fusion.34), channel_id=1, source_target_pairs={{0,1},{1,0},{2,3},{3,2},{4,5},{5,4},{6,7},{7,6},{8,9},{9,8},{10,11... | collective-permute-start | bytes 1572872 | tf_op jit(solution)/shard_map/ppermute | solution.py:442
  18.1 25.9 %collective-permute-start.1 = (bf16[128,2048]{1,0:T(8,128)(2,1)}, bf16[128,2048]{1,0:T(8,128)(2,1)}, u32[]{:S(2)}, u32[]{:S(2)}) collective-permute-start(bf16[128,2048]{1,0:T(8,128)(2,1)} %fusion.34), channel_id=1, source_target_pairs={{0,2},{1,3},{2,0},{3,1},{4,6},{5,7},{6,4},{7,5},{8,10},{9,11},{10,... | collective-permute-start | bytes 1572872 | tf_op jit(solution)/shard_map/ppermute | solution.py:442
  20.7 26.7 %collective-permute-start.4 = (bf16[128,2048]{1,0:T(8,128)(2,1)}, bf16[128,2048]{1,0:T(8,128)(2,1)}, u32[]{:S(2)}, u32[]{:S(2)}) collective-permute-start(bf16[128,2048]{1,0:T(8,128)(2,1)} %fusion.34), channel_id=1, source_target_pairs={{0,4},{4,0},{8,12},{12,8},{1,5},{5,1},{9,13},{13,9},{2,6},{6,2},{1... | collective-permute-start | bytes 1572872 | tf_op jit(solution)/shard_map/ppermute | solution.py:442
  23.1 38.5 %collective-permute-start.8 = (bf16[528,1024]{1,0:T(8,128)(2,1)}, bf16[528,1024]{1,0:T(8,128)(2,1)}, u32[]{:S(2)}, u32[]{:S(2)}) collective-permute-start(bf16[528,1024]{1,0:T(8,128)(2,1)} %copy.55), channel_id=1, source_target_pairs={{0,4},{4,0},{8,12},{12,8},{1,5},{5,1},{9,13},{13,9},{2,6},{6,2},{1... | collective-permute-start | bytes 3244040 | tf_op jit(solution)/shard_map/ppermute | solution.py:442
  25.0 38.0 %collective-permute-start.10 = (bf16[528,1024]{1,0:T(8,128)(2,1)}, bf16[528,1024]{1,0:T(8,128)(2,1)}, u32[]{:S(2)}, u32[]{:S(2)}) collective-permute-start(bf16[528,1024]{1,0:T(8,128)(2,1)} %copy.59), channel_id=1, source_target_pairs={{0,12},{4,8},{8,4},{12,0},{1,13},{5,9},{9,5},{13,1},{2,14},{6,10},... | collective-permute-start | bytes 3244040 | tf_op jit(solution)/shard_map/ppermute | solution.py:442
  44.0 13.3 %collective-permute-start.3 = (bf16[128,2048]{1,0:T(8,128)(2,1)}, bf16[128,2048]{1,0:T(8,128)(2,1)S(1)}, u32[]{:S(2)}, u32[]{:S(2)}) collective-permute-start(bf16[128,2048]{1,0:T(8,128)(2,1)} %collective-permute-done.1), channel_id=1, source_target_pairs={{2,3},{1,0},{6,7},{5,4},{10,11},{9,8},{14,15},{13,12},{18,19},{17,... | collective-permute-start | bytes 1572872 | tf_op jit(solution)/shard_map/ppermute | solution.py:489
  50.5 26.4 %collective-permute-start.9 = (bf16[528,1024]{1,0:T(8,128)(2,1)S(1)}, bf16[528,1024]{1,0:T(8,128)(2,1)}, u32[]{:S(2)}, u32[]{:S(2)}) collective-permute-start(bf16[528,1024]{1,0:T(8,128)(2,1)S(1)} %copy-done.51), channel_id=1, source_target_pairs={{0,8},{4,12},{8,0},{12,4},{1,9},{5,13},{9,1},{13,5},{2,10},{6,14},... | collective-permute-start | bytes 3244040 | tf_op jit(solution)/shard_map/ppermute | solution.py:442
  58.5 38.3 %collective-permute-start.7 = (bf16[128,2048]{1,0:T(8,128)(2,1)}, bf16[128,2048]{1,0:T(8,128)(2,1)}, u32[]{:S(2)}, u32[]{:S(2)}) collective-permute-start(bf16[128,2048]{1,0:T(8,128)(2,1)} %get-tuple-element.94), channel_id=1, source_target_pairs={{0,4},{4,0},{8,12},{12,8},{1,5},{5,1},{9,13},{13,9},{2,6},{6,2},{1... | collective-permute-start | bytes 1572872 | tf_op jit(solution)/shard_map/ppermute | solution.py:442
  98.0 24.4 %collective-permute-start.34 = (bf16[128,2048]{1,0:T(8,128)(2,1)}, bf16[128,2048]{1,0:T(8,128)(2,1)}, u32[]{:S(2)}, u32[]{:S(2)}) collective-permute-start(bf16[128,2048]{1,0:T(8,128)(2,1)} %pad_maximum_fusion.22), channel_id=1, source_target_pairs={{0,1},{1,0},{2,3},{3,2},{4,5},{5,4},{6,7},{7,6},{8,9},{9,8},{10,11... | collective-permute-start | bytes 1572872 | tf_op jit(solution)/shard_map/ppermute | solution.py:442
  101.6 24.2 %collective-permute-start.35 = (bf16[128,2048]{1,0:T(8,128)(2,1)}, bf16[128,2048]{1,0:T(8,128)(2,1)}, u32[]{:S(2)}, u32[]{:S(2)}) collective-permute-start(bf16[128,2048]{1,0:T(8,128)(2,1)} %pad_maximum_fusion.22), channel_id=1, source_target_pairs={{0,2},{1,3},{2,0},{3,1},{4,6},{5,7},{6,4},{7,5},{8,10},{9,11},{10,... | collective-permute-start | bytes 1572872 | tf_op jit(solution)/shard_map/ppermute | solution.py:442
  102.4 26.2 %collective-permute-start.38 = (bf16[128,2048]{1,0:T(8,128)(2,1)}, bf16[128,2048]{1,0:T(8,128)(2,1)S(1)}, u32[]{:S(2)}, u32[]{:S(2)}) collective-permute-start(bf16[128,2048]{1,0:T(8,128)(2,1)} %pad_maximum_fusion.22), channel_id=1, source_target_pairs={{0,4},{4,0},{8,12},{12,8},{1,5},{5,1},{9,13},{13,9},{2,6},{6,2},{1... | collective-permute-start | bytes 1572872 | tf_op jit(solution)/shard_map/ppermute | solution.py:442
  109.4 31.2 %collective-permute-start.11 = (bf16[1040,512]{1,0:T(8,128)(2,1)S(1)}, bf16[1040,512]{1,0:T(8,128)(2,1)S(1)}, u32[]{:S(2)}, u32[]{:S(2)}) collective-permute-start(bf16[1040,512]{1,0:T(8,128)(2,1)S(1)} %fusion.32), channel_id=1, source_target_pairs={{0,8},{4,12},{8,0},{12,4},{1,9},{5,13},{9,1},{13,5},{2,10},{6,14},... | collective-permute-start | bytes 3194888 | tf_op jit(solution)/shard_map/ppermute | solution.py:442
  123.0 17.5 %collective-permute-start.39 = (bf16[128,2048]{1,0:T(8,128)(2,1)}, bf16[128,2048]{1,0:T(8,128)(2,1)S(1)}, u32[]{:S(2)}, u32[]{:S(2)}) collective-permute-start(bf16[128,2048]{1,0:T(8,128)(2,1)} %collective-permute-done.34), channel_id=1, source_target_pairs={{0,4},{4,0},{8,12},{12,8},{1,5},{5,1},{9,13},{13,9},{2,6},{6,2},{1... | collective-permute-start | bytes 1572872 | tf_op jit(solution)/shard_map/ppermute | solution.py:442
  125.8 13.8 %collective-permute-start.37 = (bf16[128,2048]{1,0:T(8,128)(2,1)}, bf16[128,2048]{1,0:T(8,128)(2,1)S(1)}, u32[]{:S(2)}, u32[]{:S(2)}) collective-permute-start(bf16[128,2048]{1,0:T(8,128)(2,1)} %collective-permute-done.35), channel_id=1, source_target_pairs={{2,3},{1,0},{6,7},{5,4},{10,11},{9,8},{14,15},{13,12},{18,19},{17,... | collective-permute-start | bytes 1572872 | tf_op jit(solution)/shard_map/ppermute | solution.py:489
  128.6 14.3 %collective-permute-start.40 = (bf16[128,2048]{1,0:T(8,128)(2,1)}, bf16[128,2048]{1,0:T(8,128)(2,1)S(1)}, u32[]{:S(2)}, u32[]{:S(2)}) collective-permute-start(bf16[128,2048]{1,0:T(8,128)(2,1)} %collective-permute-done.35), channel_id=1, source_target_pairs={{0,4},{4,0},{8,12},{12,8},{1,5},{5,1},{9,13},{13,9},{2,6},{6,2},{1... | collective-permute-start | bytes 1572872 | tf_op jit(solution)/shard_map/ppermute | solution.py:442
  140.5 90.8 %collective-permute-start.41 = (bf16[128,2048]{1,0:T(8,128)(2,1)}, bf16[128,2048]{1,0:T(8,128)(2,1)}, u32[]{:S(2)}, u32[]{:S(2)}) collective-permute-start(bf16[128,2048]{1,0:T(8,128)(2,1)} %get-tuple-element.86), channel_id=1, source_target_pairs={{0,4},{4,0},{8,12},{12,8},{1,5},{5,1},{9,13},{13,9},{2,6},{6,2},{1... | collective-permute-start | bytes 1572872 | tf_op jit(solution)/shard_map/ppermute | solution.py:442
  140.7 15.1 %collective-permute-start.13 = (bf16[512,512]{1,0:T(8,128)(2,1)}, bf16[512,512]{1,0:T(8,128)(2,1)S(1)}, u32[]{:S(2)}, u32[]{:S(2)}) collective-permute-start(bf16[512,512]{1,0:T(8,128)(2,1)} %param.19), channel_id=1, source_target_pairs={{0,8},{4,12},{8,0},{12,4},{1,9},{5,13},{9,1},{13,5},{2,10},{6,14},... | collective-permute-start | bytes 1572872 | tf_op jit(solution)/shard_map/ppermute | solution.py:442
  145.1 68.3 %collective-permute-start.32 = (bf16[1408,512]{1,0:T(8,128)(2,1)S(1)}, bf16[1408,512]{1,0:T(8,128)(2,1)}, u32[]{:S(2)}, u32[]{:S(2)}) collective-permute-start(bf16[1408,512]{1,0:T(8,128)(2,1)S(1)} %copy-done.38), channel_id=1, source_target_pairs={{0,8},{4,12},{8,0},{12,4},{1,9},{5,13},{9,1},{13,5},{2,10},{6,14},... | collective-permute-start | bytes 4325384 | tf_op jit(solution)/shard_map/ppermute | solution.py:442
  156.6 47.5 %collective-permute-start.14 = (bf16[256,1024]{1,0:T(8,128)(2,1)S(1)}, bf16[256,1024]{1,0:T(8,128)(2,1)}, u32[]{:S(2)}, u32[]{:S(2)}) collective-permute-start(bf16[256,1024]{1,0:T(8,128)(2,1)S(1)} %maximum_maximum_fusion), channel_id=1, source_target_pairs={{0,4},{4,0},{8,12},{12,8},{1,5},{5,1},{9,13},{13,9},{2,6},{6,2},{1... | collective-permute-start | bytes 1572872 | tf_op jit(solution)/shard_map/ppermute | solution.py:442
  210.5 64.3 %collective-permute-start.30 = (bf16[2,512,1408]{2,1,0:T(8,128)(2,1)S(1)}, bf16[2,512,1408]{2,1,0:T(8,128)(2,1)S(1)}, u32[]{:S(2)}, u32[]{:S(2)}) collective-permute-start(bf16[2,512,1408]{2,1,0:T(8,128)(2,1)S(1)} %copy-done.31), channel_id=1, source_target_pairs={{0,8},{4,12},{8,0},{12,4},{1,9},{5,13},{9,1},{13,5},{2,10},{6,14},... | collective-permute-start | bytes 8650760 | tf_op jit(solution)/shard_map/ppermute | solution.py:442
  215.0 18.5 %collective-permute-start.33 = (bf16[768,1024]{1,0:T(8,128)(2,1)S(1)}, bf16[768,1024]{1,0:T(8,128)(2,1)S(1)}, u32[]{:S(2)}, u32[]{:S(2)}) collective-permute-start(bf16[768,1024]{1,0:T(8,128)(2,1)S(1)} %pad_maximum_fusion.6), channel_id=1, source_target_pairs={{0,4},{4,0},{8,12},{12,8},{1,5},{5,1},{9,13},{13,9},{2,6},{6,2},{1... | collective-permute-start | bytes 4718600 | tf_op jit(solution)/shard_map/ppermute | solution.py:442
  215.9 12.9 %collective-permute-start.19 = (bf16[128,2048]{1,0:T(8,128)(2,1)S(1)}, bf16[128,2048]{1,0:T(8,128)(2,1)S(1)}, u32[]{:S(2)}, u32[]{:S(2)}) collective-permute-start(bf16[128,2048]{1,0:T(8,128)(2,1)S(1)} %fusion.59), channel_id=1, source_target_pairs={{3,2},{0,1},{7,6},{4,5},{11,10},{8,9},{15,14},{12,13},{19,18},{16,... | collective-permute-start | bytes 1572872 | tf_op jit(solution)/shard_map/ppermute | solution.py:489
  217.5 16.2 %collective-permute-start.17 = (bf16[128,2048]{1,0:T(8,128)(2,1)S(1)}, bf16[128,2048]{1,0:T(8,128)(2,1)S(1)}, u32[]{:S(2)}, u32[]{:S(2)}) collective-permute-start(bf16[128,2048]{1,0:T(8,128)(2,1)S(1)} %fusion.59), channel_id=1, source_target_pairs={{1,2},{2,1},{5,6},{6,5},{9,10},{10,9},{13,14},{14,13},{17,18},{18,... | collective-permute-start | bytes 1572872 | tf_op jit(solution)/shard_map/ppermute | solution.py:489
  229.0 25.5 %collective-permute-start.20 = (bf16[128,2048]{1,0:T(8,128)(2,1)S(1)}, bf16[128,2048]{1,0:T(8,128)(2,1)S(1)}, u32[]{:S(2)}, u32[]{:S(2)}) collective-permute-start(bf16[128,2048]{1,0:T(8,128)(2,1)S(1)} %fusion.58), channel_id=1, source_target_pairs={{0,2},{1,3},{2,0},{3,1},{4,6},{5,7},{6,4},{7,5},{8,10},{9,11},{10,... | collective-permute-start | bytes 1572872 | tf_op jit(solution)/shard_map/ppermute | solution.py:442
  231.4 23.1 %collective-permute-start.18 = (bf16[128,2048]{1,0:T(8,128)(2,1)S(1)}, bf16[128,2048]{1,0:T(8,128)(2,1)S(1)}, u32[]{:S(2)}, u32[]{:S(2)}) collective-permute-start(bf16[128,2048]{1,0:T(8,128)(2,1)S(1)} %slice.1290), channel_id=1, source_target_pairs={{0,1},{1,0},{2,3},{3,2},{4,5},{5,4},{6,7},{7,6},{8,9},{9,8},{10,11... | collective-permute-start | bytes 1572872 | tf_op jit(solution)/shard_map/ppermute | solution.py:442
  233.6 62.5 %collective-permute-start.29 = (bf16[2,512,768]{2,1,0:T(8,128)(2,1)S(1)}, bf16[2,512,768]{2,1,0:T(8,128)(2,1)S(1)}, u32[]{:S(2)}, u32[]{:S(2)}) collective-permute-start(bf16[2,512,768]{2,1,0:T(8,128)(2,1)S(1)} %get-tuple-element.121), channel_id=1, source_target_pairs={{0,4},{4,0},{8,12},{12,8},{1,5},{5,1},{9,13},{13,9},{2,6},{6,2},{1... | collective-permute-start | bytes 4718600 | tf_op jit(solution)/shard_map/ppermute | solution.py:442
  255.2 23.7 %collective-permute-start.21 = (bf16[128,2048]{1,0:T(8,128)(2,1)S(1)}, bf16[128,2048]{1,0:T(8,128)(2,1)S(1)}, u32[]{:S(2)}, u32[]{:S(2)}) collective-permute-start(bf16[128,2048]{1,0:T(8,128)(2,1)S(1)} %get-tuple-element.44), channel_id=1, source_target_pairs={{0,1},{1,0},{2,3},{3,2},{4,5},{5,4},{6,7},{7,6},{8,9},{9,8},{10,11... | collective-permute-start | bytes 1572872 | tf_op jit(solution)/shard_map/ppermute | solution.py:442
  256.4 24.1 %collective-permute-start.22 = (bf16[128,2048]{1,0:T(8,128)(2,1)S(1)}, bf16[128,2048]{1,0:T(8,128)(2,1)S(1)}, u32[]{:S(2)}, u32[]{:S(2)}) collective-permute-start(bf16[128,2048]{1,0:T(8,128)(2,1)S(1)} %get-tuple-element.44), channel_id=1, source_target_pairs={{0,2},{1,3},{2,0},{3,1},{4,6},{5,7},{6,4},{7,5},{8,10},{9,11},{10,... | collective-permute-start | bytes 1572872 | tf_op jit(solution)/shard_map/ppermute | solution.py:442
  265.4 16.7 %collective-permute-start.25 = (bf16[128,2048]{1,0:T(8,128)(2,1)S(1)}, bf16[128,2048]{1,0:T(8,128)(2,1)S(1)}, u32[]{:S(2)}, u32[]{:S(2)}) collective-permute-start(bf16[128,2048]{1,0:T(8,128)(2,1)S(1)} %get-tuple-element.44), channel_id=1, source_target_pairs={{0,4},{4,0},{8,12},{12,8},{1,5},{5,1},{9,13},{13,9},{2,6},{6,2},{1... | collective-permute-start | bytes 1572872 | tf_op jit(solution)/shard_map/ppermute | solution.py:442
  275.0 21.1 %collective-permute-start.31 = (bf16[2,512,768]{2,1,0:T(8,128)(2,1)S(1)}, bf16[2,512,768]{2,1,0:T(8,128)(2,1)S(1)}, u32[]{:S(2)}, u32[]{:S(2)}) collective-permute-start(bf16[2,512,768]{2,1,0:T(8,128)(2,1)S(1)} %get-tuple-element.123), channel_id=1, source_target_pairs={{0,4},{4,0},{8,12},{12,8},{1,5},{5,1},{9,13},{13,9},{2,6},{6,2},{1... | collective-permute-start | bytes 4718600 | tf_op jit(solution)/shard_map/ppermute | solution.py:442
  280.5 13.3 %collective-permute-start.24 = (bf16[128,2048]{1,0:T(8,128)(2,1)S(1)}, bf16[128,2048]{1,0:T(8,128)(2,1)S(1)}, u32[]{:S(2)}, u32[]{:S(2)}) collective-permute-start(bf16[128,2048]{1,0:T(8,128)(2,1)S(1)} %collective-permute-done.22), channel_id=1, source_target_pairs={{2,3},{1,0},{6,7},{5,4},{10,11},{9,8},{14,15},{13,12},{18,19},{17,... | collective-permute-start | bytes 1572872 | tf_op jit(solution)/shard_map/ppermute | solution.py:489
  334.3 24.5 %collective-permute-start.87 = (bf16[1024,768]{1,0:T(8,128)(2,1)S(1)}, bf16[1024,768]{1,0:T(8,128)(2,1)S(1)}, u32[]{:S(2)}, u32[]{:S(2)}) collective-permute-start(bf16[1024,768]{1,0:T(8,128)(2,1)S(1)} %pad_maximum_fusion.8), channel_id=1, source_target_pairs={{0,4},{4,0},{8,12},{12,8},{1,5},{5,1},{9,13},{13,9},{2,6},{6,2},{1... | collective-permute-start | bytes 4718600 | tf_op jit(solution)/shard_map/ppermute | solution.py:442
  335.0 51.0 %collective-permute-start.90 = (bf16[1024,768]{1,0:T(8,128)(2,1)S(1)}, bf16[1024,768]{1,0:T(8,128)(2,1)S(1)}, u32[]{:S(2)}, u32[]{:S(2)}) collective-permute-start(bf16[1024,768]{1,0:T(8,128)(2,1)S(1)} %pad_maximum_fusion.10), channel_id=1, source_target_pairs={{0,4},{4,0},{8,12},{12,8},{1,5},{5,1},{9,13},{13,9},{2,6},{6,2},{1... | collective-permute-start | bytes 4718600 | tf_op jit(solution)/shard_map/ppermute | solution.py:442
  342.6 13.0 %collective-permute-start.46 = (bf16[128,2048]{1,0:T(8,128)(2,1)S(1)}, bf16[128,2048]{1,0:T(8,128)(2,1)S(1)}, u32[]{:S(2)}, u32[]{:S(2)}) collective-permute-start(bf16[128,2048]{1,0:T(8,128)(2,1)S(1)} %fusion.55), channel_id=1, source_target_pairs={{3,2},{0,1},{7,6},{4,5},{11,10},{8,9},{15,14},{12,13},{19,18},{16,... | collective-permute-start | bytes 1572872 | tf_op jit(solution)/shard_map/ppermute | solution.py:489
  344.1 15.4 %collective-permute-start.44 = (bf16[128,2048]{1,0:T(8,128)(2,1)S(1)}, bf16[128,2048]{1,0:T(8,128)(2,1)S(1)}, u32[]{:S(2)}, u32[]{:S(2)}) collective-permute-start(bf16[128,2048]{1,0:T(8,128)(2,1)S(1)} %fusion.55), channel_id=1, source_target_pairs={{1,2},{2,1},{5,6},{6,5},{9,10},{10,9},{13,14},{14,13},{17,18},{18,... | collective-permute-start | bytes 1572872 | tf_op jit(solution)/shard_map/ppermute | solution.py:489
  345.9 65.6 %collective-permute-start.94 = (bf16[1408,512]{1,0:T(8,128)(2,1)S(1)}, bf16[1408,512]{1,0:T(8,128)(2,1)S(1)}, u32[]{:S(2)}, u32[]{:S(2)}) collective-permute-start(bf16[1408,512]{1,0:T(8,128)(2,1)S(1)} %pad_add_fusion), channel_id=1, source_target_pairs={{0,8},{4,12},{8,0},{12,4},{1,9},{5,13},{9,1},{13,5},{2,10},{6,14},... | collective-permute-start | bytes 4325384 | tf_op jit(solution)/shard_map/ppermute | solution.py:442
  355.8 25.6 %collective-permute-start.47 = (bf16[128,2048]{1,0:T(8,128)(2,1)S(1)}, bf16[128,2048]{1,0:T(8,128)(2,1)S(1)}, u32[]{:S(2)}, u32[]{:S(2)}) collective-permute-start(bf16[128,2048]{1,0:T(8,128)(2,1)S(1)} %fusion.54), channel_id=1, source_target_pairs={{0,2},{1,3},{2,0},{3,1},{4,6},{5,7},{6,4},{7,5},{8,10},{9,11},{10,... | collective-permute-start | bytes 1572872 | tf_op jit(solution)/shard_map/ppermute | solution.py:442
  358.7 22.6 %collective-permute-start.45 = (bf16[128,2048]{1,0:T(8,128)(2,1)S(1)}, bf16[128,2048]{1,0:T(8,128)(2,1)S(1)}, u32[]{:S(2)}, u32[]{:S(2)}) collective-permute-start(bf16[128,2048]{1,0:T(8,128)(2,1)S(1)} %slice.1289), channel_id=1, source_target_pairs={{0,1},{1,0},{2,3},{3,2},{4,5},{5,4},{6,7},{7,6},{8,9},{9,8},{10,11... | collective-permute-start | bytes 1572872 | tf_op jit(solution)/shard_map/ppermute | solution.py:442
  359.6 54.2 %collective-permute-start.88 = (bf16[512,1408]{1,0:T(8,128)(2,1)S(1)}, bf16[512,1408]{1,0:T(8,128)(2,1)S(1)}, u32[]{:S(2)}, u32[]{:S(2)}) collective-permute-start(bf16[512,1408]{1,0:T(8,128)(2,1)S(1)} %pad_add_fusion.2), channel_id=1, source_target_pairs={{0,8},{4,12},{8,0},{12,4},{1,9},{5,13},{9,1},{13,5},{2,10},{6,14},... | collective-permute-start | bytes 4325384 | tf_op jit(solution)/shard_map/ppermute | solution.py:442
  383.3 23.3 %collective-permute-start.48 = (bf16[128,2048]{1,0:T(8,128)(2,1)S(1)}, bf16[128,2048]{1,0:T(8,128)(2,1)S(1)}, u32[]{:S(2)}, u32[]{:S(2)}) collective-permute-start(bf16[128,2048]{1,0:T(8,128)(2,1)S(1)} %get-tuple-element.49), channel_id=1, source_target_pairs={{0,1},{1,0},{2,3},{3,2},{4,5},{5,4},{6,7},{7,6},{8,9},{9,8},{10,11... | collective-permute-start | bytes 1572872 | tf_op jit(solution)/shard_map/ppermute | solution.py:442
  385.1 24.6 %collective-permute-start.49 = (bf16[128,2048]{1,0:T(8,128)(2,1)S(1)}, bf16[128,2048]{1,0:T(8,128)(2,1)S(1)}, u32[]{:S(2)}, u32[]{:S(2)}) collective-permute-start(bf16[128,2048]{1,0:T(8,128)(2,1)S(1)} %get-tuple-element.49), channel_id=1, source_target_pairs={{0,2},{1,3},{2,0},{3,1},{4,6},{5,7},{6,4},{7,5},{8,10},{9,11},{10,... | collective-permute-start | bytes 1572872 | tf_op jit(solution)/shard_map/ppermute | solution.py:442
  388.0 23.3 %collective-permute-start.52 = (bf16[128,2048]{1,0:T(8,128)(2,1)S(1)}, bf16[128,2048]{1,0:T(8,128)(2,1)S(1)}, u32[]{:S(2)}, u32[]{:S(2)}) collective-permute-start(bf16[128,2048]{1,0:T(8,128)(2,1)S(1)} %get-tuple-element.49), channel_id=1, source_target_pairs={{0,4},{4,0},{8,12},{12,8},{1,5},{5,1},{9,13},{13,9},{2,6},{6,2},{1... | collective-permute-start | bytes 1572872 | tf_op jit(solution)/shard_map/ppermute | solution.py:442
  413.8 72.7 %collective-permute-start.95 = (bf16[1408,512]{1,0:T(8,128)(2,1)}, bf16[1408,512]{1,0:T(8,128)(2,1)}, u32[]{:S(2)}, u32[]{:S(2)}) collective-permute-start(bf16[1408,512]{1,0:T(8,128)(2,1)} %add_convert_fusion.2), channel_id=1, source_target_pairs={{0,16},{16,0},{1,17},{17,1},{2,18},{18,2},{3,19},{19,3},{4,20},{20... | collective-permute-start | bytes 4325384 | tf_op jit(solution)/shard_map/ppermute | solution.py:442
  416.8 81.4 %collective-permute-start.89 = (bf16[512,1408]{1,0:T(8,128)(2,1)}, bf16[512,1408]{1,0:T(8,128)(2,1)}, u32[]{:S(2)}, u32[]{:S(2)}) collective-permute-start(bf16[512,1408]{1,0:T(8,128)(2,1)} %add_convert_fusion.4), channel_id=1, source_target_pairs={{0,16},{16,0},{1,17},{17,1},{2,18},{18,2},{3,19},{19,3},{4,20},{20... | collective-permute-start | bytes 4325384 | tf_op jit(solution)/shard_map/ppermute | solution.py:442
  430.8 51.0 %collective-permute-start.57 = (bf16[128,2048]{1,0:T(8,128)(2,1)}, bf16[128,2048]{1,0:T(8,128)(2,1)}, u32[]{:S(2)}, u32[]{:S(2)}) collective-permute-start(bf16[128,2048]{1,0:T(8,128)(2,1)} %slice.801), channel_id=1, source_target_pairs={{0,4},{4,0},{8,12},{12,8},{1,5},{5,1},{9,13},{13,9},{2,6},{6,2},{1... | collective-permute-start | bytes 1572872 | tf_op jit(solution)/shard_map/ppermute | solution.py:442
  430.9 125.0 %collective-permute-start.56 = (bf16[384,2048]{1,0:T(8,128)(2,1)}, bf16[384,2048]{1,0:T(8,128)(2,1)}, u32[]{:S(2)}, u32[]{:S(2)}) collective-permute-start(bf16[384,2048]{1,0:T(8,128)(2,1)} %slice.794), channel_id=1, source_target_pairs={{0,4},{4,0},{8,12},{12,8},{1,5},{5,1},{9,13},{13,9},{2,6},{6,2},{1... | collective-permute-start | bytes 4718600 | tf_op jit(solution)/shard_map/ppermute | solution.py:442
  435.8 134.5 %collective-permute-start.91 = (bf16[512,1408]{1,0:T(8,128)(2,1)}, bf16[512,1408]{1,0:T(8,128)(2,1)}, u32[]{:S(2)}, u32[]{:S(2)}) collective-permute-start(bf16[512,1408]{1,0:T(8,128)(2,1)} %pad_add_fusion.1), channel_id=1, source_target_pairs={{0,8},{4,12},{8,0},{12,4},{1,9},{5,13},{9,1},{13,5},{2,10},{6,14},... | collective-permute-start | bytes 4325384 | tf_op jit(solution)/shard_map/ppermute | solution.py:442
  481.8 14.9 %collective-permute-start.84 = (bf16[256,1024]{1,0:T(8,128)(2,1)S(1)}, bf16[256,1024]{1,0:T(8,128)(2,1)S(1)}, u32[]{:S(2)}, u32[]{:S(2)}) collective-permute-start(bf16[256,1024]{1,0:T(8,128)(2,1)S(1)} %slice.1286), channel_id=1, source_target_pairs={{0,8},{4,12},{8,0},{12,4},{1,9},{5,13},{9,1},{13,5},{2,10},{6,14},... | collective-permute-start | bytes 1572872 | tf_op jit(solution)/shard_map/ppermute | solution.py:442
  486.5 33.0 %collective-permute-start.63 = (bf16[1040,512]{1,0:T(8,128)(2,1)S(1)}, bf16[1040,512]{1,0:T(8,128)(2,1)S(1)}, u32[]{:S(2)}, u32[]{:S(2)}) collective-permute-start(bf16[1040,512]{1,0:T(8,128)(2,1)S(1)} %fusion.33), channel_id=1, source_target_pairs={{0,8},{4,12},{8,0},{12,4},{1,9},{5,13},{9,1},{13,5},{2,10},{6,14},... | collective-permute-start | bytes 3194888 | tf_op jit(solution)/shard_map/ppermute | solution.py:442
  496.6 43.7 %collective-permute-start.75 = (bf16[1024,512]{0,1:T(8,128)(2,1)S(1)}, bf16[1024,512]{0,1:T(8,128)(2,1)S(1)}, u32[]{:S(2)}, u32[]{:S(2)}) collective-permute-start(bf16[1024,512]{0,1:T(8,128)(2,1)S(1)} %slice.1284), channel_id=1, source_target_pairs={{0,8},{4,12},{8,0},{12,4},{1,9},{5,13},{9,1},{13,5},{2,10},{6,14},... | collective-permute-start | bytes 3145736 | tf_op jit(solution)/shard_map/ppermute | solution.py:442
  502.0 58.9 %collective-permute-start.60 = (bf16[128,2048]{1,0:T(8,128)(2,1)}, bf16[128,2048]{1,0:T(8,128)(2,1)}, u32[]{:S(2)}, u32[]{:S(2)}) collective-permute-start(bf16[128,2048]{1,0:T(8,128)(2,1)} %add_convert_fusion.5), channel_id=1, source_target_pairs={{3,2},{0,1},{7,6},{4,5},{11,10},{8,9},{15,14},{12,13},{19,18},{16,... | collective-permute-start | bytes 1572872 | tf_op jit(solution)/shard_map/ppermute | solution.py:489
  519.5 63.3 %collective-permute-start.58 = (bf16[128,2048]{1,0:T(8,128)(2,1)}, bf16[128,2048]{1,0:T(8,128)(2,1)}, u32[]{:S(2)}, u32[]{:S(2)}) collective-permute-start(bf16[128,2048]{1,0:T(8,128)(2,1)} %add_convert_fusion.5), channel_id=1, source_target_pairs={{1,2},{2,1},{5,6},{6,5},{9,10},{10,9},{13,14},{14,13},{17,18},{18,... | collective-permute-start | bytes 1572872 | tf_op jit(solution)/shard_map/ppermute | solution.py:489
  554.1 14.0 %collective-permute-start.86 = (bf16[512,512]{1,0:T(8,128)(2,1)}, bf16[512,512]{1,0:T(8,128)(2,1)}, u32[]{:S(2)}, u32[]{:S(2)}) collective-permute-start(bf16[512,512]{1,0:T(8,128)(2,1)} %pad_maximum_fusion.25), channel_id=1, source_target_pairs={{0,16},{16,0},{1,17},{17,1},{2,18},{18,2},{3,19},{19,3},{4,20},{20... | collective-permute-start | bytes 1572872 | tf_op jit(solution)/shard_map/ppermute | solution.py:442
  555.8 25.0 %collective-permute-start.76 = (bf16[1024,512]{0,1:T(8,128)(2,1)}, bf16[1024,512]{0,1:T(8,128)(2,1)S(1)}, u32[]{:S(2)}, u32[]{:S(2)}) collective-permute-start(bf16[1024,512]{0,1:T(8,128)(2,1)} %slice.1285), channel_id=1, source_target_pairs={{0,8},{4,12},{8,0},{12,4},{1,9},{5,13},{9,1},{13,5},{2,10},{6,14},... | collective-permute-start | bytes 3145736 | tf_op jit(solution)/shard_map/ppermute | solution.py:442
  570.3 70.0 %collective-permute-start.64 = (bf16[384,2048]{1,0:T(8,128)(2,1)}, bf16[384,2048]{1,0:T(8,128)(2,1)}, u32[]{:S(2)}, u32[]{:S(2)}) collective-permute-start(bf16[384,2048]{1,0:T(8,128)(2,1)} %slice.1036), channel_id=1, source_target_pairs={{0,4},{4,0},{8,12},{12,8},{1,5},{5,1},{9,13},{13,9},{2,6},{6,2},{1... | collective-permute-start | bytes 4718600 | tf_op jit(solution)/shard_map/ppermute | solution.py:442
  573.7 26.0 %collective-permute-start.61 = (bf16[128,2048]{1,0:T(8,128)(2,1)S(1)}, bf16[128,2048]{1,0:T(8,128)(2,1)S(1)}, u32[]{:S(2)}, u32[]{:S(2)}) collective-permute-start(bf16[128,2048]{1,0:T(8,128)(2,1)S(1)} %fusion.49), channel_id=1, source_target_pairs={{0,2},{1,3},{2,0},{3,1},{4,6},{5,7},{6,4},{7,5},{8,10},{9,11},{10,... | collective-permute-start | bytes 1572872 | tf_op jit(solution)/shard_map/ppermute | solution.py:442
  575.4 25.9 %collective-permute-start.59 = (bf16[128,2048]{1,0:T(8,128)(2,1)S(1)}, bf16[128,2048]{1,0:T(8,128)(2,1)S(1)}, u32[]{:S(2)}, u32[]{:S(2)}) collective-permute-start(bf16[128,2048]{1,0:T(8,128)(2,1)S(1)} %slice.1288), channel_id=1, source_target_pairs={{0,1},{1,0},{2,3},{3,2},{4,5},{5,4},{6,7},{7,6},{8,9},{9,8},{10,11... | collective-permute-start | bytes 1572872 | tf_op jit(solution)/shard_map/ppermute | solution.py:442
  580.8 66.7 %collective-permute-start.92 = (bf16[512,1408]{1,0:T(8,128)(2,1)}, bf16[512,1408]{1,0:T(8,128)(2,1)}, u32[]{:S(2)}, u32[]{:S(2)}) collective-permute-start(bf16[512,1408]{1,0:T(8,128)(2,1)} %add_convert_fusion.3), channel_id=1, source_target_pairs={{0,16},{16,0},{1,17},{17,1},{2,18},{18,2},{3,19},{19,3},{4,20},{20... | collective-permute-start | bytes 4325384 | tf_op jit(solution)/shard_map/ppermute | solution.py:442
  582.7 53.2 %collective-permute-start.80 = (bf16[512,1024]{0,1:T(8,128)(2,1)S(1)}, bf16[512,1024]{0,1:T(8,128)(2,1)S(1)}, u32[]{:S(2)}, u32[]{:S(2)}) collective-permute-start(bf16[512,1024]{0,1:T(8,128)(2,1)S(1)} %pad_maximum_fusion.18), channel_id=1, source_target_pairs={{0,16},{16,0},{1,17},{17,1},{2,18},{18,2},{3,19},{19,3},{4,20},{20... | collective-permute-start | bytes 3145736 | tf_op jit(solution)/shard_map/ppermute | solution.py:442
  599.7 44.5 %collective-permute-start.68 = (bf16[128,2048]{1,0:T(8,128)(2,1)}, bf16[128,2048]{1,0:T(8,128)(2,1)S(1)}, u32[]{:S(2)}, u32[]{:S(2)}) collective-permute-start(bf16[128,2048]{1,0:T(8,128)(2,1)} %fusion.45), channel_id=1, source_target_pairs={{3,2},{0,1},{7,6},{4,5},{11,10},{8,9},{15,14},{12,13},{19,18},{16,... | collective-permute-start | bytes 1572872 | tf_op jit(solution)/shard_map/ppermute | solution.py:489
  603.8 47.5 %collective-permute-start.66 = (bf16[128,2048]{1,0:T(8,128)(2,1)}, bf16[128,2048]{1,0:T(8,128)(2,1)}, u32[]{:S(2)}, u32[]{:S(2)}) collective-permute-start(bf16[128,2048]{1,0:T(8,128)(2,1)} %fusion.45), channel_id=1, source_target_pairs={{1,2},{2,1},{5,6},{6,5},{9,10},{10,9},{13,14},{14,13},{17,18},{18,... | collective-permute-start | bytes 1572872 | tf_op jit(solution)/shard_map/ppermute | solution.py:489
  635.9 58.9 %collective-permute-start.78 = (bf16[512,1024]{0,1:T(8,128)(2,1)}, bf16[512,1024]{0,1:T(8,128)(2,1)}, u32[]{:S(2)}, u32[]{:S(2)}) collective-permute-start(bf16[512,1024]{0,1:T(8,128)(2,1)} %pad_maximum_fusion.17), channel_id=1, source_target_pairs={{0,16},{16,0},{1,17},{17,1},{2,18},{18,2},{3,19},{19,3},{4,20},{20... | collective-permute-start | bytes 3145736 | tf_op jit(solution)/shard_map/ppermute | solution.py:442
  644.4 23.6 %collective-permute-start.69 = (bf16[128,2048]{1,0:T(8,128)(2,1)S(1)}, bf16[128,2048]{1,0:T(8,128)(2,1)S(1)}, u32[]{:S(2)}, u32[]{:S(2)}) collective-permute-start(bf16[128,2048]{1,0:T(8,128)(2,1)S(1)} %fusion.44), channel_id=1, source_target_pairs={{0,2},{1,3},{2,0},{3,1},{4,6},{5,7},{6,4},{7,5},{8,10},{9,11},{10,... | collective-permute-start | bytes 1572872 | tf_op jit(solution)/shard_map/ppermute | solution.py:442
  646.2 21.9 %collective-permute-start.67 = (bf16[128,2048]{1,0:T(8,128)(2,1)S(1)}, bf16[128,2048]{1,0:T(8,128)(2,1)S(1)}, u32[]{:S(2)}, u32[]{:S(2)}) collective-permute-start(bf16[128,2048]{1,0:T(8,128)(2,1)S(1)} %slice.1287), channel_id=1, source_target_pairs={{0,1},{1,0},{2,3},{3,2},{4,5},{5,4},{6,7},{7,6},{8,9},{9,8},{10,11... | collective-permute-start | bytes 1572872 | tf_op jit(solution)/shard_map/ppermute | solution.py:442
  (130 other events, 2266.9 us)

commit v4 on v3

--- a/solution.py
+++ b/solution.py
@@ -398,6 +398,7 @@
             s((total, LANES), f32),
         ],
         name="head_forward",
+        cost_estimate=pl.CostEstimate(flops=total * 20_000_000, transcendentals=0, bytes_accessed=total * 10_000),
     )(starts, info, near, far, near, far, logit, taps, gain)
     return outs[0], outs[1][0, 0], tuple(outs[2:])
 
@@ -434,6 +435,7 @@
         ),
         out_shape=[s((total, 4 * LANES), bf16), s(logit.shape, f32), s(taps.shape, f32), s((8, LANES), f32)],
         name="head_backward",
+        cost_estimate=pl.CostEstimate(flops=total * 18_000_000, transcendentals=0, bytes_accessed=total * 10_000),
     )(starts, info, near, far, logit, taps, gain, grad_near, grad_far, *kept)
 
 
@@ -489,62 +491,83 @@
     return lax.ppermute(value, "tensor", pairs)
 
 
-def gather_tensor(value):
-    if not tensor_tree():
+def gather_tensor(value, tree=True, before=()):
+    if not tree or not tensor_tree():
         return [value] + [other(value, "tensor", s) for s in range(1, lax.axis_size("tensor"))]
-    two = other(value, "tensor", 2)
+    two = after(other(value, "tensor", 2), *before)
     one = other(value, "tensor", 1)
     passed = along_tensor(two, [(2, 3), (1, 0)])
     middle = along_tensor(after(value, one), [(1, 2), (2, 1)])
     return [value, one, two, jnp.where(inner_place(), middle, passed)]
 
 
+def with_core(mine, theirs=()):
+    came = list(theirs) + [other(v, "mp", 1) for v in mine[len(theirs):]]
+    return jnp.concatenate(mine + [neighbour_order(v, 1, 1) for v in came], axis=0)
+
+
 def spread(values):
-    mine = gather_tensor(values)
-    theirs = [neighbour_order(other(v, "mp", 1), 1, 1) for v in mine]
-    return jnp.concatenate(mine + theirs, axis=0)
+    return with_core(gather_tensor(values))
 
 
 def partials(rows, body):
     return body(rows // 2, rows).astype(bf16), body(0, rows // 2)
 
 
-def collect(parts):
+def collect_pieces(parts, before=()):
     theirs, mine = parts
     ways = lax.axis_size("tensor")
     piece = mine.shape[0] // ways
+    if not tensor_tree():
+        joined = mine + neighbour_order(other(theirs, "mp", 1), 1, 1).astype(f32)
+        sent = [joined[s * piece:(s + 1) * piece].astype(bf16) for s in range(1, ways)]
+        return joined[:piece], [other(v, "tensor", s + 1) for s, v in enumerate(sent)], sent
     last = (ways - 1) * piece
     tail = mine[last:] + neighbour_order(other(theirs[last:], "mp", 1), 1, 1).astype(f32)
     rest = mine[:last] + neighbour_order(other(theirs[:last], "mp", 1), 1, 1).astype(f32)
-    if not tensor_tree():
-        joined = jnp.concatenate([rest, tail], axis=0)
-        total = joined[:piece]
-        for s in range(1, ways):
-            total = total + other(joined[s * piece:(s + 1) * piece].astype(bf16), "tensor", s).astype(f32)
-        return total
     low = tail.astype(bf16)
     passed = along_tensor(low, [(3, 2), (0, 1)])
     middle = along_tensor(low, [(1, 2), (2, 1)])
-    two = other((rest[2 * piece:] + passed.astype(f32)).astype(bf16), "tensor", 2)
-    one = other(rest[piece:2 * piece].astype(bf16), "tensor", 1)
-    return rest[:piece] + middle.astype(f32) + one.astype(f32) + two.astype(f32)
-
-
-def over_dp(value):
+    sent = [(rest[2 * piece:] + passed.astype(f32)).astype(bf16), rest[piece:2 * piece].astype(bf16)]
+    sent = list(after(sent, middle, *before))
+    return rest[:piece], [middle, other(sent[0], "tensor", 2), other(sent[1], "tensor", 1)], sent
+
+
+def added(own, received):
+    for v in received:
+        own = own + v.astype(f32)
+    return own
+
+
+def over_dp_pieces(value):
+    bit = 1
+    low = value.astype(bf16)
+    came = other(low, "dp", bit)
+    while 2 * bit < lax.axis_size("dp"):
+        bit *= 2
+        low = (low.astype(f32) + came.astype(f32)).astype(bf16)
+        came = other(low, "dp", bit)
+    return low, came
+
+
+def summed(low, came):
+    return low.astype(f32) + came.astype(f32)
+
+
+def over_all(value):
+    for axis in ("mp", "tensor"):
+        if lax.axis_size(axis) == 4:
+            one, two, three = [other(value, axis, bit) for bit in (1, 2, 3)]
+            value = (value + one) + (two + three)
+        else:
+            bit = 1
+            while bit < lax.axis_size(axis):
+                value = value + other(value, axis, bit)
+                bit *= 2
     bit = 1
     while bit < lax.axis_size("dp"):
-        low = value.astype(bf16)
-        value = low.astype(f32) + other(low, "dp", bit).astype(f32)
+        value = value + other(value, "dp", bit)
         bit *= 2
-    return value
-
-
-def over_all(value):
-    for axis in ("mp", "tensor", "dp"):
-        bit = 1
-        while bit < lax.axis_size(axis):
-            value = value + other(value, axis, bit)
-            bit *= 2
     return value
 
 
@@ -570,112 +593,118 @@
     block = w_proj.shape[1]
     near_blocks = 2 * block
 
-    inputs = own_order(tokens, m, 1).astype(f32)
-    gain_one = own_order(norm_gain, m, 0)
-    gain_two = own_order(mlp_gain, m, 0)
-    scaled, unit_one, scale_one = norm_rows(inputs, gain_one)
-    scaled = scaled.astype(bf16)
-
     pieces, _, wide = w_proj.shape
     head = wide // 4
     span = pieces * head
-    heads = [
-        lax.dynamic_slice_in_dim(w_proj, (j ^ m) * head, head, 2).transpose(1, 0, 2).reshape(block, span)
-        for j in range(4)
-    ]
-    beta_rows = own_order(w_beta.T, m, 0)
     pair = lambda values, i, j, axis: jnp.concatenate([values[i], values[j]], axis)
-
-    def with_beta(i, j):
-        row = jnp.concatenate([beta_rows[i], beta_rows[j]])[None]
-        return jnp.concatenate([pair(heads, i, j, 1), jnp.pad(row, ((0, HALO - 1), (0, 2 * span - 2 * block)))], 0)
-
-    far_sent, across_sent, core_sent = with_beta(2, 0), with_beta(3, 1), with_beta(1, 3)
-    far_got = other(far_sent, "mp", 2)
-    across_got = other(across_sent, "mp", 3)
-    core_got = other(core_sent, "mp", 1)
-    own_pair = pair(heads, 0, 2, 1)
-    normed = spread(after(scaled, far_sent, across_sent, core_sent))
-    full_proj = jnp.concatenate([own_pair, core_got[:block], far_got[:block], across_got[:block]], axis=0)
-    full_beta = jnp.concatenate(
-        [jnp.stack([beta_rows[0], beta_rows[2]])]
-        + [v[block, : 2 * block].reshape(2, block) for v in (core_got, far_got, across_got)],
-        axis=1,
-    )
+    proj_got = other(w_proj, "mp", 2)
+    beta_mine = w_beta.T
+    beta_got = other(beta_mine, "mp", 2)
+    scaled = own_order(norm_rows(tokens.astype(f32), norm_gain)[0].astype(bf16), m, 1)
+    normed = spread(scaled)
+    inputs = own_order(after(tokens, normed), m, 1).astype(f32)
+    gain_one = own_order(norm_gain, m, 0)
+    gain_two = own_order(mlp_gain, m, 0)
+    _, unit_one, scale_one = norm_rows(inputs, gain_one)
+
+    def head_blocks(v):
+        return [
+            lax.dynamic_slice_in_dim(v, (j ^ m) * head, head, 2).transpose(1, 0, 2).reshape(block, span)
+            for j in range(4)
+        ]
+
+    proj_mine, proj_far = head_blocks(w_proj), head_blocks(proj_got)
+    proj_low = jnp.concatenate([pair(proj_mine, 0, 2, 1), other(pair(proj_mine, 1, 3, 1), "mp", 1)], axis=0)
+    proj_high = jnp.concatenate([pair(proj_far, 0, 2, 1), other(pair(proj_far, 1, 3, 1), "mp", 1)], axis=0)
+    beta_both = jnp.concatenate([beta_mine, after(beta_got, proj_got)], axis=1)
+    beta_all = own_order(jnp.concatenate([beta_both, other(beta_both, "mp", 1)], axis=1), m, 0)
+    beta_all = pair([beta_all[0:1], beta_all[2:3]], 0, 1, 0)
+    full_beta = jnp.concatenate([beta_all[:, p * block:(p + 1) * block] for p in (0, 2, 1, 3)], axis=1)
     logits = matmul(full_beta, normed, ((1,), (1,))).astype(bf16)
-    far_out = matmul(normed, full_proj[:, span:]).astype(bf16)
+    normed_low, normed_high = normed[:, :near_blocks], normed[:, near_blocks:]
+    far_out = (matmul(normed_low, proj_low[:, span:]) + matmul(normed_high, proj_high[:, span:])).astype(bf16)
     count = far_out.shape[0]
     logit_rows = count // span
     far_sent = jnp.concatenate([far_out, jnp.pad(logits[1].reshape(logit_rows, span), ((0, HALO - logit_rows), (0, 0)))], 0)
-    far = other(far_sent, "mp", 2)
-    near = matmul(normed, full_proj[:, :span]).astype(bf16)
+    units = w_down.shape[0]
+    half = LANES * ((units // LANES + 1) // 2)
+    ours = lambda v, axis: lax.dynamic_slice_in_dim(v, core * (units - half), half, axis)
+    theirs = lambda v, axis: lax.dynamic_slice_in_dim(v, (1 - core) * (units - half), half, axis)
+    cot_own = own_order(cotangent, m, 1)
+    early = after((theirs(w_down, 0), theirs(w_in, 2), cot_own), far_sent)
+    down_core, in_core, cot_core = [other(v, "mp", 1) for v in early]
+    full_proj = jnp.concatenate(after((proj_low, proj_high), far_sent), axis=0)
+    far = after(other(far_sent, "mp", 2), down_core, in_core, cot_core, full_proj)
+    near_low, near_high = after((normed_low, normed_high), far_sent)
+    near = (matmul(near_low, proj_low[:, :span]) + matmul(near_high, proj_high[:, :span])).astype(bf16)
     chunk_rows = (-1, LANES)
     logit = jnp.concatenate(
         [logits[0].reshape(chunk_rows), far[count:count + logit_rows].reshape(chunk_rows)], axis=0
     ).astype(f32)
 
-    units = w_down.shape[0]
-    half = LANES * ((units // LANES + 1) // 2)
-    ours = lambda v, axis: lax.dynamic_slice_in_dim(v, core * (units - half), half, axis)
-    theirs = lambda v, axis: lax.dynamic_slice_in_dim(v, (1 - core) * (units - half), half, axis)
     live = (lax.broadcasted_iota(jnp.int32, (1, half), 1) >= core * (2 * half - units)).astype(f32)
-    w_out = after(w_out, far)
     out_blocks = lambda v: [lax.dynamic_slice_in_dim(v, (j ^ m) * head, head, 0) for j in range(4)]
-    out_mine, out_far = out_blocks(w_out), out_blocks(other(w_out, "mp", 2))
-    w_down = after(w_down, far)
-    down_far = other(w_down, "mp", 2)
-    out_core = other(jnp.concatenate([pair(out_mine, 1, 3, 0), pair(out_far, 1, 3, 0)], axis=1), "mp", 1)
-    full_out = jnp.concatenate(
-        [pair(out_mine, 0, 2, 0), out_core[:, :block], pair(out_far, 0, 2, 0), out_core[:, block:]], axis=1
-    )
-    down_core = other(jnp.concatenate([theirs(w_down, 0), theirs(down_far, 0)], axis=1), "mp", 1)
-    full_down = jnp.concatenate(
-        [ours(w_down, 0), down_core[:, :block], ours(down_far, 0), down_core[:, block:]], axis=1
-    )
-    cot_own = own_order(cotangent, m, 1)
-    cot_all = spread(after(cot_own, normed))
+    rows_sent = after(jnp.concatenate([w_out, w_down], axis=0), far)
+    rows_got = other(rows_sent, "mp", 2)
+    cot_pieces = gather_tensor(after(cot_own, far), tree=False)
 
     taps = conv_weight.reshape(3, conv_weight.shape[1], head)
     info = jnp.stack([lengths[0], place]).astype(jnp.int32)
     head_args = (near, far, logit, taps, out_gain[None], starts[0], info)
     mixed, norm_total, kept = head_forward(*head_args)
+    mixed = after(mixed, rows_got, *cot_pieces)
     mixed_far = other(mixed[count:], "mp", 2)
+    out_mine, out_far = out_blocks(w_out), out_blocks(rows_got[: w_out.shape[0]])
+    out_sent = jnp.concatenate([pair(out_mine, 1, 3, 0), pair(out_far, 1, 3, 0)], axis=1)
+    out_core = other(after(out_sent, mixed), "mp", 1)
+    full_out = jnp.concatenate(
+        [pair(out_mine, 0, 2, 0), out_core[:, :block], pair(out_far, 0, 2, 0), out_core[:, block:]], axis=1
+    )
     mixed_tok = jnp.concatenate([mixed[:count], mixed_far], axis=1)
-    branch = collect(partials(count, lambda a, b: matmul(mixed_tok[a:b], full_out)))
-
-    w_in = after(w_in, mixed_far)
-    in_far = other(w_in, "mp", 2)
-    in_core = other(theirs(w_in, 2), "mp", 1)
-    in_across = other(theirs(in_far, 2), "mp", 1)
-    full_in = jnp.concatenate([ours(w_in, 2), in_core, ours(in_far, 2), in_across], axis=1)
+    branch_parts = partials(count, lambda a, b: matmul(mixed_tok[a:b], full_out))
+    gate_first = other(after(w_in[0, : block // 2], mixed_far), "mp", 2)
+    gate_second = other(after(w_in[0, block // 2:], mixed_far), "mp", 2)
+    branch_own, branch_got, branch_sent = collect_pieces(branch_parts, before=(gate_first,))
+    branch = added(branch_own, branch_got)
+    up_far = other(after(w_in[1], branch_sent), "mp", 2)
 
     middle = inputs + branch
     scaled_two, unit_two, scale_two = norm_rows(middle, gain_two)
-    normed_two = spread(scaled_two.astype(bf16))
+    low_two = after(scaled_two.astype(bf16), gate_second)
+    down_far = after(rows_got, low_two)[w_out.shape[0]:]
+    down_across = other(theirs(down_far, 0), "mp", 1)
+    cot_across = other(after(jnp.concatenate(cot_pieces[1:], axis=0), low_two), "mp", 1)
+    piece = cot_own.shape[0]
+    theirs_cot = [cot_core] + [cot_across[s * piece:(s + 1) * piece] for s in range(len(cot_pieces) - 1)]
+    cot_all = with_core(cot_pieces, theirs_cot)
+    full_down = jnp.concatenate([ours(w_down, 0), down_core, ours(down_far, 0), down_across], axis=1)
+    d_hidden = matmul(cot_all, full_down, ((1,), (1,)))
+    two_pieces = gather_tensor(low_two, before=(up_far,))
+    normed_two = after(with_core(two_pieces), d_hidden)
+    gate_far = jnp.concatenate([after(gate_first, low_two), after(gate_second, low_two)], axis=0)
+    in_far = [gate_far, after(up_far, two_pieces[2])]
+    full_in = [
+        after(
+            jnp.concatenate([ours(w_in[i], 1), in_core[i], ours(v, 1), other(theirs(v, 1), "mp", 1)], axis=0), d_hidden
+        )
+        for i, v in enumerate(in_far)
+    ]
 
     gate = matmul(normed_two, full_in[0])
     up = matmul(normed_two, full_in[1])
     sigma = jax.nn.sigmoid(gate)
     activated = gate * sigma
     hidden = (activated * up * live).astype(bf16)
-    d_hidden = matmul(cot_all, full_down, ((1,), (1,)))
     d_hidden = d_hidden * live
     d_gate = (d_hidden * up * sigma * (1.0 + gate * (1.0 - sigma))).astype(bf16)
     d_up = (d_hidden * activated).astype(bf16)
-    d_normed_two = collect(
-        partials(
-            count,
-            lambda a, b: matmul(d_gate[a:b], full_in[0], ((1,), (1,))) + matmul(d_up[a:b], full_in[1], ((1,), (1,))),
-        )
-    )
-    d_mid_norm, g_mlp = norm_back(d_normed_two, unit_two, scale_two, gain_two)
-    d_middle = cot_own.astype(f32) + d_mid_norm
-    d_mid_all = spread(d_middle.astype(bf16))
-    d_mixed = matmul(d_mid_all, full_out, ((1,), (1,))).astype(bf16)
-    d_far = other(d_mixed[:, head:], "mp", 2)
-    feed = collect(after(partials(count, lambda a, b: matmul(hidden[a:b], full_down)), d_mid_all))
-    output = own_order((middle + feed).astype(bf16), m, 1)
-
+    two_parts = partials(
+        count,
+        lambda a, b: matmul(d_gate[a:b], full_in[0], ((1,), (1,))) + matmul(d_up[a:b], full_in[1], ((1,), (1,))),
+    )
+    two_own, two_got, two_sent = collect_pieces(two_parts)
+    d_normed_two = added(two_own, two_got)
+    hidden, d_gate, d_up = after((hidden, d_gate, d_up), two_sent)
     tn = ((0,), (0,))
     grad_dot = lambda a, b: matmul(a, b, tn)
 
@@ -686,34 +715,51 @@
         zero = jnp.zeros_like(lax.slice_in_dim(low, 0, gap, axis=axis))
         return jnp.concatenate([low, zero], axis) + jnp.concatenate([zero, high], axis)
 
-    def units_grad(product, axis, *before):
+    def units_joined(product, axis):
         cut = lambda v, p: lax.slice_in_dim(v, p * block, (p + 1) * block, axis=axis)
         two = lambda i, j: jnp.concatenate([cut(product, i), cut(product, j)], axis)
         joined = joined_units(two(0, 2), other(two(1, 3), "mp", 1), 1 - axis)
-        sent = cut(joined, 1)
-        if before:
-            sent = after(sent, *before)
-        return over_dp(cut(joined, 0).astype(f32) + other(sent, "mp", 2).astype(f32))
-
-    g_down = units_grad(grad_dot(hidden, cot_all).astype(bf16), 1)
-    g_in = jnp.stack(
-        [
-            units_grad(grad_dot(normed_two, d_gate).astype(bf16), 0),
-            units_grad(grad_dot(normed_two, d_up).astype(bf16), 0, d_far),
-        ]
-    )
+        return cut(joined, 0), cut(joined, 1)
+
+    down_product = grad_dot(hidden, cot_all).astype(bf16)
+    gate_product = grad_dot(normed_two, after(d_gate, down_product)).astype(bf16)
+    down_held, down_sent = units_joined(down_product, 1)
+    up_product = grad_dot(normed_two, after(d_up, gate_product, down_sent)).astype(bf16)
+    gate_held, gate_sent = units_joined(gate_product, 0)
+    up_held, up_sent = units_joined(up_product, 0)
+    down_got = other(down_sent, "mp", 2)
+
+    d_mid_norm, g_mlp = norm_back(d_normed_two, unit_two, scale_two, gain_two)
+    d_middle = cot_own.astype(f32) + d_mid_norm
+    d_mid_low = after(d_middle.astype(bf16), down_sent, gate_sent)
+    d_mid_pieces = gather_tensor(d_mid_low)
+    gate_got = other(after(gate_sent, d_mid_pieces[2]), "mp", 2)
+    down_sums = over_dp_pieces(summed(down_held, after(down_got, d_mid_pieces[2])))
+    feed_parts = partials(count, lambda a, b: matmul(hidden[a:b], full_down))
+    feed_theirs = other(after(feed_parts[0], d_mid_pieces[2]), "mp", 1)
+    feed_joined = feed_parts[1] + neighbour_order(feed_theirs, 1, 1).astype(f32)
+    piece_rows = feed_joined.shape[0] // lax.axis_size("tensor")
+    feed_sent = [
+        feed_joined[p * piece_rows:(p + 1) * piece_rows].astype(bf16) for p in range(1, lax.axis_size("tensor"))
+    ]
+    d_mid_all = after(with_core(d_mid_pieces), down_got, feed_sent)
+    d_mixed = matmul(d_mid_all, full_out, ((1,), (1,))).astype(bf16)
+    d_far = other(d_mixed[:, head:], "mp", 2)
+    gate_sums = over_dp_pieces(summed(gate_held, after(gate_got, down_sums[1], d_mixed)))
+    feed_got = [other(after(v, d_mid_all), "tensor", p + 1) for p, v in enumerate(feed_sent)]
+    feed_own = feed_joined[:piece_rows]
+    output = own_order((middle + added(feed_own, feed_got)).astype(bf16), m, 1)
 
     out_grad = grad_dot(mixed_tok, d_mid_all)
-    out_back = neighbour_order(other(after(out_grad[:, near_blocks:].astype(bf16), d_far), "mp", 2), 0, 1, 2)
-    out_two = (out_grad[:, :near_blocks] + out_back.astype(f32)).astype(bf16)
-    out_theirs = other(out_two[:, block:], "mp", 1)
-    out_mine = out_two[:, :block]
-    g_out = over_dp(
-        own_order(
-            jnp.concatenate([out_mine[:head], out_theirs[:head], out_mine[head:], out_theirs[head:]], axis=0), m, 0
-        )
-    )
-    d_heads, d_logit, d_taps, g_head_gain = head_backward(d_mixed[:, :head], d_far, *head_args, kept)
+    out_sent = out_grad[:, near_blocks:].astype(bf16)
+    late_sent = jnp.concatenate(
+        [up_sent, jnp.concatenate([out_sent[:, :block], out_sent[:, block:]], axis=0)], axis=1
+    )
+    late_got = other(after(late_sent, d_far), "mp", 2)
+    d_near = after(d_mixed[:, :head], gate_got, down_sums[1])
+    d_heads, d_logit, d_taps, g_head_gain = head_backward(d_near, d_far, *head_args, kept)
+    d_heads, d_logit = after((d_heads, d_logit), late_got, gate_sums[1], *feed_got)
+    d_own = d_heads[:count]
     d_logit = d_logit.astype(bf16)
     half_chunks = d_logit.shape[0] // 2
     d_sent = jnp.concatenate(
@@ -724,33 +770,43 @@
         axis=0,
     )
     d_got = other(d_sent, "mp", 2)
-    d_own = d_heads[:count]
     d_proj = jnp.concatenate([d_own, d_got[:count]], axis=1)
     d_logits = jnp.concatenate(
         [d_logit[:half_chunks].reshape(1, count), d_got[count:count + logit_rows].reshape(1, count)], axis=0
     )
-    d_normed = collect(
-        partials(
-            count,
-            lambda a, b: matmul(d_proj[a:b], full_proj, ((1,), (1,))) + matmul(d_logits[:, a:b], full_beta, tn),
-        )
-    )
-    own_grad = grad_dot(normed, d_own)
-    far_grad = grad_dot(normed, d_got[:count])
+    late_got = after(late_got, d_sent)
+    out_got = jnp.concatenate([late_got[: 2 * head, units:], late_got[2 * head:, units:]], axis=1)
+    out_two = (out_grad[:, :near_blocks] + neighbour_order(out_got, 0, 1, 2).astype(f32)).astype(bf16)
+    out_theirs = other(out_two[:, block:], "mp", 1)
+    out_mine = out_two[:, :block]
+    out_rows = jnp.concatenate([out_mine[:head], out_theirs[:head], out_mine[head:], out_theirs[head:]], axis=0)
+    up_two = summed(up_held, late_got[:, :units]).astype(bf16)
+    late_sums = over_dp_pieces(jnp.concatenate([up_two, out_rows], axis=1))
+    normed_parts = partials(
+        count,
+        lambda a, b: matmul(d_proj[a:b], full_proj, ((1,), (1,))) + matmul(d_logits[:, a:b], full_beta, tn),
+    )
+    normed_own, normed_got, normed_sent = collect_pieces(normed_parts)
+    d_normed = added(normed_own, normed_got)
+    own_grad = grad_dot(normed, after(d_own, d_sent))
+    far_grad = grad_dot(normed, after(d_got, normed_parts)[:count])
     own_back = other(own_grad[near_blocks:].astype(bf16), "mp", 2)
-    far_back = other(after(far_grad[near_blocks:].astype(bf16), own_back), "mp", 2)
+    far_back = other(after(far_grad[near_blocks:].astype(bf16), normed_sent), "mp", 2)
 
     def proj_part(held, back):
         two = (held[:near_blocks] + back.astype(f32)).astype(bf16)
-        return over_dp(jnp.concatenate([two[:block], other(two[block:], "mp", 1)], axis=1))
-
-    part_far = proj_part(far_grad, own_back)
-    part_own = proj_part(own_grad, far_back)
+        return jnp.concatenate([two[:block], other(two[block:], "mp", 1)], axis=1)
+
+    far_part = after(proj_part(far_grad, after(own_back, normed_sent)), late_sums[1])
+    far_sums = over_dp_pieces(far_part)
+    own_part = proj_part(own_grad, after(far_back, normed_got))
+    own_sums = over_dp_pieces(own_part)
+    part_far, part_own = summed(*far_sums), summed(*own_sums)
     g_heads = [part_own[:, :span], part_own[:, span:], part_far[:, :span], part_far[:, span:]]
     g_proj = own_order(
         jnp.concatenate([v.reshape(block, pieces, head).transpose(1, 0, 2) for v in g_heads], axis=2), m, 2
     )
-    beta_part = matmul(d_logits, normed)
+    beta_part = after(matmul(after(d_logits, far_part), normed), far_sums[1], own_part)
     beta_back = neighbour_order(neighbour_order(other(beta_part, "mp", 2), 0, 1, 2), 1, 1, 2)
     beta_two = beta_part + beta_back
     beta_theirs = other(beta_two[:, block:near_blocks], "mp", 1)
@@ -765,20 +821,22 @@
     cut = g_beta.size // LANES
     g_beta = small[:cut].reshape(g_beta.shape)
     d_taps = small[cut:]
-    d_in_norm, g_norm = norm_back(d_normed, unit_one, scale_one, gain_one)
+    normed_again, partial_rows = after((normed, normed_parts), far_part)
+    g_norm = (
+        jnp.sum(normed_again[: count // 2].astype(f32) * partial_rows[1], axis=0)
+        + jnp.sum(normed_again[count // 2:].astype(f32) * partial_rows[0].astype(f32), axis=0)
+    ) / gain_one
+    row = lambda v: v.reshape(-1, LANES)
+    rows_all = [own_order(row(g_norm), m, 0), own_order(row(g_mlp), m, 0), g_head_gain[:1]]
+    rows_all.append(jnp.full((1, LANES), norm_total))
+    sums = over_all(after(jnp.concatenate(rows_all, axis=0), far_sums[1], own_part))
+    d_in_norm, _ = norm_back(d_normed, unit_one, scale_one, gain_one)
     d_tokens = own_order(d_middle + d_in_norm, m, 1)
-    row = lambda v: v.reshape(-1, LANES)
-    sums = over_all(
-        jnp.concatenate(
-            [
-                row(own_order(g_norm, m, 0)),
-                row(own_order(g_mlp, m, 0)),
-                g_head_gain[:1],
-                jnp.full((1, LANES), norm_total),
-            ],
-            axis=0,
-        )
-    )
+    down_sums, gate_sums = after((down_sums, gate_sums), far_part)
+    g_down = summed(*down_sums)
+    g_late = summed(*after(late_sums, far_part))
+    g_in = jnp.stack([summed(*gate_sums), g_late[:, :units]])
+    g_out = own_order(g_late[:, units:], m, 0)
     lines = g_norm.shape[0] // LANES
     ways = lax.axis_size("mp") * lax.axis_size("tensor")
     state_norm = sums[2 * lines + 1, 0] / (ways * lax.axis_size("dp") * (2 * count // BLOCK))

time: 710 us -> 610 us (0.86)
  waiting for transfers between devices: 282 us -> 228 us
  other arithmetic: 81.8 us -> 62.7 us
  local copies, waits for them, and re-layouts: 92.2 us -> 75.2 us
    ppermute x80 -> x84, waiting for transfers between devices: 234 us -> 168 us  [other(): return lax.ppermute(value, axis, [(i, i ^ bit) for i in range(size)])]
    ppermute x16 -> x12, waiting for transfers between devices: 48.2 us -> 60.4 us  [along_tensor(): return lax.ppermute(value, 'tensor', pairs)]
    slice x25 -> x23, local copies, waits for them, and re-layouts: 17.2 us -> 9.58 us  [the longest x1 2.25 us: shards(): w_in[i]]
    dot_general x26 -> x28, matrix products: 80.1 us -> 73.5 us  [matmul(): return lax.dot_general(a, b, (dims, ((), ())), preferred_element_type=f32)]
    ppermute x16 -> x12, starting transfers between devices: 23 us -> 20.5 us  [along_tensor(): return lax.ppermute(value, 'tensor', pairs)]
    ppermute x80 -> x84, starting transfers between devices: 64.2 us -> 63.6 us  [other(): return lax.ppermute(value, axis, [(i, i ^ bit) for i in range(size)])]
    unnamed x218 -> x240, local copies, waits for them, and re-layouts: 23.5 us -> 23.5 us
  transfers between devices with their start and end apart: 96 -> 96, of which waited for: 38 -> 30; matrix products, arithmetic and copies ran while one was open for 27% -> 26% of each run, Pallas kernels for 11% -> 12%
where the time goes in v4:
time: 610 us; the launch traced here: 606 us
  waiting for transfers between devices  228 us (37%)
  starting transfers between devices  84.1 us (14%)
  Pallas kernels  75.5 us (12%)
  local copies, waits for them, and re-layouts  75.2 us (12%)
  matrix products  73.5 us (12%)
  other arithmetic  62.7 us (10%)
  between operations  6.27 us (1%)
    ppermute x84, waiting for transfers between devices, other(): return lax.ppermute(value, axis, [(i, i ^ bit) for i in range(size)])  168 us
    dot_general x28, matrix products, matmul(): return lax.dot_general(a, b, (dims, ((), ())), preferred_element_type=f32)  73.5 us
    ppermute x84, starting transfers between devices, other(): return lax.ppermute(value, axis, [(i, i ^ bit) for i in range(size)])  63.6 us
    ppermute x12, waiting for transfers between devices, along_tensor(): return lax.ppermute(value, 'tensor', pairs)  60.4 us
    pallas_call x1, Pallas kernels, head_forward(): pl.pallas_call(forward_body, grid_spec=pltpu.PrefetchScalarGridSpec(num_s...  40.7 us
    pallas_call x1, Pallas kernels, head_backward(): pl.pallas_call(backward_body, grid_spec=pltpu.PrefetchScalarGridSpec(num_...  34.7 us
    unnamed x240, local copies, waits for them, and re-layouts  23.5 us
    ppermute x12, starting transfers between devices, along_tensor(): return lax.ppermute(value, 'tensor', pairs)  20.5 us
  transfers between devices with their start and end apart: 96, of which 30 were waited for; matrix products, arithmetic and copies ran while one was open for 26% of the time, Pallas kernels for 12%

profile of v4, /device:TPU:0, one launch (start us, length us, event | category | flops | bytes accessed | tf_op | source)
XLA Modules:
  0.0 605.5 jit_solution(11898219039507075293)
XLA Ops:
  6.1 4.1 collective-permute-start.1
  13.3 4.1 copy.29
  19.2 2.3 fusion.104
  24.2 2.9 constant_dynamic-slice_fusion.58
  29.2 2.8 constant_dynamic-slice_fusion.34
  44.4 8.6 %collective-permute-done.3 = bf16[128,2048]{1,0:T(8,128)(2,1)S(1)} collective-permute-done((bf16[128,2048]{1,0:T(8,128)(2,1)}, bf16[128,2048]{1,0:T(8,128)(2,1)S(1)}, u32[]{:S(2)}, u32[]{:S(2)}) %collective-permute-start.3) | collective-permute-done | bytes 524320 | tf_op jit(solution)/shard_map/ppermute | solution.py:491
  58.6 6.9 %collective-permute-done.9 = bf16[4,512,512]{1,2,0:T(8,128)(2,1)} collective-permute-done((bf16[4,512,512]{1,2,0:T(8,128)(2,1)}, bf16[4,512,512]{1,2,0:T(8,128)(2,1)}, u32[]{:S(2)}, u32[]{:S(2)}) %collective-permute-start.9) | collective-permute-done | bytes 2097184 | tf_op jit(solution)/shard_map/ppermute | solution.py:444
  66.2 2.5 constant_dynamic-slice_fusion.54
  82.9 2.3 add_convert_fusion.5.near_ref.before_near_ref
  86.0 19.7 %collective-permute-done.13.far_ref.before_far_ref = bf16[1040,512]{1,0:T(8,128)(2,1)S(1)} collective-permute-done((bf16[1040,512]{1,0:T(8,128)(2,1)S(1)}, bf16[1040,512]{1,0:T(8,128)(2,1)S(1)}, u32[]{:S(2)}, u32[]{:S(2)}) %collective-permute-start.13) | collective-permute-done | bytes 1064992 | tf_op jit(solution)/shard_map/ppermute | solution.py:444
  107.6 2.5 collective-permute-start.18
  111.3 40.7 %head_forward.1 = (bf16[2048,128]{1,0:T(8,128)(2,1)}, f32[8,128]{1,0:T(8,128)}, f32[3,2048,128]{2,1,0:T(8,128)}, f32[2048,256]{1,0:T(8,128)}, f32[2048,128]{1,0:...) custom-call(s32[8]{0:T(128)} %bitcast.140, ...), custom_call_target="tpu_custom_call" | custom-call | flops 40960000000 | bytes 20480000 | tf_op jit(solution)/shard_map/head_forward/pallas_call | solution.py:367
  157.0 6.7 %collective-permute-done.21 = bf16[1024,128]{1,0:T(8,128)(2,1)S(1)} collective-permute-done((bf16[1024,128]{1,0:T(8,128)(2,1)S(1)}, bf16[1024,128]{1,0:T(8,128)(2,1)S(1)}, u32[]{:S(2)}, u32[]{:S(2)}) %collective-permute-start.21) | collective-permute-done | bytes 262176 | tf_op jit(solution)/shard_map/ppermute | solution.py:444
  169.0 2.3 collective-permute-start.26
  172.8 9.9 %collective-permute-done.26 = bf16[128,2048]{1,0:T(8,128)(2,1)S(1)} collective-permute-done((bf16[128,2048]{1,0:T(8,128)(2,1)S(1)}, bf16[128,2048]{1,0:T(8,128)(2,1)S(1)}, u32[]{:S(2)}, u32[]{:S(2)}) %collective-permute-start.26) | collective-permute-done | bytes 524320 | tf_op jit(solution)/shard_map/ppermute | solution.py:491
  183.5 3.0 collective-permute-start.28
  188.9 20.2 %collective-permute-done.28 = bf16[128,2048]{1,0:T(8,128)(2,1)S(1)} collective-permute-done((bf16[128,2048]{1,0:T(8,128)(2,1)S(1)}, bf16[128,2048]{1,0:T(8,128)(2,1)S(1)}, u32[]{:S(2)}, u32[]{:S(2)}) %collective-permute-start.28) | collective-permute-done | bytes 524320 | tf_op jit(solution)/shard_map/ppermute | solution.py:444
  210.0 2.7 collective-permute-start.32
  215.5 21.0 %collective-permute-done.31 = bf16[128,2048]{1,0:T(8,128)(2,1)S(1)} collective-permute-done((bf16[128,2048]{1,0:T(8,128)(2,1)S(1)}, bf16[128,2048]{1,0:T(8,128)(2,1)S(1)}, u32[]{:S(2)}, u32[]{:S(2)}) %collective-permute-start.31) | collective-permute-done | bytes 524320 | tf_op jit(solution)/shard_map/ppermute | solution.py:444
  239.8 2.0 collective-permute-done.37
  242.5 12.9 %collective-permute-done.35 = bf16[128,2048]{1,0:T(8,128)(2,1)S(1)} collective-permute-done((bf16[128,2048]{1,0:T(8,128)(2,1)S(1)}, bf16[128,2048]{1,0:T(8,128)(2,1)S(1)}, u32[]{:S(2)}, u32[]{:S(2)}) %collective-permute-start.35) | collective-permute-done | bytes 524320 | tf_op jit(solution)/shard_map/ppermute | solution.py:491
  257.4 5.1 fusion.97
  263.5 3.4 fusion.149
  266.9 5.8 multiply_convert_fusion
  277.2 3.8 fusion.52
  281.1 4.0 convolution_add_fusion
  286.0 4.3 collective-permute-start.46
  291.2 10.4 %collective-permute-done.46 = bf16[128,2048]{1,0:T(8,128)(2,1)S(1)} collective-permute-done((bf16[128,2048]{1,0:T(8,128)(2,1)S(1)}, bf16[128,2048]{1,0:T(8,128)(2,1)S(1)}, u32[]{:S(2)}, u32[]{:S(2)}) %collective-permute-start.46) | collective-permute-done | bytes 524320 | tf_op jit(solution)/shard_map/ppermute | solution.py:491
  301.8 3.2 collective-permute-start.48
  305.0 3.9 convolution_convert_fusion.2
  309.1 3.9 convolution_convert_fusion.1
  314.6 2.7 convolution_convert_fusion.4
  317.4 9.8 %collective-permute-done.48 = bf16[128,2048]{1,0:T(8,128)(2,1)S(1)} collective-permute-done((bf16[128,2048]{1,0:T(8,128)(2,1)S(1)}, bf16[128,2048]{1,0:T(8,128)(2,1)S(1)}, u32[]{:S(2)}, u32[]{:S(2)}) %collective-permute-start.48) | collective-permute-done | bytes 524320 | tf_op jit(solution)/shard_map/ppermute | solution.py:444
  334.1 3.9 convolution_convert_fusion
  338.4 17.6 %collective-permute-done.54 = bf16[128,2048]{1,0:T(8,128)(2,1)S(1)} collective-permute-done((bf16[128,2048]{1,0:T(8,128)(2,1)S(1)}, bf16[128,2048]{1,0:T(8,128)(2,1)S(1)}, u32[]{:S(2)}, u32[]{:S(2)}) %collective-permute-start.54) | collective-permute-done | bytes 524320 | tf_op jit(solution)/shard_map/ppermute | solution.py:444
  356.7 2.3 collective-permute-done.52
  363.3 8.7 %collective-permute-done.56 = bf16[128,2048]{1,0:T(8,128)(2,1)S(1)} collective-permute-done((bf16[128,2048]{1,0:T(8,128)(2,1)S(1)}, bf16[128,2048]{1,0:T(8,128)(2,1)S(1)}, u32[]{:S(2)}, u32[]{:S(2)}) %collective-permute-start.56) | collective-permute-done | bytes 524320 | tf_op jit(solution)/shard_map/ppermute | solution.py:491
  379.9 5.1 fusion.144
  389.0 2.1 collective-permute-start.63
  391.1 2.6 fusion.145
  395.1 8.4 %collective-permute-done.67.grad_far_ref = bf16[1024,128]{1,0:T(8,128)(2,1)S(1)} collective-permute-done((bf16[1024,128]{1,0:T(8,128)(2,1)S(1)}, bf16[1024,128]{1,0:T(8,128)(2,1)S(1)}, u32[]{:S(2)}, u32[]{:S(2)}) %collective-permute-start.67) | collective-permute-done | bytes 262176 | tf_op jit(solution)/shard_map/ppermute | solution.py:444
  410.3 34.7 %head_backward.1 = (bf16[2048,512]{1,0:T(8,128)(2,1)}, f32[16,128]{1,0:T(8,128)}, f32[3,4,128]{2,1,0:T(4,128)}, f32[8,128]{1,0:T(8,128)}) custom-call(s32[8]{0:T(128)} %bitcast.141, s32[2]{0:T(128)} %pad_add_fusion.3.info_ref, bf16[1024,512]{1,0:T(8,128)(2,1)} %add_convert_fusion.5.near_ref.before_near_ref, bf16[1040,512]{1,0:T(8,128)(2,1)} %copy-done.98, ...), custom_call_target="tpu_custom_call" | custom-call | flops 36864000000 | bytes 20480000 | tf_op jit(solution)/shard_map/head_backward/pallas_call | solution.py:415
  446.4 2.9 collective-permute-done.69
  449.3 3.0 fusion.107
  455.9 3.9 fusion.150
  459.8 2.8 add_convert_fusion.2
  466.1 14.1 %collective-permute-done.71 = bf16[1040,512]{1,0:T(8,128)(2,1)S(1)} collective-permute-done((bf16[1040,512]{1,0:T(8,128)(2,1)S(1)}, bf16[1040,512]{1,0:T(8,128)(2,1)S(1)}, u32[]{:S(2)}, u32[]{:S(2)}) %collective-permute-start.71) | collective-permute-done | bytes 1064992 | tf_op jit(solution)/shard_map/ppermute | solution.py:444
  483.6 2.3 add_convert_fusion
  486.1 2.4 convolution_add_fusion.1
  489.1 2.5 fusion.47
  491.7 5.3 collective-permute-start.75
  498.4 9.9 %collective-permute-done.75 = bf16[128,2048]{1,0:T(8,128)(2,1)S(1)} collective-permute-done((bf16[128,2048]{1,0:T(8,128)(2,1)S(1)}, bf16[128,2048]{1,0:T(8,128)(2,1)S(1)}, u32[]{:S(2)}, u32[]{:S(2)}) %collective-permute-start.75) | collective-permute-done | bytes 524320 | tf_op jit(solution)/shard_map/ppermute | solution.py:491
  509.1 2.0 fusion.32
  513.1 3.9 collective-permute-start.76
  522.6 18.3 %collective-permute-done.76 = bf16[128,2048]{1,0:T(8,128)(2,1)S(1)} collective-permute-done((bf16[128,2048]{1,0:T(8,128)(2,1)S(1)}, bf16[128,2048]{1,0:T(8,128)(2,1)S(1)}, u32[]{:S(2)}, u32[]{:S(2)}) %collective-permute-start.76) | collective-permute-done | bytes 524320 | tf_op jit(solution)/shard_map/ppermute | solution.py:444
  543.7 3.7 add_bitcast_fusion
  550.7 3.0 fusion.151
  553.8 2.0 convert_add_fusion.2
  560.8 2.9 pad_maximum_fusion
  572.2 2.1 collective-permute-start.90
  581.4 2.6 copy.36
  584.0 2.5 copy.37
  586.5 6.1 %collective-permute-done.95 = f32[28,128]{1,0:T(8,128)S(1)} collective-permute-done((f32[28,128]{1,0:T(8,128)S(1)}, f32[28,128]{1,0:T(8,128)S(1)}, u32[]{:S(2)}, u32[]{:S(2)}) %collective-permute-start.95) | collective-permute-done | bytes 14368 | tf_op jit(solution)/shard_map/ppermute | solution.py:444
  601.9 2.3 pad_maximum_fusion.2
  (613 shorter events, 173.0 us)
Async XLA Ops:
  6.1 31.0 %collective-permute-start.1 = (bf16[128,2048]{1,0:T(8,128)(2,1)}, bf16[128,2048]{1,0:T(8,128)(2,1)}, u32[]{:S(2)}, u32[]{:S(2)}) collective-permute-start(bf16[128,2048]{1,0:T(8,128)(2,1)} %get-tuple-element.99), channel_id=1, source_target_pairs={{0,2},{1,3},{2,0},{3,1},{4,6},{5,7},{6,4},{7,5},{8,10},{9,11},{10,... | collective-permute-start | bytes 1572872 | tf_op jit(solution)/shard_map/ppermute | solution.py:444
  10.2 28.3 %collective-permute-start = (bf16[128,2048]{1,0:T(8,128)(2,1)}, bf16[128,2048]{1,0:T(8,128)(2,1)}, u32[]{:S(2)}, u32[]{:S(2)}) collective-permute-start(bf16[128,2048]{1,0:T(8,128)(2,1)} %get-tuple-element.99), channel_id=1, source_target_pairs={{0,1},{1,0},{2,3},{3,2},{4,5},{5,4},{6,7},{7,6},{8,9},{9,8},{10,11... | collective-permute-start | bytes 1572872 | tf_op jit(solution)/shard_map/ppermute | solution.py:444
  11.8 29.5 %collective-permute-start.4 = (bf16[128,2048]{1,0:T(8,128)(2,1)}, bf16[128,2048]{1,0:T(8,128)(2,1)}, u32[]{:S(2)}, u32[]{:S(2)}) collective-permute-start(bf16[128,2048]{1,0:T(8,128)(2,1)} %get-tuple-element.99), channel_id=1, source_target_pairs={{0,4},{4,0},{8,12},{12,8},{1,5},{5,1},{9,13},{13,9},{2,6},{6,2},{1... | collective-permute-start | bytes 1572872 | tf_op jit(solution)/shard_map/ppermute | solution.py:444
  11.8 46.8 %collective-permute-start.11 = (bf16[4,512]{1,0:T(4,128)(2,1)}, bf16[4,512]{1,0:T(4,128)(2,1)}, u32[]{:S(2)}, u32[]{:S(2)}) collective-permute-start(bf16[4,512]{1,0:T(4,128)(2,1)} %bitcast.18), channel_id=1, source_target_pairs={{0,8},{4,12},{8,0},{12,4},{1,9},{5,13},{9,1},{13,5},{2,10},{6,14},... | collective-permute-start | bytes 12296 | tf_op jit(solution)/shard_map/ppermute | solution.py:444
  17.4 48.1 %collective-permute-start.9 = (bf16[4,512,512]{1,2,0:T(8,128)(2,1)}, bf16[4,512,512]{1,2,0:T(8,128)(2,1)}, u32[]{:S(2)}, u32[]{:S(2)}) collective-permute-start(bf16[4,512,512]{1,2,0:T(8,128)(2,1)} %copy.29), channel_id=1, source_target_pairs={{0,8},{4,12},{8,0},{12,4},{1,9},{5,13},{9,1},{13,5},{2,10},{6,14},... | collective-permute-start | bytes 6291464 | tf_op jit(solution)/shard_map/ppermute | solution.py:444
  37.2 15.9 %collective-permute-start.3 = (bf16[128,2048]{1,0:T(8,128)(2,1)}, bf16[128,2048]{1,0:T(8,128)(2,1)S(1)}, u32[]{:S(2)}, u32[]{:S(2)}) collective-permute-start(bf16[128,2048]{1,0:T(8,128)(2,1)} %collective-permute-done.1), channel_id=1, source_target_pairs={{2,3},{1,0},{6,7},{5,4},{10,11},{9,8},{14,15},{13,12},{18,19},{17,... | collective-permute-start | bytes 1572872 | tf_op jit(solution)/shard_map/ppermute | solution.py:491
  38.5 14.6 %collective-permute-start.2 = (bf16[128,2048]{1,0:T(8,128)(2,1)}, bf16[128,2048]{1,0:T(8,128)(2,1)S(1)}, u32[]{:S(2)}, u32[]{:S(2)}) collective-permute-start(bf16[128,2048]{1,0:T(8,128)(2,1)} %get-tuple-element.99), channel_id=1, source_target_pairs={{1,2},{2,1},{5,6},{6,5},{9,10},{10,9},{13,14},{14,13},{17,18},{18,... | collective-permute-start | bytes 1572872 | tf_op jit(solution)/shard_map/ppermute | solution.py:491
  41.3 13.2 %collective-permute-start.5 = (bf16[128,2048]{1,0:T(8,128)(2,1)}, bf16[128,2048]{1,0:T(8,128)(2,1)S(1)}, u32[]{:S(2)}, u32[]{:S(2)}) collective-permute-start(bf16[128,2048]{1,0:T(8,128)(2,1)} %collective-permute-done), channel_id=1, source_target_pairs={{0,4},{4,0},{8,12},{12,8},{1,5},{5,1},{9,13},{13,9},{2,6},{6,2},{1... | collective-permute-start | bytes 1572872 | tf_op jit(solution)/shard_map/ppermute | solution.py:444
  78.9 26.7 %collective-permute-start.15 = (bf16[2,512,768]{2,1,0:T(8,128)(2,1)S(1)}, bf16[2,512,768]{2,1,0:T(8,128)(2,1)S(1)}, u32[]{:S(2)}, u32[]{:S(2)}) collective-permute-start(bf16[2,512,768]{2,1,0:T(8,128)(2,1)S(1)} %copy-done.39), channel_id=1, source_target_pairs={{0,4},{4,0},{8,12},{12,8},{1,5},{5,1},{9,13},{13,9},{2,6},{6,2},{1... | collective-permute-start | bytes 4718600 | tf_op jit(solution)/shard_map/ppermute | solution.py:444
  80.1 25.6 %collective-permute-start.13 = (bf16[1040,512]{1,0:T(8,128)(2,1)S(1)}, bf16[1040,512]{1,0:T(8,128)(2,1)S(1)}, u32[]{:S(2)}, u32[]{:S(2)}) collective-permute-start(bf16[1040,512]{1,0:T(8,128)(2,1)S(1)} %fusion.10), channel_id=1, source_target_pairs={{0,8},{4,12},{8,0},{12,4},{1,9},{5,13},{9,1},{13,5},{2,10},{6,14},... | collective-permute-start | bytes 3194888 | tf_op jit(solution)/shard_map/ppermute | solution.py:444
  105.7 49.1 %collective-permute-start.20 = (bf16[128,2048]{1,0:T(8,128)(2,1)S(1)}, bf16[128,2048]{1,0:T(8,128)(2,1)S(1)}, u32[]{:S(2)}, u32[]{:S(2)}) collective-permute-start(bf16[128,2048]{1,0:T(8,128)(2,1)S(1)} %pad_maximum_fusion.30), channel_id=1, source_target_pairs={{0,3},{1,2},{2,1},{3,0},{4,7},{5,6},{6,5},{7,4},{8,11},{9,10},{10,... | collective-permute-start | bytes 1572872 | tf_op jit(solution)/shard_map/ppermute | solution.py:444
  106.9 47.9 %collective-permute-start.19 = (bf16[128,2048]{1,0:T(8,128)(2,1)S(1)}, bf16[128,2048]{1,0:T(8,128)(2,1)S(1)}, u32[]{:S(2)}, u32[]{:S(2)}) collective-permute-start(bf16[128,2048]{1,0:T(8,128)(2,1)S(1)} %pad_maximum_fusion.30), channel_id=1, source_target_pairs={{0,2},{1,3},{2,0},{3,1},{4,6},{5,7},{6,4},{7,5},{8,10},{9,11},{10,... | collective-permute-start | bytes 1572872 | tf_op jit(solution)/shard_map/ppermute | solution.py:444
  107.6 47.1 %collective-permute-start.18 = (bf16[128,2048]{1,0:T(8,128)(2,1)S(1)}, bf16[128,2048]{1,0:T(8,128)(2,1)S(1)}, u32[]{:S(2)}, u32[]{:S(2)}) collective-permute-start(bf16[128,2048]{1,0:T(8,128)(2,1)S(1)} %pad_maximum_fusion.30), channel_id=1, source_target_pairs={{0,1},{1,0},{2,3},{3,2},{4,5},{5,4},{6,7},{7,6},{8,9},{9,8},{10,11... | collective-permute-start | bytes 1572872 | tf_op jit(solution)/shard_map/ppermute | solution.py:444
  110.1 43.5 %collective-permute-start.17 = (bf16[1920,512]{1,0:T(8,128)(2,1)}, bf16[1920,512]{1,0:T(8,128)(2,1)}, u32[]{:S(2)}, u32[]{:S(2)}) collective-permute-start(bf16[1920,512]{1,0:T(8,128)(2,1)} %pad_maximum_fusion.8), channel_id=1, source_target_pairs={{0,8},{4,12},{8,0},{12,4},{1,9},{5,13},{9,1},{13,5},{2,10},{6,14},... | collective-permute-start | bytes 5898248 | tf_op jit(solution)/shard_map/ppermute | solution.py:444
  165.6 18.0 %collective-permute-start.27 = (bf16[256,1408]{1,0:T(8,128)(2,1)S(1)}, bf16[256,1408]{1,0:T(8,128)(2,1)S(1)}, u32[]{:S(2)}, u32[]{:S(2)}) collective-permute-start(bf16[256,1408]{1,0:T(8,128)(2,1)S(1)} %copy-done.62), channel_id=1, source_target_pairs={{0,8},{4,12},{8,0},{12,4},{1,9},{5,13},{9,1},{13,5},{2,10},{6,14},... | collective-permute-start | bytes 2162696 | tf_op jit(solution)/shard_map/ppermute | solution.py:444
  169.0 13.7 %collective-permute-start.26 = (bf16[128,2048]{1,0:T(8,128)(2,1)S(1)}, bf16[128,2048]{1,0:T(8,128)(2,1)S(1)}, u32[]{:S(2)}, u32[]{:S(2)}) collective-permute-start(bf16[128,2048]{1,0:T(8,128)(2,1)S(1)} %fusion.38), channel_id=1, source_target_pairs={{3,2},{0,1},{7,6},{4,5},{11,10},{8,9},{15,14},{12,13},{19,18},{16,... | collective-permute-start | bytes 1572872 | tf_op jit(solution)/shard_map/ppermute | solution.py:491
  171.3 12.3 %collective-permute-start.25 = (bf16[128,2048]{1,0:T(8,128)(2,1)S(1)}, bf16[128,2048]{1,0:T(8,128)(2,1)S(1)}, u32[]{:S(2)}, u32[]{:S(2)}) collective-permute-start(bf16[128,2048]{1,0:T(8,128)(2,1)S(1)} %fusion.38), channel_id=1, source_target_pairs={{1,2},{2,1},{5,6},{6,5},{9,10},{10,9},{13,14},{14,13},{17,18},{18,... | collective-permute-start | bytes 1572872 | tf_op jit(solution)/shard_map/ppermute | solution.py:491
  183.5 25.6 %collective-permute-start.28 = (bf16[128,2048]{1,0:T(8,128)(2,1)S(1)}, bf16[128,2048]{1,0:T(8,128)(2,1)S(1)}, u32[]{:S(2)}, u32[]{:S(2)}) collective-permute-start(bf16[128,2048]{1,0:T(8,128)(2,1)S(1)} %fusion.37), channel_id=1, source_target_pairs={{0,2},{1,3},{2,0},{3,1},{4,6},{5,7},{6,4},{7,5},{8,10},{9,11},{10,... | collective-permute-start | bytes 1572872 | tf_op jit(solution)/shard_map/ppermute | solution.py:444
  186.5 22.6 %collective-permute-start.29 = (bf16[128,2048]{1,0:T(8,128)(2,1)S(1)}, bf16[128,2048]{1,0:T(8,128)(2,1)S(1)}, u32[]{:S(2)}, u32[]{:S(2)}) collective-permute-start(bf16[128,2048]{1,0:T(8,128)(2,1)S(1)} %slice.1341), channel_id=1, source_target_pairs={{0,1},{1,0},{2,3},{3,2},{4,5},{5,4},{6,7},{7,6},{8,9},{9,8},{10,11... | collective-permute-start | bytes 1572872 | tf_op jit(solution)/shard_map/ppermute | solution.py:444
  186.8 23.0 %collective-permute-start.30 = (bf16[256,1408]{1,0:T(8,128)(2,1)S(1)}, bf16[256,1408]{1,0:T(8,128)(2,1)S(1)}, u32[]{:S(2)}, u32[]{:S(2)}) collective-permute-start(bf16[256,1408]{1,0:T(8,128)(2,1)S(1)} %copy-done.61), channel_id=1, source_target_pairs={{0,8},{4,12},{8,0},{12,4},{1,9},{5,13},{9,1},{13,5},{2,10},{6,14},... | collective-permute-start | bytes 2162696 | tf_op jit(solution)/shard_map/ppermute | solution.py:444
  187.4 50.9 %collective-permute-start.33 = (bf16[512,1408]{1,0:T(8,128)(2,1)S(1)}, bf16[512,1408]{1,0:T(8,128)(2,1)S(1)}, u32[]{:S(2)}, u32[]{:S(2)}) collective-permute-start(bf16[512,1408]{1,0:T(8,128)(2,1)S(1)} %copy-done.40), channel_id=1, source_target_pairs={{0,8},{4,12},{8,0},{12,4},{1,9},{5,13},{9,1},{13,5},{2,10},{6,14},... | collective-permute-start | bytes 4325384 | tf_op jit(solution)/shard_map/ppermute | solution.py:444
  209.9 26.7 %collective-permute-start.36 = (bf16[128,2048]{1,0:T(8,128)(2,1)S(1)}, bf16[128,2048]{1,0:T(8,128)(2,1)S(1)}, u32[]{:S(2)}, u32[]{:S(2)}) collective-permute-start(bf16[128,2048]{1,0:T(8,128)(2,1)S(1)} %multiply_convert_fusion.3), channel_id=1, source_target_pairs={{0,4},{4,0},{8,12},{12,8},{1,5},{5,1},{9,13},{13,9},{2,6},{6,2},{1... | collective-permute-start | bytes 1572872 | tf_op jit(solution)/shard_map/ppermute | solution.py:444
  210.0 27.7 %collective-permute-start.32 = (bf16[128,2048]{1,0:T(8,128)(2,1)S(1)}, bf16[128,2048]{1,0:T(8,128)(2,1)S(1)}, u32[]{:S(2)}, u32[]{:S(2)}) collective-permute-start(bf16[128,2048]{1,0:T(8,128)(2,1)S(1)} %multiply_convert_fusion.3), channel_id=1, source_target_pairs={{0,2},{1,3},{2,0},{3,1},{4,6},{5,7},{6,4},{7,5},{8,10},{9,11},{10,... | collective-permute-start | bytes 1572872 | tf_op jit(solution)/shard_map/ppermute | solution.py:444
  212.7 23.9 %collective-permute-start.31 = (bf16[128,2048]{1,0:T(8,128)(2,1)S(1)}, bf16[128,2048]{1,0:T(8,128)(2,1)S(1)}, u32[]{:S(2)}, u32[]{:S(2)}) collective-permute-start(bf16[128,2048]{1,0:T(8,128)(2,1)S(1)} %multiply_convert_fusion.3), channel_id=1, source_target_pairs={{0,1},{1,0},{2,3},{3,2},{4,5},{5,4},{6,7},{7,6},{8,9},{9,8},{10,11... | collective-permute-start | bytes 1572872 | tf_op jit(solution)/shard_map/ppermute | solution.py:444
  214.8 22.4 %collective-permute-start.42 = (bf16[512,768]{1,0:T(8,128)(2,1)S(1)}, bf16[512,768]{1,0:T(8,128)(2,1)S(1)}, u32[]{:S(2)}, u32[]{:S(2)}) collective-permute-start(bf16[512,768]{1,0:T(8,128)(2,1)S(1)} %get-tuple-element.285), channel_id=1, source_target_pairs={{0,4},{4,0},{8,12},{12,8},{1,5},{5,1},{9,13},{13,9},{2,6},{6,2},{1... | collective-permute-start | bytes 2359304 | tf_op jit(solution)/shard_map/ppermute | solution.py:444
  236.6 19.6 %collective-permute-start.41 = (bf16[768,512]{1,0:T(8,128)(2,1)S(1)}, bf16[768,512]{1,0:T(8,128)(2,1)S(1)}, u32[]{:S(2)}, u32[]{:S(2)}) collective-permute-start(bf16[768,512]{1,0:T(8,128)(2,1)S(1)} %get-tuple-element.291), channel_id=1, source_target_pairs={{0,4},{4,0},{8,12},{12,8},{1,5},{5,1},{9,13},{13,9},{2,6},{6,2},{1... | collective-permute-start | bytes 2359304 | tf_op jit(solution)/shard_map/ppermute | solution.py:444
  236.6 19.3 %collective-permute-start.40 = (bf16[384,2048]{1,0:T(8,128)(2,1)S(1)}, bf16[384,2048]{1,0:T(8,128)(2,1)S(1)}, u32[]{:S(2)}, u32[]{:S(2)}) collective-permute-start(bf16[384,2048]{1,0:T(8,128)(2,1)S(1)} %pad_maximum_fusion.9), channel_id=1, source_target_pairs={{0,4},{4,0},{8,12},{12,8},{1,5},{5,1},{9,13},{13,9},{2,6},{6,2},{1... | collective-permute-start | bytes 4718600 | tf_op jit(solution)/shard_map/ppermute | solution.py:444
  238.3 17.0 %collective-permute-start.35 = (bf16[128,2048]{1,0:T(8,128)(2,1)S(1)}, bf16[128,2048]{1,0:T(8,128)(2,1)S(1)}, u32[]{:S(2)}, u32[]{:S(2)}) collective-permute-start(bf16[128,2048]{1,0:T(8,128)(2,1)S(1)} %collective-permute-done.32), channel_id=1, source_target_pairs={{2,3},{1,0},{6,7},{5,4},{10,11},{9,8},{14,15},{13,12},{18,19},{17,... | collective-permute-start | bytes 1572872 | tf_op jit(solution)/shard_map/ppermute | solution.py:491
  241.8 13.9 %collective-permute-start.38 = (bf16[128,2048]{1,0:T(8,128)(2,1)S(1)}, bf16[128,2048]{1,0:T(8,128)(2,1)S(1)}, u32[]{:S(2)}, u32[]{:S(2)}) collective-permute-start(bf16[128,2048]{1,0:T(8,128)(2,1)S(1)} %collective-permute-done.32), channel_id=1, source_target_pairs={{0,4},{4,0},{8,12},{12,8},{1,5},{5,1},{9,13},{13,9},{2,6},{6,2},{1... | collective-permute-start | bytes 1572872 | tf_op jit(solution)/shard_map/ppermute | solution.py:444
  242.0 20.5 %collective-permute-start.43 = (bf16[512,768]{1,0:T(8,128)(2,1)S(1)}, bf16[512,768]{1,0:T(8,128)(2,1)S(1)}, u32[]{:S(2)}, u32[]{:S(2)}) collective-permute-start(bf16[512,768]{1,0:T(8,128)(2,1)S(1)} %get-tuple-element.287), channel_id=1, source_target_pairs={{0,4},{4,0},{8,12},{12,8},{1,5},{5,1},{9,13},{13,9},{2,6},{6,2},{1... | collective-permute-start | bytes 2359304 | tf_op jit(solution)/shard_map/ppermute | solution.py:444
  276.6 13.8 %collective-permute-start.44 = (bf16[384,2048]{1,0:T(8,128)(2,1)S(1)}, bf16[384,2048]{1,0:T(8,128)(2,1)S(1)}, u32[]{:S(2)}, u32[]{:S(2)}) collective-permute-start(bf16[384,2048]{1,0:T(8,128)(2,1)S(1)} %slice.1030), channel_id=1, source_target_pairs={{0,4},{4,0},{8,12},{12,8},{1,5},{5,1},{9,13},{13,9},{2,6},{6,2},{1... | collective-permute-start | bytes 4718600 | tf_op jit(solution)/shard_map/ppermute | solution.py:444
  285.3 16.4 %collective-permute-start.47 = (bf16[128,2048]{1,0:T(8,128)(2,1)S(1)}, bf16[128,2048]{1,0:T(8,128)(2,1)S(1)}, u32[]{:S(2)}, u32[]{:S(2)}) collective-permute-start(bf16[128,2048]{1,0:T(8,128)(2,1)S(1)} %fusion.35), channel_id=1, source_target_pairs={{1,2},{2,1},{5,6},{6,5},{9,10},{10,9},{13,14},{14,13},{17,18},{18,... | collective-permute-start | bytes 1572872 | tf_op jit(solution)/shard_map/ppermute | solution.py:491
  286.0 15.6 %collective-permute-start.46 = (bf16[128,2048]{1,0:T(8,128)(2,1)S(1)}, bf16[128,2048]{1,0:T(8,128)(2,1)S(1)}, u32[]{:S(2)}, u32[]{:S(2)}) collective-permute-start(bf16[128,2048]{1,0:T(8,128)(2,1)S(1)} %fusion.35), channel_id=1, source_target_pairs={{3,2},{0,1},{7,6},{4,5},{11,10},{8,9},{15,14},{12,13},{19,18},{16,... | collective-permute-start | bytes 1572872 | tf_op jit(solution)/shard_map/ppermute | solution.py:491
  301.8 25.4 %collective-permute-start.48 = (bf16[128,2048]{1,0:T(8,128)(2,1)S(1)}, bf16[128,2048]{1,0:T(8,128)(2,1)S(1)}, u32[]{:S(2)}, u32[]{:S(2)}) collective-permute-start(bf16[128,2048]{1,0:T(8,128)(2,1)S(1)} %fusion.36), channel_id=1, source_target_pairs={{0,2},{1,3},{2,0},{3,1},{4,6},{5,7},{6,4},{7,5},{8,10},{9,11},{10,... | collective-permute-start | bytes 1572872 | tf_op jit(solution)/shard_map/ppermute | solution.py:444
  304.9 22.2 %collective-permute-start.49 = (bf16[128,2048]{1,0:T(8,128)(2,1)S(1)}, bf16[128,2048]{1,0:T(8,128)(2,1)S(1)}, u32[]{:S(2)}, u32[]{:S(2)}) collective-permute-start(bf16[128,2048]{1,0:T(8,128)(2,1)S(1)} %slice.1340), channel_id=1, source_target_pairs={{0,1},{1,0},{2,3},{3,2},{4,5},{5,4},{6,7},{7,6},{8,9},{9,8},{10,11... | collective-permute-start | bytes 1572872 | tf_op jit(solution)/shard_map/ppermute | solution.py:444
  313.3 15.9 %collective-permute-start.51 = (bf16[1024,768]{1,0:T(8,128)(2,1)S(1)}, bf16[1024,768]{1,0:T(8,128)(2,1)S(1)}, u32[]{:S(2)}, u32[]{:S(2)}) collective-permute-start(bf16[1024,768]{1,0:T(8,128)(2,1)S(1)} %pad_maximum_fusion.13), channel_id=1, source_target_pairs={{0,4},{4,0},{8,12},{12,8},{1,5},{5,1},{9,13},{13,9},{2,6},{6,2},{1... | collective-permute-start | bytes 4718600 | tf_op jit(solution)/shard_map/ppermute | solution.py:444
  313.6 16.3 %collective-permute-start.50 = (bf16[768,1024]{1,0:T(8,128)(2,1)S(1)}, bf16[768,1024]{1,0:T(8,128)(2,1)S(1)}, u32[]{:S(2)}, u32[]{:S(2)}) collective-permute-start(bf16[768,1024]{1,0:T(8,128)(2,1)S(1)} %pad_maximum_fusion.11), channel_id=1, source_target_pairs={{0,4},{4,0},{8,12},{12,8},{1,5},{5,1},{9,13},{13,9},{2,6},{6,2},{1... | collective-permute-start | bytes 4718600 | tf_op jit(solution)/shard_map/ppermute | solution.py:444
  330.9 29.8 %collective-permute-start.57 = (bf16[128,2048]{1,0:T(8,128)(2,1)S(1)}, bf16[128,2048]{1,0:T(8,128)(2,1)S(1)}, u32[]{:S(2)}, u32[]{:S(2)}) collective-permute-start(bf16[128,2048]{1,0:T(8,128)(2,1)S(1)} %get-tuple-element.138), channel_id=1, source_target_pairs={{0,4},{4,0},{8,12},{12,8},{1,5},{5,1},{9,13},{13,9},{2,6},{6,2},{1... | collective-permute-start | bytes 1572872 | tf_op jit(solution)/shard_map/ppermute | solution.py:444
  331.0 25.0 %collective-permute-start.54 = (bf16[128,2048]{1,0:T(8,128)(2,1)S(1)}, bf16[128,2048]{1,0:T(8,128)(2,1)S(1)}, u32[]{:S(2)}, u32[]{:S(2)}) collective-permute-start(bf16[128,2048]{1,0:T(8,128)(2,1)S(1)} %get-tuple-element.138), channel_id=1, source_target_pairs={{0,1},{1,0},{2,3},{3,2},{4,5},{5,4},{6,7},{7,6},{8,9},{9,8},{10,11... | collective-permute-start | bytes 1572872 | tf_op jit(solution)/shard_map/ppermute | solution.py:444
  332.9 26.2 %collective-permute-start.52 = (bf16[128,2048]{1,0:T(8,128)(2,1)S(1)}, bf16[128,2048]{1,0:T(8,128)(2,1)S(1)}, u32[]{:S(2)}, u32[]{:S(2)}) collective-permute-start(bf16[128,2048]{1,0:T(8,128)(2,1)S(1)} %get-tuple-element.138), channel_id=1, source_target_pairs={{0,2},{1,3},{2,0},{3,1},{4,6},{5,7},{6,4},{7,5},{8,10},{9,11},{10,... | collective-permute-start | bytes 1572872 | tf_op jit(solution)/shard_map/ppermute | solution.py:444
  333.6 39.3 %collective-permute-start.61 = (bf16[1408,512]{1,0:T(8,128)(2,1)S(1)}, bf16[1408,512]{1,0:T(8,128)(2,1)S(1)}, u32[]{:S(2)}, u32[]{:S(2)}) collective-permute-start(bf16[1408,512]{1,0:T(8,128)(2,1)S(1)} %fusion.5), channel_id=1, source_target_pairs={{0,8},{4,12},{8,0},{12,4},{1,9},{5,13},{9,1},{13,5},{2,10},{6,14},... | collective-permute-start | bytes 4325384 | tf_op jit(solution)/shard_map/ppermute | solution.py:444
  359.0 13.0 %collective-permute-start.56 = (bf16[128,2048]{1,0:T(8,128)(2,1)S(1)}, bf16[128,2048]{1,0:T(8,128)(2,1)S(1)}, u32[]{:S(2)}, u32[]{:S(2)}) collective-permute-start(bf16[128,2048]{1,0:T(8,128)(2,1)S(1)} %collective-permute-done.52), channel_id=1, source_target_pairs={{2,3},{1,0},{6,7},{5,4},{10,11},{9,8},{14,15},{13,12},{18,19},{17,... | collective-permute-start | bytes 1572872 | tf_op jit(solution)/shard_map/ppermute | solution.py:491
  360.7 16.3 %collective-permute-start.68 = (bf16[1024,768]{1,0:T(8,128)(2,1)S(1)}, bf16[1024,768]{1,0:T(8,128)(2,1)S(1)}, u32[]{:S(2)}, u32[]{:S(2)}) collective-permute-start(bf16[1024,768]{1,0:T(8,128)(2,1)S(1)} %pad_maximum_fusion.15), channel_id=1, source_target_pairs={{0,4},{4,0},{8,12},{12,8},{1,5},{5,1},{9,13},{13,9},{2,6},{6,2},{1... | collective-permute-start | bytes 4718600 | tf_op jit(solution)/shard_map/ppermute | solution.py:444
  362.7 42.7 %collective-permute-start.65 = (bf16[512,1408]{1,0:T(8,128)(2,1)S(1)}, bf16[512,1408]{1,0:T(8,128)(2,1)S(1)}, u32[]{:S(2)}, u32[]{:S(2)}) collective-permute-start(bf16[512,1408]{1,0:T(8,128)(2,1)S(1)} %fusion.6), channel_id=1, source_target_pairs={{0,8},{4,12},{8,0},{12,4},{1,9},{5,13},{9,1},{13,5},{2,10},{6,14},... | collective-permute-start | bytes 4325384 | tf_op jit(solution)/shard_map/ppermute | solution.py:444
  373.6 33.6 %collective-permute-start.66 = (bf16[1408,512]{1,0:T(8,128)(2,1)S(1)}, bf16[1408,512]{1,0:T(8,128)(2,1)S(1)}, u32[]{:S(2)}, u32[]{:S(2)}) collective-permute-start(bf16[1408,512]{1,0:T(8,128)(2,1)S(1)} %add_convert_fusion.4), channel_id=1, source_target_pairs={{0,16},{16,0},{1,17},{17,1},{2,18},{18,2},{3,19},{19,3},{4,20},{20... | collective-permute-start | bytes 4325384 | tf_op jit(solution)/shard_map/ppermute | solution.py:444
  388.1 15.4 %collective-permute-start.67 = (bf16[1024,128]{1,0:T(8,128)(2,1)S(1)}, bf16[1024,128]{1,0:T(8,128)(2,1)S(1)}, u32[]{:S(2)}, u32[]{:S(2)}) collective-permute-start(bf16[1024,128]{1,0:T(8,128)(2,1)S(1)} %get-tuple-element.312), channel_id=1, source_target_pairs={{0,8},{4,12},{8,0},{12,4},{1,9},{5,13},{9,1},{13,5},{2,10},{6,14},... | collective-permute-start | bytes 786440 | tf_op jit(solution)/shard_map/ppermute | solution.py:444
  388.6 57.8 %collective-permute-start.62 = (bf16[128,2048]{1,0:T(8,128)(2,1)}, bf16[128,2048]{1,0:T(8,128)(2,1)}, u32[]{:S(2)}, u32[]{:S(2)}) collective-permute-start(bf16[128,2048]{1,0:T(8,128)(2,1)} %get-tuple-element.140), channel_id=1, source_target_pairs={{0,1},{1,0},{2,3},{3,2},{4,5},{5,4},{6,7},{7,6},{8,9},{9,8},{10,11... | collective-permute-start | bytes 1572872 | tf_op jit(solution)/shard_map/ppermute | solution.py:444
  389.0 57.4 %collective-permute-start.63 = (bf16[128,2048]{1,0:T(8,128)(2,1)}, bf16[128,2048]{1,0:T(8,128)(2,1)}, u32[]{:S(2)}, u32[]{:S(2)}) collective-permute-start(bf16[128,2048]{1,0:T(8,128)(2,1)} %get-tuple-element.141), channel_id=1, source_target_pairs={{0,2},{1,3},{2,0},{3,1},{4,6},{5,7},{6,4},{7,5},{8,10},{9,11},{10,... | collective-permute-start | bytes 1572872 | tf_op jit(solution)/shard_map/ppermute | solution.py:444
  403.5 42.9 %collective-permute-start.64 = (bf16[128,2048]{1,0:T(8,128)(2,1)S(1)}, bf16[128,2048]{1,0:T(8,128)(2,1)}, u32[]{:S(2)}, u32[]{:S(2)}) collective-permute-start(bf16[128,2048]{1,0:T(8,128)(2,1)S(1)} %get-tuple-element.142), channel_id=1, source_target_pairs={{0,3},{1,2},{2,1},{3,0},{4,7},{5,6},{6,5},{7,4},{8,11},{9,10},{10,... | collective-permute-start | bytes 1572872 | tf_op jit(solution)/shard_map/ppermute | solution.py:444
  405.4 43.9 %collective-permute-start.69 = (bf16[512,1920]{1,0:T(8,128)(2,1)}, bf16[512,1920]{1,0:T(8,128)(2,1)}, u32[]{:S(2)}, u32[]{:S(2)}) collective-permute-start(bf16[512,1920]{1,0:T(8,128)(2,1)} %maximum_maximum_fusion), channel_id=1, source_target_pairs={{0,8},{4,12},{8,0},{12,4},{1,9},{5,13},{9,1},{13,5},{2,10},{6,14},... | collective-permute-start | bytes 5898248 | tf_op jit(solution)/shard_map/ppermute | solution.py:444
  408.8 37.6 %collective-permute-start.70 = (bf16[512,1408]{1,0:T(8,128)(2,1)}, bf16[512,1408]{1,0:T(8,128)(2,1)}, u32[]{:S(2)}, u32[]{:S(2)}) collective-permute-start(bf16[512,1408]{1,0:T(8,128)(2,1)} %add_convert_fusion.3), channel_id=1, source_target_pairs={{0,16},{16,0},{1,17},{17,1},{2,18},{18,2},{3,19},{19,3},{4,20},{20... | collective-permute-start | bytes 4325384 | tf_op jit(solution)/shard_map/ppermute | solution.py:444
  453.8 26.4 %collective-permute-start.71 = (bf16[1040,512]{1,0:T(8,128)(2,1)S(1)}, bf16[1040,512]{1,0:T(8,128)(2,1)S(1)}, u32[]{:S(2)}, u32[]{:S(2)}) collective-permute-start(bf16[1040,512]{1,0:T(8,128)(2,1)S(1)} %fusion.11), channel_id=1, source_target_pairs={{0,8},{4,12},{8,0},{12,4},{1,9},{5,13},{9,1},{13,5},{2,10},{6,14},... | collective-permute-start | bytes 3194888 | tf_op jit(solution)/shard_map/ppermute | solution.py:444
  462.8 45.7 %collective-permute-start.78 = (bf16[1024,512]{0,1:T(8,128)(2,1)S(1)}, bf16[1024,512]{0,1:T(8,128)(2,1)S(1)}, u32[]{:S(2)}, u32[]{:S(2)}) collective-permute-start(bf16[1024,512]{0,1:T(8,128)(2,1)S(1)} %slice.1338), channel_id=1, source_target_pairs={{0,8},{4,12},{8,0},{12,4},{1,9},{5,13},{9,1},{13,5},{2,10},{6,14},... | collective-permute-start | bytes 3145736 | tf_op jit(solution)/shard_map/ppermute | solution.py:444
  464.5 54.1 %collective-permute-start.81 = (bf16[512,1920]{1,0:T(8,128)(2,1)S(1)}, bf16[512,1920]{1,0:T(8,128)(2,1)S(1)}, u32[]{:S(2)}, u32[]{:S(2)}) collective-permute-start(bf16[512,1920]{1,0:T(8,128)(2,1)S(1)} %maximum_maximum_fusion.1), channel_id=1, source_target_pairs={{0,16},{16,0},{1,17},{17,1},{2,18},{18,2},{3,19},{19,3},{4,20},{20... | collective-permute-start | bytes 5898248 | tf_op jit(solution)/shard_map/ppermute | solution.py:444
  486.0 11.9 %collective-permute-start.72 = (bf16[384,2048]{1,0:T(8,128)(2,1)S(1)}, bf16[384,2048]{1,0:T(8,128)(2,1)S(1)}, u32[]{:S(2)}, u32[]{:S(2)}) collective-permute-start(bf16[384,2048]{1,0:T(8,128)(2,1)S(1)} %slice.1101), channel_id=1, source_target_pairs={{0,4},{4,0},{8,12},{12,8},{1,5},{5,1},{9,13},{13,9},{2,6},{6,2},{1... | collective-permute-start | bytes 4718600 | tf_op jit(solution)/shard_map/ppermute | solution.py:444
  491.7 16.6 %collective-permute-start.75 = (bf16[128,2048]{1,0:T(8,128)(2,1)S(1)}, bf16[128,2048]{1,0:T(8,128)(2,1)S(1)}, u32[]{:S(2)}, u32[]{:S(2)}) collective-permute-start(bf16[128,2048]{1,0:T(8,128)(2,1)S(1)} %fusion.24), channel_id=1, source_target_pairs={{3,2},{0,1},{7,6},{4,5},{11,10},{8,9},{15,14},{12,13},{19,18},{16,... | collective-permute-start | bytes 1572872 | tf_op jit(solution)/shard_map/ppermute | solution.py:491
  497.0 11.5 %collective-permute-start.74 = (bf16[128,2048]{1,0:T(8,128)(2,1)S(1)}, bf16[128,2048]{1,0:T(8,128)(2,1)S(1)}, u32[]{:S(2)}, u32[]{:S(2)}) collective-permute-start(bf16[128,2048]{1,0:T(8,128)(2,1)S(1)} %fusion.24), channel_id=1, source_target_pairs={{1,2},{2,1},{5,6},{6,5},{9,10},{10,9},{13,14},{14,13},{17,18},{18,... | collective-permute-start | bytes 1572872 | tf_op jit(solution)/shard_map/ppermute | solution.py:491
  513.1 27.8 %collective-permute-start.76 = (bf16[128,2048]{1,0:T(8,128)(2,1)S(1)}, bf16[128,2048]{1,0:T(8,128)(2,1)S(1)}, u32[]{:S(2)}, u32[]{:S(2)}) collective-permute-start(bf16[128,2048]{1,0:T(8,128)(2,1)S(1)} %fusion.23), channel_id=1, source_target_pairs={{0,2},{1,3},{2,0},{3,1},{4,6},{5,7},{6,4},{7,5},{8,10},{9,11},{10,... | collective-permute-start | bytes 1572872 | tf_op jit(solution)/shard_map/ppermute | solution.py:444
  517.1 23.8 %collective-permute-start.77 = (bf16[128,2048]{1,0:T(8,128)(2,1)S(1)}, bf16[128,2048]{1,0:T(8,128)(2,1)S(1)}, u32[]{:S(2)}, u32[]{:S(2)}) collective-permute-start(bf16[128,2048]{1,0:T(8,128)(2,1)S(1)} %slice.1339), channel_id=1, source_target_pairs={{0,1},{1,0},{2,3},{3,2},{4,5},{5,4},{6,7},{7,6},{8,9},{9,8},{10,11... | collective-permute-start | bytes 1572872 | tf_op jit(solution)/shard_map/ppermute | solution.py:444
  517.1 38.8 %collective-permute-start.83 = (bf16[1024,512]{0,1:T(8,128)(2,1)}, bf16[1024,512]{0,1:T(8,128)(2,1)}, u32[]{:S(2)}, u32[]{:S(2)}) collective-permute-start(bf16[1024,512]{0,1:T(8,128)(2,1)} %slice.1337), channel_id=1, source_target_pairs={{0,8},{4,12},{8,0},{12,4},{1,9},{5,13},{9,1},{13,5},{2,10},{6,14},... | collective-permute-start | bytes 3145736 | tf_op jit(solution)/shard_map/ppermute | solution.py:444
  518.7 46.2 %collective-permute-start.82 = (bf16[512,1024]{0,1:T(8,128)(2,1)}, bf16[512,1024]{0,1:T(8,128)(2,1)}, u32[]{:S(2)}, u32[]{:S(2)}) collective-permute-start(bf16[512,1024]{0,1:T(8,128)(2,1)} %pad_maximum_fusion.22), channel_id=1, source_target_pairs={{0,16},{16,0},{1,17},{17,1},{2,18},{18,2},{3,19},{19,3},{4,20},{20... | collective-permute-start | bytes 3145736 | tf_op jit(solution)/shard_map/ppermute | solution.py:444
  566.7 29.4 %collective-permute-start.92 = (bf16[512,1024]{0,1:T(8,128)(2,1)}, bf16[512,1024]{0,1:T(8,128)(2,1)}, u32[]{:S(2)}, u32[]{:S(2)}) collective-permute-start(bf16[512,1024]{0,1:T(8,128)(2,1)} %pad_maximum_fusion.23), channel_id=1, source_target_pairs={{0,16},{16,0},{1,17},{17,1},{2,18},{18,2},{3,19},{19,3},{4,20},{20... | collective-permute-start | bytes 3145736 | tf_op jit(solution)/shard_map/ppermute | solution.py:444
  576.8 15.8 %collective-permute-start.95 = (f32[28,128]{1,0:T(8,128)S(1)}, f32[28,128]{1,0:T(8,128)S(1)}, u32[]{:S(2)}, u32[]{:S(2)}) collective-permute-start(f32[28,128]{1,0:T(8,128)S(1)} %constant_dynamic-update-slice_fusion.20), channel_id=1, source_target_pairs={{0,16},{16,0},{1,17},{17,1},{2,18},{18,2},{3,19},{19,3},{4,20},{20... | collective-permute-start | bytes 43016 | tf_op jit(solution)/shard_map/ppermute | solution.py:444
  579.3 14.5 %collective-permute-start.91 = (f32[34,128]{1,0:T(8,128)S(1)}, f32[34,128]{1,0:T(8,128)S(1)}, u32[]{:S(2)}, u32[]{:S(2)}) collective-permute-start(f32[34,128]{1,0:T(8,128)S(1)} %add_add_fusion), channel_id=1, source_target_pairs={{0,16},{16,0},{1,17},{17,1},{2,18},{18,2},{3,19},{19,3},{4,20},{20... | collective-permute-start | bytes 52232 | tf_op jit(solution)/shard_map/ppermute | solution.py:444
  (143 other events, 1572.1 us)

commit v5 on v4

--- a/solution.py
+++ b/solution.py
@@ -25,6 +25,10 @@
     a_hi, a_lo = a if isinstance(a, tuple) else halves(a)
     b_hi, b_lo = b if isinstance(b, tuple) else halves(b)
     return product(a_hi, b_hi, dims) + (product(a_hi, b_lo, dims) + product(a_lo, b_hi, dims))
+
+
+def low_dot(a, b, dims=((1,), (0,))):
+    return product(a.astype(bf16), b.astype(bf16), dims)
 
 
 NN = ((1,), (0,))
@@ -158,12 +162,13 @@
             inverse = inverse + close_dot(inverse, power)
         wu = close_dot(inverse, jnp.concatenate([jnp.where(keep, kb, 0.0), b * v], axis=1))
         wu_two = halves(wu)
-        scores = jnp.where(upto, close_dot(q, k_two, NT), 0.0)
-        cd = close_dot(scores, wu_two)
+        scores = jnp.where(upto, product(q.astype(bf16), k_two[0], NT), 0.0).astype(bf16)
+        cd = product(scores, wu_two[0], NN)
         c = jnp.where(keep, q, 0.0) - cd[:, :LANES]
         wu_ref[at] = wu
-        t_ref[at] = inverse
+        t_ref[at] = inverse.astype(bf16)
         a_ref[at] = scores
+        c = c.astype(bf16)
         c_ref[at] = c
         for h in range(2):
             inner = slice(h * BLOCK, (h + 1) * BLOCK)
@@ -179,9 +184,9 @@
     state = state_ref[...]
     results = []
     for n, (m_two, addend, c, d) in enumerate(blocks):
-        s_ref[n] = state
         s_two = halves(state)
-        results.append(close_dot(c, s_two) + d)
+        s_ref[n] = s_two[0]
+        results.append(product(c, s_two[0], NN) + d)
         state = close_dot(m_two, s_two) + addend
         square_ref[pl.ds(step * len(blocks) + n, 1), :] = jnp.sum(state * state, axis=0, keepdims=True)
     state_ref[...] = state
@@ -249,16 +254,16 @@
     logit_sig = jax.nn.sigmoid(columns(step, count, info_ref, logit_ref))
     beta = logit_sig * valid
     pairs = rows // PAIR
-    do_two = halves(d_o)
+    do_low = d_o.astype(bf16)
     pieces = [None] * (2 * pairs)
     for n in range(2 * pairs):
         inner = slice(n * BLOCK, (n + 1) * BLOCK)
-        pieces[n] = close_dot(c_ref[inner, :], (do_two[0][inner], do_two[1][inner]), TN)
+        pieces[n] = product(c_ref[inner, :], do_low[inner], TN)
     dstate = dstate_ref[...]
     dstates = [None] * (2 * pairs)
     for n in reversed(range(2 * pairs)):
         d_two = halves(dstate)
-        dstates[n] = d_two
+        dstates[n] = d_two[0]
         dstate = close_dot(m_ref[n], d_two, TN) + pieces[n]
     dstate_ref[...] = dstate
     grads = [[], [], []]
@@ -269,44 +274,37 @@
         q, k, v, b = units[0][at], units[1][at], units[2][at], beta[at]
         upto, strict, keep, eye = pair_masks(start, begins[at])
         wu = wu_ref[at, :]
-        wu_two = halves(wu)
-        a_two = halves(a_ref[at, :])
-        k_two = halves(k)
-        do_pair = (do_two[0][at], do_two[1][at])
+        wu_low = wu.astype(bf16)
+        k_low = k.astype(bf16)
+        do_pair = do_low[at]
         p_rows, dp_rows, dq_rows, dk_rows, dw_rows = [], [], [], [], []
-        later = close_dot(a_two, do_pair, TN)
+        later = product(a_ref[at, :], do_pair, TN)
         for h in range(2):
             n = g * 2 + h
             inner = slice(h * BLOCK, (h + 1) * BLOCK)
             first = start + h * BLOCK
             final = doc_start(first + BLOCK - 1, starts_ref)
             tail = place_rows(first, BLOCK) >= final
-            s_two = halves(s_ref[n])
-            ds_two = dstates[n]
-            wu_in = (wu_two[0][inner, :LANES], wu_two[1][inner, :LANES])
-            p = wu[inner, LANES:] - close_dot(wu_in, s_two)
-            p_two = halves(p)
+            s_low = s_ref[n]
+            ds_low = dstates[n]
+            p = (wu[inner, LANES:] - product(wu_low[inner, :LANES], s_low, NN)).astype(bf16)
             k_last = jnp.where(tail, k[inner], 0.0)
-            dp = later[inner] + close_dot(k_last, ds_two)
-            dp_two = halves(dp)
-            p_rows.append(p_two)
+            dp = later[inner] + low_dot(k_last, ds_low)
+            p_rows.append(p)
             dp_rows.append(dp)
-            do_in = (do_pair[0][inner], do_pair[1][inner])
-            dq_rows.append(close_dot(do_in, s_two, NT))
-            dk_rows.append(jnp.where(tail, close_dot(p_two, ds_two, NT), 0.0))
-            dw_rows.append(-close_dot(dp_two, s_two, NT))
-        p_two = tuple(jnp.concatenate([p_rows[0][i], p_rows[1][i]], axis=0) for i in range(2))
+            dq_rows.append(product(do_pair[inner], s_low, NT))
+            dk_rows.append(jnp.where(tail, product(p, ds_low, NT), 0.0))
+            dw_rows.append(-low_dot(dp, s_low, NT))
         dp = jnp.concatenate(dp_rows, axis=0)
-        da_two = halves(jnp.where(upto, close_dot(do_pair, p_two, NT), 0.0))
-        q_two = halves(q)
-        dq = jnp.where(keep, jnp.concatenate(dq_rows, axis=0), 0.0) + close_dot(da_two, k_two)
-        dk = jnp.concatenate(dk_rows, axis=0) + close_dot(da_two, q_two, TN)
+        da = jnp.where(upto, product(do_pair, jnp.concatenate(p_rows, axis=0), NT), 0.0).astype(bf16)
+        dq = jnp.where(keep, jnp.concatenate(dq_rows, axis=0), 0.0) + product(da, k_low, NN)
+        dk = jnp.concatenate(dk_rows, axis=0) + low_dot(da, q, TN)
         dwu = jnp.concatenate([jnp.concatenate(dw_rows, axis=0), dp], axis=1)
-        dbkv = close_dot(t_ref[at, :], dwu, TN)
-        dl_two = halves(jnp.where(strict, -close_dot(dbkv, wu_two, NT), 0.0))
-        dkb = close_dot(dl_two, k_two) + jnp.where(keep, dbkv[:, :LANES], 0.0)
+        dbkv = low_dot(t_ref[at, :], dwu, TN)
+        dl = jnp.where(strict, -low_dot(dbkv, wu_low, NT), 0.0).astype(bf16)
+        dkb = product(dl, k_low, NN) + jnp.where(keep, dbkv[:, :LANES], 0.0)
         dbv = dbkv[:, LANES:]
-        dk = dk + b * dkb + close_dot(dl_two, b * k, TN)
+        dk = dk + b * dkb + low_dot(dl, b * k, TN)
         grads[0].append(dq)
         grads[1].append(dk)
         grads[2].append(b * dbv)
@@ -393,8 +391,8 @@
         ),
         out_shape=[
             s((total, LANES), bf16), s((8, LANES), f32), s((3, total, LANES), f32),
-            s((total, 2 * LANES), f32), s((total, PAIR), f32), s((total, PAIR), f32), s((total, LANES), f32),
-            s((total // BLOCK, LANES, LANES), f32), s((total // BLOCK, LANES, LANES), f32),
+            s((total, 2 * LANES), f32), s((total, PAIR), bf16), s((total, PAIR), bf16), s((total, LANES), bf16),
+            s((total // BLOCK, LANES, LANES), f32), s((total // BLOCK, LANES, LANES), bf16),
             s((total, LANES), f32),
         ],
         name="head_forward",
@@ -435,7 +433,7 @@
         ),
         out_shape=[s((total, 4 * LANES), bf16), s(logit.shape, f32), s(taps.shape, f32), s((8, LANES), f32)],
         name="head_backward",
-        cost_estimate=pl.CostEstimate(flops=total * 18_000_000, transcendentals=0, bytes_accessed=total * 10_000),
+        cost_estimate=pl.CostEstimate(flops=total * 12_000_000, transcendentals=0, bytes_accessed=total * 10_000),
     )(starts, info, near, far, logit, taps, gain, grad_near, grad_far, *kept)
 
 
@@ -703,7 +701,6 @@
         lambda a, b: matmul(d_gate[a:b], full_in[0], ((1,), (1,))) + matmul(d_up[a:b], full_in[1], ((1,), (1,))),
     )
     two_own, two_got, two_sent = collect_pieces(two_parts)
-    d_normed_two = added(two_own, two_got)
     hidden, d_gate, d_up = after((hidden, d_gate, d_up), two_sent)
     tn = ((0,), (0,))
     grad_dot = lambda a, b: matmul(a, b, tn)
@@ -729,6 +726,7 @@
     up_held, up_sent = units_joined(up_product, 0)
     down_got = other(down_sent, "mp", 2)
 
+    d_normed_two = added(after(two_own, down_sent), two_got)
     d_mid_norm, g_mlp = norm_back(d_normed_two, unit_two, scale_two, gain_two)
     d_middle = cot_own.astype(f32) + d_mid_norm
     d_mid_low = after(d_middle.astype(bf16), down_sent, gate_sent)
@@ -745,20 +743,17 @@
     d_mid_all = after(with_core(d_mid_pieces), down_got, feed_sent)
     d_mixed = matmul(d_mid_all, full_out, ((1,), (1,))).astype(bf16)
     d_far = other(d_mixed[:, head:], "mp", 2)
-    gate_sums = over_dp_pieces(summed(gate_held, after(gate_got, down_sums[1], d_mixed)))
+    gate_sums = over_dp_pieces(summed(gate_held, after(gate_got, down_sums[1], d_far)))
     feed_got = [other(after(v, d_mid_all), "tensor", p + 1) for p, v in enumerate(feed_sent)]
     feed_own = feed_joined[:piece_rows]
     output = own_order((middle + added(feed_own, feed_got)).astype(bf16), m, 1)
 
     out_grad = grad_dot(mixed_tok, d_mid_all)
     out_sent = out_grad[:, near_blocks:].astype(bf16)
-    late_sent = jnp.concatenate(
-        [up_sent, jnp.concatenate([out_sent[:, :block], out_sent[:, block:]], axis=0)], axis=1
-    )
-    late_got = other(after(late_sent, d_far), "mp", 2)
+    up_got = other(after(up_sent, d_far), "mp", 2)
     d_near = after(d_mixed[:, :head], gate_got, down_sums[1])
     d_heads, d_logit, d_taps, g_head_gain = head_backward(d_near, d_far, *head_args, kept)
-    d_heads, d_logit = after((d_heads, d_logit), late_got, gate_sums[1], *feed_got)
+    d_heads, d_logit = after((d_heads, d_logit), up_got, gate_sums[1], *feed_got)
     d_own = d_heads[:count]
     d_logit = d_logit.astype(bf16)
     half_chunks = d_logit.shape[0] // 2
@@ -774,20 +769,19 @@
     d_logits = jnp.concatenate(
         [d_logit[:half_chunks].reshape(1, count), d_got[count:count + logit_rows].reshape(1, count)], axis=0
     )
-    late_got = after(late_got, d_sent)
-    out_got = jnp.concatenate([late_got[: 2 * head, units:], late_got[2 * head:, units:]], axis=1)
+    up_sums = over_dp_pieces(summed(up_held, after(up_got, d_sent)))
+    out_got = other(after(out_sent, d_sent), "mp", 2)
+    normed_parts = partials(
+        count,
+        lambda a, b: matmul(d_proj[a:b], full_proj, ((1,), (1,))) + matmul(d_logits[:, a:b], full_beta, tn),
+    )
+    normed_own, normed_got, normed_sent = collect_pieces(normed_parts)
+    out_got = after(out_got, normed_parts)
     out_two = (out_grad[:, :near_blocks] + neighbour_order(out_got, 0, 1, 2).astype(f32)).astype(bf16)
     out_theirs = other(out_two[:, block:], "mp", 1)
     out_mine = out_two[:, :block]
     out_rows = jnp.concatenate([out_mine[:head], out_theirs[:head], out_mine[head:], out_theirs[head:]], axis=0)
-    up_two = summed(up_held, late_got[:, :units]).astype(bf16)
-    late_sums = over_dp_pieces(jnp.concatenate([up_two, out_rows], axis=1))
-    normed_parts = partials(
-        count,
-        lambda a, b: matmul(d_proj[a:b], full_proj, ((1,), (1,))) + matmul(d_logits[:, a:b], full_beta, tn),
-    )
-    normed_own, normed_got, normed_sent = collect_pieces(normed_parts)
-    d_normed = added(normed_own, normed_got)
+    out_sums = over_dp_pieces(out_rows)
     own_grad = grad_dot(normed, after(d_own, d_sent))
     far_grad = grad_dot(normed, after(d_got, normed_parts)[:count])
     own_back = other(own_grad[near_blocks:].astype(bf16), "mp", 2)
@@ -797,8 +791,24 @@
         two = (held[:near_blocks] + back.astype(f32)).astype(bf16)
         return jnp.concatenate([two[:block], other(two[block:], "mp", 1)], axis=1)
 
-    far_part = after(proj_part(far_grad, after(own_back, normed_sent)), late_sums[1])
+    far_part = after(proj_part(far_grad, after(own_back, normed_sent)), up_sums[1], out_sums[1])
     far_sums = over_dp_pieces(far_part)
+    down_sums, gate_sums = after((down_sums, gate_sums), far_part)
+    g_down = summed(*down_sums)
+    up_sums, out_sums = after((up_sums, out_sums), far_part)
+    g_in = jnp.stack([summed(*gate_sums), summed(*up_sums)])
+    g_out = own_order(summed(*out_sums), m, 0)
+    normed_again, partial_rows = after((normed, normed_parts), far_part)
+    g_norm = (
+        jnp.sum(normed_again[: count // 2].astype(f32) * partial_rows[1], axis=0)
+        + jnp.sum(normed_again[count // 2:].astype(f32) * partial_rows[0].astype(f32), axis=0)
+    ) / gain_one
+    row = lambda v: v.reshape(-1, LANES)
+    rows_all = [own_order(row(g_norm), m, 0), own_order(row(g_mlp), m, 0), g_head_gain[:1]]
+    rows_all.append(jnp.full((1, LANES), norm_total))
+    rows_here = jnp.concatenate(rows_all, axis=0)
+    beta_here = matmul(after(d_logits, far_part), normed)
+    d_normed = added(after(normed_own, g_down, g_in, g_out, rows_here, beta_here), normed_got)
     own_part = proj_part(own_grad, after(far_back, normed_got))
     own_sums = over_dp_pieces(own_part)
     part_far, part_own = summed(*far_sums), summed(*own_sums)
@@ -806,7 +816,7 @@
     g_proj = own_order(
         jnp.concatenate([v.reshape(block, pieces, head).transpose(1, 0, 2) for v in g_heads], axis=2), m, 2
     )
-    beta_part = after(matmul(after(d_logits, far_part), normed), far_sums[1], own_part)
+    beta_part = after(beta_here, far_sums[1], own_part)
     beta_back = neighbour_order(neighbour_order(other(beta_part, "mp", 2), 0, 1, 2), 1, 1, 2)
     beta_two = beta_part + beta_back
     beta_theirs = other(beta_two[:, block:near_blocks], "mp", 1)
@@ -821,22 +831,9 @@
     cut = g_beta.size // LANES
     g_beta = small[:cut].reshape(g_beta.shape)
     d_taps = small[cut:]
-    normed_again, partial_rows = after((normed, normed_parts), far_part)
-    g_norm = (
-        jnp.sum(normed_again[: count // 2].astype(f32) * partial_rows[1], axis=0)
-        + jnp.sum(normed_again[count // 2:].astype(f32) * partial_rows[0].astype(f32), axis=0)
-    ) / gain_one
-    row = lambda v: v.reshape(-1, LANES)
-    rows_all = [own_order(row(g_norm), m, 0), own_order(row(g_mlp), m, 0), g_head_gain[:1]]
-    rows_all.append(jnp.full((1, LANES), norm_total))
-    sums = over_all(after(jnp.concatenate(rows_all, axis=0), far_sums[1], own_part))
+    sums = over_all(after(rows_here, far_sums[1], own_part))
     d_in_norm, _ = norm_back(d_normed, unit_one, scale_one, gain_one)
     d_tokens = own_order(d_middle + d_in_norm, m, 1)
-    down_sums, gate_sums = after((down_sums, gate_sums), far_part)
-    g_down = summed(*down_sums)
-    g_late = summed(*after(late_sums, far_part))
-    g_in = jnp.stack([summed(*gate_sums), g_late[:, :units]])
-    g_out = own_order(g_late[:, units:], m, 0)
     lines = g_norm.shape[0] // LANES
     ways = lax.axis_size("mp") * lax.axis_size("tensor")
     state_norm = sums[2 * lines + 1, 0] / (ways * lax.axis_size("dp") * (2 * count // BLOCK))

time: 610 us -> 593 us (0.972)
  Pallas kernels: 75.5 us -> 66.7 us
  waiting for transfers between devices: 228 us -> 220 us
  local copies, waits for them, and re-layouts: 75.2 us -> 69.1 us
    ppermute x84 -> x86, waiting for transfers between devices: 168 us -> 159 us  [other(): return lax.ppermute(value, axis, [(i, i ^ bit) for i in range(size)])]
    pallas_call x1, Pallas kernels: 34.7 us -> 26.5 us  [head_backward(): pl.pallas_call(backward_body, grid_spec=pltpu.PrefetchScalarGridSpec(num_...]
    ppermute x84 -> x86, starting transfers between devices: 63.6 us -> 67.6 us  [other(): return lax.ppermute(value, axis, [(i, i ^ bit) for i in range(size)])]
    unnamed x240 -> x224, local copies, waits for them, and re-layouts: 23.5 us -> 20.3 us
  transfers between devices with their start and end apart: 96 -> 98, of which waited for: 30 -> 31; matrix products, arithmetic and copies ran while one was open for 26% -> 27% of each run, Pallas kernels for 12% -> 11%
where the time goes in v5:
time: 593 us; the launch traced here: 589 us
  waiting for transfers between devices  220 us (37%)
  starting transfers between devices  89.6 us (15%)
  local copies, waits for them, and re-layouts  69.1 us (12%)
  other arithmetic  68.6 us (12%)
  matrix products  68.4 us (12%)
  Pallas kernels  66.7 us (11%)
  between operations  6.13 us (1%)
    ppermute x86, waiting for transfers between devices, other(): return lax.ppermute(value, axis, [(i, i ^ bit) for i in range(size)])  159 us
    dot_general x28, matrix products, matmul(): return lax.dot_general(a, b, (dims, ((), ())), preferred_element_type=f32)  68.4 us
    ppermute x86, starting transfers between devices, other(): return lax.ppermute(value, axis, [(i, i ^ bit) for i in range(size)])  67.6 us
    ppermute x12, waiting for transfers between devices, along_tensor(): return lax.ppermute(value, 'tensor', pairs)  61.3 us
    pallas_call x1, Pallas kernels, head_forward(): pl.pallas_call(forward_body, grid_spec=pltpu.PrefetchScalarGridSpec(num_s...  40.2 us
    pallas_call x1, Pallas kernels, head_backward(): pl.pallas_call(backward_body, grid_spec=pltpu.PrefetchScalarGridSpec(num_...  26.5 us
    ppermute x12, starting transfers between devices, along_tensor(): return lax.ppermute(value, 'tensor', pairs)  22 us
    unnamed x224, local copies, waits for them, and re-layouts  20.3 us
  transfers between devices with their start and end apart: 98, of which 31 were waited for; matrix products, arithmetic and copies ran while one was open for 27% of the time, Pallas kernels for 11%

profile of v5, /device:TPU:0, one launch (start us, length us, event | category | flops | bytes accessed | tf_op | source)
XLA Modules:
  0.0 588.9 jit_solution(7507476150435574244)
XLA Ops:
  6.2 4.1 collective-permute-start.1
  13.3 4.1 copy.29
  19.2 2.3 fusion.98
  24.3 2.9 constant_dynamic-slice_fusion.58
  29.3 2.8 constant_dynamic-slice_fusion.34
  44.5 8.6 %collective-permute-done.3 = bf16[128,2048]{1,0:T(8,128)(2,1)S(1)} collective-permute-done((bf16[128,2048]{1,0:T(8,128)(2,1)}, bf16[128,2048]{1,0:T(8,128)(2,1)S(1)}, u32[]{:S(2)}, u32[]{:S(2)}) %collective-permute-start.3) | collective-permute-done | bytes 524320 | tf_op jit(solution)/shard_map/ppermute | solution.py:489
  58.7 6.8 %collective-permute-done.9 = bf16[4,512,512]{1,2,0:T(8,128)(2,1)} collective-permute-done((bf16[4,512,512]{1,2,0:T(8,128)(2,1)}, bf16[4,512,512]{1,2,0:T(8,128)(2,1)}, u32[]{:S(2)}, u32[]{:S(2)}) %collective-permute-start.9) | collective-permute-done | bytes 2097184 | tf_op jit(solution)/shard_map/ppermute | solution.py:442
  66.2 2.5 constant_dynamic-slice_fusion.54
  82.9 2.3 add_convert_fusion.5.near_ref.before_near_ref
  86.0 19.6 %collective-permute-done.13.far_ref.before_far_ref = bf16[1040,512]{1,0:T(8,128)(2,1)S(1)} collective-permute-done((bf16[1040,512]{1,0:T(8,128)(2,1)S(1)}, bf16[1040,512]{1,0:T(8,128)(2,1)S(1)}, u32[]{:S(2)}, u32[]{:S(2)}) %collective-permute-start.13) | collective-permute-done | bytes 1064992 | tf_op jit(solution)/shard_map/ppermute | solution.py:442
  107.7 2.5 collective-permute-start.18
  111.3 40.2 %head_forward.1 = (bf16[2048,128]{1,0:T(8,128)(2,1)}, f32[8,128]{1,0:T(8,128)}, f32[3,2048,128]{2,1,0:T(8,128)}, f32[2048,256]{1,0:T(8,128)}, bf16[2048,128]{1,0...) custom-call(s32[8]{0:T(128)} %bitcast.140, ...), custom_call_target="tpu_custom_call" | custom-call | flops 40960000000 | bytes 20480000 | tf_op jit(solution)/shard_map/head_forward/pallas_call | solution.py:365
  151.5 2.1 collective-permute-done.17
  156.9 6.8 %collective-permute-done.21 = bf16[1024,128]{1,0:T(8,128)(2,1)S(1)} collective-permute-done((bf16[1024,128]{1,0:T(8,128)(2,1)S(1)}, bf16[1024,128]{1,0:T(8,128)(2,1)S(1)}, u32[]{:S(2)}, u32[]{:S(2)}) %collective-permute-start.21) | collective-permute-done | bytes 262176 | tf_op jit(solution)/shard_map/ppermute | solution.py:442
  166.8 2.0 collective-permute-done.24
  169.0 2.3 collective-permute-start.26
  172.8 9.9 %collective-permute-done.26 = bf16[128,2048]{1,0:T(8,128)(2,1)S(1)} collective-permute-done((bf16[128,2048]{1,0:T(8,128)(2,1)S(1)}, bf16[128,2048]{1,0:T(8,128)(2,1)S(1)}, u32[]{:S(2)}, u32[]{:S(2)}) %collective-permute-start.26) | collective-permute-done | bytes 524320 | tf_op jit(solution)/shard_map/ppermute | solution.py:489
  183.5 3.0 collective-permute-start.28
  188.9 20.2 %collective-permute-done.28 = bf16[128,2048]{1,0:T(8,128)(2,1)S(1)} collective-permute-done((bf16[128,2048]{1,0:T(8,128)(2,1)S(1)}, bf16[128,2048]{1,0:T(8,128)(2,1)S(1)}, u32[]{:S(2)}, u32[]{:S(2)}) %collective-permute-start.28) | collective-permute-done | bytes 524320 | tf_op jit(solution)/shard_map/ppermute | solution.py:442
  209.9 2.7 collective-permute-start.32
  215.6 21.0 %collective-permute-done.31 = bf16[128,2048]{1,0:T(8,128)(2,1)S(1)} collective-permute-done((bf16[128,2048]{1,0:T(8,128)(2,1)S(1)}, bf16[128,2048]{1,0:T(8,128)(2,1)S(1)}, u32[]{:S(2)}, u32[]{:S(2)}) %collective-permute-start.31) | collective-permute-done | bytes 524320 | tf_op jit(solution)/shard_map/ppermute | solution.py:442
  239.8 2.0 collective-permute-done.37
  242.5 12.8 %collective-permute-done.35 = bf16[128,2048]{1,0:T(8,128)(2,1)S(1)} collective-permute-done((bf16[128,2048]{1,0:T(8,128)(2,1)S(1)}, bf16[128,2048]{1,0:T(8,128)(2,1)S(1)}, u32[]{:S(2)}, u32[]{:S(2)}) %collective-permute-start.35) | collective-permute-done | bytes 524320 | tf_op jit(solution)/shard_map/ppermute | solution.py:489
  257.1 5.1 fusion.90
  263.2 3.4 fusion.141
  266.6 5.8 multiply_convert_fusion
  276.9 3.8 fusion.47
  280.8 4.0 convolution_add_fusion
  285.7 4.4 collective-permute-start.46
  291.0 10.4 %collective-permute-done.46 = bf16[128,2048]{1,0:T(8,128)(2,1)S(1)} collective-permute-done((bf16[128,2048]{1,0:T(8,128)(2,1)S(1)}, bf16[128,2048]{1,0:T(8,128)(2,1)S(1)}, u32[]{:S(2)}, u32[]{:S(2)}) %collective-permute-start.46) | collective-permute-done | bytes 524320 | tf_op jit(solution)/shard_map/ppermute | solution.py:489
  301.6 3.2 collective-permute-start.49
  304.8 3.9 convolution_convert_fusion.2
  309.2 3.9 convolution_convert_fusion.1
  313.9 2.7 convolution_convert_fusion.4
  317.7 9.3 %collective-permute-done.49 = bf16[128,2048]{1,0:T(8,128)(2,1)S(1)} collective-permute-done((bf16[128,2048]{1,0:T(8,128)(2,1)S(1)}, bf16[128,2048]{1,0:T(8,128)(2,1)S(1)}, u32[]{:S(2)}, u32[]{:S(2)}) %collective-permute-start.49) | collective-permute-done | bytes 524320 | tf_op jit(solution)/shard_map/ppermute | solution.py:442
  333.8 3.8 convolution_convert_fusion
  338.1 17.6 %collective-permute-done.54 = bf16[128,2048]{1,0:T(8,128)(2,1)S(1)} collective-permute-done((bf16[128,2048]{1,0:T(8,128)(2,1)S(1)}, bf16[128,2048]{1,0:T(8,128)(2,1)S(1)}, u32[]{:S(2)}, u32[]{:S(2)}) %collective-permute-start.54) | collective-permute-done | bytes 524320 | tf_op jit(solution)/shard_map/ppermute | solution.py:442
  356.4 2.3 collective-permute-done.52
  363.0 8.8 %collective-permute-done.56 = bf16[128,2048]{1,0:T(8,128)(2,1)S(1)} collective-permute-done((bf16[128,2048]{1,0:T(8,128)(2,1)S(1)}, bf16[128,2048]{1,0:T(8,128)(2,1)S(1)}, u32[]{:S(2)}, u32[]{:S(2)}) %collective-permute-start.56) | collective-permute-done | bytes 524320 | tf_op jit(solution)/shard_map/ppermute | solution.py:489
  380.4 5.1 fusion.137
  389.6 4.2 collective-permute-start.63
  395.2 8.1 %collective-permute-done.67.grad_far_ref = bf16[1024,128]{1,0:T(8,128)(2,1)S(1)} collective-permute-done((bf16[1024,128]{1,0:T(8,128)(2,1)S(1)}, bf16[1024,128]{1,0:T(8,128)(2,1)S(1)}, u32[]{:S(2)}, u32[]{:S(2)}) %collective-permute-start.67) | collective-permute-done | bytes 262176 | tf_op jit(solution)/shard_map/ppermute | solution.py:442
  410.1 26.5 %head_backward.1 = (bf16[2048,512]{1,0:T(8,128)(2,1)}, f32[16,128]{1,0:T(8,128)}, f32[3,4,128]{2,1,0:T(4,128)}, f32[8,128]{1,0:T(8,128)}) custom-call(s32[8]{0:T(128)} %bitcast.141, s32[2]{0:T(128)} %pad_add_fusion.3.info_ref, bf16[1024,512]{1,0:T(8,128)(2,1)} %add_convert_fusion.5.near_ref.before_near_ref, bf16[1040,512]{1,0:T(8,128)(2,1)} %copy-done.95, ...), custom_call_target="tpu_custom_call" | custom-call | flops 24576000000 | bytes 20480000 | tf_op jit(solution)/shard_map/head_backward/pallas_call | solution.py:413
  438.0 2.9 fusion.29
  443.5 2.2 add_convert_fusion.2
  448.5 2.5 fusion.142
  452.1 17.2 %collective-permute-done.71 = bf16[1040,512]{1,0:T(8,128)(2,1)S(1)} collective-permute-done((bf16[1040,512]{1,0:T(8,128)(2,1)S(1)}, bf16[1040,512]{1,0:T(8,128)(2,1)S(1)}, u32[]{:S(2)}, u32[]{:S(2)}) %collective-permute-start.71) | collective-permute-done | bytes 1064992 | tf_op jit(solution)/shard_map/ppermute | solution.py:442
  472.3 2.3 add_convert_fusion
  474.8 2.4 convolution_add_fusion.1
  477.2 3.3 collective-permute-done.79
  481.4 2.5 fusion.42
  484.8 6.9 %collective-permute-start.75 = (bf16[128,2048]{1,0:T(8,128)(2,1)S(1)}, bf16[128,2048]{1,0:T(8,128)(2,1)S(1)}, u32[]{:S(2)}, u32[]{:S(2)}) collective-permute-start(bf16[128,2048]{1,0:T(8,128)(2,1)S(1)} %fusion.23), channel_id=1, source_target_pairs={{3,2},{0,1},{7,6},{4,5},{11,10},{8,9},{15,14},{12,13},{19,18},{16,... | collective-permute-start | bytes 1572872 | tf_op jit(solution)/shard_map/ppermute | solution.py:489
  492.3 10.7 %collective-permute-done.75 = bf16[128,2048]{1,0:T(8,128)(2,1)S(1)} collective-permute-done((bf16[128,2048]{1,0:T(8,128)(2,1)S(1)}, bf16[128,2048]{1,0:T(8,128)(2,1)S(1)}, u32[]{:S(2)}, u32[]{:S(2)}) %collective-permute-start.75) | collective-permute-done | bytes 524320 | tf_op jit(solution)/shard_map/ppermute | solution.py:489
  508.8 2.6 collective-permute-start.82
  514.1 6.2 %collective-permute-done.81 = bf16[512,512]{1,0:T(8,128)(2,1)S(1)} collective-permute-done((bf16[512,512]{1,0:T(8,128)(2,1)S(1)}, bf16[512,512]{1,0:T(8,128)(2,1)S(1)}, u32[]{:S(2)}, u32[]{:S(2)}) %collective-permute-start.81) | collective-permute-done | bytes 524320 | tf_op jit(solution)/shard_map/ppermute | solution.py:442
  526.3 2.0 convert_add_fusion.1
  528.3 3.7 add_bitcast_fusion.1
  532.7 2.2 pad_maximum_fusion.22
  534.9 4.9 pad_maximum_fusion
  556.7 2.1 collective-permute-start.91
  565.0 2.6 copy.36
  567.6 2.5 copy.37
  570.1 5.9 collective-permute-done.97
  585.3 2.3 pad_maximum_fusion.2
  (597 shorter events, 172.8 us)
Async XLA Ops:
  6.2 31.1 %collective-permute-start.1 = (bf16[128,2048]{1,0:T(8,128)(2,1)}, bf16[128,2048]{1,0:T(8,128)(2,1)}, u32[]{:S(2)}, u32[]{:S(2)}) collective-permute-start(bf16[128,2048]{1,0:T(8,128)(2,1)} %get-tuple-element.105), channel_id=1, source_target_pairs={{0,2},{1,3},{2,0},{3,1},{4,6},{5,7},{6,4},{7,5},{8,10},{9,11},{10,... | collective-permute-start | bytes 1572872 | tf_op jit(solution)/shard_map/ppermute | solution.py:442
  10.3 28.3 %collective-permute-start = (bf16[128,2048]{1,0:T(8,128)(2,1)}, bf16[128,2048]{1,0:T(8,128)(2,1)}, u32[]{:S(2)}, u32[]{:S(2)}) collective-permute-start(bf16[128,2048]{1,0:T(8,128)(2,1)} %get-tuple-element.105), channel_id=1, source_target_pairs={{0,1},{1,0},{2,3},{3,2},{4,5},{5,4},{6,7},{7,6},{8,9},{9,8},{10,11... | collective-permute-start | bytes 1572872 | tf_op jit(solution)/shard_map/ppermute | solution.py:442
  11.8 29.5 %collective-permute-start.4 = (bf16[128,2048]{1,0:T(8,128)(2,1)}, bf16[128,2048]{1,0:T(8,128)(2,1)}, u32[]{:S(2)}, u32[]{:S(2)}) collective-permute-start(bf16[128,2048]{1,0:T(8,128)(2,1)} %get-tuple-element.105), channel_id=1, source_target_pairs={{0,4},{4,0},{8,12},{12,8},{1,5},{5,1},{9,13},{13,9},{2,6},{6,2},{1... | collective-permute-start | bytes 1572872 | tf_op jit(solution)/shard_map/ppermute | solution.py:442
  11.8 46.9 %collective-permute-start.11 = (bf16[4,512]{1,0:T(4,128)(2,1)}, bf16[4,512]{1,0:T(4,128)(2,1)}, u32[]{:S(2)}, u32[]{:S(2)}) collective-permute-start(bf16[4,512]{1,0:T(4,128)(2,1)} %bitcast.18), channel_id=1, source_target_pairs={{0,8},{4,12},{8,0},{12,4},{1,9},{5,13},{9,1},{13,5},{2,10},{6,14},... | collective-permute-start | bytes 12296 | tf_op jit(solution)/shard_map/ppermute | solution.py:442
  17.5 48.1 %collective-permute-start.9 = (bf16[4,512,512]{1,2,0:T(8,128)(2,1)}, bf16[4,512,512]{1,2,0:T(8,128)(2,1)}, u32[]{:S(2)}, u32[]{:S(2)}) collective-permute-start(bf16[4,512,512]{1,2,0:T(8,128)(2,1)} %copy.29), channel_id=1, source_target_pairs={{0,8},{4,12},{8,0},{12,4},{1,9},{5,13},{9,1},{13,5},{2,10},{6,14},... | collective-permute-start | bytes 6291464 | tf_op jit(solution)/shard_map/ppermute | solution.py:442
  37.3 15.9 %collective-permute-start.3 = (bf16[128,2048]{1,0:T(8,128)(2,1)}, bf16[128,2048]{1,0:T(8,128)(2,1)S(1)}, u32[]{:S(2)}, u32[]{:S(2)}) collective-permute-start(bf16[128,2048]{1,0:T(8,128)(2,1)} %collective-permute-done.1), channel_id=1, source_target_pairs={{2,3},{1,0},{6,7},{5,4},{10,11},{9,8},{14,15},{13,12},{18,19},{17,... | collective-permute-start | bytes 1572872 | tf_op jit(solution)/shard_map/ppermute | solution.py:489
  38.6 14.6 %collective-permute-start.2 = (bf16[128,2048]{1,0:T(8,128)(2,1)}, bf16[128,2048]{1,0:T(8,128)(2,1)S(1)}, u32[]{:S(2)}, u32[]{:S(2)}) collective-permute-start(bf16[128,2048]{1,0:T(8,128)(2,1)} %get-tuple-element.105), channel_id=1, source_target_pairs={{1,2},{2,1},{5,6},{6,5},{9,10},{10,9},{13,14},{14,13},{17,18},{18,... | collective-permute-start | bytes 1572872 | tf_op jit(solution)/shard_map/ppermute | solution.py:489
  41.4 13.2 %collective-permute-start.5 = (bf16[128,2048]{1,0:T(8,128)(2,1)}, bf16[128,2048]{1,0:T(8,128)(2,1)S(1)}, u32[]{:S(2)}, u32[]{:S(2)}) collective-permute-start(bf16[128,2048]{1,0:T(8,128)(2,1)} %collective-permute-done), channel_id=1, source_target_pairs={{0,4},{4,0},{8,12},{12,8},{1,5},{5,1},{9,13},{13,9},{2,6},{6,2},{1... | collective-permute-start | bytes 1572872 | tf_op jit(solution)/shard_map/ppermute | solution.py:442
  79.0 26.7 %collective-permute-start.15 = (bf16[2,512,768]{2,1,0:T(8,128)(2,1)S(1)}, bf16[2,512,768]{2,1,0:T(8,128)(2,1)S(1)}, u32[]{:S(2)}, u32[]{:S(2)}) collective-permute-start(bf16[2,512,768]{2,1,0:T(8,128)(2,1)S(1)} %copy-done.38), channel_id=1, source_target_pairs={{0,4},{4,0},{8,12},{12,8},{1,5},{5,1},{9,13},{13,9},{2,6},{6,2},{1... | collective-permute-start | bytes 4718600 | tf_op jit(solution)/shard_map/ppermute | solution.py:442
  80.1 25.6 %collective-permute-start.13 = (bf16[1040,512]{1,0:T(8,128)(2,1)S(1)}, bf16[1040,512]{1,0:T(8,128)(2,1)S(1)}, u32[]{:S(2)}, u32[]{:S(2)}) collective-permute-start(bf16[1040,512]{1,0:T(8,128)(2,1)S(1)} %fusion.10), channel_id=1, source_target_pairs={{0,8},{4,12},{8,0},{12,4},{1,9},{5,13},{9,1},{13,5},{2,10},{6,14},... | collective-permute-start | bytes 3194888 | tf_op jit(solution)/shard_map/ppermute | solution.py:442
  105.7 49.1 %collective-permute-start.20 = (bf16[128,2048]{1,0:T(8,128)(2,1)S(1)}, bf16[128,2048]{1,0:T(8,128)(2,1)S(1)}, u32[]{:S(2)}, u32[]{:S(2)}) collective-permute-start(bf16[128,2048]{1,0:T(8,128)(2,1)S(1)} %pad_maximum_fusion.29), channel_id=1, source_target_pairs={{0,3},{1,2},{2,1},{3,0},{4,7},{5,6},{6,5},{7,4},{8,11},{9,10},{10,... | collective-permute-start | bytes 1572872 | tf_op jit(solution)/shard_map/ppermute | solution.py:442
  106.8 47.9 %collective-permute-start.19 = (bf16[128,2048]{1,0:T(8,128)(2,1)S(1)}, bf16[128,2048]{1,0:T(8,128)(2,1)S(1)}, u32[]{:S(2)}, u32[]{:S(2)}) collective-permute-start(bf16[128,2048]{1,0:T(8,128)(2,1)S(1)} %pad_maximum_fusion.29), channel_id=1, source_target_pairs={{0,2},{1,3},{2,0},{3,1},{4,6},{5,7},{6,4},{7,5},{8,10},{9,11},{10,... | collective-permute-start | bytes 1572872 | tf_op jit(solution)/shard_map/ppermute | solution.py:442
  107.7 47.1 %collective-permute-start.18 = (bf16[128,2048]{1,0:T(8,128)(2,1)S(1)}, bf16[128,2048]{1,0:T(8,128)(2,1)S(1)}, u32[]{:S(2)}, u32[]{:S(2)}) collective-permute-start(bf16[128,2048]{1,0:T(8,128)(2,1)S(1)} %pad_maximum_fusion.29), channel_id=1, source_target_pairs={{0,1},{1,0},{2,3},{3,2},{4,5},{5,4},{6,7},{7,6},{8,9},{9,8},{10,11... | collective-permute-start | bytes 1572872 | tf_op jit(solution)/shard_map/ppermute | solution.py:442
  110.1 43.5 %collective-permute-start.17 = (bf16[1920,512]{1,0:T(8,128)(2,1)}, bf16[1920,512]{1,0:T(8,128)(2,1)}, u32[]{:S(2)}, u32[]{:S(2)}) collective-permute-start(bf16[1920,512]{1,0:T(8,128)(2,1)} %pad_maximum_fusion.8), channel_id=1, source_target_pairs={{0,8},{4,12},{8,0},{12,4},{1,9},{5,13},{9,1},{13,5},{2,10},{6,14},... | collective-permute-start | bytes 5898248 | tf_op jit(solution)/shard_map/ppermute | solution.py:442
  165.6 18.0 %collective-permute-start.27 = (bf16[256,1408]{1,0:T(8,128)(2,1)S(1)}, bf16[256,1408]{1,0:T(8,128)(2,1)S(1)}, u32[]{:S(2)}, u32[]{:S(2)}) collective-permute-start(bf16[256,1408]{1,0:T(8,128)(2,1)S(1)} %copy-done.59), channel_id=1, source_target_pairs={{0,8},{4,12},{8,0},{12,4},{1,9},{5,13},{9,1},{13,5},{2,10},{6,14},... | collective-permute-start | bytes 2162696 | tf_op jit(solution)/shard_map/ppermute | solution.py:442
  169.0 13.7 %collective-permute-start.26 = (bf16[128,2048]{1,0:T(8,128)(2,1)S(1)}, bf16[128,2048]{1,0:T(8,128)(2,1)S(1)}, u32[]{:S(2)}, u32[]{:S(2)}) collective-permute-start(bf16[128,2048]{1,0:T(8,128)(2,1)S(1)} %fusion.33), channel_id=1, source_target_pairs={{3,2},{0,1},{7,6},{4,5},{11,10},{8,9},{15,14},{12,13},{19,18},{16,... | collective-permute-start | bytes 1572872 | tf_op jit(solution)/shard_map/ppermute | solution.py:489
  171.3 12.3 %collective-permute-start.25 = (bf16[128,2048]{1,0:T(8,128)(2,1)S(1)}, bf16[128,2048]{1,0:T(8,128)(2,1)S(1)}, u32[]{:S(2)}, u32[]{:S(2)}) collective-permute-start(bf16[128,2048]{1,0:T(8,128)(2,1)S(1)} %fusion.33), channel_id=1, source_target_pairs={{1,2},{2,1},{5,6},{6,5},{9,10},{10,9},{13,14},{14,13},{17,18},{18,... | collective-permute-start | bytes 1572872 | tf_op jit(solution)/shard_map/ppermute | solution.py:489
  183.5 25.6 %collective-permute-start.28 = (bf16[128,2048]{1,0:T(8,128)(2,1)S(1)}, bf16[128,2048]{1,0:T(8,128)(2,1)S(1)}, u32[]{:S(2)}, u32[]{:S(2)}) collective-permute-start(bf16[128,2048]{1,0:T(8,128)(2,1)S(1)} %fusion.32), channel_id=1, source_target_pairs={{0,2},{1,3},{2,0},{3,1},{4,6},{5,7},{6,4},{7,5},{8,10},{9,11},{10,... | collective-permute-start | bytes 1572872 | tf_op jit(solution)/shard_map/ppermute | solution.py:442
  186.5 22.6 %collective-permute-start.29 = (bf16[128,2048]{1,0:T(8,128)(2,1)S(1)}, bf16[128,2048]{1,0:T(8,128)(2,1)S(1)}, u32[]{:S(2)}, u32[]{:S(2)}) collective-permute-start(bf16[128,2048]{1,0:T(8,128)(2,1)S(1)} %slice.1287), channel_id=1, source_target_pairs={{0,1},{1,0},{2,3},{3,2},{4,5},{5,4},{6,7},{7,6},{8,9},{9,8},{10,11... | collective-permute-start | bytes 1572872 | tf_op jit(solution)/shard_map/ppermute | solution.py:442
  186.8 23.0 %collective-permute-start.30 = (bf16[256,1408]{1,0:T(8,128)(2,1)S(1)}, bf16[256,1408]{1,0:T(8,128)(2,1)S(1)}, u32[]{:S(2)}, u32[]{:S(2)}) collective-permute-start(bf16[256,1408]{1,0:T(8,128)(2,1)S(1)} %copy-done.58), channel_id=1, source_target_pairs={{0,8},{4,12},{8,0},{12,4},{1,9},{5,13},{9,1},{13,5},{2,10},{6,14},... | collective-permute-start | bytes 2162696 | tf_op jit(solution)/shard_map/ppermute | solution.py:442
  187.4 51.0 %collective-permute-start.33 = (bf16[512,1408]{1,0:T(8,128)(2,1)S(1)}, bf16[512,1408]{1,0:T(8,128)(2,1)S(1)}, u32[]{:S(2)}, u32[]{:S(2)}) collective-permute-start(bf16[512,1408]{1,0:T(8,128)(2,1)S(1)} %copy-done.39), channel_id=1, source_target_pairs={{0,8},{4,12},{8,0},{12,4},{1,9},{5,13},{9,1},{13,5},{2,10},{6,14},... | collective-permute-start | bytes 4325384 | tf_op jit(solution)/shard_map/ppermute | solution.py:442
  209.9 26.7 %collective-permute-start.36 = (bf16[128,2048]{1,0:T(8,128)(2,1)S(1)}, bf16[128,2048]{1,0:T(8,128)(2,1)S(1)}, u32[]{:S(2)}, u32[]{:S(2)}) collective-permute-start(bf16[128,2048]{1,0:T(8,128)(2,1)S(1)} %multiply_convert_fusion.3), channel_id=1, source_target_pairs={{0,4},{4,0},{8,12},{12,8},{1,5},{5,1},{9,13},{13,9},{2,6},{6,2},{1... | collective-permute-start | bytes 1572872 | tf_op jit(solution)/shard_map/ppermute | solution.py:442
  209.9 27.7 %collective-permute-start.32 = (bf16[128,2048]{1,0:T(8,128)(2,1)S(1)}, bf16[128,2048]{1,0:T(8,128)(2,1)S(1)}, u32[]{:S(2)}, u32[]{:S(2)}) collective-permute-start(bf16[128,2048]{1,0:T(8,128)(2,1)S(1)} %multiply_convert_fusion.3), channel_id=1, source_target_pairs={{0,2},{1,3},{2,0},{3,1},{4,6},{5,7},{6,4},{7,5},{8,10},{9,11},{10,... | collective-permute-start | bytes 1572872 | tf_op jit(solution)/shard_map/ppermute | solution.py:442
  212.7 23.9 %collective-permute-start.31 = (bf16[128,2048]{1,0:T(8,128)(2,1)S(1)}, bf16[128,2048]{1,0:T(8,128)(2,1)S(1)}, u32[]{:S(2)}, u32[]{:S(2)}) collective-permute-start(bf16[128,2048]{1,0:T(8,128)(2,1)S(1)} %multiply_convert_fusion.3), channel_id=1, source_target_pairs={{0,1},{1,0},{2,3},{3,2},{4,5},{5,4},{6,7},{7,6},{8,9},{9,8},{10,11... | collective-permute-start | bytes 1572872 | tf_op jit(solution)/shard_map/ppermute | solution.py:442
  214.8 22.4 %collective-permute-start.42 = (bf16[512,768]{1,0:T(8,128)(2,1)S(1)}, bf16[512,768]{1,0:T(8,128)(2,1)S(1)}, u32[]{:S(2)}, u32[]{:S(2)}) collective-permute-start(bf16[512,768]{1,0:T(8,128)(2,1)S(1)} %get-tuple-element.299), channel_id=1, source_target_pairs={{0,4},{4,0},{8,12},{12,8},{1,5},{5,1},{9,13},{13,9},{2,6},{6,2},{1... | collective-permute-start | bytes 2359304 | tf_op jit(solution)/shard_map/ppermute | solution.py:442
  236.6 19.5 %collective-permute-start.41 = (bf16[768,512]{1,0:T(8,128)(2,1)S(1)}, bf16[768,512]{1,0:T(8,128)(2,1)S(1)}, u32[]{:S(2)}, u32[]{:S(2)}) collective-permute-start(bf16[768,512]{1,0:T(8,128)(2,1)S(1)} %get-tuple-element.305), channel_id=1, source_target_pairs={{0,4},{4,0},{8,12},{12,8},{1,5},{5,1},{9,13},{13,9},{2,6},{6,2},{1... | collective-permute-start | bytes 2359304 | tf_op jit(solution)/shard_map/ppermute | solution.py:442
  236.6 19.2 %collective-permute-start.40 = (bf16[384,2048]{1,0:T(8,128)(2,1)S(1)}, bf16[384,2048]{1,0:T(8,128)(2,1)S(1)}, u32[]{:S(2)}, u32[]{:S(2)}) collective-permute-start(bf16[384,2048]{1,0:T(8,128)(2,1)S(1)} %pad_maximum_fusion.9), channel_id=1, source_target_pairs={{0,4},{4,0},{8,12},{12,8},{1,5},{5,1},{9,13},{13,9},{2,6},{6,2},{1... | collective-permute-start | bytes 4718600 | tf_op jit(solution)/shard_map/ppermute | solution.py:442
  238.4 16.9 %collective-permute-start.35 = (bf16[128,2048]{1,0:T(8,128)(2,1)S(1)}, bf16[128,2048]{1,0:T(8,128)(2,1)S(1)}, u32[]{:S(2)}, u32[]{:S(2)}) collective-permute-start(bf16[128,2048]{1,0:T(8,128)(2,1)S(1)} %collective-permute-done.32), channel_id=1, source_target_pairs={{2,3},{1,0},{6,7},{5,4},{10,11},{9,8},{14,15},{13,12},{18,19},{17,... | collective-permute-start | bytes 1572872 | tf_op jit(solution)/shard_map/ppermute | solution.py:489
  241.9 13.8 %collective-permute-start.38 = (bf16[128,2048]{1,0:T(8,128)(2,1)S(1)}, bf16[128,2048]{1,0:T(8,128)(2,1)S(1)}, u32[]{:S(2)}, u32[]{:S(2)}) collective-permute-start(bf16[128,2048]{1,0:T(8,128)(2,1)S(1)} %collective-permute-done.32), channel_id=1, source_target_pairs={{0,4},{4,0},{8,12},{12,8},{1,5},{5,1},{9,13},{13,9},{2,6},{6,2},{1... | collective-permute-start | bytes 1572872 | tf_op jit(solution)/shard_map/ppermute | solution.py:442
  242.1 20.2 %collective-permute-start.43 = (bf16[512,768]{1,0:T(8,128)(2,1)S(1)}, bf16[512,768]{1,0:T(8,128)(2,1)S(1)}, u32[]{:S(2)}, u32[]{:S(2)}) collective-permute-start(bf16[512,768]{1,0:T(8,128)(2,1)S(1)} %get-tuple-element.301), channel_id=1, source_target_pairs={{0,4},{4,0},{8,12},{12,8},{1,5},{5,1},{9,13},{13,9},{2,6},{6,2},{1... | collective-permute-start | bytes 2359304 | tf_op jit(solution)/shard_map/ppermute | solution.py:442
  276.3 13.8 %collective-permute-start.44 = (bf16[384,2048]{1,0:T(8,128)(2,1)S(1)}, bf16[384,2048]{1,0:T(8,128)(2,1)S(1)}, u32[]{:S(2)}, u32[]{:S(2)}) collective-permute-start(bf16[384,2048]{1,0:T(8,128)(2,1)S(1)} %slice.1003), channel_id=1, source_target_pairs={{0,4},{4,0},{8,12},{12,8},{1,5},{5,1},{9,13},{13,9},{2,6},{6,2},{1... | collective-permute-start | bytes 4718600 | tf_op jit(solution)/shard_map/ppermute | solution.py:442
  285.0 16.6 %collective-permute-start.47 = (bf16[128,2048]{1,0:T(8,128)(2,1)S(1)}, bf16[128,2048]{1,0:T(8,128)(2,1)S(1)}, u32[]{:S(2)}, u32[]{:S(2)}) collective-permute-start(bf16[128,2048]{1,0:T(8,128)(2,1)S(1)} %fusion.30), channel_id=1, source_target_pairs={{1,2},{2,1},{5,6},{6,5},{9,10},{10,9},{13,14},{14,13},{17,18},{18,... | collective-permute-start | bytes 1572872 | tf_op jit(solution)/shard_map/ppermute | solution.py:489
  285.7 15.7 %collective-permute-start.46 = (bf16[128,2048]{1,0:T(8,128)(2,1)S(1)}, bf16[128,2048]{1,0:T(8,128)(2,1)S(1)}, u32[]{:S(2)}, u32[]{:S(2)}) collective-permute-start(bf16[128,2048]{1,0:T(8,128)(2,1)S(1)} %fusion.30), channel_id=1, source_target_pairs={{3,2},{0,1},{7,6},{4,5},{11,10},{8,9},{15,14},{12,13},{19,18},{16,... | collective-permute-start | bytes 1572872 | tf_op jit(solution)/shard_map/ppermute | solution.py:489
  301.6 25.4 %collective-permute-start.49 = (bf16[128,2048]{1,0:T(8,128)(2,1)S(1)}, bf16[128,2048]{1,0:T(8,128)(2,1)S(1)}, u32[]{:S(2)}, u32[]{:S(2)}) collective-permute-start(bf16[128,2048]{1,0:T(8,128)(2,1)S(1)} %get-tuple-element.137), channel_id=1, source_target_pairs={{0,2},{1,3},{2,0},{3,1},{4,6},{5,7},{6,4},{7,5},{8,10},{9,11},{10,... | collective-permute-start | bytes 1572872 | tf_op jit(solution)/shard_map/ppermute | solution.py:442
  304.8 22.2 %collective-permute-start.50 = (bf16[128,2048]{1,0:T(8,128)(2,1)S(1)}, bf16[128,2048]{1,0:T(8,128)(2,1)S(1)}, u32[]{:S(2)}, u32[]{:S(2)}) collective-permute-start(bf16[128,2048]{1,0:T(8,128)(2,1)S(1)} %slice.1286), channel_id=1, source_target_pairs={{0,1},{1,0},{2,3},{3,2},{4,5},{5,4},{6,7},{7,6},{8,9},{9,8},{10,11... | collective-permute-start | bytes 1572872 | tf_op jit(solution)/shard_map/ppermute | solution.py:442
  313.4 14.2 %collective-permute-start.51 = (bf16[1024,768]{1,0:T(8,128)(2,1)S(1)}, bf16[1024,768]{1,0:T(8,128)(2,1)S(1)}, u32[]{:S(2)}, u32[]{:S(2)}) collective-permute-start(bf16[1024,768]{1,0:T(8,128)(2,1)S(1)} %pad_maximum_fusion.13), channel_id=1, source_target_pairs={{0,4},{4,0},{8,12},{12,8},{1,5},{5,1},{9,13},{13,9},{2,6},{6,2},{1... | collective-permute-start | bytes 4718600 | tf_op jit(solution)/shard_map/ppermute | solution.py:442
  330.7 29.7 %collective-permute-start.57 = (bf16[128,2048]{1,0:T(8,128)(2,1)S(1)}, bf16[128,2048]{1,0:T(8,128)(2,1)S(1)}, u32[]{:S(2)}, u32[]{:S(2)}) collective-permute-start(bf16[128,2048]{1,0:T(8,128)(2,1)S(1)} %get-tuple-element.145), channel_id=1, source_target_pairs={{0,4},{4,0},{8,12},{12,8},{1,5},{5,1},{9,13},{13,9},{2,6},{6,2},{1... | collective-permute-start | bytes 1572872 | tf_op jit(solution)/shard_map/ppermute | solution.py:442
  330.7 25.0 %collective-permute-start.54 = (bf16[128,2048]{1,0:T(8,128)(2,1)S(1)}, bf16[128,2048]{1,0:T(8,128)(2,1)S(1)}, u32[]{:S(2)}, u32[]{:S(2)}) collective-permute-start(bf16[128,2048]{1,0:T(8,128)(2,1)S(1)} %get-tuple-element.145), channel_id=1, source_target_pairs={{0,1},{1,0},{2,3},{3,2},{4,5},{5,4},{6,7},{7,6},{8,9},{9,8},{10,11... | collective-permute-start | bytes 1572872 | tf_op jit(solution)/shard_map/ppermute | solution.py:442
  332.5 26.2 %collective-permute-start.52 = (bf16[128,2048]{1,0:T(8,128)(2,1)S(1)}, bf16[128,2048]{1,0:T(8,128)(2,1)S(1)}, u32[]{:S(2)}, u32[]{:S(2)}) collective-permute-start(bf16[128,2048]{1,0:T(8,128)(2,1)S(1)} %get-tuple-element.145), channel_id=1, source_target_pairs={{0,2},{1,3},{2,0},{3,1},{4,6},{5,7},{6,4},{7,5},{8,10},{9,11},{10,... | collective-permute-start | bytes 1572872 | tf_op jit(solution)/shard_map/ppermute | solution.py:442
  333.3 39.5 %collective-permute-start.61 = (bf16[1408,512]{1,0:T(8,128)(2,1)S(1)}, bf16[1408,512]{1,0:T(8,128)(2,1)S(1)}, u32[]{:S(2)}, u32[]{:S(2)}) collective-permute-start(bf16[1408,512]{1,0:T(8,128)(2,1)S(1)} %fusion.5), channel_id=1, source_target_pairs={{0,8},{4,12},{8,0},{12,4},{1,9},{5,13},{9,1},{13,5},{2,10},{6,14},... | collective-permute-start | bytes 4325384 | tf_op jit(solution)/shard_map/ppermute | solution.py:442
  358.7 13.1 %collective-permute-start.56 = (bf16[128,2048]{1,0:T(8,128)(2,1)S(1)}, bf16[128,2048]{1,0:T(8,128)(2,1)S(1)}, u32[]{:S(2)}, u32[]{:S(2)}) collective-permute-start(bf16[128,2048]{1,0:T(8,128)(2,1)S(1)} %collective-permute-done.52), channel_id=1, source_target_pairs={{2,3},{1,0},{6,7},{5,4},{10,11},{9,8},{14,15},{13,12},{18,19},{17,... | collective-permute-start | bytes 1572872 | tf_op jit(solution)/shard_map/ppermute | solution.py:489
  360.4 16.4 %collective-permute-start.68 = (bf16[1024,768]{1,0:T(8,128)(2,1)S(1)}, bf16[1024,768]{1,0:T(8,128)(2,1)S(1)}, u32[]{:S(2)}, u32[]{:S(2)}) collective-permute-start(bf16[1024,768]{1,0:T(8,128)(2,1)S(1)} %pad_maximum_fusion.15), channel_id=1, source_target_pairs={{0,4},{4,0},{8,12},{12,8},{1,5},{5,1},{9,13},{13,9},{2,6},{6,2},{1... | collective-permute-start | bytes 4718600 | tf_op jit(solution)/shard_map/ppermute | solution.py:442
  362.4 42.7 %collective-permute-start.65 = (bf16[512,1408]{1,0:T(8,128)(2,1)S(1)}, bf16[512,1408]{1,0:T(8,128)(2,1)S(1)}, u32[]{:S(2)}, u32[]{:S(2)}) collective-permute-start(bf16[512,1408]{1,0:T(8,128)(2,1)S(1)} %fusion.6), channel_id=1, source_target_pairs={{0,8},{4,12},{8,0},{12,4},{1,9},{5,13},{9,1},{13,5},{2,10},{6,14},... | collective-permute-start | bytes 4325384 | tf_op jit(solution)/shard_map/ppermute | solution.py:442
  373.4 33.6 %collective-permute-start.66 = (bf16[1408,512]{1,0:T(8,128)(2,1)S(1)}, bf16[1408,512]{1,0:T(8,128)(2,1)S(1)}, u32[]{:S(2)}, u32[]{:S(2)}) collective-permute-start(bf16[1408,512]{1,0:T(8,128)(2,1)S(1)} %add_convert_fusion.4), channel_id=1, source_target_pairs={{0,16},{16,0},{1,17},{17,1},{2,18},{18,2},{3,19},{19,3},{4,20},{20... | collective-permute-start | bytes 4325384 | tf_op jit(solution)/shard_map/ppermute | solution.py:442
  388.7 14.5 %collective-permute-start.67 = (bf16[1024,128]{1,0:T(8,128)(2,1)S(1)}, bf16[1024,128]{1,0:T(8,128)(2,1)S(1)}, u32[]{:S(2)}, u32[]{:S(2)}) collective-permute-start(bf16[1024,128]{1,0:T(8,128)(2,1)S(1)} %get-tuple-element.326), channel_id=1, source_target_pairs={{0,8},{4,12},{8,0},{12,4},{1,9},{5,13},{9,1},{13,5},{2,10},{6,14},... | collective-permute-start | bytes 786440 | tf_op jit(solution)/shard_map/ppermute | solution.py:442
  389.3 48.7 %collective-permute-start.62 = (bf16[128,2048]{1,0:T(8,128)(2,1)}, bf16[128,2048]{1,0:T(8,128)(2,1)}, u32[]{:S(2)}, u32[]{:S(2)}) collective-permute-start(bf16[128,2048]{1,0:T(8,128)(2,1)} %get-tuple-element.147), channel_id=1, source_target_pairs={{0,1},{1,0},{2,3},{3,2},{4,5},{5,4},{6,7},{7,6},{8,9},{9,8},{10,11... | collective-permute-start | bytes 1572872 | tf_op jit(solution)/shard_map/ppermute | solution.py:442
  389.6 48.4 %collective-permute-start.63 = (bf16[128,2048]{1,0:T(8,128)(2,1)}, bf16[128,2048]{1,0:T(8,128)(2,1)}, u32[]{:S(2)}, u32[]{:S(2)}) collective-permute-start(bf16[128,2048]{1,0:T(8,128)(2,1)} %get-tuple-element.148), channel_id=1, source_target_pairs={{0,2},{1,3},{2,0},{3,1},{4,6},{5,7},{6,4},{7,5},{8,10},{9,11},{10,... | collective-permute-start | bytes 1572872 | tf_op jit(solution)/shard_map/ppermute | solution.py:442
  403.3 34.7 %collective-permute-start.64 = (bf16[128,2048]{1,0:T(8,128)(2,1)}, bf16[128,2048]{1,0:T(8,128)(2,1)}, u32[]{:S(2)}, u32[]{:S(2)}) collective-permute-start(bf16[128,2048]{1,0:T(8,128)(2,1)} %get-tuple-element.149), channel_id=1, source_target_pairs={{0,3},{1,2},{2,1},{3,0},{4,7},{5,6},{6,5},{7,4},{8,11},{9,10},{10,... | collective-permute-start | bytes 1572872 | tf_op jit(solution)/shard_map/ppermute | solution.py:442
  405.1 35.8 %collective-permute-start.69 = (bf16[512,1408]{1,0:T(8,128)(2,1)}, bf16[512,1408]{1,0:T(8,128)(2,1)}, u32[]{:S(2)}, u32[]{:S(2)}) collective-permute-start(bf16[512,1408]{1,0:T(8,128)(2,1)} %fusion.7), channel_id=1, source_target_pairs={{0,8},{4,12},{8,0},{12,4},{1,9},{5,13},{9,1},{13,5},{2,10},{6,14},... | collective-permute-start | bytes 4325384 | tf_op jit(solution)/shard_map/ppermute | solution.py:442
  408.5 33.1 %collective-permute-start.70 = (bf16[512,1408]{1,0:T(8,128)(2,1)}, bf16[512,1408]{1,0:T(8,128)(2,1)}, u32[]{:S(2)}, u32[]{:S(2)}) collective-permute-start(bf16[512,1408]{1,0:T(8,128)(2,1)} %add_convert_fusion.3), channel_id=1, source_target_pairs={{0,16},{16,0},{1,17},{17,1},{2,18},{18,2},{3,19},{19,3},{4,20},{20... | collective-permute-start | bytes 4325384 | tf_op jit(solution)/shard_map/ppermute | solution.py:442
  442.8 26.4 %collective-permute-start.71 = (bf16[1040,512]{1,0:T(8,128)(2,1)S(1)}, bf16[1040,512]{1,0:T(8,128)(2,1)S(1)}, u32[]{:S(2)}, u32[]{:S(2)}) collective-permute-start(bf16[1040,512]{1,0:T(8,128)(2,1)S(1)} %fusion.11), channel_id=1, source_target_pairs={{0,8},{4,12},{8,0},{12,4},{1,9},{5,13},{9,1},{13,5},{2,10},{6,14},... | collective-permute-start | bytes 3194888 | tf_op jit(solution)/shard_map/ppermute | solution.py:442
  445.8 68.3 %collective-permute-start.78 = (bf16[512,1408]{1,0:T(8,128)(2,1)S(1)}, bf16[512,1408]{1,0:T(8,128)(2,1)S(1)}, u32[]{:S(2)}, u32[]{:S(2)}) collective-permute-start(bf16[512,1408]{1,0:T(8,128)(2,1)S(1)} %add_convert_fusion.2), channel_id=1, source_target_pairs={{0,16},{16,0},{1,17},{17,1},{2,18},{18,2},{3,19},{19,3},{4,20},{20... | collective-permute-start | bytes 4325384 | tf_op jit(solution)/shard_map/ppermute | solution.py:442
  447.3 33.2 %collective-permute-start.79 = (bf16[256,1024]{1,0:T(8,128)(2,1)S(1)}, bf16[256,1024]{1,0:T(8,128)(2,1)S(1)}, u32[]{:S(2)}, u32[]{:S(2)}) collective-permute-start(bf16[256,1024]{1,0:T(8,128)(2,1)S(1)} %slice.1284), channel_id=1, source_target_pairs={{0,8},{4,12},{8,0},{12,4},{1,9},{5,13},{9,1},{13,5},{2,10},{6,14},... | collective-permute-start | bytes 1572872 | tf_op jit(solution)/shard_map/ppermute | solution.py:442
  451.2 54.1 %collective-permute-start.73 = (bf16[1024,512]{0,1:T(8,128)(2,1)S(1)}, bf16[1024,512]{0,1:T(8,128)(2,1)S(1)}, u32[]{:S(2)}, u32[]{:S(2)}) collective-permute-start(bf16[1024,512]{0,1:T(8,128)(2,1)S(1)} %slice.1283), channel_id=1, source_target_pairs={{0,8},{4,12},{8,0},{12,4},{1,9},{5,13},{9,1},{13,5},{2,10},{6,14},... | collective-permute-start | bytes 3145736 | tf_op jit(solution)/shard_map/ppermute | solution.py:442
  484.1 21.1 %collective-permute-start.76 = (bf16[128,2048]{1,0:T(8,128)(2,1)S(1)}, bf16[128,2048]{1,0:T(8,128)(2,1)S(1)}, u32[]{:S(2)}, u32[]{:S(2)}) collective-permute-start(bf16[128,2048]{1,0:T(8,128)(2,1)S(1)} %fusion.23), channel_id=1, source_target_pairs={{1,2},{2,1},{5,6},{6,5},{9,10},{10,9},{13,14},{14,13},{17,18},{18,... | collective-permute-start | bytes 1572872 | tf_op jit(solution)/shard_map/ppermute | solution.py:489
  484.8 18.2 %collective-permute-start.75 = (bf16[128,2048]{1,0:T(8,128)(2,1)S(1)}, bf16[128,2048]{1,0:T(8,128)(2,1)S(1)}, u32[]{:S(2)}, u32[]{:S(2)}) collective-permute-start(bf16[128,2048]{1,0:T(8,128)(2,1)S(1)} %fusion.23), channel_id=1, source_target_pairs={{3,2},{0,1},{7,6},{4,5},{11,10},{8,9},{15,14},{12,13},{19,18},{16,... | collective-permute-start | bytes 1572872 | tf_op jit(solution)/shard_map/ppermute | solution.py:489
  505.9 14.4 %collective-permute-start.81 = (bf16[512,512]{1,0:T(8,128)(2,1)S(1)}, bf16[512,512]{1,0:T(8,128)(2,1)S(1)}, u32[]{:S(2)}, u32[]{:S(2)}) collective-permute-start(bf16[512,512]{1,0:T(8,128)(2,1)S(1)} %pad_maximum_fusion.31), channel_id=1, source_target_pairs={{0,16},{16,0},{1,17},{17,1},{2,18},{18,2},{3,19},{19,3},{4,20},{20... | collective-permute-start | bytes 1572872 | tf_op jit(solution)/shard_map/ppermute | solution.py:442
  508.8 31.0 %collective-permute-start.82 = (bf16[128,2048]{1,0:T(8,128)(2,1)}, bf16[128,2048]{1,0:T(8,128)(2,1)}, u32[]{:S(2)}, u32[]{:S(2)}) collective-permute-start(bf16[128,2048]{1,0:T(8,128)(2,1)} %get-tuple-element.171), channel_id=1, source_target_pairs={{0,2},{1,3},{2,0},{3,1},{4,6},{5,7},{6,4},{7,5},{8,10},{9,11},{10,... | collective-permute-start | bytes 1572872 | tf_op jit(solution)/shard_map/ppermute | solution.py:442
  511.4 28.4 %collective-permute-start.83 = (bf16[128,2048]{1,0:T(8,128)(2,1)}, bf16[128,2048]{1,0:T(8,128)(2,1)}, u32[]{:S(2)}, u32[]{:S(2)}) collective-permute-start(bf16[128,2048]{1,0:T(8,128)(2,1)} %slice.1285), channel_id=1, source_target_pairs={{0,1},{1,0},{2,3},{3,2},{4,5},{5,4},{6,7},{7,6},{8,9},{9,8},{10,11... | collective-permute-start | bytes 1572872 | tf_op jit(solution)/shard_map/ppermute | solution.py:442
  511.5 30.1 %collective-permute-start.85 = (bf16[1024,512]{0,1:T(8,128)(2,1)}, bf16[1024,512]{0,1:T(8,128)(2,1)}, u32[]{:S(2)}, u32[]{:S(2)}) collective-permute-start(bf16[1024,512]{0,1:T(8,128)(2,1)} %slice.1282), channel_id=1, source_target_pairs={{0,8},{4,12},{8,0},{12,4},{1,9},{5,13},{9,1},{13,5},{2,10},{6,14},... | collective-permute-start | bytes 3145736 | tf_op jit(solution)/shard_map/ppermute | solution.py:442
  520.3 27.3 %collective-permute-start.84 = (bf16[512,1024]{0,1:T(8,128)(2,1)}, bf16[512,1024]{0,1:T(8,128)(2,1)}, u32[]{:S(2)}, u32[]{:S(2)}) collective-permute-start(bf16[512,1024]{0,1:T(8,128)(2,1)} %pad_maximum_fusion.21), channel_id=1, source_target_pairs={{0,16},{16,0},{1,17},{17,1},{2,18},{18,2},{3,19},{19,3},{4,20},{20... | collective-permute-start | bytes 3145736 | tf_op jit(solution)/shard_map/ppermute | solution.py:442
  549.7 29.9 %collective-permute-start.94 = (bf16[512,1024]{0,1:T(8,128)(2,1)}, bf16[512,1024]{0,1:T(8,128)(2,1)}, u32[]{:S(2)}, u32[]{:S(2)}) collective-permute-start(bf16[512,1024]{0,1:T(8,128)(2,1)} %pad_maximum_fusion.24), channel_id=1, source_target_pairs={{0,16},{16,0},{1,17},{17,1},{2,18},{18,2},{3,19},{19,3},{4,20},{20... | collective-permute-start | bytes 3145736 | tf_op jit(solution)/shard_map/ppermute | solution.py:442
  559.4 16.7 %collective-permute-start.97 = (f32[28,128]{1,0:T(8,128)S(1)}, f32[28,128]{1,0:T(8,128)S(1)}, u32[]{:S(2)}, u32[]{:S(2)}) collective-permute-start(f32[28,128]{1,0:T(8,128)S(1)} %constant_dynamic-update-slice_fusion.20), channel_id=1, source_target_pairs={{0,16},{16,0},{1,17},{17,1},{2,18},{18,2},{3,19},{19,3},{4,20},{20... | collective-permute-start | bytes 43016 | tf_op jit(solution)/shard_map/ppermute | solution.py:442
  562.6 14.7 %collective-permute-start.93 = (f32[34,128]{1,0:T(8,128)S(1)}, f32[34,128]{1,0:T(8,128)S(1)}, u32[]{:S(2)}, u32[]{:S(2)}) collective-permute-start(f32[34,128]{1,0:T(8,128)S(1)} %add_add_fusion), channel_id=1, source_target_pairs={{0,16},{16,0},{1,17},{17,1},{2,18},{18,2},{3,19},{19,3},{4,20},{20... | collective-permute-start | bytes 52232 | tf_op jit(solution)/shard_map/ppermute | solution.py:442
  (136 other events, 1434.3 us)

commit v6 on v5

--- a/solution.py
+++ b/solution.py
@@ -348,7 +348,7 @@
     return pl.BlockSpec(shape, lambda i, *_: (0,) * len(shape))
 
 
-def head_forward(near, far, logit, taps, gain, starts, info, rows=256):
+def head_forward(near, far, logit, taps, gain, starts, info, rows=512):
     total = 2 * near.shape[0]
     steps = total // rows
     count = rows // PAIR
@@ -401,7 +401,7 @@
     return outs[0], outs[1][0, 0], tuple(outs[2:])
 
 
-def head_backward(grad_near, grad_far, near, far, logit, taps, gain, starts, info, kept, rows=256):
+def head_backward(grad_near, grad_far, near, far, logit, taps, gain, starts, info, kept, rows=512):
     total = 2 * near.shape[0]
     steps = total // rows
     count = rows // PAIR

time: 593 us -> 593 us (level)
  transfers between devices with their start and end apart: 98 -> 98, of which waited for: 31 -> 30; matrix products, arithmetic and copies ran while one was open for 27% -> 27% of each run, Pallas kernels for 11% -> 11%
where the time goes in v6:
time: 593 us; the launch traced here: 589 us
  waiting for transfers between devices  221 us (37%)
  starting transfers between devices  90.9 us (15%)
  local copies, waits for them, and re-layouts  69.1 us (12%)
  matrix products  68.5 us (12%)
  other arithmetic  68.3 us (12%)
  Pallas kernels  64.5 us (11%)
  between operations  6.17 us (1%)
    ppermute x86, waiting for transfers between devices, other(): return lax.ppermute(value, axis, [(i, i ^ bit) for i in range(size)])  160 us
    ppermute x86, starting transfers between devices, other(): return lax.ppermute(value, axis, [(i, i ^ bit) for i in range(size)])  69.4 us
    dot_general x28, matrix products, matmul(): return lax.dot_general(a, b, (dims, ((), ())), preferred_element_type=f32)  68.5 us
    ppermute x12, waiting for transfers between devices, along_tensor(): return lax.ppermute(value, 'tensor', pairs)  61.1 us
    pallas_call x1, Pallas kernels, head_forward(): pl.pallas_call(forward_body, grid_spec=pltpu.PrefetchScalarGridSpec(num_s...  39.2 us
    pallas_call x1, Pallas kernels, head_backward(): pl.pallas_call(backward_body, grid_spec=pltpu.PrefetchScalarGridSpec(num_...  25.3 us
    ppermute x12, starting transfers between devices, along_tensor(): return lax.ppermute(value, 'tensor', pairs)  21.5 us
    unnamed x224, local copies, waits for them, and re-layouts  20.3 us
  transfers between devices with their start and end apart: 98, of which 30 were waited for; matrix products, arithmetic and copies ran while one was open for 27% of the time, Pallas kernels for 11%

profile of v6, /device:TPU:0, one launch (start us, length us, event | category | flops | bytes accessed | tf_op | source)
XLA Modules:
  0.0 588.5 jit_solution(14821359809105621191)
XLA Ops:
  6.2 4.1 collective-permute-start.1
  13.3 4.1 copy.29
  19.2 2.3 fusion.98
  24.3 2.9 constant_dynamic-slice_fusion.58
  29.3 2.8 constant_dynamic-slice_fusion.34
  44.5 8.6 %collective-permute-done.3 = bf16[128,2048]{1,0:T(8,128)(2,1)S(1)} collective-permute-done((bf16[128,2048]{1,0:T(8,128)(2,1)}, bf16[128,2048]{1,0:T(8,128)(2,1)S(1)}, u32[]{:S(2)}, u32[]{:S(2)}) %collective-permute-start.3) | collective-permute-done | bytes 524320 | tf_op jit(solution)/shard_map/ppermute | solution.py:489
  58.7 6.8 %collective-permute-done.9 = bf16[4,512,512]{1,2,0:T(8,128)(2,1)} collective-permute-done((bf16[4,512,512]{1,2,0:T(8,128)(2,1)}, bf16[4,512,512]{1,2,0:T(8,128)(2,1)}, u32[]{:S(2)}, u32[]{:S(2)}) %collective-permute-start.9) | collective-permute-done | bytes 2097184 | tf_op jit(solution)/shard_map/ppermute | solution.py:442
  66.2 2.5 constant_dynamic-slice_fusion.54
  82.9 2.3 add_convert_fusion.5.near_ref.before_near_ref
  86.0 19.6 %collective-permute-done.13.far_ref.before_far_ref = bf16[1040,512]{1,0:T(8,128)(2,1)S(1)} collective-permute-done((bf16[1040,512]{1,0:T(8,128)(2,1)S(1)}, bf16[1040,512]{1,0:T(8,128)(2,1)S(1)}, u32[]{:S(2)}, u32[]{:S(2)}) %collective-permute-start.13) | collective-permute-done | bytes 1064992 | tf_op jit(solution)/shard_map/ppermute | solution.py:442
  107.7 2.5 collective-permute-start.18
  111.3 39.2 %head_forward.1 = (bf16[2048,128]{1,0:T(8,128)(2,1)}, f32[8,128]{1,0:T(8,128)}, f32[3,2048,128]{2,1,0:T(8,128)}, f32[2048,256]{1,0:T(8,128)}, bf16[2048,128]{1,0...) custom-call(s32[8]{0:T(128)} %bitcast.140, ...), custom_call_target="tpu_custom_call" | custom-call | flops 40960000000 | bytes 20480000 | tf_op jit(solution)/shard_map/head_forward/pallas_call | solution.py:365
  150.5 3.1 collective-permute-done.17
  156.9 6.8 %collective-permute-done.21 = bf16[1024,128]{1,0:T(8,128)(2,1)S(1)} collective-permute-done((bf16[1024,128]{1,0:T(8,128)(2,1)S(1)}, bf16[1024,128]{1,0:T(8,128)(2,1)S(1)}, u32[]{:S(2)}, u32[]{:S(2)}) %collective-permute-start.21) | collective-permute-done | bytes 262176 | tf_op jit(solution)/shard_map/ppermute | solution.py:442
  166.8 2.0 collective-permute-done.24
  169.0 2.3 collective-permute-start.26
  172.8 9.9 %collective-permute-done.26 = bf16[128,2048]{1,0:T(8,128)(2,1)S(1)} collective-permute-done((bf16[128,2048]{1,0:T(8,128)(2,1)S(1)}, bf16[128,2048]{1,0:T(8,128)(2,1)S(1)}, u32[]{:S(2)}, u32[]{:S(2)}) %collective-permute-start.26) | collective-permute-done | bytes 524320 | tf_op jit(solution)/shard_map/ppermute | solution.py:489
  183.5 3.0 collective-permute-start.28
  188.9 20.2 %collective-permute-done.28 = bf16[128,2048]{1,0:T(8,128)(2,1)S(1)} collective-permute-done((bf16[128,2048]{1,0:T(8,128)(2,1)S(1)}, bf16[128,2048]{1,0:T(8,128)(2,1)S(1)}, u32[]{:S(2)}, u32[]{:S(2)}) %collective-permute-start.28) | collective-permute-done | bytes 524320 | tf_op jit(solution)/shard_map/ppermute | solution.py:442
  209.9 2.7 collective-permute-start.32
  215.6 21.0 %collective-permute-done.31 = bf16[128,2048]{1,0:T(8,128)(2,1)S(1)} collective-permute-done((bf16[128,2048]{1,0:T(8,128)(2,1)S(1)}, bf16[128,2048]{1,0:T(8,128)(2,1)S(1)}, u32[]{:S(2)}, u32[]{:S(2)}) %collective-permute-start.31) | collective-permute-done | bytes 524320 | tf_op jit(solution)/shard_map/ppermute | solution.py:442
  239.8 2.0 collective-permute-done.37
  242.5 12.8 %collective-permute-done.35 = bf16[128,2048]{1,0:T(8,128)(2,1)S(1)} collective-permute-done((bf16[128,2048]{1,0:T(8,128)(2,1)S(1)}, bf16[128,2048]{1,0:T(8,128)(2,1)S(1)}, u32[]{:S(2)}, u32[]{:S(2)}) %collective-permute-start.35) | collective-permute-done | bytes 524320 | tf_op jit(solution)/shard_map/ppermute | solution.py:489
  257.1 5.1 fusion.90
  262.9 3.4 fusion.141
  266.3 5.8 multiply_convert_fusion
  276.6 3.8 fusion.47
  280.6 4.0 convolution_add_fusion
  285.5 4.4 collective-permute-start.46
  290.7 10.4 %collective-permute-done.46 = bf16[128,2048]{1,0:T(8,128)(2,1)S(1)} collective-permute-done((bf16[128,2048]{1,0:T(8,128)(2,1)S(1)}, bf16[128,2048]{1,0:T(8,128)(2,1)S(1)}, u32[]{:S(2)}, u32[]{:S(2)}) %collective-permute-start.46) | collective-permute-done | bytes 524320 | tf_op jit(solution)/shard_map/ppermute | solution.py:489
  301.3 3.2 collective-permute-start.49
  304.5 3.9 convolution_convert_fusion.2
  309.0 3.9 convolution_convert_fusion.1
  313.7 2.7 convolution_convert_fusion.4
  317.4 9.3 %collective-permute-done.49 = bf16[128,2048]{1,0:T(8,128)(2,1)S(1)} collective-permute-done((bf16[128,2048]{1,0:T(8,128)(2,1)S(1)}, bf16[128,2048]{1,0:T(8,128)(2,1)S(1)}, u32[]{:S(2)}, u32[]{:S(2)}) %collective-permute-start.49) | collective-permute-done | bytes 524320 | tf_op jit(solution)/shard_map/ppermute | solution.py:442
  333.5 3.9 convolution_convert_fusion
  337.8 17.7 %collective-permute-done.54 = bf16[128,2048]{1,0:T(8,128)(2,1)S(1)} collective-permute-done((bf16[128,2048]{1,0:T(8,128)(2,1)S(1)}, bf16[128,2048]{1,0:T(8,128)(2,1)S(1)}, u32[]{:S(2)}, u32[]{:S(2)}) %collective-permute-start.54) | collective-permute-done | bytes 524320 | tf_op jit(solution)/shard_map/ppermute | solution.py:442
  356.1 2.3 collective-permute-done.52
  362.9 8.6 %collective-permute-done.56 = bf16[128,2048]{1,0:T(8,128)(2,1)S(1)} collective-permute-done((bf16[128,2048]{1,0:T(8,128)(2,1)S(1)}, bf16[128,2048]{1,0:T(8,128)(2,1)S(1)}, u32[]{:S(2)}, u32[]{:S(2)}) %collective-permute-start.56) | collective-permute-done | bytes 524320 | tf_op jit(solution)/shard_map/ppermute | solution.py:489
  380.1 5.1 fusion.137
  389.3 4.2 collective-permute-start.63
  394.9 8.1 %collective-permute-done.67.grad_far_ref = bf16[1024,128]{1,0:T(8,128)(2,1)S(1)} collective-permute-done((bf16[1024,128]{1,0:T(8,128)(2,1)S(1)}, bf16[1024,128]{1,0:T(8,128)(2,1)S(1)}, u32[]{:S(2)}, u32[]{:S(2)}) %collective-permute-start.67) | collective-permute-done | bytes 262176 | tf_op jit(solution)/shard_map/ppermute | solution.py:442
  409.8 25.3 %head_backward.1 = (bf16[2048,512]{1,0:T(8,128)(2,1)}, f32[16,128]{1,0:T(8,128)}, f32[3,4,128]{2,1,0:T(4,128)}, f32[8,128]{1,0:T(8,128)}) custom-call(s32[8]{0:T(128)} %bitcast.141, s32[2]{0:T(128)} %pad_add_fusion.3.info_ref, bf16[1024,512]{1,0:T(8,128)(2,1)} %add_convert_fusion.5.near_ref.before_near_ref, bf16[1040,512]{1,0:T(8,128)(2,1)} %copy-done.95, ...), custom_call_target="tpu_custom_call" | custom-call | flops 24576000000 | bytes 20480000 | tf_op jit(solution)/shard_map/head_backward/pallas_call | solution.py:413
  436.5 2.9 fusion.29
  443.2 2.2 add_convert_fusion.2
  448.2 2.5 fusion.142
  451.8 17.2 %collective-permute-done.71 = bf16[1040,512]{1,0:T(8,128)(2,1)S(1)} collective-permute-done((bf16[1040,512]{1,0:T(8,128)(2,1)S(1)}, bf16[1040,512]{1,0:T(8,128)(2,1)S(1)}, u32[]{:S(2)}, u32[]{:S(2)}) %collective-permute-start.71) | collective-permute-done | bytes 1064992 | tf_op jit(solution)/shard_map/ppermute | solution.py:442
  472.0 2.3 add_convert_fusion
  474.6 2.4 convolution_add_fusion.1
  476.9 3.3 collective-permute-done.79
  481.2 2.5 fusion.42
  484.6 6.2 %collective-permute-start.75 = (bf16[128,2048]{1,0:T(8,128)(2,1)S(1)}, bf16[128,2048]{1,0:T(8,128)(2,1)S(1)}, u32[]{:S(2)}, u32[]{:S(2)}) collective-permute-start(bf16[128,2048]{1,0:T(8,128)(2,1)S(1)} %fusion.23), channel_id=1, source_target_pairs={{3,2},{0,1},{7,6},{4,5},{11,10},{8,9},{15,14},{12,13},{19,18},{16,... | collective-permute-start | bytes 1572872 | tf_op jit(solution)/shard_map/ppermute | solution.py:489
  491.3 10.7 %collective-permute-done.75 = bf16[128,2048]{1,0:T(8,128)(2,1)S(1)} collective-permute-done((bf16[128,2048]{1,0:T(8,128)(2,1)S(1)}, bf16[128,2048]{1,0:T(8,128)(2,1)S(1)}, u32[]{:S(2)}, u32[]{:S(2)}) %collective-permute-start.75) | collective-permute-done | bytes 524320 | tf_op jit(solution)/shard_map/ppermute | solution.py:489
  508.4 2.7 collective-permute-start.82
  513.7 5.5 collective-permute-done.81
  525.9 2.0 convert_add_fusion.1
  527.9 3.7 add_bitcast_fusion.1
  532.2 2.2 pad_maximum_fusion.22
  534.5 4.9 pad_maximum_fusion
  555.3 2.4 collective-permute-start.91
  564.6 2.6 copy.36
  567.2 2.5 copy.37
  569.7 5.9 collective-permute-done.97
  584.9 2.3 pad_maximum_fusion.2
  (597 shorter events, 174.7 us)
Async XLA Ops:
  6.2 31.1 %collective-permute-start.1 = (bf16[128,2048]{1,0:T(8,128)(2,1)}, bf16[128,2048]{1,0:T(8,128)(2,1)}, u32[]{:S(2)}, u32[]{:S(2)}) collective-permute-start(bf16[128,2048]{1,0:T(8,128)(2,1)} %get-tuple-element.105), channel_id=1, source_target_pairs={{0,2},{1,3},{2,0},{3,1},{4,6},{5,7},{6,4},{7,5},{8,10},{9,11},{10,... | collective-permute-start | bytes 1572872 | tf_op jit(solution)/shard_map/ppermute | solution.py:442
  10.3 28.3 %collective-permute-start = (bf16[128,2048]{1,0:T(8,128)(2,1)}, bf16[128,2048]{1,0:T(8,128)(2,1)}, u32[]{:S(2)}, u32[]{:S(2)}) collective-permute-start(bf16[128,2048]{1,0:T(8,128)(2,1)} %get-tuple-element.105), channel_id=1, source_target_pairs={{0,1},{1,0},{2,3},{3,2},{4,5},{5,4},{6,7},{7,6},{8,9},{9,8},{10,11... | collective-permute-start | bytes 1572872 | tf_op jit(solution)/shard_map/ppermute | solution.py:442
  11.8 29.5 %collective-permute-start.4 = (bf16[128,2048]{1,0:T(8,128)(2,1)}, bf16[128,2048]{1,0:T(8,128)(2,1)}, u32[]{:S(2)}, u32[]{:S(2)}) collective-permute-start(bf16[128,2048]{1,0:T(8,128)(2,1)} %get-tuple-element.105), channel_id=1, source_target_pairs={{0,4},{4,0},{8,12},{12,8},{1,5},{5,1},{9,13},{13,9},{2,6},{6,2},{1... | collective-permute-start | bytes 1572872 | tf_op jit(solution)/shard_map/ppermute | solution.py:442
  11.8 46.9 %collective-permute-start.11 = (bf16[4,512]{1,0:T(4,128)(2,1)}, bf16[4,512]{1,0:T(4,128)(2,1)}, u32[]{:S(2)}, u32[]{:S(2)}) collective-permute-start(bf16[4,512]{1,0:T(4,128)(2,1)} %bitcast.18), channel_id=1, source_target_pairs={{0,8},{4,12},{8,0},{12,4},{1,9},{5,13},{9,1},{13,5},{2,10},{6,14},... | collective-permute-start | bytes 12296 | tf_op jit(solution)/shard_map/ppermute | solution.py:442
  17.5 48.1 %collective-permute-start.9 = (bf16[4,512,512]{1,2,0:T(8,128)(2,1)}, bf16[4,512,512]{1,2,0:T(8,128)(2,1)}, u32[]{:S(2)}, u32[]{:S(2)}) collective-permute-start(bf16[4,512,512]{1,2,0:T(8,128)(2,1)} %copy.29), channel_id=1, source_target_pairs={{0,8},{4,12},{8,0},{12,4},{1,9},{5,13},{9,1},{13,5},{2,10},{6,14},... | collective-permute-start | bytes 6291464 | tf_op jit(solution)/shard_map/ppermute | solution.py:442
  37.3 15.9 %collective-permute-start.3 = (bf16[128,2048]{1,0:T(8,128)(2,1)}, bf16[128,2048]{1,0:T(8,128)(2,1)S(1)}, u32[]{:S(2)}, u32[]{:S(2)}) collective-permute-start(bf16[128,2048]{1,0:T(8,128)(2,1)} %collective-permute-done.1), channel_id=1, source_target_pairs={{2,3},{1,0},{6,7},{5,4},{10,11},{9,8},{14,15},{13,12},{18,19},{17,... | collective-permute-start | bytes 1572872 | tf_op jit(solution)/shard_map/ppermute | solution.py:489
  38.6 14.6 %collective-permute-start.2 = (bf16[128,2048]{1,0:T(8,128)(2,1)}, bf16[128,2048]{1,0:T(8,128)(2,1)S(1)}, u32[]{:S(2)}, u32[]{:S(2)}) collective-permute-start(bf16[128,2048]{1,0:T(8,128)(2,1)} %get-tuple-element.105), channel_id=1, source_target_pairs={{1,2},{2,1},{5,6},{6,5},{9,10},{10,9},{13,14},{14,13},{17,18},{18,... | collective-permute-start | bytes 1572872 | tf_op jit(solution)/shard_map/ppermute | solution.py:489
  41.4 13.2 %collective-permute-start.5 = (bf16[128,2048]{1,0:T(8,128)(2,1)}, bf16[128,2048]{1,0:T(8,128)(2,1)S(1)}, u32[]{:S(2)}, u32[]{:S(2)}) collective-permute-start(bf16[128,2048]{1,0:T(8,128)(2,1)} %collective-permute-done), channel_id=1, source_target_pairs={{0,4},{4,0},{8,12},{12,8},{1,5},{5,1},{9,13},{13,9},{2,6},{6,2},{1... | collective-permute-start | bytes 1572872 | tf_op jit(solution)/shard_map/ppermute | solution.py:442
  79.0 26.7 %collective-permute-start.15 = (bf16[2,512,768]{2,1,0:T(8,128)(2,1)S(1)}, bf16[2,512,768]{2,1,0:T(8,128)(2,1)S(1)}, u32[]{:S(2)}, u32[]{:S(2)}) collective-permute-start(bf16[2,512,768]{2,1,0:T(8,128)(2,1)S(1)} %copy-done.38), channel_id=1, source_target_pairs={{0,4},{4,0},{8,12},{12,8},{1,5},{5,1},{9,13},{13,9},{2,6},{6,2},{1... | collective-permute-start | bytes 4718600 | tf_op jit(solution)/shard_map/ppermute | solution.py:442
  80.1 25.6 %collective-permute-start.13 = (bf16[1040,512]{1,0:T(8,128)(2,1)S(1)}, bf16[1040,512]{1,0:T(8,128)(2,1)S(1)}, u32[]{:S(2)}, u32[]{:S(2)}) collective-permute-start(bf16[1040,512]{1,0:T(8,128)(2,1)S(1)} %fusion.10), channel_id=1, source_target_pairs={{0,8},{4,12},{8,0},{12,4},{1,9},{5,13},{9,1},{13,5},{2,10},{6,14},... | collective-permute-start | bytes 3194888 | tf_op jit(solution)/shard_map/ppermute | solution.py:442
  105.7 49.1 %collective-permute-start.20 = (bf16[128,2048]{1,0:T(8,128)(2,1)S(1)}, bf16[128,2048]{1,0:T(8,128)(2,1)S(1)}, u32[]{:S(2)}, u32[]{:S(2)}) collective-permute-start(bf16[128,2048]{1,0:T(8,128)(2,1)S(1)} %pad_maximum_fusion.29), channel_id=1, source_target_pairs={{0,3},{1,2},{2,1},{3,0},{4,7},{5,6},{6,5},{7,4},{8,11},{9,10},{10,... | collective-permute-start | bytes 1572872 | tf_op jit(solution)/shard_map/ppermute | solution.py:442
  106.8 47.9 %collective-permute-start.19 = (bf16[128,2048]{1,0:T(8,128)(2,1)S(1)}, bf16[128,2048]{1,0:T(8,128)(2,1)S(1)}, u32[]{:S(2)}, u32[]{:S(2)}) collective-permute-start(bf16[128,2048]{1,0:T(8,128)(2,1)S(1)} %pad_maximum_fusion.29), channel_id=1, source_target_pairs={{0,2},{1,3},{2,0},{3,1},{4,6},{5,7},{6,4},{7,5},{8,10},{9,11},{10,... | collective-permute-start | bytes 1572872 | tf_op jit(solution)/shard_map/ppermute | solution.py:442
  107.7 47.1 %collective-permute-start.18 = (bf16[128,2048]{1,0:T(8,128)(2,1)S(1)}, bf16[128,2048]{1,0:T(8,128)(2,1)S(1)}, u32[]{:S(2)}, u32[]{:S(2)}) collective-permute-start(bf16[128,2048]{1,0:T(8,128)(2,1)S(1)} %pad_maximum_fusion.29), channel_id=1, source_target_pairs={{0,1},{1,0},{2,3},{3,2},{4,5},{5,4},{6,7},{7,6},{8,9},{9,8},{10,11... | collective-permute-start | bytes 1572872 | tf_op jit(solution)/shard_map/ppermute | solution.py:442
  110.1 43.5 %collective-permute-start.17 = (bf16[1920,512]{1,0:T(8,128)(2,1)}, bf16[1920,512]{1,0:T(8,128)(2,1)}, u32[]{:S(2)}, u32[]{:S(2)}) collective-permute-start(bf16[1920,512]{1,0:T(8,128)(2,1)} %pad_maximum_fusion.8), channel_id=1, source_target_pairs={{0,8},{4,12},{8,0},{12,4},{1,9},{5,13},{9,1},{13,5},{2,10},{6,14},... | collective-permute-start | bytes 5898248 | tf_op jit(solution)/shard_map/ppermute | solution.py:442
  165.6 18.0 %collective-permute-start.27 = (bf16[256,1408]{1,0:T(8,128)(2,1)S(1)}, bf16[256,1408]{1,0:T(8,128)(2,1)S(1)}, u32[]{:S(2)}, u32[]{:S(2)}) collective-permute-start(bf16[256,1408]{1,0:T(8,128)(2,1)S(1)} %copy-done.59), channel_id=1, source_target_pairs={{0,8},{4,12},{8,0},{12,4},{1,9},{5,13},{9,1},{13,5},{2,10},{6,14},... | collective-permute-start | bytes 2162696 | tf_op jit(solution)/shard_map/ppermute | solution.py:442
  169.0 13.7 %collective-permute-start.26 = (bf16[128,2048]{1,0:T(8,128)(2,1)S(1)}, bf16[128,2048]{1,0:T(8,128)(2,1)S(1)}, u32[]{:S(2)}, u32[]{:S(2)}) collective-permute-start(bf16[128,2048]{1,0:T(8,128)(2,1)S(1)} %fusion.33), channel_id=1, source_target_pairs={{3,2},{0,1},{7,6},{4,5},{11,10},{8,9},{15,14},{12,13},{19,18},{16,... | collective-permute-start | bytes 1572872 | tf_op jit(solution)/shard_map/ppermute | solution.py:489
  171.3 12.3 %collective-permute-start.25 = (bf16[128,2048]{1,0:T(8,128)(2,1)S(1)}, bf16[128,2048]{1,0:T(8,128)(2,1)S(1)}, u32[]{:S(2)}, u32[]{:S(2)}) collective-permute-start(bf16[128,2048]{1,0:T(8,128)(2,1)S(1)} %fusion.33), channel_id=1, source_target_pairs={{1,2},{2,1},{5,6},{6,5},{9,10},{10,9},{13,14},{14,13},{17,18},{18,... | collective-permute-start | bytes 1572872 | tf_op jit(solution)/shard_map/ppermute | solution.py:489
  183.5 25.6 %collective-permute-start.28 = (bf16[128,2048]{1,0:T(8,128)(2,1)S(1)}, bf16[128,2048]{1,0:T(8,128)(2,1)S(1)}, u32[]{:S(2)}, u32[]{:S(2)}) collective-permute-start(bf16[128,2048]{1,0:T(8,128)(2,1)S(1)} %fusion.32), channel_id=1, source_target_pairs={{0,2},{1,3},{2,0},{3,1},{4,6},{5,7},{6,4},{7,5},{8,10},{9,11},{10,... | collective-permute-start | bytes 1572872 | tf_op jit(solution)/shard_map/ppermute | solution.py:442
  186.5 22.6 %collective-permute-start.29 = (bf16[128,2048]{1,0:T(8,128)(2,1)S(1)}, bf16[128,2048]{1,0:T(8,128)(2,1)S(1)}, u32[]{:S(2)}, u32[]{:S(2)}) collective-permute-start(bf16[128,2048]{1,0:T(8,128)(2,1)S(1)} %slice.1287), channel_id=1, source_target_pairs={{0,1},{1,0},{2,3},{3,2},{4,5},{5,4},{6,7},{7,6},{8,9},{9,8},{10,11... | collective-permute-start | bytes 1572872 | tf_op jit(solution)/shard_map/ppermute | solution.py:442
  186.8 23.0 %collective-permute-start.30 = (bf16[256,1408]{1,0:T(8,128)(2,1)S(1)}, bf16[256,1408]{1,0:T(8,128)(2,1)S(1)}, u32[]{:S(2)}, u32[]{:S(2)}) collective-permute-start(bf16[256,1408]{1,0:T(8,128)(2,1)S(1)} %copy-done.58), channel_id=1, source_target_pairs={{0,8},{4,12},{8,0},{12,4},{1,9},{5,13},{9,1},{13,5},{2,10},{6,14},... | collective-permute-start | bytes 2162696 | tf_op jit(solution)/shard_map/ppermute | solution.py:442
  187.4 51.0 %collective-permute-start.33 = (bf16[512,1408]{1,0:T(8,128)(2,1)S(1)}, bf16[512,1408]{1,0:T(8,128)(2,1)S(1)}, u32[]{:S(2)}, u32[]{:S(2)}) collective-permute-start(bf16[512,1408]{1,0:T(8,128)(2,1)S(1)} %copy-done.39), channel_id=1, source_target_pairs={{0,8},{4,12},{8,0},{12,4},{1,9},{5,13},{9,1},{13,5},{2,10},{6,14},... | collective-permute-start | bytes 4325384 | tf_op jit(solution)/shard_map/ppermute | solution.py:442
  209.9 26.7 %collective-permute-start.36 = (bf16[128,2048]{1,0:T(8,128)(2,1)S(1)}, bf16[128,2048]{1,0:T(8,128)(2,1)S(1)}, u32[]{:S(2)}, u32[]{:S(2)}) collective-permute-start(bf16[128,2048]{1,0:T(8,128)(2,1)S(1)} %multiply_convert_fusion.3), channel_id=1, source_target_pairs={{0,4},{4,0},{8,12},{12,8},{1,5},{5,1},{9,13},{13,9},{2,6},{6,2},{1... | collective-permute-start | bytes 1572872 | tf_op jit(solution)/shard_map/ppermute | solution.py:442
  209.9 27.7 %collective-permute-start.32 = (bf16[128,2048]{1,0:T(8,128)(2,1)S(1)}, bf16[128,2048]{1,0:T(8,128)(2,1)S(1)}, u32[]{:S(2)}, u32[]{:S(2)}) collective-permute-start(bf16[128,2048]{1,0:T(8,128)(2,1)S(1)} %multiply_convert_fusion.3), channel_id=1, source_target_pairs={{0,2},{1,3},{2,0},{3,1},{4,6},{5,7},{6,4},{7,5},{8,10},{9,11},{10,... | collective-permute-start | bytes 1572872 | tf_op jit(solution)/shard_map/ppermute | solution.py:442
  212.7 23.9 %collective-permute-start.31 = (bf16[128,2048]{1,0:T(8,128)(2,1)S(1)}, bf16[128,2048]{1,0:T(8,128)(2,1)S(1)}, u32[]{:S(2)}, u32[]{:S(2)}) collective-permute-start(bf16[128,2048]{1,0:T(8,128)(2,1)S(1)} %multiply_convert_fusion.3), channel_id=1, source_target_pairs={{0,1},{1,0},{2,3},{3,2},{4,5},{5,4},{6,7},{7,6},{8,9},{9,8},{10,11... | collective-permute-start | bytes 1572872 | tf_op jit(solution)/shard_map/ppermute | solution.py:442
  214.8 22.4 %collective-permute-start.42 = (bf16[512,768]{1,0:T(8,128)(2,1)S(1)}, bf16[512,768]{1,0:T(8,128)(2,1)S(1)}, u32[]{:S(2)}, u32[]{:S(2)}) collective-permute-start(bf16[512,768]{1,0:T(8,128)(2,1)S(1)} %get-tuple-element.299), channel_id=1, source_target_pairs={{0,4},{4,0},{8,12},{12,8},{1,5},{5,1},{9,13},{13,9},{2,6},{6,2},{1... | collective-permute-start | bytes 2359304 | tf_op jit(solution)/shard_map/ppermute | solution.py:442
  236.6 19.5 %collective-permute-start.41 = (bf16[768,512]{1,0:T(8,128)(2,1)S(1)}, bf16[768,512]{1,0:T(8,128)(2,1)S(1)}, u32[]{:S(2)}, u32[]{:S(2)}) collective-permute-start(bf16[768,512]{1,0:T(8,128)(2,1)S(1)} %get-tuple-element.305), channel_id=1, source_target_pairs={{0,4},{4,0},{8,12},{12,8},{1,5},{5,1},{9,13},{13,9},{2,6},{6,2},{1... | collective-permute-start | bytes 2359304 | tf_op jit(solution)/shard_map/ppermute | solution.py:442
  236.6 19.2 %collective-permute-start.40 = (bf16[384,2048]{1,0:T(8,128)(2,1)S(1)}, bf16[384,2048]{1,0:T(8,128)(2,1)S(1)}, u32[]{:S(2)}, u32[]{:S(2)}) collective-permute-start(bf16[384,2048]{1,0:T(8,128)(2,1)S(1)} %pad_maximum_fusion.9), channel_id=1, source_target_pairs={{0,4},{4,0},{8,12},{12,8},{1,5},{5,1},{9,13},{13,9},{2,6},{6,2},{1... | collective-permute-start | bytes 4718600 | tf_op jit(solution)/shard_map/ppermute | solution.py:442
  238.4 16.9 %collective-permute-start.35 = (bf16[128,2048]{1,0:T(8,128)(2,1)S(1)}, bf16[128,2048]{1,0:T(8,128)(2,1)S(1)}, u32[]{:S(2)}, u32[]{:S(2)}) collective-permute-start(bf16[128,2048]{1,0:T(8,128)(2,1)S(1)} %collective-permute-done.32), channel_id=1, source_target_pairs={{2,3},{1,0},{6,7},{5,4},{10,11},{9,8},{14,15},{13,12},{18,19},{17,... | collective-permute-start | bytes 1572872 | tf_op jit(solution)/shard_map/ppermute | solution.py:489
  241.9 13.8 %collective-permute-start.38 = (bf16[128,2048]{1,0:T(8,128)(2,1)S(1)}, bf16[128,2048]{1,0:T(8,128)(2,1)S(1)}, u32[]{:S(2)}, u32[]{:S(2)}) collective-permute-start(bf16[128,2048]{1,0:T(8,128)(2,1)S(1)} %collective-permute-done.32), channel_id=1, source_target_pairs={{0,4},{4,0},{8,12},{12,8},{1,5},{5,1},{9,13},{13,9},{2,6},{6,2},{1... | collective-permute-start | bytes 1572872 | tf_op jit(solution)/shard_map/ppermute | solution.py:442
  242.1 20.2 %collective-permute-start.43 = (bf16[512,768]{1,0:T(8,128)(2,1)S(1)}, bf16[512,768]{1,0:T(8,128)(2,1)S(1)}, u32[]{:S(2)}, u32[]{:S(2)}) collective-permute-start(bf16[512,768]{1,0:T(8,128)(2,1)S(1)} %get-tuple-element.301), channel_id=1, source_target_pairs={{0,4},{4,0},{8,12},{12,8},{1,5},{5,1},{9,13},{13,9},{2,6},{6,2},{1... | collective-permute-start | bytes 2359304 | tf_op jit(solution)/shard_map/ppermute | solution.py:442
  276.0 13.8 %collective-permute-start.44 = (bf16[384,2048]{1,0:T(8,128)(2,1)S(1)}, bf16[384,2048]{1,0:T(8,128)(2,1)S(1)}, u32[]{:S(2)}, u32[]{:S(2)}) collective-permute-start(bf16[384,2048]{1,0:T(8,128)(2,1)S(1)} %slice.1003), channel_id=1, source_target_pairs={{0,4},{4,0},{8,12},{12,8},{1,5},{5,1},{9,13},{13,9},{2,6},{6,2},{1... | collective-permute-start | bytes 4718600 | tf_op jit(solution)/shard_map/ppermute | solution.py:442
  284.8 16.6 %collective-permute-start.47 = (bf16[128,2048]{1,0:T(8,128)(2,1)S(1)}, bf16[128,2048]{1,0:T(8,128)(2,1)S(1)}, u32[]{:S(2)}, u32[]{:S(2)}) collective-permute-start(bf16[128,2048]{1,0:T(8,128)(2,1)S(1)} %fusion.30), channel_id=1, source_target_pairs={{1,2},{2,1},{5,6},{6,5},{9,10},{10,9},{13,14},{14,13},{17,18},{18,... | collective-permute-start | bytes 1572872 | tf_op jit(solution)/shard_map/ppermute | solution.py:489
  285.5 15.7 %collective-permute-start.46 = (bf16[128,2048]{1,0:T(8,128)(2,1)S(1)}, bf16[128,2048]{1,0:T(8,128)(2,1)S(1)}, u32[]{:S(2)}, u32[]{:S(2)}) collective-permute-start(bf16[128,2048]{1,0:T(8,128)(2,1)S(1)} %fusion.30), channel_id=1, source_target_pairs={{3,2},{0,1},{7,6},{4,5},{11,10},{8,9},{15,14},{12,13},{19,18},{16,... | collective-permute-start | bytes 1572872 | tf_op jit(solution)/shard_map/ppermute | solution.py:489
  301.3 25.4 %collective-permute-start.49 = (bf16[128,2048]{1,0:T(8,128)(2,1)S(1)}, bf16[128,2048]{1,0:T(8,128)(2,1)S(1)}, u32[]{:S(2)}, u32[]{:S(2)}) collective-permute-start(bf16[128,2048]{1,0:T(8,128)(2,1)S(1)} %get-tuple-element.137), channel_id=1, source_target_pairs={{0,2},{1,3},{2,0},{3,1},{4,6},{5,7},{6,4},{7,5},{8,10},{9,11},{10,... | collective-permute-start | bytes 1572872 | tf_op jit(solution)/shard_map/ppermute | solution.py:442
  304.5 22.2 %collective-permute-start.50 = (bf16[128,2048]{1,0:T(8,128)(2,1)S(1)}, bf16[128,2048]{1,0:T(8,128)(2,1)S(1)}, u32[]{:S(2)}, u32[]{:S(2)}) collective-permute-start(bf16[128,2048]{1,0:T(8,128)(2,1)S(1)} %slice.1286), channel_id=1, source_target_pairs={{0,1},{1,0},{2,3},{3,2},{4,5},{5,4},{6,7},{7,6},{8,9},{9,8},{10,11... | collective-permute-start | bytes 1572872 | tf_op jit(solution)/shard_map/ppermute | solution.py:442
  313.1 14.2 %collective-permute-start.51 = (bf16[1024,768]{1,0:T(8,128)(2,1)S(1)}, bf16[1024,768]{1,0:T(8,128)(2,1)S(1)}, u32[]{:S(2)}, u32[]{:S(2)}) collective-permute-start(bf16[1024,768]{1,0:T(8,128)(2,1)S(1)} %pad_maximum_fusion.13), channel_id=1, source_target_pairs={{0,4},{4,0},{8,12},{12,8},{1,5},{5,1},{9,13},{13,9},{2,6},{6,2},{1... | collective-permute-start | bytes 4718600 | tf_op jit(solution)/shard_map/ppermute | solution.py:442
  330.4 29.9 %collective-permute-start.57 = (bf16[128,2048]{1,0:T(8,128)(2,1)S(1)}, bf16[128,2048]{1,0:T(8,128)(2,1)S(1)}, u32[]{:S(2)}, u32[]{:S(2)}) collective-permute-start(bf16[128,2048]{1,0:T(8,128)(2,1)S(1)} %get-tuple-element.145), channel_id=1, source_target_pairs={{0,4},{4,0},{8,12},{12,8},{1,5},{5,1},{9,13},{13,9},{2,6},{6,2},{1... | collective-permute-start | bytes 1572872 | tf_op jit(solution)/shard_map/ppermute | solution.py:442
  330.4 25.0 %collective-permute-start.54 = (bf16[128,2048]{1,0:T(8,128)(2,1)S(1)}, bf16[128,2048]{1,0:T(8,128)(2,1)S(1)}, u32[]{:S(2)}, u32[]{:S(2)}) collective-permute-start(bf16[128,2048]{1,0:T(8,128)(2,1)S(1)} %get-tuple-element.145), channel_id=1, source_target_pairs={{0,1},{1,0},{2,3},{3,2},{4,5},{5,4},{6,7},{7,6},{8,9},{9,8},{10,11... | collective-permute-start | bytes 1572872 | tf_op jit(solution)/shard_map/ppermute | solution.py:442
  332.2 26.2 %collective-permute-start.52 = (bf16[128,2048]{1,0:T(8,128)(2,1)S(1)}, bf16[128,2048]{1,0:T(8,128)(2,1)S(1)}, u32[]{:S(2)}, u32[]{:S(2)}) collective-permute-start(bf16[128,2048]{1,0:T(8,128)(2,1)S(1)} %get-tuple-element.145), channel_id=1, source_target_pairs={{0,2},{1,3},{2,0},{3,1},{4,6},{5,7},{6,4},{7,5},{8,10},{9,11},{10,... | collective-permute-start | bytes 1572872 | tf_op jit(solution)/shard_map/ppermute | solution.py:442
  333.0 39.5 %collective-permute-start.61 = (bf16[1408,512]{1,0:T(8,128)(2,1)S(1)}, bf16[1408,512]{1,0:T(8,128)(2,1)S(1)}, u32[]{:S(2)}, u32[]{:S(2)}) collective-permute-start(bf16[1408,512]{1,0:T(8,128)(2,1)S(1)} %fusion.5), channel_id=1, source_target_pairs={{0,8},{4,12},{8,0},{12,4},{1,9},{5,13},{9,1},{13,5},{2,10},{6,14},... | collective-permute-start | bytes 4325384 | tf_op jit(solution)/shard_map/ppermute | solution.py:442
  358.4 13.1 %collective-permute-start.56 = (bf16[128,2048]{1,0:T(8,128)(2,1)S(1)}, bf16[128,2048]{1,0:T(8,128)(2,1)S(1)}, u32[]{:S(2)}, u32[]{:S(2)}) collective-permute-start(bf16[128,2048]{1,0:T(8,128)(2,1)S(1)} %collective-permute-done.52), channel_id=1, source_target_pairs={{2,3},{1,0},{6,7},{5,4},{10,11},{9,8},{14,15},{13,12},{18,19},{17,... | collective-permute-start | bytes 1572872 | tf_op jit(solution)/shard_map/ppermute | solution.py:489
  360.3 16.2 %collective-permute-start.68 = (bf16[1024,768]{1,0:T(8,128)(2,1)S(1)}, bf16[1024,768]{1,0:T(8,128)(2,1)S(1)}, u32[]{:S(2)}, u32[]{:S(2)}) collective-permute-start(bf16[1024,768]{1,0:T(8,128)(2,1)S(1)} %pad_maximum_fusion.15), channel_id=1, source_target_pairs={{0,4},{4,0},{8,12},{12,8},{1,5},{5,1},{9,13},{13,9},{2,6},{6,2},{1... | collective-permute-start | bytes 4718600 | tf_op jit(solution)/shard_map/ppermute | solution.py:442
  362.3 42.5 %collective-permute-start.65 = (bf16[512,1408]{1,0:T(8,128)(2,1)S(1)}, bf16[512,1408]{1,0:T(8,128)(2,1)S(1)}, u32[]{:S(2)}, u32[]{:S(2)}) collective-permute-start(bf16[512,1408]{1,0:T(8,128)(2,1)S(1)} %fusion.6), channel_id=1, source_target_pairs={{0,8},{4,12},{8,0},{12,4},{1,9},{5,13},{9,1},{13,5},{2,10},{6,14},... | collective-permute-start | bytes 4325384 | tf_op jit(solution)/shard_map/ppermute | solution.py:442
  373.1 33.6 %collective-permute-start.66 = (bf16[1408,512]{1,0:T(8,128)(2,1)S(1)}, bf16[1408,512]{1,0:T(8,128)(2,1)S(1)}, u32[]{:S(2)}, u32[]{:S(2)}) collective-permute-start(bf16[1408,512]{1,0:T(8,128)(2,1)S(1)} %add_convert_fusion.4), channel_id=1, source_target_pairs={{0,16},{16,0},{1,17},{17,1},{2,18},{18,2},{3,19},{19,3},{4,20},{20... | collective-permute-start | bytes 4325384 | tf_op jit(solution)/shard_map/ppermute | solution.py:442
  388.4 14.5 %collective-permute-start.67 = (bf16[1024,128]{1,0:T(8,128)(2,1)S(1)}, bf16[1024,128]{1,0:T(8,128)(2,1)S(1)}, u32[]{:S(2)}, u32[]{:S(2)}) collective-permute-start(bf16[1024,128]{1,0:T(8,128)(2,1)S(1)} %get-tuple-element.326), channel_id=1, source_target_pairs={{0,8},{4,12},{8,0},{12,4},{1,9},{5,13},{9,1},{13,5},{2,10},{6,14},... | collective-permute-start | bytes 786440 | tf_op jit(solution)/shard_map/ppermute | solution.py:442
  389.0 47.5 %collective-permute-start.62 = (bf16[128,2048]{1,0:T(8,128)(2,1)}, bf16[128,2048]{1,0:T(8,128)(2,1)}, u32[]{:S(2)}, u32[]{:S(2)}) collective-permute-start(bf16[128,2048]{1,0:T(8,128)(2,1)} %get-tuple-element.147), channel_id=1, source_target_pairs={{0,1},{1,0},{2,3},{3,2},{4,5},{5,4},{6,7},{7,6},{8,9},{9,8},{10,11... | collective-permute-start | bytes 1572872 | tf_op jit(solution)/shard_map/ppermute | solution.py:442
  389.3 47.2 %collective-permute-start.63 = (bf16[128,2048]{1,0:T(8,128)(2,1)}, bf16[128,2048]{1,0:T(8,128)(2,1)}, u32[]{:S(2)}, u32[]{:S(2)}) collective-permute-start(bf16[128,2048]{1,0:T(8,128)(2,1)} %get-tuple-element.148), channel_id=1, source_target_pairs={{0,2},{1,3},{2,0},{3,1},{4,6},{5,7},{6,4},{7,5},{8,10},{9,11},{10,... | collective-permute-start | bytes 1572872 | tf_op jit(solution)/shard_map/ppermute | solution.py:442
  403.0 33.5 %collective-permute-start.64 = (bf16[128,2048]{1,0:T(8,128)(2,1)}, bf16[128,2048]{1,0:T(8,128)(2,1)}, u32[]{:S(2)}, u32[]{:S(2)}) collective-permute-start(bf16[128,2048]{1,0:T(8,128)(2,1)} %get-tuple-element.149), channel_id=1, source_target_pairs={{0,3},{1,2},{2,1},{3,0},{4,7},{5,6},{6,5},{7,4},{8,11},{9,10},{10,... | collective-permute-start | bytes 1572872 | tf_op jit(solution)/shard_map/ppermute | solution.py:442
  404.8 34.6 %collective-permute-start.69 = (bf16[512,1408]{1,0:T(8,128)(2,1)}, bf16[512,1408]{1,0:T(8,128)(2,1)}, u32[]{:S(2)}, u32[]{:S(2)}) collective-permute-start(bf16[512,1408]{1,0:T(8,128)(2,1)} %fusion.7), channel_id=1, source_target_pairs={{0,8},{4,12},{8,0},{12,4},{1,9},{5,13},{9,1},{13,5},{2,10},{6,14},... | collective-permute-start | bytes 4325384 | tf_op jit(solution)/shard_map/ppermute | solution.py:442
  408.3 33.1 %collective-permute-start.70 = (bf16[512,1408]{1,0:T(8,128)(2,1)}, bf16[512,1408]{1,0:T(8,128)(2,1)}, u32[]{:S(2)}, u32[]{:S(2)}) collective-permute-start(bf16[512,1408]{1,0:T(8,128)(2,1)} %add_convert_fusion.3), channel_id=1, source_target_pairs={{0,16},{16,0},{1,17},{17,1},{2,18},{18,2},{3,19},{19,3},{4,20},{20... | collective-permute-start | bytes 4325384 | tf_op jit(solution)/shard_map/ppermute | solution.py:442
  442.6 26.4 %collective-permute-start.71 = (bf16[1040,512]{1,0:T(8,128)(2,1)S(1)}, bf16[1040,512]{1,0:T(8,128)(2,1)S(1)}, u32[]{:S(2)}, u32[]{:S(2)}) collective-permute-start(bf16[1040,512]{1,0:T(8,128)(2,1)S(1)} %fusion.11), channel_id=1, source_target_pairs={{0,8},{4,12},{8,0},{12,4},{1,9},{5,13},{9,1},{13,5},{2,10},{6,14},... | collective-permute-start | bytes 3194888 | tf_op jit(solution)/shard_map/ppermute | solution.py:442
  445.5 68.3 %collective-permute-start.78 = (bf16[512,1408]{1,0:T(8,128)(2,1)S(1)}, bf16[512,1408]{1,0:T(8,128)(2,1)S(1)}, u32[]{:S(2)}, u32[]{:S(2)}) collective-permute-start(bf16[512,1408]{1,0:T(8,128)(2,1)S(1)} %add_convert_fusion.2), channel_id=1, source_target_pairs={{0,16},{16,0},{1,17},{17,1},{2,18},{18,2},{3,19},{19,3},{4,20},{20... | collective-permute-start | bytes 4325384 | tf_op jit(solution)/shard_map/ppermute | solution.py:442
  447.0 33.2 %collective-permute-start.79 = (bf16[256,1024]{1,0:T(8,128)(2,1)S(1)}, bf16[256,1024]{1,0:T(8,128)(2,1)S(1)}, u32[]{:S(2)}, u32[]{:S(2)}) collective-permute-start(bf16[256,1024]{1,0:T(8,128)(2,1)S(1)} %slice.1284), channel_id=1, source_target_pairs={{0,8},{4,12},{8,0},{12,4},{1,9},{5,13},{9,1},{13,5},{2,10},{6,14},... | collective-permute-start | bytes 1572872 | tf_op jit(solution)/shard_map/ppermute | solution.py:442
  450.9 53.3 %collective-permute-start.73 = (bf16[1024,512]{0,1:T(8,128)(2,1)S(1)}, bf16[1024,512]{0,1:T(8,128)(2,1)S(1)}, u32[]{:S(2)}, u32[]{:S(2)}) collective-permute-start(bf16[1024,512]{0,1:T(8,128)(2,1)S(1)} %slice.1283), channel_id=1, source_target_pairs={{0,8},{4,12},{8,0},{12,4},{1,9},{5,13},{9,1},{13,5},{2,10},{6,14},... | collective-permute-start | bytes 3145736 | tf_op jit(solution)/shard_map/ppermute | solution.py:442
  483.9 20.4 %collective-permute-start.76 = (bf16[128,2048]{1,0:T(8,128)(2,1)S(1)}, bf16[128,2048]{1,0:T(8,128)(2,1)S(1)}, u32[]{:S(2)}, u32[]{:S(2)}) collective-permute-start(bf16[128,2048]{1,0:T(8,128)(2,1)S(1)} %fusion.23), channel_id=1, source_target_pairs={{1,2},{2,1},{5,6},{6,5},{9,10},{10,9},{13,14},{14,13},{17,18},{18,... | collective-permute-start | bytes 1572872 | tf_op jit(solution)/shard_map/ppermute | solution.py:489
  484.6 17.4 %collective-permute-start.75 = (bf16[128,2048]{1,0:T(8,128)(2,1)S(1)}, bf16[128,2048]{1,0:T(8,128)(2,1)S(1)}, u32[]{:S(2)}, u32[]{:S(2)}) collective-permute-start(bf16[128,2048]{1,0:T(8,128)(2,1)S(1)} %fusion.23), channel_id=1, source_target_pairs={{3,2},{0,1},{7,6},{4,5},{11,10},{8,9},{15,14},{12,13},{19,18},{16,... | collective-permute-start | bytes 1572872 | tf_op jit(solution)/shard_map/ppermute | solution.py:489
  504.8 14.4 %collective-permute-start.81 = (bf16[512,512]{1,0:T(8,128)(2,1)S(1)}, bf16[512,512]{1,0:T(8,128)(2,1)S(1)}, u32[]{:S(2)}, u32[]{:S(2)}) collective-permute-start(bf16[512,512]{1,0:T(8,128)(2,1)S(1)} %pad_maximum_fusion.31), channel_id=1, source_target_pairs={{0,16},{16,0},{1,17},{17,1},{2,18},{18,2},{3,19},{19,3},{4,20},{20... | collective-permute-start | bytes 1572872 | tf_op jit(solution)/shard_map/ppermute | solution.py:442
  508.4 31.0 %collective-permute-start.82 = (bf16[128,2048]{1,0:T(8,128)(2,1)}, bf16[128,2048]{1,0:T(8,128)(2,1)}, u32[]{:S(2)}, u32[]{:S(2)}) collective-permute-start(bf16[128,2048]{1,0:T(8,128)(2,1)} %get-tuple-element.171), channel_id=1, source_target_pairs={{0,2},{1,3},{2,0},{3,1},{4,6},{5,7},{6,4},{7,5},{8,10},{9,11},{10,... | collective-permute-start | bytes 1572872 | tf_op jit(solution)/shard_map/ppermute | solution.py:442
  511.1 28.3 %collective-permute-start.83 = (bf16[128,2048]{1,0:T(8,128)(2,1)}, bf16[128,2048]{1,0:T(8,128)(2,1)}, u32[]{:S(2)}, u32[]{:S(2)}) collective-permute-start(bf16[128,2048]{1,0:T(8,128)(2,1)} %slice.1285), channel_id=1, source_target_pairs={{0,1},{1,0},{2,3},{3,2},{4,5},{5,4},{6,7},{7,6},{8,9},{9,8},{10,11... | collective-permute-start | bytes 1572872 | tf_op jit(solution)/shard_map/ppermute | solution.py:442
  511.1 30.1 %collective-permute-start.85 = (bf16[1024,512]{0,1:T(8,128)(2,1)}, bf16[1024,512]{0,1:T(8,128)(2,1)}, u32[]{:S(2)}, u32[]{:S(2)}) collective-permute-start(bf16[1024,512]{0,1:T(8,128)(2,1)} %slice.1282), channel_id=1, source_target_pairs={{0,8},{4,12},{8,0},{12,4},{1,9},{5,13},{9,1},{13,5},{2,10},{6,14},... | collective-permute-start | bytes 3145736 | tf_op jit(solution)/shard_map/ppermute | solution.py:442
  519.2 27.9 %collective-permute-start.84 = (bf16[512,1024]{0,1:T(8,128)(2,1)}, bf16[512,1024]{0,1:T(8,128)(2,1)}, u32[]{:S(2)}, u32[]{:S(2)}) collective-permute-start(bf16[512,1024]{0,1:T(8,128)(2,1)} %pad_maximum_fusion.21), channel_id=1, source_target_pairs={{0,16},{16,0},{1,17},{17,1},{2,18},{18,2},{3,19},{19,3},{4,20},{20... | collective-permute-start | bytes 3145736 | tf_op jit(solution)/shard_map/ppermute | solution.py:442
  549.2 29.9 %collective-permute-start.94 = (bf16[512,1024]{0,1:T(8,128)(2,1)}, bf16[512,1024]{0,1:T(8,128)(2,1)}, u32[]{:S(2)}, u32[]{:S(2)}) collective-permute-start(bf16[512,1024]{0,1:T(8,128)(2,1)} %pad_maximum_fusion.24), channel_id=1, source_target_pairs={{0,16},{16,0},{1,17},{17,1},{2,18},{18,2},{3,19},{19,3},{4,20},{20... | collective-permute-start | bytes 3145736 | tf_op jit(solution)/shard_map/ppermute | solution.py:442
  558.3 17.3 %collective-permute-start.97 = (f32[28,128]{1,0:T(8,128)S(1)}, f32[28,128]{1,0:T(8,128)S(1)}, u32[]{:S(2)}, u32[]{:S(2)}) collective-permute-start(f32[28,128]{1,0:T(8,128)S(1)} %constant_dynamic-update-slice_fusion.20), channel_id=1, source_target_pairs={{0,16},{16,0},{1,17},{17,1},{2,18},{18,2},{3,19},{19,3},{4,20},{20... | collective-permute-start | bytes 43016 | tf_op jit(solution)/shard_map/ppermute | solution.py:442
  561.5 15.3 %collective-permute-start.93 = (f32[34,128]{1,0:T(8,128)S(1)}, f32[34,128]{1,0:T(8,128)S(1)}, u32[]{:S(2)}, u32[]{:S(2)}) collective-permute-start(f32[34,128]{1,0:T(8,128)S(1)} %add_add_fusion), channel_id=1, source_target_pairs={{0,16},{16,0},{1,17},{17,1},{2,18},{18,2},{3,19},{19,3},{4,20},{20... | collective-permute-start | bytes 52232 | tf_op jit(solution)/shard_map/ppermute | solution.py:442
  (136 other events, 1436.4 us)
